TPU v7x, 256 devices: a whole 4x4x8 slice. The times are simulated.
256 devices in a mesh: row: 8 (over y, core), col: 32 (over z, x).
Axes of the slice: x: 4, y: 4, z: 8, core: 2. Of those that a mesh axis runs over, the one named last changes fastest.
Arguments:
- fields: float32 [4096, 5, 4096], P(('row', 'col')), as said below
- counts: int32 [8, 32], P('row', 'col'), may hold values from 1 to 16, 256 in all within a row
Outputs:
- fields_out: float32 [4096, 5, 4096], P(('row', 'col'))
Inputs may be any that keep to these rules, and one draw needn't show every extreme that they name: `fields`: in every slot, also those that hold no patch, density lies in 0.5 to 3, pressure 0.4 (E - |m|^2 / (2 rho)) in 0.5 to 2 and each velocity component in -0.5 to 0.5. Each index of row holds 256 patches in all: the entries of counts[r] sum to 256, and some device of each index of row holds 16.
All inputs are finite; a program needn't handle non-finite values.
Results may differ from a plain program's by a relative error of at most 0.0003.
Values sent between devices are 32-bit elements; how exact they have to be, the bound alone decides.
No kernel may reach another device: no remote copies, remote signals or barrier semaphores. Data moves between devices by JAX's collectives and lax.ppermute only.
A program may use at most 128 MiB of HBM per device.

v0:
```python
import math

import jax
import jax.numpy as jnp
from jax import lax
from jax.sharding import PartitionSpec as P

PE = 16
GX = 256
GY = 256
GZ = 128


gamma_gas = 1.4
speed_bound = 4.0
time_step = 0.03
four_pi_g = 10.0


def padded(block, sides, width):
    for axis, dim in sides:
        count = lax.axis_size(axis)
        forward = [(i, i + 1) for i in range(count - 1)]
        forward.append((count - 1, 0))
        backward = [(target, source) for source, target in forward]
        low = lax.ppermute(
            lax.slice_in_dim(block, block.shape[dim] - width, None, axis=dim), axis, forward
        )
        high = lax.ppermute(lax.slice_in_dim(block, 0, width, axis=dim), axis, backward)
        block = jnp.concatenate([low, block, high], axis=dim)
    return block


def minmod_slope(lower_gap, upper_gap):
    return (
        0.5
        * (jnp.sign(lower_gap) + jnp.sign(upper_gap))
        * jnp.minimum(jnp.abs(lower_gap), jnp.abs(upper_gap))
    )


def normal_flux(states, direction):
    density = states[0]
    momenta = states[1:4]
    energy = states[4]
    velocity = momenta[direction] / density
    kinetic = (
        0.5
        * (momenta[0] * momenta[0] + momenta[1] * momenta[1] + momenta[2] * momenta[2])
        / density
    )
    pressure = (gamma_gas - 1.0) * (energy - kinetic)
    pieces = [momenta[direction]]
    for component in range(3):
        flux_term = momenta[component] * velocity
        if component == direction:
            flux_term = flux_term + pressure
        pieces.append(flux_term)
    pieces.append((energy + pressure) * velocity)
    return jnp.stack(pieces)


def cut_range(array, dim_index, first_cell, count_cells):
    return lax.slice_in_dim(array, first_cell, first_cell + count_cells, axis=dim_index)


def face_rates(states):
    total_rate = None
    for direction in range(3):
        dim_index = direction + 1
        trimmed = states
        for other_dim in (1, 2):
            if other_dim != dim_index:
                trimmed = cut_range(trimmed, other_dim, 2, trimmed.shape[other_dim] - 4)
        if direction < 2:
            length = trimmed.shape[dim_index]
            lower_cell = cut_range(trimmed, dim_index, 0, length - 3)
            centre = cut_range(trimmed, dim_index, 1, length - 3)
            upper_cell = cut_range(trimmed, dim_index, 2, length - 3)
            far_cell = cut_range(trimmed, dim_index, 3, length - 3)
        else:
            lower_cell = jnp.roll(trimmed, 1, 3)
            centre = trimmed
            upper_cell = jnp.roll(trimmed, -1, 3)
            far_cell = jnp.roll(trimmed, -2, 3)
        left_state = centre + 0.5 * minmod_slope(centre - lower_cell, upper_cell - centre)
        right_state = upper_cell - 0.5 * minmod_slope(upper_cell - centre, far_cell - upper_cell)
        face_flux = 0.5 * (
            normal_flux(left_state, direction) + normal_flux(right_state, direction)
        ) - 0.5 * speed_bound * (right_state - left_state)
        if direction < 2:
            change = cut_range(face_flux, dim_index, 1, length - 4) - cut_range(
                face_flux, dim_index, 0, length - 4
            )
        else:
            change = face_flux - jnp.roll(face_flux, 1, 3)
        total_rate = change if total_rate is None else total_rate + change
    return -total_rate


def crop_plane(array, margin):
    return array[:, margin : array.shape[1] - margin, margin : array.shape[2] - margin, :]


def advance(extended):
    first = crop_plane(extended, 2) + time_step * face_rates(extended)
    second = crop_plane(first, 2) + time_step * face_rates(first)
    return 0.5 * crop_plane(extended, 4) + 0.5 * second


def lap_eigen(wave, length):
    return 2.0 * jnp.cos(2.0 * math.pi / length * wave) - 2.0


def apply_kick(stepped, gradient):
    density = stepped[0]
    momenta = stepped[1:4]
    new_momenta = momenta - time_step * density[None] * gradient
    work_done = momenta[0] * gradient[0] + momenta[1] * gradient[1] + momenta[2] * gradient[2]
    new_energy = stepped[4] - time_step * work_done
    return jnp.concatenate([stepped[0:1], new_momenta, new_energy[None]], axis=0)


def dft_tables(length):
    indices = jnp.arange(length, dtype=jnp.int32)
    wrapped = indices[:, None] * indices[None, :] % length
    angles = 2.0 * math.pi / length * wrapped.astype(jnp.float32)
    return (jnp.cos(angles), jnp.sin(angles))


def right_mul(values, matrix):
    return jnp.matmul(values, matrix, precision=lax.Precision.HIGHEST)


def left_mul(matrix, values):
    return jnp.einsum("yk,...km->...ym", matrix, values, precision=lax.Precision.HIGHEST)


def on_device(fields, counts):
    rows_count = lax.axis_size("row")
    cols_count = lax.axis_size("col")
    my_row = lax.axis_index("row")
    my_column = lax.axis_index("col")
    capacity = fields.shape[0]
    block_x = GX // rows_count
    block_y = GY // cols_count
    lat_x = block_x // PE
    lat_y = GY // PE
    lat_z = GZ // PE
    brick_y = min(PE, block_y)
    per_patch = PE // brick_y
    per_pencil_y = block_y // brick_y
    repeat_y = max(1, block_y // PE)
    per_peer = (capacity + lat_y - 1) // lat_y * repeat_y
    brick_cells = 5 * PE * brick_y * PE
    buffer_rows = cols_count * per_peer
    row_counts = lax.all_gather(counts, "col", axis=1, tiled=True).reshape(cols_count)
    starts = jnp.cumsum(row_counts) - row_counts
    column_ids = jnp.arange(cols_count, dtype=jnp.int32)
    own_start = jnp.sum(jnp.where(column_ids == my_column, starts, 0))
    own_count = counts[0, 0]
    slot_ids = jnp.arange(capacity, dtype=jnp.int32)
    brick_ids = jnp.arange(per_patch, dtype=jnp.int32)
    y_patch = (own_start + slot_ids) % lat_y
    global_y = y_patch[:, None] * PE + brick_ids[None, :] * brick_y
    slot_inner = (slot_ids // lat_y * repeat_y + y_patch % repeat_y)[:, None]
    dest_index = (global_y // block_y * per_peer + slot_inner).reshape(-1)
    live_slots = jnp.broadcast_to((slot_ids < own_count)[:, None], (capacity, per_patch)).reshape(
        -1
    )
    buffer_ids = jnp.arange(buffer_rows, dtype=jnp.int32)
    send_select = ((buffer_ids[:, None] == dest_index[None, :]) & live_slots[None, :]).astype(
        jnp.float32
    )
    grid_xl = jnp.arange(lat_x, dtype=jnp.int32)[:, None, None]
    grid_w = jnp.arange(per_pencil_y, dtype=jnp.int32)[None, :, None]
    grid_zl = jnp.arange(lat_z, dtype=jnp.int32)[None, None, :]
    pencil_y = (my_column * block_y + grid_w * brick_y) // PE
    curve_pos = (grid_xl * lat_z + grid_zl) * lat_y + pencil_y
    curve_pos = curve_pos.reshape(-1)
    y_flat = jnp.broadcast_to(pencil_y, (lat_x, per_pencil_y, lat_z)).reshape(-1)
    owner = jnp.sum((starts[None, :] <= curve_pos[:, None]).astype(jnp.int32), axis=1) - 1
    owner_start = jnp.sum(
        jnp.where(column_ids[None, :] == owner[:, None], starts[None, :], 0), axis=1
    )
    source_index = (
        owner * per_peer + (curve_pos - owner_start) // lat_y * repeat_y + y_flat % repeat_y
    )
    recv_select = (buffer_ids[None, :] == source_index[:, None]).astype(jnp.float32)
    patch_bricks = (
        fields.reshape(capacity, 5, PE, per_patch, brick_y, PE)
        .transpose(0, 3, 1, 2, 4, 5)
        .reshape(capacity * per_patch, brick_cells)
    )
    send_buffer = jnp.matmul(send_select, patch_bricks, precision=lax.Precision.HIGHEST)
    arrived = lax.all_to_all(send_buffer, "col", split_axis=0, concat_axis=0, tiled=True)
    pencil_bricks = jnp.matmul(recv_select, arrived, precision=lax.Precision.HIGHEST)
    pencil = (
        pencil_bricks.reshape(lat_x, per_pencil_y, lat_z, 5, PE, brick_y, PE)
        .transpose(3, 0, 4, 1, 5, 2, 6)
        .reshape(5, block_x, block_y, GZ)
    )
    extended = padded(pencil, (("row", 1), ("col", 2)), 4)
    stepped = advance(extended)
    rows_y = GY // rows_count
    cols_z = GZ // cols_count
    cos_x, sin_x = dft_tables(GX)
    cos_y, sin_y = dft_tables(GY)
    cos_z, sin_z = dft_tables(GZ)
    density = stepped[0]
    along_re = right_mul(density, cos_z)
    along_im = -right_mul(density, sin_z)
    packed = (
        jnp.stack([along_re, along_im])
        .reshape(2, block_x, block_y, cols_count, cols_z)
        .transpose(3, 2, 0, 4, 1)
    )
    paired = lax.all_to_all(packed, "col", split_axis=0, concat_axis=0, tiled=True)
    paired = paired.reshape(GY, 2, cols_z * block_x)
    mid_re = paired[:, 0]
    mid_im = paired[:, 1]
    spec_re = left_mul(cos_y, mid_re) + left_mul(sin_y, mid_im)
    spec_im = left_mul(cos_y, mid_im) - left_mul(sin_y, mid_re)
    packed = (
        jnp.stack([spec_re, spec_im])
        .reshape(2, rows_count, rows_y, cols_z * block_x)
        .transpose(1, 0, 2, 3)
    )
    paired = lax.all_to_all(packed, "row", split_axis=0, concat_axis=0, tiled=True)
    paired = (
        paired.reshape(rows_count, 2, rows_y, cols_z, block_x)
        .transpose(1, 2, 3, 0, 4)
        .reshape(2, rows_y * cols_z, GX)
    )
    spec_re = right_mul(paired[0], cos_x) + right_mul(paired[1], sin_x)
    spec_im = right_mul(paired[1], cos_x) - right_mul(paired[0], sin_x)
    index_x = jnp.arange(GX, dtype=jnp.int32)
    index_y = my_row * rows_y + jnp.arange(rows_y, dtype=jnp.int32)
    index_z = my_column * cols_z + jnp.arange(cols_z, dtype=jnp.int32)
    wave_x = index_x.astype(jnp.float32)
    wave_y = index_y.astype(jnp.float32)
    wave_z = index_z.astype(jnp.float32)
    eigen = (
        lap_eigen(wave_x, GX)[None, None, :]
        + lap_eigen(wave_y, GY)[:, None, None]
        + lap_eigen(wave_z, GZ)[None, :, None]
    )
    zero_mode = (
        (index_x == 0)[None, None, :]
        & (index_y == 0)[:, None, None]
        & (index_z == 0)[None, :, None]
    )
    green = jnp.where(zero_mode, 0.0, four_pi_g / jnp.where(zero_mode, -1.0, eigen)).reshape(
        rows_y * cols_z, GX
    )
    pot_re = spec_re * green
    pot_im = spec_im * green
    scale = 1.0 / (GX * GY * GZ)
    sine_x = jnp.sin(2.0 * math.pi / GX * wave_x)[None, :]
    sine_y = jnp.broadcast_to(
        jnp.sin(2.0 * math.pi / GY * wave_y)[:, None], (rows_y, cols_z)
    ).reshape(rows_y * cols_z, 1)
    sine_z = jnp.broadcast_to(
        jnp.sin(2.0 * math.pi / GZ * wave_z)[None, :], (rows_y, cols_z)
    ).reshape(rows_y * cols_z, 1)
    grad_re = jnp.stack([-(sine_x * pot_im), -(sine_y * pot_im), -(sine_z * pot_im)])
    grad_im = jnp.stack([sine_x * pot_re, sine_y * pot_re, sine_z * pot_re])
    back_re = right_mul(grad_re, cos_x) - right_mul(grad_im, sin_x)
    back_im = right_mul(grad_im, cos_x) + right_mul(grad_re, sin_x)
    packed = (
        jnp.stack([back_re, back_im], axis=1)
        .reshape(3, 2, rows_y, cols_z, rows_count, block_x)
        .transpose(4, 0, 1, 2, 3, 5)
    )
    returned = lax.all_to_all(packed, "row", split_axis=0, concat_axis=0, tiled=True)
    returned = returned.transpose(1, 2, 0, 3, 4, 5).reshape(3, 2, GY, cols_z * block_x)
    mid_re = left_mul(cos_y, returned[:, 0]) - left_mul(sin_y, returned[:, 1])
    mid_im = left_mul(cos_y, returned[:, 1]) + left_mul(sin_y, returned[:, 0])
    packed = (
        jnp.stack([mid_re, mid_im], axis=1)
        .reshape(3, 2, cols_count, block_y, cols_z * block_x)
        .transpose(2, 0, 1, 3, 4)
    )
    returned = lax.all_to_all(packed, "col", split_axis=0, concat_axis=0, tiled=True)
    returned = (
        returned.reshape(cols_count, 3, 2, block_y, cols_z, block_x)
        .transpose(1, 2, 5, 3, 0, 4)
        .reshape(3, 2, block_x, block_y, GZ)
    )
    gradient = (right_mul(returned[:, 0], cos_z) - right_mul(returned[:, 1], sin_z)) * scale
    kicked = apply_kick(stepped, gradient)
    back_bricks = (
        kicked.reshape(5, lat_x, PE, per_pencil_y, brick_y, lat_z, PE)
        .transpose(1, 3, 5, 0, 2, 4, 6)
        .reshape(lat_x * per_pencil_y * lat_z, brick_cells)
    )
    return_buffer = jnp.matmul(recv_select.T, back_bricks, precision=lax.Precision.HIGHEST)
    came_back = lax.all_to_all(return_buffer, "col", split_axis=0, concat_axis=0, tiled=True)
    slot_bricks = jnp.matmul(send_select.T, came_back, precision=lax.Precision.HIGHEST)
    return (
        slot_bricks.reshape(capacity, per_patch, 5, PE, brick_y, PE)
        .transpose(0, 2, 3, 1, 4, 5)
        .reshape(capacity, 5, PE * PE * PE)
    )


def solution(mesh):
    return jax.shard_map(
        on_device,
        mesh=mesh,
        in_specs=(P(("row", "col"), None, None), P("row", "col")),
        out_specs=P(("row", "col"), None, None),
        check_vma=False,
    )
```

profile of v0, /device:TPU:2, one launch (start us, length us, event | category | flops | bytes accessed | tf_op | source)
XLA Modules:
  0.0 405.6 jit_solution(16840905404594072980)
XLA Ops:
  0.0 7.2 %reshape.446 = f32[16,5,16,2,8,16]{5,4,3,2,0,1:T(8,128)} reshape(f32[16,5,4096]{2,0,1:T(8,128)} %param.2) | data formatting | bytes 2621440 | tf_op jit(solution)/shard_map/reshape | solution.py:191
  7.3 9.3 %copy.158 = f32[16,5,16,2,8,16]{5,4,2,1,3,0:T(8,128)} copy(f32[16,5,16,2,8,16]{5,4,3,2,0,1:T(8,128)} %reshape.446) | data formatting | bytes 2621440 | tf_op jit(solution)/shard_map/reshape | solution.py:191
  16.6 9.9 %reshape.447 = f32[32,10240]{1,0:T(8,128)S(1)} reshape(f32[16,2,5,16,8,16]{5,4,3,2,1,0:T(8,128)} %bitcast.229) | data formatting | bytes 2621440 | tf_op jit(solution)/shard_map/reshape | solution.py:193
  28.6 22.5 %all-reduce = s32[32]{0:T(128)S(1)} all-reduce(s32[32]{0:T(128)S(1)} %bitcast_dynamic-update-slice_fusion), channel_id=1, replica_groups=mesh['row'=8,'col'=32] {'col'}, use_global_device_ids=true, to_apply=%add | all-reduce | flops 32 | bytes 256 | tf_op jit(solution)/shard_map/reshape | solution.py:157
  53.8 2.4 copy.119
  56.2 5.6 %all-to-all-start = ((f32[32,1,10240]{2,1,0:T(1,128)}), f32[32,1,10240]{2,1,0:T(1,128)S(1)}, u32[]{:S(2)}, u32[]{:S(2)}) async-start(f32[32,1,10240]{2,1,0:T(1,128)} %copy.119), calls=%async_computation | async-start | bytes 2621440 | tf_op jit(solution)/shard_map/all_to_all | solution.py:196
  62.7 28.4 %all-to-all-done = f32[32,1,10240]{2,1,0:T(1,128)S(1)} async-done(((f32[32,1,10240]{2,1,0:T(1,128)}), f32[32,1,10240]{2,1,0:T(1,128)S(1)}, u32[]{:S(2)}, u32[]{:S(2)}) %all-to-all-start) | async-done | bytes 1310752 | tf_op jit(solution)/shard_map/all_to_all | solution.py:196
  91.1 4.1 %copy.120 = f32[32,1,10240]{0,2,1:T(8,128)} copy(f32[32,1,10240]{2,1,0:T(1,128)S(1)} %all-to-all-done) | data formatting | bytes 2621440 | tf_op jit(solution)/shard_map/all_to_all | solution.py:196
  95.2 20.9 %convolution_bitcast_fusion.3 = f32[5,2,16,1,8,8,16]{6,5,4,2,0,1,3:T(8,128)S(1)} fusion(f32[5,16,8,16,32,1]{4,3,2,1,0,5:T(8,128)} %bitcast.232, s32[2,8]{1,0:T(2,128)S(1)} %fusion.108), kind=kOutput, calls=%fused_computation.6 | convolution fusion | flops 62915072 | bytes 1966144 | tf_op jit(solution)/shard_map/dot_general | solution.py:197
  116.1 3.0 copy.121
  119.1 3.8 reshape.448
  123.1 3.0 collective-permute-start.1
  126.0 2.1 collective-permute-done
  128.9 1.6 collective-permute-start.2
  131.0 9.2 %collective-permute-done.3 = f32[5,40,4,128]{3,2,1,0:T(4,128)S(1)} collective-permute-done((f32[5,40,4,128]{3,2,1,0:T(4,128)S(1)}, f32[5,40,4,128]{3,2,1,0:T(4,128)S(1)}, u32[]{:S(2)}, u32[]{:S(2)}) %collective-permute-start.3) | collective-permute-done | bytes 409632 | tf_op jit(solution)/shard_map/ppermute | solution.py:29
  141.0 2.1 multiply_add_fusion.2
  143.1 2.1 multiply_add_fusion
  148.0 2.7 multiply_add_fusion.1
  154.5 1.9 multiply_add_fusion.3
  164.2 1.2 copy.125
  166.6 10.1 %all-to-all-start.1 = ((f32[32,1,2048]{2,1,0:T(1,128)}), f32[32,1,2048]{2,1,0:T(1,128)S(1)}, u32[]{:S(2)}, u32[]{:S(2)}) async-start(f32[32,1,2048]{2,1,0:T(1,128)} %reshape.477), calls=%async_computation.1 | async-start | bytes 524288 | tf_op jit(solution)/shard_map/all_to_all | solution.py:218
  176.9 10.6 %all-to-all-done.1 = f32[32,1,2048]{2,1,0:T(1,128)S(1)} async-done(((f32[32,1,2048]{2,1,0:T(1,128)}), f32[32,1,2048]{2,1,0:T(1,128)S(1)}, u32[]{:S(2)}, u32[]{:S(2)}) %all-to-all-start.1) | async-done | bytes 262176 | tf_op jit(solution)/shard_map/all_to_all | solution.py:218
  188.1 1.3 reduce.2
  190.5 1.3 fusion.53
  191.8 1.3 fusion.55
  193.2 1.3 convolution_subtract_fusion.4
  194.5 1.3 convolution_add_fusion.3
  196.6 5.1 %all-to-all-start.2 = ((f32[8,2,32,128]{3,2,1,0:T(8,128)}), f32[8,2,32,128]{3,2,1,0:T(8,128)S(1)}, u32[]{:S(2)}, u32[]{:S(2)}) async-start(f32[8,2,32,128]{3,2,1,0:T(8,128)} %maximum_bitcast_fusion.4), calls=%async_computation.2 | async-start | bytes 524288 | tf_op jit(solution)/shard_map/all_to_all | solution.py:229
  202.4 6.3 %all-to-all-done.2 = f32[8,2,32,128]{3,2,1,0:T(8,128)S(1)} async-done(((f32[8,2,32,128]{3,2,1,0:T(8,128)}), f32[8,2,32,128]{3,2,1,0:T(8,128)S(1)}, u32[]{:S(2)}, u32[]{:S(2)}) %all-to-all-start.2) | async-done | bytes 262176 | tf_op jit(solution)/shard_map/all_to_all | solution.py:229
  209.8 1.2 fusion.48
  211.6 1.2 fusion.51
  212.8 1.3 fusion.7
  214.1 1.3 multiply_bitcast_fusion.3
  215.4 1.5 fusion.21
  216.9 1.5 fusion.22
  218.3 1.5 convolution_add_fusion.1
  220.2 1.8 copy.132
  221.9 1.5 convolution_subtract_fusion.2
  226.1 2.8 reshape.479
  228.9 16.7 %all_to_all.44 = f32[8,1,24576]{2,1,0:T(1,128)S(1)} all-to-all(f32[8,1,24576]{2,1,0:T(1,128)} %reshape.479), channel_id=1, replica_groups=mesh['row'=8,'col'=32] {'row'}, dimensions={0} | all-to-all | bytes 1572864 | tf_op jit(solution)/shard_map/all_to_all | solution.py:275
  245.6 2.5 reduce.3
  248.2 3.2 reshape.480
  251.4 2.1 bitcast_bitcast_fusion
  253.5 2.8 copy.133
  256.3 2.4 reshape.452
  258.7 1.5 fusion.20
  260.1 1.5 fusion.19
  261.6 1.5 fusion.5
  263.2 1.5 fusion.6
  265.9 6.7 %all-to-all-start.4 = ((f32[32,3,2,8,128]{4,3,1,2,0:T(8,128)}), f32[32,3,2,8,128]{4,3,1,2,0:T(8,128)}, u32[]{:S(2)}, u32[]{:S(2)}) async-start(f32[32,3,2,8,128]{4,3,1,2,0:T(8,128)} %copy.136), calls=%async_computation.4 | async-start | bytes 1572864 | tf_op jit(solution)/shard_map/all_to_all | solution.py:284
  272.6 22.3 %all-to-all-done.4 = f32[32,3,2,8,128]{4,3,1,2,0:T(8,128)} async-done(((f32[32,3,2,8,128]{4,3,1,2,0:T(8,128)}), f32[32,3,2,8,128]{4,3,1,2,0:T(8,128)}, u32[]{:S(2)}, u32[]{:S(2)}) %all-to-all-start.4) | async-done | bytes 786464 | tf_op jit(solution)/shard_map/all_to_all | solution.py:284
  295.0 2.5 reshape.453
  303.8 2.2 copy.141
  306.0 1.3 concatenate.60
  307.3 1.5 copy.140
  308.8 4.1 %maximum_bitcast_fusion = f32[2,1,8,5,16,8,16]{6,5,4,3,2,0,1:T(8,128)} fusion(f32[1,2,16,1,8,8,16]{6,4,2,0,5,1,3:T(8,128)} %copy.142, f32[3,2,16,1,8,8,16]{6,4,2,0,5,1,3:T(8,128)S(1)} %copy-done, f32[1,2,16,1,8,8,16]{6,4,2,0,5,1,3:T(8,128)S(1)} %copy.140), kind=kLoop, calls=%fused_computation.3 | loop fusion | flops 327680 | bytes 1310720 | tf_op jit(solution)/shard_map/transpose | solution.py:294
  312.9 5.8 %reshape.455 = f32[16,10240]{1,0:T(8,128)S(1)} reshape(f32[2,1,8,5,16,8,16]{6,5,4,3,2,0,1:T(8,128)} %maximum_bitcast_fusion) | data formatting | bytes 1310720 | tf_op jit(solution)/shard_map/reshape | solution.py:295
  319.5 2.4 copy.143
  321.9 5.9 %all-to-all-start.5 = ((f32[32,1,10240]{2,1,0:T(1,128)}), f32[32,1,10240]{2,1,0:T(1,128)S(1)}, u32[]{:S(2)}, u32[]{:S(2)}) async-start(f32[32,1,10240]{2,1,0:T(1,128)} %copy.143), calls=%async_computation.5 | async-start | bytes 2621440 | tf_op jit(solution)/shard_map/all_to_all | solution.py:298
  327.8 32.3 %all-to-all-done.5 = f32[32,1,10240]{2,1,0:T(1,128)S(1)} async-done(((f32[32,1,10240]{2,1,0:T(1,128)}), f32[32,1,10240]{2,1,0:T(1,128)S(1)}, u32[]{:S(2)}, u32[]{:S(2)}) %all-to-all-start.5) | async-done | bytes 1310752 | tf_op jit(solution)/shard_map/all_to_all | solution.py:298
  360.1 4.1 %copy.144 = f32[32,1,10240]{0,2,1:T(8,128)} copy(f32[32,1,10240]{2,1,0:T(1,128)S(1)} %all-to-all-done.5) | data formatting | bytes 2621440 | tf_op jit(solution)/shard_map/all_to_all | solution.py:298
  364.2 23.6 %convolution_bitcast_fusion.2 = f32[16,5,16,2,8,16]{5,0,4,2,1,3:T(8,128)S(1)} fusion(f32[5,16,8,16,32,1]{4,3,2,1,0,5:T(8,128)} %bitcast.231, s32[16,2]{0,1:T(2,128)S(1)} %copy.117, pred[16]{0:T(512)(128)(4,1)S(1)} %iota_compare_fusion.7), kind=kOutput, calls=%fused_computation.4 | convolution fusion | flops 125831168 | bytes 2621584 | tf_op jit(solution)/shard_map/dot_general | solution.py:299
  387.8 7.3 %copy.145 = f32[16,5,16,2,8,16]{5,4,3,2,0,1:T(8,128)} copy(f32[16,5,16,2,8,16]{5,0,4,2,1,3:T(8,128)S(1)} %convolution_bitcast_fusion.2) | data formatting | bytes 2621440 | tf_op jit(solution)/shard_map/transpose | solution.py:302
  395.1 10.3 %reshape.456 = f32[16,5,4096]{2,0,1:T(8,128)} reshape(f32[16,5,16,2,8,16]{5,4,3,2,0,1:T(8,128)} %copy.145) | data formatting | bytes 2621440 | tf_op jit(solution)/shard_map/reshape | solution.py:303
  (190 shorter events, 38.3 us)
Async XLA Ops:
  16.6 10.8 %copy-start.5 = (u32[256]{0:T(256)S(1)}, u32[256]{0:T(256)}, u32[]{:S(2)}) copy-start(u32[256]{0:T(256)} %constant.206) | copy-start | bytes 3076
  56.2 34.9 %all-to-all-start = ((f32[32,1,10240]{2,1,0:T(1,128)}), f32[32,1,10240]{2,1,0:T(1,128)S(1)}, u32[]{:S(2)}, u32[]{:S(2)}) async-start(f32[32,1,10240]{2,1,0:T(1,128)} %copy.119), calls=%async_computation | async-start | bytes 2621440 | tf_op jit(solution)/shard_map/all_to_all | solution.py:196
  123.0 5.1 %collective-permute-start = (f32[5,4,8,128]{3,2,1,0:T(8,128)S(1)}, f32[5,4,8,128]{3,2,1,0:T(8,128)S(1)}, u32[]{:S(2)}, u32[]{:S(2)}) collective-permute-start(f32[5,4,8,128]{3,2,1,0:T(8,128)S(1)} %get-tuple-element.79), channel_id=1, source_target_pairs={{0,32},{32,64},{64,96},{96,128},{128,160},{160,192},{192,224},{224... | collective-permute-start | bytes 245768 | tf_op jit(solution)/shard_map/ppermute | solution.py:26
  123.1 5.1 %collective-permute-start.1 = (f32[5,4,8,128]{3,2,1,0:T(8,128)S(1)}, f32[5,4,8,128]{3,2,1,0:T(8,128)S(1)}, u32[]{:S(2)}, u32[]{:S(2)}) collective-permute-start(f32[5,4,8,128]{3,2,1,0:T(8,128)S(1)} %get-tuple-element.78), channel_id=1, source_target_pairs={{32,0},{64,32},{96,64},{128,96},{160,128},{192,160},{224,192},{0,2... | collective-permute-start | bytes 245768 | tf_op jit(solution)/shard_map/ppermute | solution.py:29
  128.3 11.9 %collective-permute-start.3 = (f32[5,40,4,128]{3,2,1,0:T(4,128)S(1)}, f32[5,40,4,128]{3,2,1,0:T(4,128)S(1)}, u32[]{:S(2)}, u32[]{:S(2)}) collective-permute-start(f32[5,40,4,128]{3,2,1,0:T(4,128)S(1)} %get-tuple-element.74), channel_id=1, source_target_pairs={{1,0},{2,1},{3,2},{4,3},{5,4},{6,5},{7,6},{8,7},{9,8},{10,9},{11,1... | collective-permute-start | bytes 1228808 | tf_op jit(solution)/shard_map/ppermute | solution.py:29
  128.9 11.7 %collective-permute-start.2 = (f32[5,40,4,128]{3,2,1,0:T(4,128)S(1)}, f32[5,40,4,128]{3,2,1,0:T(4,128)S(1)}, u32[]{:S(2)}, u32[]{:S(2)}) collective-permute-start(f32[5,40,4,128]{3,2,1,0:T(4,128)S(1)} %get-tuple-element.73), channel_id=1, source_target_pairs={{0,1},{1,2},{2,3},{3,4},{4,5},{5,6},{6,7},{7,8},{8,9},{9,10},{10,1... | collective-permute-start | bytes 1228808 | tf_op jit(solution)/shard_map/ppermute | solution.py:26
  162.1 2.1 copy-start.2
  166.6 20.9 %all-to-all-start.1 = ((f32[32,1,2048]{2,1,0:T(1,128)}), f32[32,1,2048]{2,1,0:T(1,128)S(1)}, u32[]{:S(2)}, u32[]{:S(2)}) async-start(f32[32,1,2048]{2,1,0:T(1,128)} %reshape.477), calls=%async_computation.1 | async-start | bytes 524288 | tf_op jit(solution)/shard_map/all_to_all | solution.py:218
  196.6 12.2 %all-to-all-start.2 = ((f32[8,2,32,128]{3,2,1,0:T(8,128)}), f32[8,2,32,128]{3,2,1,0:T(8,128)S(1)}, u32[]{:S(2)}, u32[]{:S(2)}) async-start(f32[8,2,32,128]{3,2,1,0:T(8,128)} %maximum_bitcast_fusion.4), calls=%async_computation.2 | async-start | bytes 524288 | tf_op jit(solution)/shard_map/all_to_all | solution.py:229
  223.8 1.4 copy-start.1
  265.9 29.1 %all-to-all-start.4 = ((f32[32,3,2,8,128]{4,3,1,2,0:T(8,128)}), f32[32,3,2,8,128]{4,3,1,2,0:T(8,128)}, u32[]{:S(2)}, u32[]{:S(2)}) async-start(f32[32,3,2,8,128]{4,3,1,2,0:T(8,128)} %copy.136), calls=%async_computation.4 | async-start | bytes 1572864 | tf_op jit(solution)/shard_map/all_to_all | solution.py:284
  299.3 1.2 copy-start.3
  303.8 2.2 copy-start.4
  306.0 2.8 copy-start
  321.9 38.3 %all-to-all-start.5 = ((f32[32,1,10240]{2,1,0:T(1,128)}), f32[32,1,10240]{2,1,0:T(1,128)S(1)}, u32[]{:S(2)}, u32[]{:S(2)}) async-start(f32[32,1,10240]{2,1,0:T(1,128)} %copy.143), calls=%async_computation.5 | async-start | bytes 2621440 | tf_op jit(solution)/shard_map/all_to_all | solution.py:298
where the time goes:
time: 412 us; the launch traced here: 406 us
  local copies, waits for them, and re-layouts  113 us (27%)
  waiting for transfers between devices  112 us (27%)
  matrix products  70.7 us (17%)
  blocking collectives  39.2 us (10%)
  starting transfers between devices  38.7 us (9%)
  other arithmetic  30.6 us (7%)
    all_to_all x2, waiting for transfers between devices, on_device(): lax.all_to_all(packed, 'col', split_axis=0, concat_axis=0, tiled=True)  32.9 us
    all_to_all x1, waiting for transfers between devices, on_device(): lax.all_to_all(return_buffer, 'col', split_axis=0, concat_axis=0, tiled=T...  32.3 us
    all_to_all x1, waiting for transfers between devices, on_device(): lax.all_to_all(send_buffer, 'col', split_axis=0, concat_axis=0, tiled=True)  28.4 us
    dot_general x1, matrix products, on_device(): jnp.matmul(send_select.T, came_back, precision=lax.Precision.HIGHEST)  23.6 us
    reshape x1, blocking collectives, on_device(): lax.all_gather(counts, 'col', axis=1, tiled=True).reshape(cols_count)  22.5 us
    dot_general x1, matrix products, on_device(): jnp.matmul(recv_select, arrived, precision=lax.Precision.HIGHEST)  20.9 us
    all_to_all x2, starting transfers between devices, on_device(): lax.all_to_all(packed, 'col', split_axis=0, concat_axis=0, tiled=True)  16.9 us
    all_to_all x1, blocking collectives, on_device(): lax.all_to_all(packed, 'row', split_axis=0, concat_axis=0, tiled=True)  16.7 us
  transfers between devices with their start and end apart: 9, of which 8 were waited for; matrix products, arithmetic and copies ran while one was open for 1% of the time, Pallas kernels for 0%

commit v1 on v0

--- a/solution.py
+++ b/solution.py
@@ -155,8 +155,10 @@
     brick_cells = 5 * PE * brick_y * PE
     buffer_rows = cols_count * per_peer
     row_counts = lax.all_gather(counts, "col", axis=1, tiled=True).reshape(cols_count)
-    starts = jnp.cumsum(row_counts) - row_counts
     column_ids = jnp.arange(cols_count, dtype=jnp.int32)
+    starts = jnp.sum(
+        jnp.where(column_ids[None, :] < column_ids[:, None], row_counts[None, :], 0), axis=1
+    )
     own_start = jnp.sum(jnp.where(column_ids == my_column, starts, 0))
     own_count = counts[0, 0]
     slot_ids = jnp.arange(capacity, dtype=jnp.int32)

time: 412 us -> 412 us (level)
    reshape x1 -> x0, blocking collectives: 22.5 us -> none  [on_device(): lax.all_gather(counts, 'col', axis=1, tiled=True).reshape(cols_count)]
    unnamed x0 -> x1, blocking collectives: none -> 22.5 us
where the time goes in v1:
time: 412 us; the launch traced here: 405 us
  local copies, waits for them, and re-layouts  113 us (27%)
  waiting for transfers between devices  112 us (27%)
  matrix products  70.7 us (17%)
  blocking collectives  39.2 us (10%)
  starting transfers between devices  38.7 us (9%)
  other arithmetic  30.5 us (7%)
    all_to_all x2, waiting for transfers between devices, on_device(): lax.all_to_all(packed, 'col', split_axis=0, concat_axis=0, tiled=True)  32.9 us
    all_to_all x1, waiting for transfers between devices, on_device(): lax.all_to_all(return_buffer, 'col', split_axis=0, concat_axis=0, tiled=T...  32.3 us
    all_to_all x1, waiting for transfers between devices, on_device(): lax.all_to_all(send_buffer, 'col', split_axis=0, concat_axis=0, tiled=True)  28.4 us
    dot_general x1, matrix products, on_device(): jnp.matmul(send_select.T, came_back, precision=lax.Precision.HIGHEST)  23.6 us
    unnamed x1, blocking collectives  22.5 us
    dot_general x1, matrix products, on_device(): jnp.matmul(recv_select, arrived, precision=lax.Precision.HIGHEST)  20.9 us
    all_to_all x2, starting transfers between devices, on_device(): lax.all_to_all(packed, 'col', split_axis=0, concat_axis=0, tiled=True)  16.9 us
    all_to_all x1, blocking collectives, on_device(): lax.all_to_all(packed, 'row', split_axis=0, concat_axis=0, tiled=True)  16.7 us
  transfers between devices with their start and end apart: 9, of which 8 were waited for; matrix products, arithmetic and copies ran while one was open for 1% of the time, Pallas kernels for 0%

profile of v1, /device:TPU:2, one launch (start us, length us, event | category | flops | bytes accessed | tf_op | source)
XLA Modules:
  0.0 405.4 jit_solution(17611532026228184675)
XLA Ops:
  0.0 7.2 %reshape.430 = f32[16,5,16,2,8,16]{5,4,3,2,0,1:T(8,128)} reshape(f32[16,5,4096]{2,0,1:T(8,128)} %param.2) | data formatting | bytes 2621440 | tf_op jit(solution)/shard_map/reshape | solution.py:193
  7.2 9.3 %copy.152 = f32[16,5,16,2,8,16]{5,4,2,1,3,0:T(8,128)} copy(f32[16,5,16,2,8,16]{5,4,3,2,0,1:T(8,128)} %reshape.430) | data formatting | bytes 2621440 | tf_op jit(solution)/shard_map/reshape | solution.py:193
  16.6 9.9 %reshape.431 = f32[32,10240]{1,0:T(8,128)S(1)} reshape(f32[16,2,5,16,8,16]{5,4,3,2,1,0:T(8,128)} %bitcast.220) | data formatting | bytes 2621440 | tf_op jit(solution)/shard_map/reshape | solution.py:195
  28.4 22.5 %all-reduce = s32[32]{0:T(128)S(1)} all-reduce(s32[32]{0:T(128)S(1)} %bitcast_dynamic-update-slice_fusion), channel_id=1, replica_groups=mesh['row'=8,'col'=32] {'col'}, use_global_device_ids=true, to_apply=%add | all-reduce | flops 32 | bytes 256
  53.6 2.4 copy.113
  56.0 5.6 %all-to-all-start = ((f32[32,1,10240]{2,1,0:T(1,128)}), f32[32,1,10240]{2,1,0:T(1,128)S(1)}, u32[]{:S(2)}, u32[]{:S(2)}) async-start(f32[32,1,10240]{2,1,0:T(1,128)} %copy.113), calls=%async_computation | async-start | bytes 2621440 | tf_op jit(solution)/shard_map/all_to_all | solution.py:198
  62.6 28.4 %all-to-all-done = f32[32,1,10240]{2,1,0:T(1,128)S(1)} async-done(((f32[32,1,10240]{2,1,0:T(1,128)}), f32[32,1,10240]{2,1,0:T(1,128)S(1)}, u32[]{:S(2)}, u32[]{:S(2)}) %all-to-all-start) | async-done | bytes 1310752 | tf_op jit(solution)/shard_map/all_to_all | solution.py:198
  90.9 4.1 %copy.114 = f32[32,1,10240]{0,2,1:T(8,128)} copy(f32[32,1,10240]{2,1,0:T(1,128)S(1)} %all-to-all-done) | data formatting | bytes 2621440 | tf_op jit(solution)/shard_map/all_to_all | solution.py:198
  95.0 20.9 %convolution_bitcast_fusion.3 = f32[5,2,16,1,8,8,16]{6,5,4,2,0,1,3:T(8,128)S(1)} fusion(f32[5,16,8,16,32,1]{4,3,2,1,0,5:T(8,128)} %bitcast.223, s32[2,8]{1,0:T(2,128)S(1)} %fusion.108), kind=kOutput, calls=%fused_computation.6 | convolution fusion | flops 62915072 | bytes 1966144 | tf_op jit(solution)/shard_map/dot_general | solution.py:199
  115.9 3.0 copy.115
  118.9 3.8 reshape.432
  122.9 3.0 collective-permute-start.1
  125.8 2.1 collective-permute-done
  128.8 1.6 collective-permute-start.2
  130.8 9.2 %collective-permute-done.3 = f32[5,40,4,128]{3,2,1,0:T(4,128)S(1)} collective-permute-done((f32[5,40,4,128]{3,2,1,0:T(4,128)S(1)}, f32[5,40,4,128]{3,2,1,0:T(4,128)S(1)}, u32[]{:S(2)}, u32[]{:S(2)}) %collective-permute-start.3) | collective-permute-done | bytes 409632 | tf_op jit(solution)/shard_map/ppermute | solution.py:29
  140.8 2.1 multiply_add_fusion.2
  142.9 2.1 multiply_add_fusion
  147.7 2.7 multiply_add_fusion.1
  154.4 1.9 multiply_add_fusion.3
  164.2 1.2 copy.119
  166.6 10.1 %all-to-all-start.1 = ((f32[32,1,2048]{2,1,0:T(1,128)}), f32[32,1,2048]{2,1,0:T(1,128)S(1)}, u32[]{:S(2)}, u32[]{:S(2)}) async-start(f32[32,1,2048]{2,1,0:T(1,128)} %reshape.458), calls=%async_computation.1 | async-start | bytes 524288 | tf_op jit(solution)/shard_map/all_to_all | solution.py:220
  176.9 10.6 %all-to-all-done.1 = f32[32,1,2048]{2,1,0:T(1,128)S(1)} async-done(((f32[32,1,2048]{2,1,0:T(1,128)}), f32[32,1,2048]{2,1,0:T(1,128)S(1)}, u32[]{:S(2)}, u32[]{:S(2)}) %all-to-all-start.1) | async-done | bytes 262176 | tf_op jit(solution)/shard_map/all_to_all | solution.py:220
  188.0 1.2 reduce
  190.4 1.3 fusion.53
  191.7 1.3 fusion.55
  193.1 1.3 convolution_subtract_fusion.4
  194.4 1.3 convolution_add_fusion.3
  196.5 5.1 %all-to-all-start.2 = ((f32[8,2,32,128]{3,2,1,0:T(8,128)}), f32[8,2,32,128]{3,2,1,0:T(8,128)S(1)}, u32[]{:S(2)}, u32[]{:S(2)}) async-start(f32[8,2,32,128]{3,2,1,0:T(8,128)} %maximum_bitcast_fusion.4), calls=%async_computation.2 | async-start | bytes 524288 | tf_op jit(solution)/shard_map/all_to_all | solution.py:231
  202.3 6.3 %all-to-all-done.2 = f32[8,2,32,128]{3,2,1,0:T(8,128)S(1)} async-done(((f32[8,2,32,128]{3,2,1,0:T(8,128)}), f32[8,2,32,128]{3,2,1,0:T(8,128)S(1)}, u32[]{:S(2)}, u32[]{:S(2)}) %all-to-all-start.2) | async-done | bytes 262176 | tf_op jit(solution)/shard_map/all_to_all | solution.py:231
  209.7 1.2 fusion.48
  211.5 1.2 fusion.51
  212.7 1.3 fusion.7
  214.0 1.3 multiply_bitcast_fusion.3
  215.3 1.5 fusion.21
  216.8 1.5 fusion.22
  218.2 1.5 convolution_add_fusion.1
  220.1 1.8 copy.126
  221.8 1.5 convolution_subtract_fusion.2
  226.0 2.8 reshape.460
  228.8 16.7 %all_to_all.44 = f32[8,1,24576]{2,1,0:T(1,128)S(1)} all-to-all(f32[8,1,24576]{2,1,0:T(1,128)} %reshape.460), channel_id=1, replica_groups=mesh['row'=8,'col'=32] {'row'}, dimensions={0} | all-to-all | bytes 1572864 | tf_op jit(solution)/shard_map/all_to_all | solution.py:277
  245.5 2.5 reduce.1
  248.0 3.2 reshape.461
  251.3 2.1 bitcast_bitcast_fusion
  253.4 2.8 copy.127
  256.1 2.4 reshape.436
  258.5 1.5 fusion.20
  260.0 1.5 fusion.19
  261.5 1.5 fusion.5
  263.1 1.5 fusion.6
  265.7 6.7 %all-to-all-start.4 = ((f32[32,3,2,8,128]{4,3,1,2,0:T(8,128)}), f32[32,3,2,8,128]{4,3,1,2,0:T(8,128)}, u32[]{:S(2)}, u32[]{:S(2)}) async-start(f32[32,3,2,8,128]{4,3,1,2,0:T(8,128)} %copy.130), calls=%async_computation.4 | async-start | bytes 1572864 | tf_op jit(solution)/shard_map/all_to_all | solution.py:286
  272.5 22.3 %all-to-all-done.4 = f32[32,3,2,8,128]{4,3,1,2,0:T(8,128)} async-done(((f32[32,3,2,8,128]{4,3,1,2,0:T(8,128)}), f32[32,3,2,8,128]{4,3,1,2,0:T(8,128)}, u32[]{:S(2)}, u32[]{:S(2)}) %all-to-all-start.4) | async-done | bytes 786464 | tf_op jit(solution)/shard_map/all_to_all | solution.py:286
  294.8 2.5 reshape.437
  303.6 2.2 copy.135
  305.9 1.3 concatenate.60
  307.2 1.4 copy.134
  308.6 4.1 %maximum_bitcast_fusion = f32[2,1,8,5,16,8,16]{6,5,4,3,2,0,1:T(8,128)} fusion(f32[1,2,16,1,8,8,16]{6,4,2,0,5,1,3:T(8,128)} %copy.136, f32[3,2,16,1,8,8,16]{6,4,2,0,5,1,3:T(8,128)S(1)} %copy-done, f32[1,2,16,1,8,8,16]{6,4,2,0,5,1,3:T(8,128)S(1)} %copy.134), kind=kLoop, calls=%fused_computation.3 | loop fusion | flops 327680 | bytes 1310720 | tf_op jit(solution)/shard_map/transpose | solution.py:296
  312.7 5.8 %reshape.439 = f32[16,10240]{1,0:T(8,128)S(1)} reshape(f32[2,1,8,5,16,8,16]{6,5,4,3,2,0,1:T(8,128)} %maximum_bitcast_fusion) | data formatting | bytes 1310720 | tf_op jit(solution)/shard_map/reshape | solution.py:297
  319.3 2.4 copy.137
  321.7 5.9 %all-to-all-start.5 = ((f32[32,1,10240]{2,1,0:T(1,128)}), f32[32,1,10240]{2,1,0:T(1,128)S(1)}, u32[]{:S(2)}, u32[]{:S(2)}) async-start(f32[32,1,10240]{2,1,0:T(1,128)} %copy.137), calls=%async_computation.5 | async-start | bytes 2621440 | tf_op jit(solution)/shard_map/all_to_all | solution.py:300
  327.7 32.3 %all-to-all-done.5 = f32[32,1,10240]{2,1,0:T(1,128)S(1)} async-done(((f32[32,1,10240]{2,1,0:T(1,128)}), f32[32,1,10240]{2,1,0:T(1,128)S(1)}, u32[]{:S(2)}, u32[]{:S(2)}) %all-to-all-start.5) | async-done | bytes 1310752 | tf_op jit(solution)/shard_map/all_to_all | solution.py:300
  360.0 4.1 %copy.138 = f32[32,1,10240]{0,2,1:T(8,128)} copy(f32[32,1,10240]{2,1,0:T(1,128)S(1)} %all-to-all-done.5) | data formatting | bytes 2621440 | tf_op jit(solution)/shard_map/all_to_all | solution.py:300
  364.0 23.6 %convolution_bitcast_fusion.2 = f32[16,5,16,2,8,16]{5,0,4,2,1,3:T(8,128)S(1)} fusion(f32[5,16,8,16,32,1]{4,3,2,1,0,5:T(8,128)} %bitcast.222, s32[16,2]{0,1:T(2,128)S(1)} %copy.111, pred[16]{0:T(512)(128)(4,1)S(1)} %iota_compare_fusion.8), kind=kOutput, calls=%fused_computation.4 | convolution fusion | flops 125831168 | bytes 2621584 | tf_op jit(solution)/shard_map/dot_general | solution.py:301
  387.6 7.3 %copy.139 = f32[16,5,16,2,8,16]{5,4,3,2,0,1:T(8,128)} copy(f32[16,5,16,2,8,16]{5,0,4,2,1,3:T(8,128)S(1)} %convolution_bitcast_fusion.2) | data formatting | bytes 2621440 | tf_op jit(solution)/shard_map/transpose | solution.py:304
  394.9 10.3 %reshape.440 = f32[16,5,4096]{2,0,1:T(8,128)} reshape(f32[16,5,16,2,8,16]{5,4,3,2,0,1:T(8,128)} %copy.139) | data formatting | bytes 2621440 | tf_op jit(solution)/shard_map/reshape | solution.py:305
  (189 shorter events, 38.3 us)
Async XLA Ops:
  16.5 10.6 %copy-start.5 = (u32[256]{0:T(256)S(1)}, u32[256]{0:T(256)}, u32[]{:S(2)}) copy-start(u32[256]{0:T(256)} %constant.203) | copy-start | bytes 3076
  56.0 34.9 %all-to-all-start = ((f32[32,1,10240]{2,1,0:T(1,128)}), f32[32,1,10240]{2,1,0:T(1,128)S(1)}, u32[]{:S(2)}, u32[]{:S(2)}) async-start(f32[32,1,10240]{2,1,0:T(1,128)} %copy.113), calls=%async_computation | async-start | bytes 2621440 | tf_op jit(solution)/shard_map/all_to_all | solution.py:198
  122.8 5.1 %collective-permute-start = (f32[5,4,8,128]{3,2,1,0:T(8,128)S(1)}, f32[5,4,8,128]{3,2,1,0:T(8,128)S(1)}, u32[]{:S(2)}, u32[]{:S(2)}) collective-permute-start(f32[5,4,8,128]{3,2,1,0:T(8,128)S(1)} %get-tuple-element.79), channel_id=1, source_target_pairs={{0,32},{32,64},{64,96},{96,128},{128,160},{160,192},{192,224},{224... | collective-permute-start | bytes 245768 | tf_op jit(solution)/shard_map/ppermute | solution.py:26
  122.9 5.1 %collective-permute-start.1 = (f32[5,4,8,128]{3,2,1,0:T(8,128)S(1)}, f32[5,4,8,128]{3,2,1,0:T(8,128)S(1)}, u32[]{:S(2)}, u32[]{:S(2)}) collective-permute-start(f32[5,4,8,128]{3,2,1,0:T(8,128)S(1)} %get-tuple-element.78), channel_id=1, source_target_pairs={{32,0},{64,32},{96,64},{128,96},{160,128},{192,160},{224,192},{0,2... | collective-permute-start | bytes 245768 | tf_op jit(solution)/shard_map/ppermute | solution.py:29
  128.1 11.9 %collective-permute-start.3 = (f32[5,40,4,128]{3,2,1,0:T(4,128)S(1)}, f32[5,40,4,128]{3,2,1,0:T(4,128)S(1)}, u32[]{:S(2)}, u32[]{:S(2)}) collective-permute-start(f32[5,40,4,128]{3,2,1,0:T(4,128)S(1)} %get-tuple-element.74), channel_id=1, source_target_pairs={{1,0},{2,1},{3,2},{4,3},{5,4},{6,5},{7,6},{8,7},{9,8},{10,9},{11,1... | collective-permute-start | bytes 1228808 | tf_op jit(solution)/shard_map/ppermute | solution.py:29
  128.8 11.7 %collective-permute-start.2 = (f32[5,40,4,128]{3,2,1,0:T(4,128)S(1)}, f32[5,40,4,128]{3,2,1,0:T(4,128)S(1)}, u32[]{:S(2)}, u32[]{:S(2)}) collective-permute-start(f32[5,40,4,128]{3,2,1,0:T(4,128)S(1)} %get-tuple-element.73), channel_id=1, source_target_pairs={{0,1},{1,2},{2,3},{3,4},{4,5},{5,6},{6,7},{7,8},{8,9},{9,10},{10,1... | collective-permute-start | bytes 1228808 | tf_op jit(solution)/shard_map/ppermute | solution.py:26
  162.1 2.1 copy-start.2
  166.6 20.9 %all-to-all-start.1 = ((f32[32,1,2048]{2,1,0:T(1,128)}), f32[32,1,2048]{2,1,0:T(1,128)S(1)}, u32[]{:S(2)}, u32[]{:S(2)}) async-start(f32[32,1,2048]{2,1,0:T(1,128)} %reshape.458), calls=%async_computation.1 | async-start | bytes 524288 | tf_op jit(solution)/shard_map/all_to_all | solution.py:220
  196.5 12.2 %all-to-all-start.2 = ((f32[8,2,32,128]{3,2,1,0:T(8,128)}), f32[8,2,32,128]{3,2,1,0:T(8,128)S(1)}, u32[]{:S(2)}, u32[]{:S(2)}) async-start(f32[8,2,32,128]{3,2,1,0:T(8,128)} %maximum_bitcast_fusion.4), calls=%async_computation.2 | async-start | bytes 524288 | tf_op jit(solution)/shard_map/all_to_all | solution.py:231
  223.7 1.4 copy-start.1
  265.7 29.0 %all-to-all-start.4 = ((f32[32,3,2,8,128]{4,3,1,2,0:T(8,128)}), f32[32,3,2,8,128]{4,3,1,2,0:T(8,128)}, u32[]{:S(2)}, u32[]{:S(2)}) async-start(f32[32,3,2,8,128]{4,3,1,2,0:T(8,128)} %copy.130), calls=%async_computation.4 | async-start | bytes 1572864 | tf_op jit(solution)/shard_map/all_to_all | solution.py:286
  299.2 1.3 copy-start.3
  303.6 2.2 copy-start.4
  305.9 2.8 copy-start
  321.7 38.3 %all-to-all-start.5 = ((f32[32,1,10240]{2,1,0:T(1,128)}), f32[32,1,10240]{2,1,0:T(1,128)S(1)}, u32[]{:S(2)}, u32[]{:S(2)}) async-start(f32[32,1,10240]{2,1,0:T(1,128)} %copy.137), calls=%async_computation.5 | async-start | bytes 2621440 | tf_op jit(solution)/shard_map/all_to_all | solution.py:300

commit v2 on v1

v2 whole, which is shorter than its diff:
```python
import math

import jax
import jax.numpy as jnp
import numpy as np
from jax import lax
from jax.experimental import pallas as pl
from jax.experimental.pallas import tpu as pltpu
from jax.sharding import PartitionSpec as P

PE = 16
GX = 256
GY = 256
GZ = 128
ROWS = 8
COLS = 32
BX = GX // ROWS
BY = GY // COLS
CAP = 16
LINES = 16
BRICK = 5 * PE
HALO = 4

time_step = 0.03
four_pi_g = 10.0

PARAMS = pltpu.CompilerParams(vmem_limit_bytes=40 * 2**20)
VM = pl.BlockSpec(memory_space=pltpu.VMEM)
SM = pl.BlockSpec(memory_space=pltpu.SMEM)


def hartley(length):
    index = np.arange(length)
    angle = 2.0 * np.pi / length * (index[:, None] * index[None, :] % length)
    return ((np.cos(angle) + np.sin(angle)) / math.sqrt(length)).astype(np.float32)


def eigenvalues(length):
    return (-4.0 * np.sin(np.pi * np.arange(length) / length) ** 2).astype(np.float32)


def dot(left, right, dims=((1,), (0,))):
    return lax.dot_general(
        left,
        right,
        (dims, ((), ())),
        precision=lax.Precision.HIGHEST,
        preferred_element_type=jnp.float32,
    )


def swap_groups(arrays, group):
    count = len(arrays)
    lane = lax.broadcasted_iota(jnp.int32, arrays[0].shape, 1) // group
    arrays = list(arrays)
    distance = count // 2
    while distance:
        upper = (lane & distance) != 0
        for i in range(count):
            if i & distance:
                continue
            low, high = arrays[i], arrays[i + distance]
            arrays[i] = jnp.where(upper, pltpu.roll(high, distance * group, 1), low)
            arrays[i + distance] = jnp.where(
                upper, high, pltpu.roll(low, 128 - distance * group, 1)
            )
        distance //= 2
    return arrays


def pack_kernel(start_ref, fields_ref, out_ref):
    shift = start_ref[0]
    for q in range(5):
        for tile in range(2 * PE):
            a, half = tile // 2, tile % 2
            slots = fields_ref[q, :, tile * 128 : (tile + 1) * 128]
            turned = pltpu.roll(slots, shift, 0)
            out_ref[pl.ds(half * BRICK + q * PE + a, CAP, stride=2 * BRICK), :] = turned


def unpack_kernel(owner_ref, recv_ref, own_ref, xfirst_ref, xlast_ref, yfirst_ref, ylast_ref, flat_ref):
    for q in range(5):
        for xl in range(2):
            for part in range(2):
                rows = q * PE + part * 8
                lines = [
                    recv_ref[owner_ref[xl * 8 + zl], rows : rows + 8, :] for zl in range(8)
                ]
                for b, value in enumerate(swap_groups(lines, PE)):
                    base = (q * BX + xl * PE + part * 8) * BY + b
                    flat_ref[pl.ds(base, 8, stride=BY), :] = value
    block = flat_ref[...].reshape(5, BX, BY, GZ)
    own_ref[...] = block
    xfirst_ref[...] = block[:, :HALO]
    xlast_ref[...] = block[:, BX - HALO :]
    yfirst_ref[...] = block[:, :, :HALO]
    ylast_ref[...] = block[:, :, BY - HALO :]


def minmod(p, q):
    return jnp.maximum(jnp.minimum(p, q), 0.0) + jnp.minimum(jnp.maximum(p, q), 0.0)


def half_flux(states, direction, sign):
    density, energy = states[0], states[4]
    inverse = 1.0 / density
    velocity = 0.5 * states[1 + direction] * inverse
    squares = states[1] * states[1] + states[2] * states[2] + states[3] * states[3]
    pressure = 0.4 * energy - (0.2 * squares) * inverse
    pieces = [0.5 * states[1 + direction]]
    for component in range(3):
        term = states[1 + component] * velocity
        if component == direction:
            term = term + 0.5 * pressure
        pieces.append(term)
    pieces.append((energy + pressure) * velocity)
    if sign > 0:
        return [piece + 2.0 * state for piece, state in zip(pieces, states)]
    return [piece - 2.0 * state for piece, state in zip(pieces, states)]


def edge_terms(states, slopes, direction):
    halves = [0.5 * slope for slope in slopes]
    upper = half_flux([u + h for u, h in zip(states, halves)], direction, 1)
    lower = half_flux([u - h for u, h in zip(states, halves)], direction, -1)
    return upper, lower


def line_change(states, direction, axis):
    size = states[0].shape[axis]
    gaps = [pltpu.roll(u, size - 1, axis) - u for u in states]
    slopes = [minmod(pltpu.roll(g, 1, axis), g) for g in gaps]
    upper, lower = edge_terms(states, slopes, direction)
    faces = [u + pltpu.roll(w, size - 1, axis) for u, w in zip(upper, lower)]
    return [f - pltpu.roll(f, 1, axis) for f in faces]


def euler_stage(load, store, first_row, count, keep):
    def slopes_of(low, mid, high):
        return [minmod(b - a, c - b) for a, b, c in zip(low, mid, high)]

    cut = lambda states: [u[:keep] for u in states]
    r0, r1, r2, r3 = [cut(load(first_row + k)) for k in (-2, -1, 0, 1)]
    upper_prev, _ = edge_terms(r1, slopes_of(r0, r1, r2), 0)
    upper_now, lower_now = edge_terms(r2, slopes_of(r1, r2, r3), 0)
    face = [u + w for u, w in zip(upper_prev, lower_now)]

    def step(k, carry):
        face_low, upper_here = carry
        i = first_row + k
        here, above, far = load(i), cut(load(i + 1)), cut(load(i + 2))
        mine = cut(here)
        upper_next, lower_next = edge_terms(above, slopes_of(mine, above, far), 0)
        face_high = [u + w for u, w in zip(upper_here, lower_next)]
        change = [h - l for h, l in zip(face_high, face_low)]
        along_y = cut(line_change(here, 1, 0))
        along_z = line_change(mine, 2, 1)
        rate = [-(a + b + c) for a, b, c in zip(change, along_y, along_z)]
        store(i, mine, rate)
        return tuple(face_high), tuple(upper_next)

    lax.fori_loop(0, count, step, (tuple(face), tuple(upper_now)))


def euler_kernel(
    own_ref, xlow_ref, xhigh_ref, ylow_ref, yhigh_ref, clow_ref, chigh_ref, table_ref,
    stepped_ref, modes_ref, ext_ref, first_ref, flat_ref,
):
    low, high = slice(BY + HALO, BY + 2 * HALO), slice(BY, BY + HALO)
    inner = slice(HALO, HALO + BX)
    ext_ref[:, inner, 0:BY] = own_ref[...]
    ext_ref[:, 0:HALO, 0:BY] = xlow_ref[...]
    ext_ref[:, HALO + BX :, 0:BY] = xhigh_ref[...]
    ext_ref[:, inner, high] = yhigh_ref[...]
    ext_ref[:, inner, low] = ylow_ref[...]
    for part, ref in ((low, clow_ref), (high, chigh_ref)):
        corner = ref[...]
        ext_ref[:, 0:2, part] = corner[:, 0:2]
        ext_ref[:, 2:4, part] = corner[:, 0:2]
        ext_ref[:, HALO + BX : HALO + BX + 2, part] = corner[:, 2:4]
        ext_ref[:, HALO + BX + 2 :, part] = corner[:, 2:4]

    def load_ext(i):
        return [ext_ref[q, i] for q in range(5)]

    def store_first(i, states, rates):
        for q in range(5):
            first_ref[q, i] = states[q] + time_step * rates[q]

    euler_stage(load_ext, store_first, 2, BX + 4, BY + 2 * HALO)

    def load_first(i):
        return [first_ref[q, i] for q in range(5)]

    def store_stepped(i, states, rates):
        for q in range(5):
            second = states[q] + time_step * rates[q]
            value = 0.5 * ext_ref[q, i, 0:BY] + 0.5 * second
            stepped_ref[q, i - HALO] = value
            if q == 0:
                flat_ref[pl.ds(pl.multiple_of((i - HALO) * BY, BY), BY), :] = value

    euler_stage(load_first, store_stepped, HALO, BX, BY)
    density = jnp.concatenate(
        [flat_ref[pl.ds(b, BX, stride=BY), :] for b in range(BY)], axis=0
    )
    spread = dot(table_ref[...], density, ((1,), (1,)))
    modes_ref[pl.ds(0, 256, stride=2), :] = spread[:, :128]
    modes_ref[pl.ds(1, 256, stride=2), :] = spread[:, 128:]


def plane_kernel(place_ref, wave_ref, modes_ref, table_ref, eigx_ref, eigy_ref, out_ref, plane_ref, wide_ref):
    for high in range(2):
        for tile in range(2):
            lines = [
                modes_ref[pl.ds((high * 4 + r) * COLS * 2 + tile, COLS, stride=2), :]
                for r in range(4)
            ]
            for p, value in enumerate(swap_groups(lines, 32)):
                plane_ref[pl.ds(high * GY + tile * 4 + p, COLS, stride=BY), :] = value
    half = pl.multiple_of(place_ref[0] * 128, 128)
    table = table_ref[...]
    half_table = table_ref[pl.ds(half, 128), :]
    plane = jnp.concatenate([plane_ref[0:GY, :], plane_ref[GY:, :]], axis=1)
    spectrum = dot(dot(half_table, plane), table)
    eigen = eigx_ref[...] + eigy_ref[pl.ds(half, 128), :][:, 0:1] + wave_ref[0]
    flat = eigen >= 0.0
    green = jnp.where(flat, 0.0, four_pi_g / jnp.where(flat, -1.0, eigen))
    back = dot(spectrum * green, table)
    potential = dot(half_table, back, ((0,), (0,)))
    for high in range(2):
        base, side = high * (GY + 16), potential[:, high * 128 : high * 128 + 128]
        wide_ref[base + 8 : base + 8 + GY, :] = side
        wide_ref[base : base + 8, :] = side[GY - 8 :]
        wide_ref[base + 8 + GY : base + 16 + GY, :] = side[:8]

    def strip(row):
        return jnp.concatenate(
            [wide_ref[pl.ds(b + row, COLS, stride=BY), :] for b in (0, GY + 16)], axis=1
        )

    strips = [strip(8 + yl) for yl in range(BY)]
    below, above = strip(7), strip(16)
    lane = lax.broadcasted_iota(jnp.int32, (COLS, GX), 1) % 32
    sides = jnp.zeros((COLS, GX), jnp.float32)
    for yl in range(BY):
        sides = jnp.where(lane == yl, pltpu.roll(strips[yl], 1 + yl, 1), sides)
        sides = jnp.where(lane == 8 + yl, pltpu.roll(strips[yl], GX - 24 + yl, 1), sides)
    strips = strips + [below, above, sides, sides]
    for high in range(2):
        for quad in range(3):
            lines = [s[:, high * 128 : high * 128 + 128] for s in strips[quad * 4 : quad * 4 + 4]]
            for p, value in enumerate(swap_groups(lines, 32)):
                out_ref[pl.ds((high * 4 + p) * COLS * 3 + quad, COLS, stride=3), :] = value


def kick_kernel(owner_ref, stepped_ref, modes_ref, table_ref, out_ref, phi_ref, kicked_ref):
    table = table_ref[...]
    parts = []
    for quad in range(3):
        block = modes_ref[pl.ds(quad, 256, stride=3), :]
        parts.append(dot(block, table, ((0,), (0,))))
    for yl in range(BY):
        phi_ref[pl.ds(BY + yl, BX, stride=BY), :] = parts[yl // 4][(yl % 4) * 32 : (yl % 4) * 32 + 32]
    phi_ref[0:BY, :] = parts[2][64 : 64 + BY]
    phi_ref[BY + BX * BY :, :] = parts[2][64 + BY : 64 + 2 * BY]
    phi = phi_ref[...].reshape(BX + 2, BY, GZ)
    mid = phi[1 : 1 + BX]
    below = parts[2][0:32].reshape(BX, 1, GZ)
    above = parts[2][32:64].reshape(BX, 1, GZ)
    grad_x = 0.5 * (phi[2:] - phi[:BX])
    lower = jnp.concatenate([below, mid[:, : BY - 1]], axis=1)
    upper = jnp.concatenate([mid[:, 1:], above], axis=1)
    grad_y = 0.5 * (upper - lower)
    grad_z = 0.5 * (pltpu.roll(mid, GZ - 1, 2) - pltpu.roll(mid, 1, 2))
    grads = (grad_x, grad_y, grad_z)
    density = stepped_ref[0]
    momenta = [stepped_ref[1 + d] for d in range(3)]
    work = momenta[0] * grad_x + momenta[1] * grad_y + momenta[2] * grad_z
    cells = BX * BY
    kicked_ref[0:cells, :] = density.reshape(cells, GZ)
    for d in range(3):
        value = momenta[d] - time_step * density * grads[d]
        kicked_ref[(1 + d) * cells : (2 + d) * cells, :] = value.reshape(cells, GZ)
    kicked_ref[4 * cells :, :] = (stepped_ref[4] - time_step * work).reshape(cells, GZ)
    for q in range(5):
        for xl in range(2):
            for part in range(2):
                base = (q * BX + xl * PE + part * 8) * BY
                lines = [kicked_ref[pl.ds(base + b, 8, stride=BY), :] for b in range(BY)]
                rows = q * PE + part * 8
                for zl, value in enumerate(swap_groups(lines, PE)):
                    out_ref[owner_ref[xl * 8 + zl], rows : rows + 8, :] = value


def spread_kernel(place_ref, recv_ref, out_ref):
    shift = place_ref[0]
    live = lax.broadcasted_iota(jnp.int32, (CAP, 128), 0) < place_ref[1]
    for q in range(5):
        for tile in range(2 * PE):
            a, half = tile // 2, tile % 2
            lines = recv_ref[pl.ds(half * BRICK + q * PE + a, CAP, stride=2 * BRICK), :]
            turned = pltpu.roll(lines, shift, 0)
            out_ref[q, :, tile * 128 : (tile + 1) * 128] = jnp.where(live, turned, 0.0)


def call(kernel, outs, ins, scratch=()):
    shapes = [jax.ShapeDtypeStruct(s, jnp.float32) for s in outs]
    many = len(outs) > 1
    return pl.pallas_call(
        kernel,
        out_shape=tuple(shapes) if many else shapes[0],
        in_specs=[SM if i in ins[1] else VM for i in range(ins[0])],
        out_specs=tuple([VM] * len(outs)) if many else VM,
        scratch_shapes=[pltpu.VMEM(s, jnp.float32) for s in scratch],
        compiler_params=PARAMS,
    )


def gather_counts(counts):
    return lax.all_gather(counts, "col", axis=1, tiled=True).reshape(COLS)


def on_device(fields, counts):
    my_row = lax.axis_index("row")
    my_column = lax.axis_index("col")
    row_counts = gather_counts(counts)
    column_ids = jnp.arange(COLS, dtype=jnp.int32)
    starts = jnp.sum(
        jnp.where(column_ids[None, :] < column_ids[:, None], row_counts[None, :], 0), axis=1
    )
    own_start = jnp.sum(jnp.where(column_ids < my_column, row_counts, 0))
    y_patch = my_column // 2
    wanted = jnp.arange(LINES, dtype=jnp.int32) * 16 + y_patch
    owners = jnp.sum((starts[None, :] <= wanted[:, None]).astype(jnp.int32), axis=1) - 1
    turn = own_start % CAP

    sent = call(pack_kernel, [(COLS * BRICK, 128)], (2, (0,)))(
        turn.reshape(1), fields.transpose(1, 0, 2)
    )
    arrived = lax.all_to_all(
        sent.reshape(COLS, BRICK, 128), "col", split_axis=0, concat_axis=0, tiled=True
    )
    own, xfirst, xlast, yfirst, ylast = call(
        unpack_kernel,
        [
            (5, BX, BY, GZ),
            (5, HALO, BY, GZ),
            (5, HALO, BY, GZ),
            (5, BX, HALO, GZ),
            (5, BX, HALO, GZ),
        ],
        (2, (0,)),
        [(5 * BX * BY, GZ)],
    )(owners, arrived)

    def ring(count, step):
        return [(i, (i + step) % count) for i in range(count)]

    xlow = lax.ppermute(xlast, "row", ring(ROWS, 1))
    xhigh = lax.ppermute(xfirst, "row", ring(ROWS, -1))
    ylow = lax.ppermute(ylast, "col", ring(COLS, 1))
    yhigh = lax.ppermute(yfirst, "col", ring(COLS, -1))
    edges = jnp.concatenate([xlow[:, 2:4], xhigh[:, 0:2]], axis=1)
    clow = lax.ppermute(edges[:, :, BY - HALO :], "col", ring(COLS, 1))
    chigh = lax.ppermute(edges[:, :, :HALO], "col", ring(COLS, -1))

    table_z = hartley(GZ)
    table_x = hartley(GX)
    modes_of = np.arange(256) % GZ
    stepped, modes = call(
        euler_kernel,
        [(5, BX, BY, GZ), (512, 128)],
        (8, ()),
        [(5, BX + 2 * HALO, BY + 2 * HALO, GZ), (5, BX + 2 * HALO, BY + 2 * HALO, GZ), (BX * BY, GZ)],
    )(own, xlow, xhigh, ylow, yhigh, clow, chigh, jnp.asarray(table_z[modes_of]))
    planes = lax.all_to_all(
        modes.reshape(256, 2, 128), ("row", "col"), split_axis=0, concat_axis=0, tiled=True
    )
    place = my_row * COLS + my_column
    wave_z = place % GZ
    eig = eigenvalues(GX)
    eig_z = -4.0 * jnp.sin((math.pi / GZ) * wave_z.astype(jnp.float32)) ** 2
    strips = call(plane_kernel, [(768, 128)], (6, (0, 1)), [(2 * GY, 128), (2 * (GY + 16), 128)])(
        (place // GZ).reshape(1),
        eig_z.reshape(1),
        planes.reshape(512, 128),
        jnp.asarray(table_x),
        jnp.asarray(eig[None, :]),
        jnp.asarray(np.broadcast_to(eig[:, None], (GX, 128))),
    )
    strips = lax.all_to_all(
        strips.reshape(256, 3, 128), ("row", "col"), split_axis=0, concat_axis=0, tiled=True
    )
    returned = call(
        kick_kernel,
        [(COLS, BRICK, 128)],
        (4, (0,)),
        [((BX + 2) * BY, GZ), (5 * BX * BY, GZ)],
    )(owners, stepped, strips.reshape(768, 128), jnp.asarray(table_z[modes_of]))
    came_back = lax.all_to_all(returned, "col", split_axis=0, concat_axis=0, tiled=True)
    home = jnp.stack([(CAP - turn) % CAP, counts[0, 0]])
    result = call(spread_kernel, [(5, CAP, PE * PE * PE)], (2, (0,)))(
        home, came_back.reshape(COLS * BRICK, 128)
    )
    return result.transpose(1, 0, 2)


def solution(mesh):
    return jax.shard_map(
        on_device,
        mesh=mesh,
        in_specs=(P(("row", "col"), None, None), P("row", "col")),
        out_specs=P(("row", "col"), None, None),
        check_vma=False,
    )
```

time: 412 us -> 205 us (0.50); the launches traced: 405 us -> 205 us
  local copies, waits for them, and re-layouts: 113 us -> 3.71 us
  matrix products: 70.7 us -> 0 us
  Pallas kernels: 0 us -> 34.1 us
  other arithmetic: 30.5 us -> 1.03 us
  waiting for transfers between devices: 112 us -> 82.9 us
  blocking collectives: 39.2 us -> 48.5 us
  starting transfers between devices: 38.7 us -> 31.8 us
    dot_general x24 -> x0, matrix products: 70.7 us -> none  [the longest x1 23.6 us: on_device(): jnp.matmul(send_select.T, came_back, precision=lax.Precision.HIGHEST)]
    reshape x11 -> x2, local copies, waits for them, and re-layouts: 52.7 us -> 0.34 us  [the longest x1 0.18 us: on_device(): strips.reshape(768, 128)]
    pallas_call x0 -> x6, Pallas kernels: none -> 34.1 us  [the longest x1 22 us: on_device(): call(euler_kernel, [(5, BX, BY, GZ), (512, 128)], (8, ()), [(5, BX + 2 *...]
    all_to_all x5 -> x3, waiting for transfers between devices: 99.9 us -> 76.3 us  [the longest x1 33.3 us: on_device(): lax.all_to_all(returned, 'col', split_axis=0, concat_axis=0, tiled=True)]
    reshape x0 -> x1, blocking collectives: none -> 22.5 us  [gather_counts(): return lax.all_gather(counts, 'col', axis=1, tiled=True).reshape(COLS)]
    unnamed x1 -> x0, blocking collectives: 22.5 us -> none
    transpose x6 -> x0, local copies, waits for them, and re-layouts: 17.3 us -> none  [the longest x1 7.26 us: on_device(): return slot_bricks.reshape(capacity, per_patch, 5, PE, brick_y, PE).trans...]
    all_to_all x6 -> x0, local copies, waits for them, and re-layouts: 13.8 us -> none  [the longest x2 6.46 us: on_device(): lax.all_to_all(send_buffer, 'col', split_axis=0, concat_axis=0, tiled=True)]
  transfers between devices with their start and end apart: 9 -> 9, of which waited for: 8 -> 6; matrix products, arithmetic and copies ran while one was open for 1% -> 0% of each run, Pallas kernels for 0% -> 0%
where the time goes in v2:
time: 205 us
  waiting for transfers between devices  82.9 us (40%)
  blocking collectives  48.5 us (24%)
  Pallas kernels  34.1 us (17%)
  starting transfers between devices  31.8 us (16%)
  local copies, waits for them, and re-layouts  3.71 us (2%)
  between operations  2.88 us (1%)
    all_to_all x1, waiting for transfers between devices, on_device(): lax.all_to_all(returned, 'col', split_axis=0, concat_axis=0, tiled=True)  33.3 us
    all_to_all x1, waiting for transfers between devices, on_device(): lax.all_to_all(sent.reshape(COLS, BRICK, 128), 'col', split_axis=0, conca...  29.1 us
    all_to_all x1, blocking collectives, on_device(): lax.all_to_all(strips.reshape(256, 3, 128), ('row', 'col'), split_axis=0,...  26 us
    reshape x1, blocking collectives, gather_counts(): return lax.all_gather(counts, 'col', axis=1, tiled=True).reshape(COLS)  22.5 us
    pallas_call x1, Pallas kernels, on_device(): call(euler_kernel, [(5, BX, BY, GZ), (512, 128)], (8, ()), [(5, BX + 2 *...  22 us
    all_to_all x1, waiting for transfers between devices, on_device(): lax.all_to_all(modes.reshape(256, 2, 128), ('row', 'col'), split_axis=0,...  13.9 us
    all_to_all x1, starting transfers between devices, on_device(): lax.all_to_all(modes.reshape(256, 2, 128), ('row', 'col'), split_axis=0,...  13.8 us
    all_to_all x1, starting transfers between devices, on_device(): lax.all_to_all(returned, 'col', split_axis=0, concat_axis=0, tiled=True)  5.96 us
  transfers between devices with their start and end apart: 9, of which 6 were waited for; matrix products, arithmetic and copies ran while one was open for 0% of the time, Pallas kernels for 0%

profile of v2, /device:TPU:2, one launch (start us, length us, event | category | flops | bytes accessed | tf_op | source)
XLA Modules:
  0.0 204.8 jit_solution(15908875128763073817)
XLA Ops:
  0.7 1.3 dynamic-slice
  1.9 0.7 bitcast_dynamic-update-slice_fusion
  2.6 22.5 %all-reduce = s32[32]{0:T(128)S(1)} all-reduce(s32[32]{0:T(128)S(1)} %bitcast_dynamic-update-slice_fusion), channel_id=1, replica_groups=mesh['row'=8,'col'=32] {'col'}, use_global_device_ids=true, to_apply=%add | all-reduce | flops 32 | bytes 256 | tf_op jit(solution)/shard_map/reshape | solution.py:321
  25.1 0.6 fusion.1
  27.7 0.0 copy-start
  27.7 1.3 copy-done
  29.0 2.1 %shard_map.73 = f32[2560,128]{1,0:T(8,128)} custom-call(s32[1]{0:T(128)} %bitcast.3.start_ref, f32[5,16,4096]{2,1,0:T(8,128)S(1)} %bitcast.15), custom_call_target="tpu_custom_call" | custom-call | tf_op jit(solution)/shard_map/pallas_call | solution.py:338
  31.1 5.3 %all-to-all-start = ((f32[32,80,128]{2,1,0:T(8,128)}), f32[32,80,128]{2,1,0:T(8,128)S(1)}, u32[]{:S(2)}, u32[]{:S(2)}) async-start(f32[32,80,128]{2,1,0:T(8,128)} %bitcast.5), calls=%async_computation | async-start | bytes 2621440 | tf_op jit(solution)/shard_map/all_to_all | solution.py:341
  36.5 0.0 copy-start.1
  36.5 0.1 select_reduce_fusion
  36.6 0.2 convert_reduce_fusion
  36.8 29.1 %all-to-all-done.recv_ref = f32[32,80,128]{2,1,0:T(8,128)S(1)} async-done(((f32[32,80,128]{2,1,0:T(8,128)}), f32[32,80,128]{2,1,0:T(8,128)S(1)}, u32[]{:S(2)}, u32[]{:S(2)}) %all-to-all-start) | async-done | bytes 1310752 | tf_op jit(solution)/shard_map/all_to_all | solution.py:341
  65.9 2.7 %shard_map.74 = (f32[5,32,8,128]{3,2,1,0:T(8,128)S(1)}, f32[5,4,8,128]{3,2,1,0:T(8,128)S(1)}, f32[5,4,8,128]{3,2,1,0:T(8,128)S(1)}, f32[5,32,4,128]{3,2,1,0:T(4,128)S(1)}, f32[5,32,4,128]{3,2,1,0:T(4,128)S(1)}) custom-call(s32[16]{0:T(128)S(1)} %broadcast_add_fusion.owner_ref, f32[32,80,128]{2,1,0:T(8,128)S(1)} %all-to-all-done.recv_ref), custom_call_target="tpu_custom_call" | custom-call | tf_op jit(solution)/shard_map/pallas_call | solution.py:344
  68.5 0.0 copy-start.4
  68.6 1.5 collective-permute-start.2
  70.1 0.6 collective-permute-start.3
  70.7 0.0 collective-permute-start.1
  70.7 0.5 collective-permute-start
  71.2 1.6 collective-permute-done.1.xhigh_ref
  72.7 0.0 copy-start.2
  72.7 0.0 copy-start.3
  72.7 3.2 %collective-permute-done.xlow_ref = f32[5,4,8,128]{3,2,1,0:T(8,128)S(1)} collective-permute-done((f32[5,4,8,128]{3,2,1,0:T(8,128)S(1)}, f32[5,4,8,128]{3,2,1,0:T(8,128)S(1)}, u32[]{:S(2)}, u32[]{:S(2)}) %collective-permute-start) | collective-permute-done | bytes 81952 | tf_op jit(solution)/shard_map/ppermute | solution.py:360
  75.9 1.5 collective-permute-start.4
  77.5 2.5 %collective-permute-start.5 = (f32[5,4,4,128]{3,2,1,0:T(4,128)S(1)}, f32[5,4,4,128]{3,2,1,0:T(4,128)S(1)}, u32[]{:S(2)}, u32[]{:S(2)}) collective-permute-start(f32[5,4,4,128]{3,2,1,0:T(4,128)S(1)} %get-tuple-element.19), channel_id=1, source_target_pairs={{0,31},{1,0},{2,1},{3,2},{4,3},{5,4},{6,5},{7,6},{8,7},{9,8},{10,9... | collective-permute-start | bytes 122888 | tf_op jit(solution)/shard_map/ppermute | solution.py:366
  80.0 1.9 collective-permute-done.4.clow_ref
  81.9 0.0 collective-permute-done.5.chigh_ref
  81.9 0.0 collective-permute-done.2.ylow_ref
  81.9 0.0 collective-permute-done.3.yhigh_ref
  81.9 0.0 copy-done.1
  81.9 22.0 %shard_map.75 = (f32[5,32,8,128]{3,2,1,0:T(8,128)S(1)}, f32[512,128]{1,0:T(8,128)}) custom-call(f32[5,32,8,128]{3,2,1,0:T(8,128)S(1)} %get-tuple-element.12.own_ref, f32[5,4,8,128]{3,2,1,0:T(8,128)S(1)} %collective-permute-done.xlow_ref, f32[5,4,8,128]{3,2,1,0:T(8,128)S(1)} %collective-permute-done.1.xhigh_ref, ...), custom_call_target="tpu_custom_call" | custom-call | tf_op jit(solution)/shard_map/pallas_call | solution.py:371
  103.9 13.8 %all-to-all-start.1 = ((f32[256,2,128]{2,1,0:T(2,128)}), f32[256,2,128]{2,1,0:T(2,128)S(1)}, u32[]{:S(2)}, u32[]{:S(2)}) async-start(f32[256,2,128]{2,1,0:T(2,128)} %bitcast.8), calls=%async_computation.1 | async-start | bytes 524288 | tf_op jit(solution)/shard_map/all_to_all | solution.py:377
  117.8 13.9 %all-to-all-done.1 = f32[256,2,128]{2,1,0:T(2,128)S(1)} async-done(((f32[256,2,128]{2,1,0:T(2,128)}), f32[256,2,128]{2,1,0:T(2,128)S(1)}, u32[]{:S(2)}, u32[]{:S(2)}) %all-to-all-start.1) | async-done | bytes 262176 | tf_op jit(solution)/shard_map/all_to_all | solution.py:377
  131.7 0.0 copy-done.4
  131.7 0.1 jit_solution_.3.eigy_ref
  131.8 0.0 copy-done.2
  131.9 0.0 copy-done.3
  131.9 2.0 shard_map.76
  133.9 0.2 reshape.43
  134.1 26.0 %all_to_all.20 = f32[256,3,128]{2,1,0:T(4,128)S(1)} all-to-all(f32[256,3,128]{2,1,0:T(4,128)S(1)} %reshape.43), channel_id=1, replica_groups=mesh['row'=8,'col'=32] {'row','col'}, dimensions={0} | all-to-all | bytes 786432 | tf_op jit(solution)/shard_map/all_to_all | solution.py:392
  160.0 0.2 reshape.44.modes_ref
  160.2 2.9 %shard_map.77 = f32[32,80,128]{2,1,0:T(8,128)} custom-call(s32[16]{0:T(128)S(1)} %broadcast_add_fusion.owner_ref, f32[5,32,8,128]{3,2,1,0:T(8,128)S(1)} %get-tuple-element.17.stepped_ref, f32[768,128]{1,0:T(8,128)S(1)} %reshape.44.modes_ref, f32[256,128]{1,0:T(8,128)S(1)} %copy-done.1), custom_call_target="tpu_custom_call" | custom-call | tf_op jit(solution)/shard_map/pallas_call | solution.py:395
  163.1 6.0 %all-to-all-start.3 = ((f32[32,80,128]{2,1,0:T(8,128)}), f32[32,80,128]{2,1,0:T(8,128)S(1)}, u32[]{:S(2)}, u32[]{:S(2)}) async-start(f32[32,80,128]{2,1,0:T(8,128)} %shard_map.77), calls=%async_computation.3 | async-start | bytes 2621440 | tf_op jit(solution)/shard_map/all_to_all | solution.py:401
  169.1 0.1 pad_add_fusion.place_ref
  169.2 33.3 %all-to-all-done.3 = f32[32,80,128]{2,1,0:T(8,128)S(1)} async-done(((f32[32,80,128]{2,1,0:T(8,128)}), f32[32,80,128]{2,1,0:T(8,128)S(1)}, u32[]{:S(2)}, u32[]{:S(2)}) %all-to-all-start.3) | async-done | bytes 1310752 | tf_op jit(solution)/shard_map/all_to_all | solution.py:401
  202.5 2.4 %shard_map.78 = f32[5,16,4096]{2,1,0:T(8,128)} custom-call(s32[2]{0:T(128)S(1)} %pad_add_fusion.place_ref, f32[2560,128]{1,0:T(8,128)S(1)} %bitcast.14), custom_call_target="tpu_custom_call" | custom-call | tf_op jit(solution)/shard_map/pallas_call | solution.py:403
  (6 shorter events, 0.0 us)
Async XLA Ops:
  27.7 1.3 copy-start
  31.1 34.7 %all-to-all-start = ((f32[32,80,128]{2,1,0:T(8,128)}), f32[32,80,128]{2,1,0:T(8,128)S(1)}, u32[]{:S(2)}, u32[]{:S(2)}) async-start(f32[32,80,128]{2,1,0:T(8,128)} %bitcast.5), calls=%async_computation | async-start | bytes 2621440 | tf_op jit(solution)/shard_map/all_to_all | solution.py:341
  36.5 45.4 %copy-start.1 = (f32[256,128]{1,0:T(8,128)S(1)}, f32[256,128]{1,0:T(8,128)}, u32[]{:S(2)}) copy-start(f32[256,128]{1,0:T(8,128)} %constant.76.clone.table_ref) | copy-start | bytes 393220
  68.5 63.2 %copy-start.4 = (f32[256]{0:T(256)S(1)}, f32[256]{0:T(256)}, u32[]{:S(2)}) copy-start(f32[256]{0:T(256)} %constant.79.clone) | copy-start | bytes 3076
  68.6 13.3 %collective-permute-start.2 = (f32[5,32,4,128]{3,2,1,0:T(4,128)S(1)}, f32[5,32,4,128]{3,2,1,0:T(4,128)S(1)}, u32[]{:S(2)}, u32[]{:S(2)}) collective-permute-start(f32[5,32,4,128]{3,2,1,0:T(4,128)S(1)} %get-tuple-element.15), channel_id=1, source_target_pairs={{0,1},{1,2},{2,3},{3,4},{4,5},{5,6},{6,7},{7,8},{8,9},{9,10},{10,1... | collective-permute-start | bytes 983048 | tf_op jit(solution)/shard_map/ppermute | solution.py:362
  70.1 11.8 %collective-permute-start.3 = (f32[5,32,4,128]{3,2,1,0:T(4,128)S(1)}, f32[5,32,4,128]{3,2,1,0:T(4,128)S(1)}, u32[]{:S(2)}, u32[]{:S(2)}) collective-permute-start(f32[5,32,4,128]{3,2,1,0:T(4,128)S(1)} %get-tuple-element.16), channel_id=1, source_target_pairs={{0,31},{1,0},{2,1},{3,2},{4,3},{5,4},{6,5},{7,6},{8,7},{9,8},{10,9... | collective-permute-start | bytes 983048 | tf_op jit(solution)/shard_map/ppermute | solution.py:363
  70.7 2.1 %collective-permute-start.1 = (f32[5,4,8,128]{3,2,1,0:T(8,128)S(1)}, f32[5,4,8,128]{3,2,1,0:T(8,128)S(1)}, u32[]{:S(2)}, u32[]{:S(2)}) collective-permute-start(f32[5,4,8,128]{3,2,1,0:T(8,128)S(1)} %get-tuple-element.14), channel_id=1, source_target_pairs={{0,224},{32,0},{64,32},{96,64},{128,96},{160,128},{192,160},{224,1... | collective-permute-start | bytes 245768 | tf_op jit(solution)/shard_map/ppermute | solution.py:361
  70.7 5.2 %collective-permute-start = (f32[5,4,8,128]{3,2,1,0:T(8,128)S(1)}, f32[5,4,8,128]{3,2,1,0:T(8,128)S(1)}, u32[]{:S(2)}, u32[]{:S(2)}) collective-permute-start(f32[5,4,8,128]{3,2,1,0:T(8,128)S(1)} %get-tuple-element.13), channel_id=1, source_target_pairs={{0,32},{32,64},{64,96},{96,128},{128,160},{160,192},{192,224},{224... | collective-permute-start | bytes 245768 | tf_op jit(solution)/shard_map/ppermute | solution.py:360
  72.7 59.1 %copy-start.2 = (f32[256,256]{1,0:T(8,128)S(1)}, f32[256,256]{1,0:T(8,128)}, u32[]{:S(2)}) copy-start(f32[256,256]{1,0:T(8,128)} %constant.77.clone.table_ref) | copy-start | bytes 786436
  72.7 59.1 %copy-start.3 = (f32[1,256]{1,0:T(1,128)S(1)}, f32[1,256]{1,0:T(1,128)}, u32[]{:S(2)}) copy-start(f32[1,256]{1,0:T(1,128)} %constant.78.clone.eigx_ref) | copy-start | bytes 3076
  75.9 6.0 %collective-permute-start.4 = (f32[5,4,4,128]{3,2,1,0:T(4,128)S(1)}, f32[5,4,4,128]{3,2,1,0:T(4,128)S(1)}, u32[]{:S(2)}, u32[]{:S(2)}) collective-permute-start(f32[5,4,4,128]{3,2,1,0:T(4,128)S(1)} %get-tuple-element.20), channel_id=1, source_target_pairs={{0,1},{1,2},{2,3},{3,4},{4,5},{5,6},{6,7},{7,8},{8,9},{9,10},{10,1... | collective-permute-start | bytes 122888 | tf_op jit(solution)/shard_map/ppermute | solution.py:365
  77.5 4.4 %collective-permute-start.5 = (f32[5,4,4,128]{3,2,1,0:T(4,128)S(1)}, f32[5,4,4,128]{3,2,1,0:T(4,128)S(1)}, u32[]{:S(2)}, u32[]{:S(2)}) collective-permute-start(f32[5,4,4,128]{3,2,1,0:T(4,128)S(1)} %get-tuple-element.19), channel_id=1, source_target_pairs={{0,31},{1,0},{2,1},{3,2},{4,3},{5,4},{6,5},{7,6},{8,7},{9,8},{10,9... | collective-permute-start | bytes 122888 | tf_op jit(solution)/shard_map/ppermute | solution.py:366
  103.9 27.9 %all-to-all-start.1 = ((f32[256,2,128]{2,1,0:T(2,128)}), f32[256,2,128]{2,1,0:T(2,128)S(1)}, u32[]{:S(2)}, u32[]{:S(2)}) async-start(f32[256,2,128]{2,1,0:T(2,128)} %bitcast.8), calls=%async_computation.1 | async-start | bytes 524288 | tf_op jit(solution)/shard_map/all_to_all | solution.py:377
  163.1 39.3 %all-to-all-start.3 = ((f32[32,80,128]{2,1,0:T(8,128)}), f32[32,80,128]{2,1,0:T(8,128)S(1)}, u32[]{:S(2)}, u32[]{:S(2)}) async-start(f32[32,80,128]{2,1,0:T(8,128)} %shard_map.77), calls=%async_computation.3 | async-start | bytes 2621440 | tf_op jit(solution)/shard_map/all_to_all | solution.py:401

commit v3 on v2

--- a/solution.py
+++ b/solution.py
@@ -20,6 +20,7 @@
 LINES = 16
 BRICK = 5 * PE
 HALO = 4
+CORNERS = ((1, 1), (-1, 1), (1, -1), (-1, -1))
 
 time_step = 0.03
 four_pi_g = 10.0
@@ -78,7 +79,10 @@
             out_ref[pl.ds(half * BRICK + q * PE + a, CAP, stride=2 * BRICK), :] = turned
 
 
-def unpack_kernel(owner_ref, recv_ref, own_ref, xfirst_ref, xlast_ref, yfirst_ref, ylast_ref, flat_ref):
+def unpack_kernel(
+    owner_ref, recv_ref, own_ref, xfirst_ref, xlast_ref, yfirst_ref, ylast_ref, *rest
+):
+    corner_refs, flat_ref = rest[:4], rest[4]
     for q in range(5):
         for xl in range(2):
             for part in range(2):
@@ -95,6 +99,9 @@
     xlast_ref[...] = block[:, BX - HALO :]
     yfirst_ref[...] = block[:, :, :HALO]
     ylast_ref[...] = block[:, :, BY - HALO :]
+    for ref, (row_step, col_step) in zip(corner_refs, CORNERS):
+        part = block[:, BX - 2 :] if row_step > 0 else block[:, :2]
+        ref[...] = part[:, :, BY - HALO :] if col_step > 0 else part[:, :, :HALO]
 
 
 def minmod(p, q):
@@ -163,7 +170,7 @@
 
 
 def euler_kernel(
-    own_ref, xlow_ref, xhigh_ref, ylow_ref, yhigh_ref, clow_ref, chigh_ref, table_ref,
+    own_ref, xlow_ref, xhigh_ref, ylow_ref, yhigh_ref, c0_ref, c1_ref, c2_ref, c3_ref, table_ref,
     stepped_ref, modes_ref, ext_ref, first_ref, flat_ref,
 ):
     low, high = slice(BY + HALO, BY + 2 * HALO), slice(BY, BY + HALO)
@@ -173,12 +180,12 @@
     ext_ref[:, HALO + BX :, 0:BY] = xhigh_ref[...]
     ext_ref[:, inner, high] = yhigh_ref[...]
     ext_ref[:, inner, low] = ylow_ref[...]
-    for part, ref in ((low, clow_ref), (high, chigh_ref)):
+    for ref, (row_step, col_step) in zip((c0_ref, c1_ref, c2_ref, c3_ref), CORNERS):
+        part = low if col_step > 0 else high
         corner = ref[...]
-        ext_ref[:, 0:2, part] = corner[:, 0:2]
-        ext_ref[:, 2:4, part] = corner[:, 0:2]
-        ext_ref[:, HALO + BX : HALO + BX + 2, part] = corner[:, 2:4]
-        ext_ref[:, HALO + BX + 2 :, part] = corner[:, 2:4]
+        outer = 0 if row_step > 0 else HALO + BX
+        ext_ref[:, outer : outer + 2, part] = corner
+        ext_ref[:, outer + 2 : outer + 4, part] = corner
 
     def load_ext(i):
         return [ext_ref[q, i] for q in range(5)]
@@ -317,14 +324,30 @@
     )
 
 
-def gather_counts(counts):
-    return lax.all_gather(counts, "col", axis=1, tiled=True).reshape(COLS)
+def ring(count, step):
+    return [(i, (i + step) % count) for i in range(count)]
+
+
+def gather_counts(counts, column):
+    own = counts.reshape(1)
+    inner, outer = column % 4, column // 4
+    quad = jnp.arange(4, dtype=jnp.int32)
+    four = jnp.where(quad == inner, own, 0)
+    for k in range(1, 4):
+        pairs = [(c, c // 4 * 4 + (c + k) % 4) for c in range(COLS)]
+        four = jnp.where(quad == (inner - k) % 4, lax.ppermute(own, "col", pairs), four)
+    groups = jnp.arange(8, dtype=jnp.int32)[:, None]
+    every = jnp.where(groups == outer, four[None, :], 0)
+    for k in range(1, 8):
+        moved = lax.ppermute(four, "col", ring(COLS, 4 * k))
+        every = jnp.where(groups == (outer - k) % 8, moved[None, :], every)
+    return every.reshape(COLS)
 
 
 def on_device(fields, counts):
     my_row = lax.axis_index("row")
     my_column = lax.axis_index("col")
-    row_counts = gather_counts(counts)
+    row_counts = gather_counts(counts, my_column)
     column_ids = jnp.arange(COLS, dtype=jnp.int32)
     starts = jnp.sum(
         jnp.where(column_ids[None, :] < column_ids[:, None], row_counts[None, :], 0), axis=1
@@ -341,7 +364,7 @@
     arrived = lax.all_to_all(
         sent.reshape(COLS, BRICK, 128), "col", split_axis=0, concat_axis=0, tiled=True
     )
-    own, xfirst, xlast, yfirst, ylast = call(
+    own, xfirst, xlast, yfirst, ylast, *edges = call(
         unpack_kernel,
         [
             (5, BX, BY, GZ),
@@ -349,21 +372,28 @@
             (5, HALO, BY, GZ),
             (5, BX, HALO, GZ),
             (5, BX, HALO, GZ),
-        ],
+        ]
+        + [(5, 2, HALO, GZ)] * 4,
         (2, (0,)),
         [(5 * BX * BY, GZ)],
     )(owners, arrived)
 
-    def ring(count, step):
-        return [(i, (i + step) % count) for i in range(count)]
+    def diagonal(row_step, col_step):
+        return [
+            (r * COLS + c, (r + row_step) % ROWS * COLS + (c + col_step) % COLS)
+            for r in range(ROWS)
+            for c in range(COLS)
+        ]
 
     xlow = lax.ppermute(xlast, "row", ring(ROWS, 1))
     xhigh = lax.ppermute(xfirst, "row", ring(ROWS, -1))
     ylow = lax.ppermute(ylast, "col", ring(COLS, 1))
     yhigh = lax.ppermute(yfirst, "col", ring(COLS, -1))
-    edges = jnp.concatenate([xlow[:, 2:4], xhigh[:, 0:2]], axis=1)
-    clow = lax.ppermute(edges[:, :, BY - HALO :], "col", ring(COLS, 1))
-    chigh = lax.ppermute(edges[:, :, :HALO], "col", ring(COLS, -1))
+    both = ("row", "col")
+    corners = [
+        lax.ppermute(corner, both, diagonal(row_step, col_step))
+        for corner, (row_step, col_step) in zip(edges, CORNERS)
+    ]
 
     table_z = hartley(GZ)
     table_x = hartley(GX)
@@ -371,9 +401,9 @@
     stepped, modes = call(
         euler_kernel,
         [(5, BX, BY, GZ), (512, 128)],
-        (8, ()),
+        (10, ()),
         [(5, BX + 2 * HALO, BY + 2 * HALO, GZ), (5, BX + 2 * HALO, BY + 2 * HALO, GZ), (BX * BY, GZ)],
-    )(own, xlow, xhigh, ylow, yhigh, clow, chigh, jnp.asarray(table_z[modes_of]))
+    )(own, xlow, xhigh, ylow, yhigh, *corners, jnp.asarray(table_z[modes_of]))
     planes = lax.all_to_all(
         modes.reshape(256, 2, 128), ("row", "col"), split_axis=0, concat_axis=0, tiled=True
     )

time: 205 us -> 224 us (1.093)
  starting transfers between devices: 31.8 us -> 68.2 us
  blocking collectives: 48.5 us -> 26 us
  waiting for transfers between devices: 82.9 us -> 87.2 us
    ppermute x2 -> x14, starting transfers between devices: 4.06 us -> 36 us  [the longest x7 17.3 us: gather_counts(): moved = lax.ppermute(four, 'col', ring(COLS, 4 * k))]
    reshape x1 -> x0, blocking collectives: 22.5 us -> none  [gather_counts(): return lax.all_gather(counts, 'col', axis=1, tiled=True).reshape(COLS)]
    ppermute x2 -> x14, waiting for transfers between devices: 1.89 us -> 10.9 us  [the longest x4 6.13 us: on_device(): lax.ppermute(corner, both, diagonal(row_step, col_step))]
    ppermute x1, waiting for transfers between devices: 3.18 us -> 0.01 us  [on_device(): xlow = lax.ppermute(xlast, 'row', ring(ROWS, 1))]
  transfers between devices with their start and end apart: 9 -> 21, of which waited for: 6 -> 11; matrix products, arithmetic and copies ran while one was open for 0% -> 0% of each run, Pallas kernels for 0% -> 0%
where the time goes in v3:
time: 224 us
  waiting for transfers between devices  87.2 us (39%)
  starting transfers between devices  68.2 us (30%)
  Pallas kernels  34.1 us (15%)
  blocking collectives  26 us (12%)
  between operations  3.24 us (1%)
  other arithmetic  3.05 us (1%)
    all_to_all x1, waiting for transfers between devices, on_device(): lax.all_to_all(returned, 'col', split_axis=0, concat_axis=0, tiled=True)  33.3 us
    all_to_all x1, waiting for transfers between devices, on_device(): lax.all_to_all(sent.reshape(COLS, BRICK, 128), 'col', split_axis=0, conca...  29 us
    all_to_all x1, blocking collectives, on_device(): lax.all_to_all(strips.reshape(256, 3, 128), ('row', 'col'), split_axis=0,...  26 us
    pallas_call x1, Pallas kernels, on_device(): call(euler_kernel, [(5, BX, BY, GZ), (512, 128)], (10, ()), [(5, BX + 2 *...  22 us
    ppermute x7, starting transfers between devices, gather_counts(): moved = lax.ppermute(four, 'col', ring(COLS, 4 * k))  17.3 us
    ppermute x4, starting transfers between devices, on_device(): lax.ppermute(corner, both, diagonal(row_step, col_step))  14 us
    all_to_all x1, waiting for transfers between devices, on_device(): lax.all_to_all(modes.reshape(256, 2, 128), ('row', 'col'), split_axis=0,...  13.9 us
    all_to_all x1, starting transfers between devices, on_device(): lax.all_to_all(modes.reshape(256, 2, 128), ('row', 'col'), split_axis=0,...  12.9 us
  transfers between devices with their start and end apart: 21, of which 11 were waited for; matrix products, arithmetic and copies ran while one was open for 0% of the time, Pallas kernels for 0%

profile of v3, /device:TPU:2, one launch (start us, length us, event | category | flops | bytes accessed | tf_op | source)
XLA Modules:
  0.0 223.5 jit_solution(5834722256006137649)
XLA Ops:
  0.0 1.5 collective-permute-start.2
  1.5 2.8 %collective-permute-start.1 = (s32[1]{0:T(128)}, s32[1]{0:T(128)}, u32[]{:S(2)}, u32[]{:S(2)}) collective-permute-start(s32[1]{0:T(128)} %bitcast), channel_id=1, source_target_pairs={{0,2},{1,3},{2,0},{3,1},{4,6},{5,7},{6,4},{7,5},{8,10},{9,11},{10,... | collective-permute-start | bytes 20 | tf_op jit(solution)/shard_map/ppermute | solution.py:338
  4.3 0.4 collective-permute-start
  5.7 0.0 collective-permute-done.2
  5.8 1.0 collective-permute-done.1
  6.8 1.2 collective-permute-done
  8.0 1.9 compare_select_fusion.3
  9.9 0.8 collective-permute-start.9
  10.7 3.3 %collective-permute-start.8 = (s32[4]{0:T(128)S(1)}, s32[4]{0:T(128)S(1)}, u32[]{:S(2)}, u32[]{:S(2)}) collective-permute-start(s32[4]{0:T(128)S(1)} %compare_select_fusion.3), channel_id=1, source_target_pairs={{0,8},{1,9},{2,10},{3,11},{4,12},{5,13},{6,14},{7,15},{8,16},{9,17... | collective-permute-start | bytes 56 | tf_op jit(solution)/shard_map/ppermute | solution.py:342
  14.0 4.0 %collective-permute-start.7 = (s32[4]{0:T(128)S(1)}, s32[4]{0:T(128)S(1)}, u32[]{:S(2)}, u32[]{:S(2)}) collective-permute-start(s32[4]{0:T(128)S(1)} %compare_select_fusion.3), channel_id=1, source_target_pairs={{0,12},{1,13},{2,14},{3,15},{4,16},{5,17},{6,18},{7,19},{8,20},{9,... | collective-permute-start | bytes 56 | tf_op jit(solution)/shard_map/ppermute | solution.py:342
  18.0 0.5 collective-permute-start.6
  18.6 4.9 %collective-permute-start.5 = (s32[4]{0:T(128)S(1)}, s32[4]{0:T(128)S(1)}, u32[]{:S(2)}, u32[]{:S(2)}) collective-permute-start(s32[4]{0:T(128)S(1)} %compare_select_fusion.3), channel_id=1, source_target_pairs={{0,20},{1,21},{2,22},{3,23},{4,24},{5,25},{6,26},{7,27},{8,28},{9,... | collective-permute-start | bytes 56 | tf_op jit(solution)/shard_map/ppermute | solution.py:342
  23.5 0.0 collective-permute-done.9
  23.5 2.7 %collective-permute-start.4 = (s32[4]{0:T(128)S(1)}, s32[4]{0:T(128)S(1)}, u32[]{:S(2)}, u32[]{:S(2)}) collective-permute-start(s32[4]{0:T(128)S(1)} %compare_select_fusion.3), channel_id=1, source_target_pairs={{0,24},{1,25},{2,26},{3,27},{4,28},{5,29},{6,30},{7,31},{8,0},{9,1... | collective-permute-start | bytes 56 | tf_op jit(solution)/shard_map/ppermute | solution.py:342
  26.2 0.0 collective-permute-done.8
  26.2 1.0 collective-permute-start.3
  27.2 0.0 collective-permute-done.7
  27.2 0.0 collective-permute-done.6
  27.2 0.0 collective-permute-done.5
  27.2 0.8 collective-permute-done.4
  28.0 1.8 collective-permute-done.3
  29.7 0.7 select_reduce_fusion.1
  32.4 0.0 copy-start
  32.4 1.3 copy-done
  33.7 2.1 shard_map.73
  35.8 7.3 %all-to-all-start = ((f32[32,80,128]{2,1,0:T(8,128)}), f32[32,80,128]{2,1,0:T(8,128)S(1)}, u32[]{:S(2)}, u32[]{:S(2)}) async-start(f32[32,80,128]{2,1,0:T(8,128)} %bitcast.8), calls=%async_computation | async-start | bytes 2621440 | tf_op jit(solution)/shard_map/all_to_all | solution.py:364
  43.2 0.0 copy-start.1
  43.2 0.1 reshape.238
  43.3 0.1 select_reduce_fusion
  43.4 0.2 convert_reduce_fusion
  43.6 29.0 %all-to-all-done.recv_ref = f32[32,80,128]{2,1,0:T(8,128)S(1)} async-done(((f32[32,80,128]{2,1,0:T(8,128)}), f32[32,80,128]{2,1,0:T(8,128)S(1)}, u32[]{:S(2)}, u32[]{:S(2)}) %all-to-all-start) | async-done | bytes 1310752 | tf_op jit(solution)/shard_map/all_to_all | solution.py:364
  72.7 2.7 %shard_map.74 = (f32[5,32,8,128]{3,2,1,0:T(8,128)S(1)}, f32[5,4,8,128]{3,2,1,0:T(8,128)S(1)}, f32[5,4,8,128]{3,2,1,0:T(8,128)S(1)}, f32[5,32,4,128]{3,2,1,0:T(4,...) custom-call(s32[16]{0:T(128)S(1)} %broadcast_add_fusion.owner_ref, ...), custom_call_target="tpu_custom_call" | custom-call | tf_op jit(solution)/shard_map/pallas_call | solution.py:367
  75.3 0.0 copy-start.4
  75.3 0.0 copy-start.2
  75.4 0.0 copy-start.3
  75.4 1.5 collective-permute-start.12
  76.9 0.6 collective-permute-start.13
  77.5 0.0 collective-permute-start.14
  77.5 2.6 %collective-permute-start.10 = (f32[5,4,8,128]{3,2,1,0:T(8,128)S(1)}, f32[5,4,8,128]{3,2,1,0:T(8,128)S(1)}, u32[]{:S(2)}, u32[]{:S(2)}) collective-permute-start(f32[5,4,8,128]{3,2,1,0:T(8,128)S(1)} %get-tuple-element.17), channel_id=1, source_target_pairs={{0,32},{32,64},{64,96},{96,128},{128,160},{160,192},{192,224},{224... | collective-permute-start | bytes 245768 | tf_op jit(solution)/shard_map/ppermute | solution.py:388
  80.1 1.3 collective-permute-start.11
  81.3 1.7 collective-permute-done.14.c0_ref
  83.0 3.6 %collective-permute-start.15 = (f32[5,2,4,128]{3,2,1,0:T(4,128)S(1)}, f32[5,2,4,128]{3,2,1,0:T(4,128)S(1)}, u32[]{:S(2)}, u32[]{:S(2)}) collective-permute-start(f32[5,2,4,128]{3,2,1,0:T(4,128)S(1)} %get-tuple-element.22), channel_id=1, source_target_pairs={{0,225},{1,226},{2,227},{3,228},{4,229},{5,230},{6,231},{7,232},{8... | collective-permute-start | bytes 61448 | tf_op jit(solution)/shard_map/ppermute | solution.py:394
  86.6 1.5 collective-permute-done.15.c1_ref
  88.1 5.0 %collective-permute-start.16 = (f32[5,2,4,128]{3,2,1,0:T(4,128)S(1)}, f32[5,2,4,128]{3,2,1,0:T(4,128)S(1)}, u32[]{:S(2)}, u32[]{:S(2)}) collective-permute-start(f32[5,2,4,128]{3,2,1,0:T(4,128)S(1)} %get-tuple-element.23), channel_id=1, source_target_pairs={{0,63},{1,32},{2,33},{3,34},{4,35},{5,36},{6,37},{7,38},{8,39},{9,... | collective-permute-start | bytes 61448 | tf_op jit(solution)/shard_map/ppermute | solution.py:394
  93.1 1.5 collective-permute-done.16.c2_ref
  94.6 5.4 %collective-permute-start.17 = (f32[5,2,4,128]{3,2,1,0:T(4,128)S(1)}, f32[5,2,4,128]{3,2,1,0:T(4,128)S(1)}, u32[]{:S(2)}, u32[]{:S(2)}) collective-permute-start(f32[5,2,4,128]{3,2,1,0:T(4,128)S(1)} %get-tuple-element.24), channel_id=1, source_target_pairs={{0,255},{1,224},{2,225},{3,226},{4,227},{5,228},{6,229},{7,230},{8... | collective-permute-start | bytes 61448 | tf_op jit(solution)/shard_map/ppermute | solution.py:394
  100.0 1.5 collective-permute-done.17.c3_ref
  101.5 0.0 collective-permute-done.10.xlow_ref
  101.5 0.0 collective-permute-done.11.xhigh_ref
  101.5 0.0 collective-permute-done.12.ylow_ref
  101.5 0.0 collective-permute-done.13.yhigh_ref
  101.5 22.0 %shard_map.75 = (f32[5,32,8,128]{3,2,1,0:T(8,128)S(1)}, f32[512,128]{1,0:T(8,128)}) custom-call(f32[5,32,8,128]{3,2,1,0:T(8,128)S(1)} %get-tuple-element.16.own_ref, f32[5,4,8,128]{3,2,1,0:T(8,128)S(1)} %collective-permute-done.10.xlow_ref, f32[5,4,8,128]{3,2,1,0:T(8,128)S(1)} %collective-permute-done.11.xhigh_ref, ...), custom_call_target="tpu_custom_call" | custom-call | tf_op jit(solution)/shard_map/pallas_call | solution.py:401
  123.5 12.9 %all-to-all-start.1 = ((f32[256,2,128]{2,1,0:T(2,128)}), f32[256,2,128]{2,1,0:T(2,128)S(1)}, u32[]{:S(2)}, u32[]{:S(2)}) async-start(f32[256,2,128]{2,1,0:T(2,128)} %bitcast.11), calls=%async_computation.1 | async-start | bytes 524288 | tf_op jit(solution)/shard_map/all_to_all | solution.py:407
  136.5 13.9 %all-to-all-done.1 = f32[256,2,128]{2,1,0:T(2,128)S(1)} async-done(((f32[256,2,128]{2,1,0:T(2,128)}), f32[256,2,128]{2,1,0:T(2,128)S(1)}, u32[]{:S(2)}, u32[]{:S(2)}) %all-to-all-start.1) | async-done | bytes 262176 | tf_op jit(solution)/shard_map/all_to_all | solution.py:407
  150.4 0.1 jit_solution_.3.eigy_ref
  150.6 2.0 shard_map.76
  152.6 0.2 reshape.232
  152.8 26.0 %all_to_all.20 = f32[256,3,128]{2,1,0:T(4,128)S(1)} all-to-all(f32[256,3,128]{2,1,0:T(4,128)S(1)} %reshape.232), channel_id=1, replica_groups=mesh['row'=8,'col'=32] {'row','col'}, dimensions={0} | all-to-all | bytes 786432 | tf_op jit(solution)/shard_map/all_to_all | solution.py:422
  178.7 0.2 reshape.233.modes_ref
  178.9 2.9 %shard_map.77 = f32[32,80,128]{2,1,0:T(8,128)} custom-call(s32[16]{0:T(128)S(1)} %broadcast_add_fusion.owner_ref, f32[5,32,8,128]{3,2,1,0:T(8,128)S(1)} %get-tuple-element.25.stepped_ref, f32[768,128]{1,0:T(8,128)S(1)} %reshape.233.modes_ref, f32[256,128]{1,0:T(8,128)S(1)} %copy-done.1), custom_call_target="tpu_custom_call" | custom-call | tf_op jit(solution)/shard_map/pallas_call | solution.py:425
  181.8 6.0 %all-to-all-start.3 = ((f32[32,80,128]{2,1,0:T(8,128)}), f32[32,80,128]{2,1,0:T(8,128)S(1)}, u32[]{:S(2)}, u32[]{:S(2)}) async-start(f32[32,80,128]{2,1,0:T(8,128)} %shard_map.77), calls=%async_computation.3 | async-start | bytes 2621440 | tf_op jit(solution)/shard_map/all_to_all | solution.py:431
  187.8 0.1 pad_add_fusion.place_ref
  187.9 33.3 %all-to-all-done.3 = f32[32,80,128]{2,1,0:T(8,128)S(1)} async-done(((f32[32,80,128]{2,1,0:T(8,128)}), f32[32,80,128]{2,1,0:T(8,128)S(1)}, u32[]{:S(2)}, u32[]{:S(2)}) %all-to-all-start.3) | async-done | bytes 1310752 | tf_op jit(solution)/shard_map/all_to_all | solution.py:431
  221.2 2.4 %shard_map.78 = f32[5,16,4096]{2,1,0:T(8,128)} custom-call(s32[2]{0:T(128)S(1)} %pad_add_fusion.place_ref, f32[2560,128]{1,0:T(8,128)S(1)} %bitcast.17), custom_call_target="tpu_custom_call" | custom-call | tf_op jit(solution)/shard_map/pallas_call | solution.py:433
  (10 shorter events, 0.0 us)
Async XLA Ops:
  0.0 5.7 %collective-permute-start.2 = (s32[1]{0:T(128)}, s32[1]{0:T(128)}, u32[]{:S(2)}, u32[]{:S(2)}) collective-permute-start(s32[1]{0:T(128)} %bitcast), channel_id=1, source_target_pairs={{0,1},{1,2},{2,3},{3,0},{4,5},{5,6},{6,7},{7,4},{8,9},{9,10},{10,1... | collective-permute-start | bytes 20 | tf_op jit(solution)/shard_map/ppermute | solution.py:338
  1.5 5.3 %collective-permute-start.1 = (s32[1]{0:T(128)}, s32[1]{0:T(128)}, u32[]{:S(2)}, u32[]{:S(2)}) collective-permute-start(s32[1]{0:T(128)} %bitcast), channel_id=1, source_target_pairs={{0,2},{1,3},{2,0},{3,1},{4,6},{5,7},{6,4},{7,5},{8,10},{9,11},{10,... | collective-permute-start | bytes 20 | tf_op jit(solution)/shard_map/ppermute | solution.py:338
  4.3 3.6 %collective-permute-start = (s32[1]{0:T(128)}, s32[1]{0:T(128)}, u32[]{:S(2)}, u32[]{:S(2)}) collective-permute-start(s32[1]{0:T(128)} %bitcast), channel_id=1, source_target_pairs={{0,3},{1,0},{2,1},{3,2},{4,7},{5,4},{6,5},{7,6},{8,11},{9,8},{10,9... | collective-permute-start | bytes 20 | tf_op jit(solution)/shard_map/ppermute | solution.py:338
  9.9 13.6 %collective-permute-start.9 = (s32[4]{0:T(128)S(1)}, s32[4]{0:T(128)S(1)}, u32[]{:S(2)}, u32[]{:S(2)}) collective-permute-start(s32[4]{0:T(128)S(1)} %compare_select_fusion.3), channel_id=1, source_target_pairs={{0,4},{1,5},{2,6},{3,7},{4,8},{5,9},{6,10},{7,11},{8,12},{9,13},{1... | collective-permute-start | bytes 56 | tf_op jit(solution)/shard_map/ppermute | solution.py:342
  10.7 15.5 %collective-permute-start.8 = (s32[4]{0:T(128)S(1)}, s32[4]{0:T(128)S(1)}, u32[]{:S(2)}, u32[]{:S(2)}) collective-permute-start(s32[4]{0:T(128)S(1)} %compare_select_fusion.3), channel_id=1, source_target_pairs={{0,8},{1,9},{2,10},{3,11},{4,12},{5,13},{6,14},{7,15},{8,16},{9,17... | collective-permute-start | bytes 56 | tf_op jit(solution)/shard_map/ppermute | solution.py:342
  14.0 13.2 %collective-permute-start.7 = (s32[4]{0:T(128)S(1)}, s32[4]{0:T(128)S(1)}, u32[]{:S(2)}, u32[]{:S(2)}) collective-permute-start(s32[4]{0:T(128)S(1)} %compare_select_fusion.3), channel_id=1, source_target_pairs={{0,12},{1,13},{2,14},{3,15},{4,16},{5,17},{6,18},{7,19},{8,20},{9,... | collective-permute-start | bytes 56 | tf_op jit(solution)/shard_map/ppermute | solution.py:342
  18.0 9.2 %collective-permute-start.6 = (s32[4]{0:T(128)S(1)}, s32[4]{0:T(128)S(1)}, u32[]{:S(2)}, u32[]{:S(2)}) collective-permute-start(s32[4]{0:T(128)S(1)} %compare_select_fusion.3), channel_id=1, source_target_pairs={{0,16},{1,17},{2,18},{3,19},{4,20},{5,21},{6,22},{7,23},{8,24},{9,... | collective-permute-start | bytes 56 | tf_op jit(solution)/shard_map/ppermute | solution.py:342
  18.6 8.6 %collective-permute-start.5 = (s32[4]{0:T(128)S(1)}, s32[4]{0:T(128)S(1)}, u32[]{:S(2)}, u32[]{:S(2)}) collective-permute-start(s32[4]{0:T(128)S(1)} %compare_select_fusion.3), channel_id=1, source_target_pairs={{0,20},{1,21},{2,22},{3,23},{4,24},{5,25},{6,26},{7,27},{8,28},{9,... | collective-permute-start | bytes 56 | tf_op jit(solution)/shard_map/ppermute | solution.py:342
  23.5 4.4 %collective-permute-start.4 = (s32[4]{0:T(128)S(1)}, s32[4]{0:T(128)S(1)}, u32[]{:S(2)}, u32[]{:S(2)}) collective-permute-start(s32[4]{0:T(128)S(1)} %compare_select_fusion.3), channel_id=1, source_target_pairs={{0,24},{1,25},{2,26},{3,27},{4,28},{5,29},{6,30},{7,31},{8,0},{9,1... | collective-permute-start | bytes 56 | tf_op jit(solution)/shard_map/ppermute | solution.py:342
  26.2 3.5 %collective-permute-start.3 = (s32[4]{0:T(128)S(1)}, s32[4]{0:T(128)S(1)}, u32[]{:S(2)}, u32[]{:S(2)}) collective-permute-start(s32[4]{0:T(128)S(1)} %compare_select_fusion.3), channel_id=1, source_target_pairs={{0,28},{1,29},{2,30},{3,31},{4,0},{5,1},{6,2},{7,3},{8,4},{9,5},{1... | collective-permute-start | bytes 56 | tf_op jit(solution)/shard_map/ppermute | solution.py:342
  32.4 1.3 copy-start
  35.8 36.8 %all-to-all-start = ((f32[32,80,128]{2,1,0:T(8,128)}), f32[32,80,128]{2,1,0:T(8,128)S(1)}, u32[]{:S(2)}, u32[]{:S(2)}) async-start(f32[32,80,128]{2,1,0:T(8,128)} %bitcast.8), calls=%async_computation | async-start | bytes 2621440 | tf_op jit(solution)/shard_map/all_to_all | solution.py:364
  43.2 58.3 %copy-start.1 = (f32[256,128]{1,0:T(8,128)S(1)}, f32[256,128]{1,0:T(8,128)}, u32[]{:S(2)}) copy-start(f32[256,128]{1,0:T(8,128)} %constant.162.clone.table_ref) | copy-start | bytes 393220
  75.3 75.1 %copy-start.4 = (f32[256]{0:T(256)S(1)}, f32[256]{0:T(256)}, u32[]{:S(2)}) copy-start(f32[256]{0:T(256)} %constant.165.clone) | copy-start | bytes 3076
  75.3 75.2 %copy-start.2 = (f32[256,256]{1,0:T(8,128)S(1)}, f32[256,256]{1,0:T(8,128)}, u32[]{:S(2)}) copy-start(f32[256,256]{1,0:T(8,128)} %constant.163.clone.table_ref) | copy-start | bytes 786436
  75.4 75.2 %copy-start.3 = (f32[1,256]{1,0:T(1,128)S(1)}, f32[1,256]{1,0:T(1,128)}, u32[]{:S(2)}) copy-start(f32[1,256]{1,0:T(1,128)} %constant.164.clone.eigx_ref) | copy-start | bytes 3076
  75.4 26.1 %collective-permute-start.12 = (f32[5,32,4,128]{3,2,1,0:T(4,128)S(1)}, f32[5,32,4,128]{3,2,1,0:T(4,128)S(1)}, u32[]{:S(2)}, u32[]{:S(2)}) collective-permute-start(f32[5,32,4,128]{3,2,1,0:T(4,128)S(1)} %get-tuple-element.19), channel_id=1, source_target_pairs={{0,1},{1,2},{2,3},{3,4},{4,5},{5,6},{6,7},{7,8},{8,9},{9,10},{10,1... | collective-permute-start | bytes 983048 | tf_op jit(solution)/shard_map/ppermute | solution.py:390
  76.9 24.6 %collective-permute-start.13 = (f32[5,32,4,128]{3,2,1,0:T(4,128)S(1)}, f32[5,32,4,128]{3,2,1,0:T(4,128)S(1)}, u32[]{:S(2)}, u32[]{:S(2)}) collective-permute-start(f32[5,32,4,128]{3,2,1,0:T(4,128)S(1)} %get-tuple-element.20), channel_id=1, source_target_pairs={{0,31},{1,0},{2,1},{3,2},{4,3},{5,4},{6,5},{7,6},{8,7},{9,8},{10,9... | collective-permute-start | bytes 983048 | tf_op jit(solution)/shard_map/ppermute | solution.py:391
  77.5 5.5 %collective-permute-start.14 = (f32[5,2,4,128]{3,2,1,0:T(4,128)S(1)}, f32[5,2,4,128]{3,2,1,0:T(4,128)S(1)}, u32[]{:S(2)}, u32[]{:S(2)}) collective-permute-start(f32[5,2,4,128]{3,2,1,0:T(4,128)S(1)} %get-tuple-element.21), channel_id=1, source_target_pairs={{0,33},{1,34},{2,35},{3,36},{4,37},{5,38},{6,39},{7,40},{8,41},{9,... | collective-permute-start | bytes 61448 | tf_op jit(solution)/shard_map/ppermute | solution.py:394
  77.5 24.0 %collective-permute-start.10 = (f32[5,4,8,128]{3,2,1,0:T(8,128)S(1)}, f32[5,4,8,128]{3,2,1,0:T(8,128)S(1)}, u32[]{:S(2)}, u32[]{:S(2)}) collective-permute-start(f32[5,4,8,128]{3,2,1,0:T(8,128)S(1)} %get-tuple-element.17), channel_id=1, source_target_pairs={{0,32},{32,64},{64,96},{96,128},{128,160},{160,192},{192,224},{224... | collective-permute-start | bytes 245768 | tf_op jit(solution)/shard_map/ppermute | solution.py:388
  80.1 21.4 %collective-permute-start.11 = (f32[5,4,8,128]{3,2,1,0:T(8,128)S(1)}, f32[5,4,8,128]{3,2,1,0:T(8,128)S(1)}, u32[]{:S(2)}, u32[]{:S(2)}) collective-permute-start(f32[5,4,8,128]{3,2,1,0:T(8,128)S(1)} %get-tuple-element.18), channel_id=1, source_target_pairs={{0,224},{32,0},{64,32},{96,64},{128,96},{160,128},{192,160},{224,1... | collective-permute-start | bytes 245768 | tf_op jit(solution)/shard_map/ppermute | solution.py:389
  83.0 5.1 %collective-permute-start.15 = (f32[5,2,4,128]{3,2,1,0:T(4,128)S(1)}, f32[5,2,4,128]{3,2,1,0:T(4,128)S(1)}, u32[]{:S(2)}, u32[]{:S(2)}) collective-permute-start(f32[5,2,4,128]{3,2,1,0:T(4,128)S(1)} %get-tuple-element.22), channel_id=1, source_target_pairs={{0,225},{1,226},{2,227},{3,228},{4,229},{5,230},{6,231},{7,232},{8... | collective-permute-start | bytes 61448 | tf_op jit(solution)/shard_map/ppermute | solution.py:394
  88.1 6.5 %collective-permute-start.16 = (f32[5,2,4,128]{3,2,1,0:T(4,128)S(1)}, f32[5,2,4,128]{3,2,1,0:T(4,128)S(1)}, u32[]{:S(2)}, u32[]{:S(2)}) collective-permute-start(f32[5,2,4,128]{3,2,1,0:T(4,128)S(1)} %get-tuple-element.23), channel_id=1, source_target_pairs={{0,63},{1,32},{2,33},{3,34},{4,35},{5,36},{6,37},{7,38},{8,39},{9,... | collective-permute-start | bytes 61448 | tf_op jit(solution)/shard_map/ppermute | solution.py:394
  94.6 6.9 %collective-permute-start.17 = (f32[5,2,4,128]{3,2,1,0:T(4,128)S(1)}, f32[5,2,4,128]{3,2,1,0:T(4,128)S(1)}, u32[]{:S(2)}, u32[]{:S(2)}) collective-permute-start(f32[5,2,4,128]{3,2,1,0:T(4,128)S(1)} %get-tuple-element.24), channel_id=1, source_target_pairs={{0,255},{1,224},{2,225},{3,226},{4,227},{5,228},{6,229},{7,230},{8... | collective-permute-start | bytes 61448 | tf_op jit(solution)/shard_map/ppermute | solution.py:394
  123.5 27.0 %all-to-all-start.1 = ((f32[256,2,128]{2,1,0:T(2,128)}), f32[256,2,128]{2,1,0:T(2,128)S(1)}, u32[]{:S(2)}, u32[]{:S(2)}) async-start(f32[256,2,128]{2,1,0:T(2,128)} %bitcast.11), calls=%async_computation.1 | async-start | bytes 524288 | tf_op jit(solution)/shard_map/all_to_all | solution.py:407
  181.8 39.3 %all-to-all-start.3 = ((f32[32,80,128]{2,1,0:T(8,128)}), f32[32,80,128]{2,1,0:T(8,128)S(1)}, u32[]{:S(2)}, u32[]{:S(2)}) async-start(f32[32,80,128]{2,1,0:T(8,128)} %shard_map.77), calls=%async_computation.3 | async-start | bytes 2621440 | tf_op jit(solution)/shard_map/all_to_all | solution.py:431

commit v4 on v2

--- a/solution.py
+++ b/solution.py
@@ -159,7 +159,7 @@
         store(i, mine, rate)
         return tuple(face_high), tuple(upper_next)
 
-    lax.fori_loop(0, count, step, (tuple(face), tuple(upper_now)))
+    lax.fori_loop(0, count, step, (tuple(face), tuple(upper_now)), unroll=4)
 
 
 def euler_kernel(
@@ -318,7 +318,8 @@
 
 
 def gather_counts(counts):
-    return lax.all_gather(counts, "col", axis=1, tiled=True).reshape(COLS)
+    copies = jnp.broadcast_to(counts.reshape(1, 1, 1), (COLS, 1, 128))
+    return lax.all_to_all(copies, "col", split_axis=0, concat_axis=0, tiled=True)[:, 0, 0]
 
 
 def on_device(fields, counts):

time: 205 us -> 194 us (0.946)
  blocking collectives: 48.5 us -> 26.2 us
  waiting for transfers between devices: 82.9 us -> 94.6 us
  Pallas kernels: 34.1 us -> 22.6 us
  starting transfers between devices: 31.8 us -> 43.1 us
    reshape x1 -> x0, blocking collectives: 22.5 us -> none  [gather_counts(): return lax.all_gather(counts, 'col', axis=1, tiled=True).reshape(COLS)]
    all_to_all x0 -> x1, starting transfers between devices: none -> 11.6 us  [gather_counts(): lax.all_to_all(copies, 'col', split_axis=0, concat_axis=0, tiled=True)]
    pallas_call x1, Pallas kernels: 22 us -> 10.6 us  [on_device(): call(euler_kernel, [(5, BX, BY, GZ), (512, 128)], (8, ()), [(5, BX + 2 *...]
    all_to_all x0 -> x1, waiting for transfers between devices: none -> 8.44 us  [gather_counts(): lax.all_to_all(copies, 'col', split_axis=0, concat_axis=0, tiled=True)]
    all_to_all x1, waiting for transfers between devices: 29.1 us -> 32.3 us  [on_device(): lax.all_to_all(sent.reshape(COLS, BRICK, 128), 'col', split_axis=0, conca...]
  transfers between devices with their start and end apart: 9 -> 10, of which waited for: 6 -> 7; matrix products, arithmetic and copies ran while one was open for 0% -> 0% of each run, Pallas kernels for 0% -> 0%
where the time goes in v4:
time: 194 us; the launch traced here: 193 us
  waiting for transfers between devices  94.6 us (49%)
  starting transfers between devices  43.1 us (22%)
  blocking collectives  26.2 us (14%)
  Pallas kernels  22.6 us (12%)
  local copies, waits for them, and re-layouts  3.06 us (2%)
  between operations  2.89 us (1%)
    all_to_all x1, waiting for transfers between devices, on_device(): lax.all_to_all(returned, 'col', split_axis=0, concat_axis=0, tiled=True)  33.3 us
    all_to_all x1, waiting for transfers between devices, on_device(): lax.all_to_all(sent.reshape(COLS, BRICK, 128), 'col', split_axis=0, conca...  32.3 us
    all_to_all x1, blocking collectives, on_device(): lax.all_to_all(strips.reshape(256, 3, 128), ('row', 'col'), split_axis=0,...  26.2 us
    all_to_all x1, waiting for transfers between devices, on_device(): lax.all_to_all(modes.reshape(256, 2, 128), ('row', 'col'), split_axis=0,...  13.9 us
    all_to_all x1, starting transfers between devices, on_device(): lax.all_to_all(modes.reshape(256, 2, 128), ('row', 'col'), split_axis=0,...  13.8 us
    all_to_all x1, starting transfers between devices, gather_counts(): lax.all_to_all(copies, 'col', split_axis=0, concat_axis=0, tiled=True)  11.6 us
    pallas_call x1, Pallas kernels, on_device(): call(euler_kernel, [(5, BX, BY, GZ), (512, 128)], (8, ()), [(5, BX + 2 *...  10.6 us
    all_to_all x1, waiting for transfers between devices, gather_counts(): lax.all_to_all(copies, 'col', split_axis=0, concat_axis=0, tiled=True)  8.44 us
  transfers between devices with their start and end apart: 10, of which 7 were waited for; matrix products, arithmetic and copies ran while one was open for 0% of the time, Pallas kernels for 0%

profile of v4, /device:TPU:2, one launch (start us, length us, event | category | flops | bytes accessed | tf_op | source)
XLA Modules:
  0.0 193.5 jit_solution(9152403416333799597)
XLA Ops:
  0.7 0.6 broadcast_in_dim.28
  1.3 11.6 %all-to-all-start = ((s32[32,1,128]{2,1,0:T(1,128)}), s32[32,1,128]{2,1,0:T(1,128)S(1)}, u32[]{:S(2)}, u32[]{:S(2)}) async-start(s32[32,1,128]{2,1,0:T(1,128)} %broadcast_in_dim.28), calls=%async_computation | async-start | bytes 32768 | tf_op jit(solution)/shard_map/all_to_all | solution.py:322
  12.9 8.4 %all-to-all-done = s32[32,1,128]{2,1,0:T(1,128)S(1)} async-done(((s32[32,1,128]{2,1,0:T(1,128)}), s32[32,1,128]{2,1,0:T(1,128)S(1)}, u32[]{:S(2)}, u32[]{:S(2)}) %all-to-all-start) | async-done | bytes 16416 | tf_op jit(solution)/shard_map/all_to_all | solution.py:322
  21.3 0.7 slice_reduce_fusion
  22.0 0.6 fusion.1
  24.6 0.0 copy-start
  24.6 1.3 copy-done
  25.9 2.1 %shard_map.73 = f32[2560,128]{1,0:T(8,128)} custom-call(s32[1]{0:T(128)} %bitcast.3.start_ref, f32[5,16,4096]{2,1,0:T(8,128)S(1)} %bitcast.15), custom_call_target="tpu_custom_call" | custom-call | tf_op jit(solution)/shard_map/pallas_call | solution.py:339
  28.1 5.1 %all-to-all-start.1 = ((f32[32,80,128]{2,1,0:T(8,128)}), f32[32,80,128]{2,1,0:T(8,128)S(1)}, u32[]{:S(2)}, u32[]{:S(2)}) async-start(f32[32,80,128]{2,1,0:T(8,128)} %bitcast.5), calls=%async_computation.1 | async-start | bytes 2621440 | tf_op jit(solution)/shard_map/all_to_all | solution.py:342
  33.1 0.0 copy-start.1
  33.2 0.1 select_reduce_fusion
  33.3 0.2 convert_reduce_fusion
  33.5 32.3 %all-to-all-done.1.recv_ref = f32[32,80,128]{2,1,0:T(8,128)S(1)} async-done(((f32[32,80,128]{2,1,0:T(8,128)}), f32[32,80,128]{2,1,0:T(8,128)S(1)}, u32[]{:S(2)}, u32[]{:S(2)}) %all-to-all-start.1) | async-done | bytes 1310752 | tf_op jit(solution)/shard_map/all_to_all | solution.py:342
  65.7 2.7 %shard_map.74 = (f32[5,32,8,128]{3,2,1,0:T(8,128)S(1)}, f32[5,4,8,128]{3,2,1,0:T(8,128)S(1)}, f32[5,4,8,128]{3,2,1,0:T(8,128)S(1)}, f32[5,32,4,128]{3,2,1,0:T(4,128)S(1)}, f32[5,32,4,128]{3,2,1,0:T(4,128)S(1)}) custom-call(s32[16]{0:T(128)S(1)} %broadcast_add_fusion.owner_ref, f32[32,80,128]{2,1,0:T(8,128)S(1)} %all-to-all-done.1.recv_ref), custom_call_target="tpu_custom_call" | custom-call | tf_op jit(solution)/shard_map/pallas_call | solution.py:345
  68.4 0.0 copy-start.4
  68.4 1.5 collective-permute-start.2
  70.0 0.6 collective-permute-start.3
  70.5 0.0 collective-permute-start.1
  70.5 0.5 collective-permute-start
  71.0 1.6 collective-permute-done.1.xhigh_ref
  72.6 0.0 copy-start.2
  72.6 0.0 copy-start.3
  72.6 3.2 %collective-permute-done.xlow_ref = f32[5,4,8,128]{3,2,1,0:T(8,128)S(1)} collective-permute-done((f32[5,4,8,128]{3,2,1,0:T(8,128)S(1)}, f32[5,4,8,128]{3,2,1,0:T(8,128)S(1)}, u32[]{:S(2)}, u32[]{:S(2)}) %collective-permute-start) | collective-permute-done | bytes 81952 | tf_op jit(solution)/shard_map/ppermute | solution.py:361
  75.8 1.5 collective-permute-start.4
  77.4 2.5 %collective-permute-start.5 = (f32[5,4,4,128]{3,2,1,0:T(4,128)S(1)}, f32[5,4,4,128]{3,2,1,0:T(4,128)S(1)}, u32[]{:S(2)}, u32[]{:S(2)}) collective-permute-start(f32[5,4,4,128]{3,2,1,0:T(4,128)S(1)} %get-tuple-element.19), channel_id=1, source_target_pairs={{0,31},{1,0},{2,1},{3,2},{4,3},{5,4},{6,5},{7,6},{8,7},{9,8},{10,9... | collective-permute-start | bytes 122888 | tf_op jit(solution)/shard_map/ppermute | solution.py:367
  79.9 1.9 collective-permute-done.4.clow_ref
  81.8 0.0 collective-permute-done.5.chigh_ref
  81.8 0.0 collective-permute-done.2.ylow_ref
  81.8 0.0 collective-permute-done.3.yhigh_ref
  81.8 0.0 copy-done.1
  81.8 10.6 %shard_map.75 = (f32[5,32,8,128]{3,2,1,0:T(8,128)S(1)}, f32[512,128]{1,0:T(8,128)}) custom-call(f32[5,32,8,128]{3,2,1,0:T(8,128)S(1)} %get-tuple-element.12.own_ref, f32[5,4,8,128]{3,2,1,0:T(8,128)S(1)} %collective-permute-done.xlow_ref, f32[5,4,8,128]{3,2,1,0:T(8,128)S(1)} %collective-permute-done.1.xhigh_ref, ...), custom_call_target="tpu_custom_call" | custom-call | tf_op jit(solution)/shard_map/pallas_call | solution.py:372
  92.3 13.8 %all-to-all-start.2 = ((f32[256,2,128]{2,1,0:T(2,128)}), f32[256,2,128]{2,1,0:T(2,128)S(1)}, u32[]{:S(2)}, u32[]{:S(2)}) async-start(f32[256,2,128]{2,1,0:T(2,128)} %bitcast.8), calls=%async_computation.2 | async-start | bytes 524288 | tf_op jit(solution)/shard_map/all_to_all | solution.py:378
  106.2 13.9 %all-to-all-done.2 = f32[256,2,128]{2,1,0:T(2,128)S(1)} async-done(((f32[256,2,128]{2,1,0:T(2,128)}), f32[256,2,128]{2,1,0:T(2,128)S(1)}, u32[]{:S(2)}, u32[]{:S(2)}) %all-to-all-start.2) | async-done | bytes 262176 | tf_op jit(solution)/shard_map/all_to_all | solution.py:378
  120.2 0.0 copy-done.4
  120.2 0.1 jit_solution_.3.eigy_ref
  120.3 0.0 copy-done.2
  120.3 0.0 copy-done.3
  120.3 2.0 %shard_map.76 = f32[768,128]{1,0:T(8,128)S(1)} custom-call(s32[1]{0:T(128)} %bitcast.6.place_ref, f32[1]{0:T(128)} %bitcast.7.wave_ref, f32[512,128]{1,0:T(8,128)S(1)} %bitcast.16, f32[256,256]{1,0:T(8,128)S(1)} %copy-done.2, f32[1,256]{1,0:T(1,128)S(1)} %copy-done.3, f32[256,128]{1,0:T(8,128)S(1)} %jit_solution_.3.eigy_ref), custom_call_target="tpu_custom_call" | custom-call | tf_op jit(solution)/shard_map/pallas_call | solution.py:385
  122.3 0.2 reshape.44
  122.5 26.2 %all_to_all.25 = f32[256,3,128]{2,1,0:T(4,128)S(1)} all-to-all(f32[256,3,128]{2,1,0:T(4,128)S(1)} %reshape.44), channel_id=1, replica_groups=mesh['row'=8,'col'=32] {'row','col'}, dimensions={0} | all-to-all | bytes 786432 | tf_op jit(solution)/shard_map/all_to_all | solution.py:393
  148.7 0.2 reshape.45.modes_ref
  148.9 2.9 %shard_map.77 = f32[32,80,128]{2,1,0:T(8,128)} custom-call(s32[16]{0:T(128)S(1)} %broadcast_add_fusion.owner_ref, f32[5,32,8,128]{3,2,1,0:T(8,128)S(1)} %get-tuple-element.17.stepped_ref, f32[768,128]{1,0:T(8,128)S(1)} %reshape.45.modes_ref, f32[256,128]{1,0:T(8,128)S(1)} %copy-done.1), custom_call_target="tpu_custom_call" | custom-call | tf_op jit(solution)/shard_map/pallas_call | solution.py:396
  151.8 6.0 %all-to-all-start.4 = ((f32[32,80,128]{2,1,0:T(8,128)}), f32[32,80,128]{2,1,0:T(8,128)S(1)}, u32[]{:S(2)}, u32[]{:S(2)}) async-start(f32[32,80,128]{2,1,0:T(8,128)} %shard_map.77), calls=%async_computation.4 | async-start | bytes 2621440 | tf_op jit(solution)/shard_map/all_to_all | solution.py:402
  157.7 0.1 pad_add_fusion.place_ref
  157.8 33.3 %all-to-all-done.4 = f32[32,80,128]{2,1,0:T(8,128)S(1)} async-done(((f32[32,80,128]{2,1,0:T(8,128)}), f32[32,80,128]{2,1,0:T(8,128)S(1)}, u32[]{:S(2)}, u32[]{:S(2)}) %all-to-all-start.4) | async-done | bytes 1310752 | tf_op jit(solution)/shard_map/all_to_all | solution.py:402
  191.1 2.4 %shard_map.78 = f32[5,16,4096]{2,1,0:T(8,128)} custom-call(s32[2]{0:T(128)S(1)} %pad_add_fusion.place_ref, f32[2560,128]{1,0:T(8,128)S(1)} %bitcast.14), custom_call_target="tpu_custom_call" | custom-call | tf_op jit(solution)/shard_map/pallas_call | solution.py:404
  (5 shorter events, 0.0 us)
Async XLA Ops:
  1.3 20.1 %all-to-all-start = ((s32[32,1,128]{2,1,0:T(1,128)}), s32[32,1,128]{2,1,0:T(1,128)S(1)}, u32[]{:S(2)}, u32[]{:S(2)}) async-start(s32[32,1,128]{2,1,0:T(1,128)} %broadcast_in_dim.28), calls=%async_computation | async-start | bytes 32768 | tf_op jit(solution)/shard_map/all_to_all | solution.py:322
  24.6 1.3 copy-start
  28.1 37.7 %all-to-all-start.1 = ((f32[32,80,128]{2,1,0:T(8,128)}), f32[32,80,128]{2,1,0:T(8,128)S(1)}, u32[]{:S(2)}, u32[]{:S(2)}) async-start(f32[32,80,128]{2,1,0:T(8,128)} %bitcast.5), calls=%async_computation.1 | async-start | bytes 2621440 | tf_op jit(solution)/shard_map/all_to_all | solution.py:342
  33.1 48.6 %copy-start.1 = (f32[256,128]{1,0:T(8,128)S(1)}, f32[256,128]{1,0:T(8,128)}, u32[]{:S(2)}) copy-start(f32[256,128]{1,0:T(8,128)} %constant.76.clone.table_ref) | copy-start | bytes 393220
  68.4 51.8 %copy-start.4 = (f32[256]{0:T(256)S(1)}, f32[256]{0:T(256)}, u32[]{:S(2)}) copy-start(f32[256]{0:T(256)} %constant.79.clone) | copy-start | bytes 3076
  68.4 13.3 %collective-permute-start.2 = (f32[5,32,4,128]{3,2,1,0:T(4,128)S(1)}, f32[5,32,4,128]{3,2,1,0:T(4,128)S(1)}, u32[]{:S(2)}, u32[]{:S(2)}) collective-permute-start(f32[5,32,4,128]{3,2,1,0:T(4,128)S(1)} %get-tuple-element.15), channel_id=1, source_target_pairs={{0,1},{1,2},{2,3},{3,4},{4,5},{5,6},{6,7},{7,8},{8,9},{9,10},{10,1... | collective-permute-start | bytes 983048 | tf_op jit(solution)/shard_map/ppermute | solution.py:363
  70.0 11.8 %collective-permute-start.3 = (f32[5,32,4,128]{3,2,1,0:T(4,128)S(1)}, f32[5,32,4,128]{3,2,1,0:T(4,128)S(1)}, u32[]{:S(2)}, u32[]{:S(2)}) collective-permute-start(f32[5,32,4,128]{3,2,1,0:T(4,128)S(1)} %get-tuple-element.16), channel_id=1, source_target_pairs={{0,31},{1,0},{2,1},{3,2},{4,3},{5,4},{6,5},{7,6},{8,7},{9,8},{10,9... | collective-permute-start | bytes 983048 | tf_op jit(solution)/shard_map/ppermute | solution.py:364
  70.5 2.1 %collective-permute-start.1 = (f32[5,4,8,128]{3,2,1,0:T(8,128)S(1)}, f32[5,4,8,128]{3,2,1,0:T(8,128)S(1)}, u32[]{:S(2)}, u32[]{:S(2)}) collective-permute-start(f32[5,4,8,128]{3,2,1,0:T(8,128)S(1)} %get-tuple-element.14), channel_id=1, source_target_pairs={{0,224},{32,0},{64,32},{96,64},{128,96},{160,128},{192,160},{224,1... | collective-permute-start | bytes 245768 | tf_op jit(solution)/shard_map/ppermute | solution.py:362
  70.5 5.2 %collective-permute-start = (f32[5,4,8,128]{3,2,1,0:T(8,128)S(1)}, f32[5,4,8,128]{3,2,1,0:T(8,128)S(1)}, u32[]{:S(2)}, u32[]{:S(2)}) collective-permute-start(f32[5,4,8,128]{3,2,1,0:T(8,128)S(1)} %get-tuple-element.13), channel_id=1, source_target_pairs={{0,32},{32,64},{64,96},{96,128},{128,160},{160,192},{192,224},{224... | collective-permute-start | bytes 245768 | tf_op jit(solution)/shard_map/ppermute | solution.py:361
  72.6 47.7 %copy-start.2 = (f32[256,256]{1,0:T(8,128)S(1)}, f32[256,256]{1,0:T(8,128)}, u32[]{:S(2)}) copy-start(f32[256,256]{1,0:T(8,128)} %constant.77.clone.table_ref) | copy-start | bytes 786436
  72.6 47.7 %copy-start.3 = (f32[1,256]{1,0:T(1,128)S(1)}, f32[1,256]{1,0:T(1,128)}, u32[]{:S(2)}) copy-start(f32[1,256]{1,0:T(1,128)} %constant.78.clone.eigx_ref) | copy-start | bytes 3076
  75.8 5.9 %collective-permute-start.4 = (f32[5,4,4,128]{3,2,1,0:T(4,128)S(1)}, f32[5,4,4,128]{3,2,1,0:T(4,128)S(1)}, u32[]{:S(2)}, u32[]{:S(2)}) collective-permute-start(f32[5,4,4,128]{3,2,1,0:T(4,128)S(1)} %get-tuple-element.20), channel_id=1, source_target_pairs={{0,1},{1,2},{2,3},{3,4},{4,5},{5,6},{6,7},{7,8},{8,9},{9,10},{10,1... | collective-permute-start | bytes 122888 | tf_op jit(solution)/shard_map/ppermute | solution.py:366
  77.4 4.4 %collective-permute-start.5 = (f32[5,4,4,128]{3,2,1,0:T(4,128)S(1)}, f32[5,4,4,128]{3,2,1,0:T(4,128)S(1)}, u32[]{:S(2)}, u32[]{:S(2)}) collective-permute-start(f32[5,4,4,128]{3,2,1,0:T(4,128)S(1)} %get-tuple-element.19), channel_id=1, source_target_pairs={{0,31},{1,0},{2,1},{3,2},{4,3},{5,4},{6,5},{7,6},{8,7},{9,8},{10,9... | collective-permute-start | bytes 122888 | tf_op jit(solution)/shard_map/ppermute | solution.py:367
  92.3 27.9 %all-to-all-start.2 = ((f32[256,2,128]{2,1,0:T(2,128)}), f32[256,2,128]{2,1,0:T(2,128)S(1)}, u32[]{:S(2)}, u32[]{:S(2)}) async-start(f32[256,2,128]{2,1,0:T(2,128)} %bitcast.8), calls=%async_computation.2 | async-start | bytes 524288 | tf_op jit(solution)/shard_map/all_to_all | solution.py:378
  151.8 39.3 %all-to-all-start.4 = ((f32[32,80,128]{2,1,0:T(8,128)}), f32[32,80,128]{2,1,0:T(8,128)S(1)}, u32[]{:S(2)}, u32[]{:S(2)}) async-start(f32[32,80,128]{2,1,0:T(8,128)} %shard_map.77), calls=%async_computation.4 | async-start | bytes 2621440 | tf_op jit(solution)/shard_map/all_to_all | solution.py:402

commit v5 on v4

--- a/solution.py
+++ b/solution.py
@@ -162,9 +162,20 @@
     lax.fori_loop(0, count, step, (tuple(face), tuple(upper_now)), unroll=4)
 
 
+def send_home(owner_ref, cells_ref, out_ref, fields):
+    for q in range(fields):
+        for xl in range(2):
+            for part in range(2):
+                base = (q * BX + xl * PE + part * 8) * BY
+                lines = [cells_ref[pl.ds(base + b, 8, stride=BY), :] for b in range(BY)]
+                rows = q * PE + part * 8
+                for zl, value in enumerate(swap_groups(lines, PE)):
+                    out_ref[owner_ref[xl * 8 + zl], rows : rows + 8, :] = value
+
+
 def euler_kernel(
-    own_ref, xlow_ref, xhigh_ref, ylow_ref, yhigh_ref, clow_ref, chigh_ref, table_ref,
-    stepped_ref, modes_ref, ext_ref, first_ref, flat_ref,
+    owner_ref, own_ref, xlow_ref, xhigh_ref, ylow_ref, yhigh_ref, clow_ref, chigh_ref, table_ref,
+    home_ref, modes_ref, ext_ref, first_ref, cells_ref,
 ):
     low, high = slice(BY + HALO, BY + 2 * HALO), slice(BY, BY + HALO)
     inner = slice(HALO, HALO + BX)
@@ -196,17 +207,17 @@
         for q in range(5):
             second = states[q] + time_step * rates[q]
             value = 0.5 * ext_ref[q, i, 0:BY] + 0.5 * second
-            stepped_ref[q, i - HALO] = value
-            if q == 0:
-                flat_ref[pl.ds(pl.multiple_of((i - HALO) * BY, BY), BY), :] = value
+            row = pl.multiple_of((q * BX + i - HALO) * BY, BY)
+            cells_ref[pl.ds(row, BY), :] = value
 
     euler_stage(load_first, store_stepped, HALO, BX, BY)
     density = jnp.concatenate(
-        [flat_ref[pl.ds(b, BX, stride=BY), :] for b in range(BY)], axis=0
+        [cells_ref[pl.ds(b, BX, stride=BY), :] for b in range(BY)], axis=0
     )
     spread = dot(table_ref[...], density, ((1,), (1,)))
     modes_ref[pl.ds(0, 256, stride=2), :] = spread[:, :128]
     modes_ref[pl.ds(1, 256, stride=2), :] = spread[:, 128:]
+    send_home(owner_ref, cells_ref, home_ref, 5)
 
 
 def plane_kernel(place_ref, wave_ref, modes_ref, table_ref, eigx_ref, eigy_ref, out_ref, plane_ref, wide_ref):
@@ -254,7 +265,7 @@
                 out_ref[pl.ds((high * 4 + p) * COLS * 3 + quad, COLS, stride=3), :] = value
 
 
-def kick_kernel(owner_ref, stepped_ref, modes_ref, table_ref, out_ref, phi_ref, kicked_ref):
+def gradient_kernel(owner_ref, modes_ref, table_ref, out_ref, phi_ref, cells_ref):
     table = table_ref[...]
     parts = []
     for quad in range(3):
@@ -268,39 +279,36 @@
     mid = phi[1 : 1 + BX]
     below = parts[2][0:32].reshape(BX, 1, GZ)
     above = parts[2][32:64].reshape(BX, 1, GZ)
-    grad_x = 0.5 * (phi[2:] - phi[:BX])
     lower = jnp.concatenate([below, mid[:, : BY - 1]], axis=1)
     upper = jnp.concatenate([mid[:, 1:], above], axis=1)
-    grad_y = 0.5 * (upper - lower)
-    grad_z = 0.5 * (pltpu.roll(mid, GZ - 1, 2) - pltpu.roll(mid, 1, 2))
-    grads = (grad_x, grad_y, grad_z)
-    density = stepped_ref[0]
-    momenta = [stepped_ref[1 + d] for d in range(3)]
-    work = momenta[0] * grad_x + momenta[1] * grad_y + momenta[2] * grad_z
     cells = BX * BY
-    kicked_ref[0:cells, :] = density.reshape(cells, GZ)
-    for d in range(3):
-        value = momenta[d] - time_step * density * grads[d]
-        kicked_ref[(1 + d) * cells : (2 + d) * cells, :] = value.reshape(cells, GZ)
-    kicked_ref[4 * cells :, :] = (stepped_ref[4] - time_step * work).reshape(cells, GZ)
-    for q in range(5):
-        for xl in range(2):
-            for part in range(2):
-                base = (q * BX + xl * PE + part * 8) * BY
-                lines = [kicked_ref[pl.ds(base + b, 8, stride=BY), :] for b in range(BY)]
-                rows = q * PE + part * 8
-                for zl, value in enumerate(swap_groups(lines, PE)):
-                    out_ref[owner_ref[xl * 8 + zl], rows : rows + 8, :] = value
-
-
-def spread_kernel(place_ref, recv_ref, out_ref):
+    cells_ref[0:cells, :] = (0.5 * (phi[2:] - phi[:BX])).reshape(cells, GZ)
+    cells_ref[cells : 2 * cells, :] = (0.5 * (upper - lower)).reshape(cells, GZ)
+    turned = pltpu.roll(mid, GZ - 1, 2) - pltpu.roll(mid, 1, 2)
+    cells_ref[2 * cells :, :] = (0.5 * turned).reshape(cells, GZ)
+    send_home(owner_ref, cells_ref, out_ref, 3)
+
+
+def kick_kernel(place_ref, state_ref, gradient_ref, out_ref):
     shift = place_ref[0]
     live = lax.broadcasted_iota(jnp.int32, (CAP, 128), 0) < place_ref[1]
-    for q in range(5):
-        for tile in range(2 * PE):
-            a, half = tile // 2, tile % 2
-            lines = recv_ref[pl.ds(half * BRICK + q * PE + a, CAP, stride=2 * BRICK), :]
-            turned = pltpu.roll(lines, shift, 0)
+
+    def rows(ref, fields, tile):
+        a, half = tile // 2, tile % 2
+        bricks = fields * PE
+        return [
+            ref[pl.ds(half * bricks + q * PE + a, CAP, stride=2 * bricks), :]
+            for q in range(fields)
+        ]
+
+    for tile in range(2 * PE):
+        density, mx, my, mz, energy = rows(state_ref, 5, tile)
+        gx, gy, gz = rows(gradient_ref, 3, tile)
+        pull = time_step * density
+        energy = energy - time_step * (mx * gx + my * gy + mz * gz)
+        kicked = (density, mx - pull * gx, my - pull * gy, mz - pull * gz, energy)
+        for q in range(5):
+            turned = pltpu.roll(kicked[q], shift, 0)
             out_ref[q, :, tile * 128 : (tile + 1) * 128] = jnp.where(live, turned, 0.0)
 
 
@@ -369,40 +377,46 @@
     table_z = hartley(GZ)
     table_x = hartley(GX)
     modes_of = np.arange(256) % GZ
-    stepped, modes = call(
+    home, modes = call(
         euler_kernel,
-        [(5, BX, BY, GZ), (512, 128)],
-        (8, ()),
-        [(5, BX + 2 * HALO, BY + 2 * HALO, GZ), (5, BX + 2 * HALO, BY + 2 * HALO, GZ), (BX * BY, GZ)],
-    )(own, xlow, xhigh, ylow, yhigh, clow, chigh, jnp.asarray(table_z[modes_of]))
-    planes = lax.all_to_all(
-        modes.reshape(256, 2, 128), ("row", "col"), split_axis=0, concat_axis=0, tiled=True
-    )
+        [(COLS, BRICK, 128), (512, 128)],
+        (9, (0,)),
+        [(5, BX + 2 * HALO, BY + 2 * HALO, GZ), (5, BX + 2 * HALO, BY + 2 * HALO, GZ), (5 * BX * BY, GZ)],
+    )(owners, own, xlow, xhigh, ylow, yhigh, clow, chigh, jnp.asarray(table_z[modes_of]))
+    state = lax.all_to_all(home, "col", split_axis=0, concat_axis=0, tiled=True)
     place = my_row * COLS + my_column
     wave_z = place % GZ
     eig = eigenvalues(GX)
     eig_z = -4.0 * jnp.sin((math.pi / GZ) * wave_z.astype(jnp.float32)) ** 2
-    strips = call(plane_kernel, [(768, 128)], (6, (0, 1)), [(2 * GY, 128), (2 * (GY + 16), 128)])(
-        (place // GZ).reshape(1),
-        eig_z.reshape(1),
-        planes.reshape(512, 128),
-        jnp.asarray(table_x),
-        jnp.asarray(eig[None, :]),
-        jnp.asarray(np.broadcast_to(eig[:, None], (GX, 128))),
-    )
-    strips = lax.all_to_all(
-        strips.reshape(256, 3, 128), ("row", "col"), split_axis=0, concat_axis=0, tiled=True
-    )
-    returned = call(
-        kick_kernel,
-        [(COLS, BRICK, 128)],
-        (4, (0,)),
-        [((BX + 2) * BY, GZ), (5 * BX * BY, GZ)],
-    )(owners, stepped, strips.reshape(768, 128), jnp.asarray(table_z[modes_of]))
-    came_back = lax.all_to_all(returned, "col", split_axis=0, concat_axis=0, tiled=True)
-    home = jnp.stack([(CAP - turn) % CAP, counts[0, 0]])
-    result = call(spread_kernel, [(5, CAP, PE * PE * PE)], (2, (0,)))(
-        home, came_back.reshape(COLS * BRICK, 128)
+    def poisson(step, strips):
+        planes = lax.all_to_all(
+            modes.reshape(256, 2, 128), ("row", "col"), split_axis=0, concat_axis=0, tiled=True
+        )
+        strips = call(plane_kernel, [(768, 128)], (6, (0, 1)), [(2 * GY, 128), (2 * (GY + 16), 128)])(
+            (place // GZ).reshape(1),
+            eig_z.reshape(1),
+            planes.reshape(512, 128),
+            jnp.asarray(table_x),
+            jnp.asarray(eig[None, :]),
+            jnp.asarray(np.broadcast_to(eig[:, None], (GX, 128))),
+        )
+        strips = lax.all_to_all(
+            strips.reshape(256, 3, 128), ("row", "col"), split_axis=0, concat_axis=0, tiled=True
+        )
+        return strips
+
+    strips = lax.fori_loop(0, jnp.minimum(counts[0, 0], 1), poisson, jnp.zeros((256, 3, 128), jnp.float32))
+    pulls = call(
+        gradient_kernel,
+        [(COLS, 3 * PE, 128)],
+        (3, (0,)),
+        [((BX + 2) * BY, GZ), (3 * BX * BY, GZ)],
+    )(owners, strips.reshape(768, 128), jnp.asarray(table_z[modes_of]))
+    gradient = lax.all_to_all(pulls, "col", split_axis=0, concat_axis=0, tiled=True)
+    result = call(kick_kernel, [(5, CAP, PE * PE * PE)], (3, (0,)))(
+        jnp.stack([(CAP - turn) % CAP, counts[0, 0]]),
+        state.reshape(COLS * BRICK, 128),
+        gradient.reshape(COLS * 3 * PE, 128),
     )
     return result.transpose(1, 0, 2)
 

time: 194 us -> 221 us (1.14)
  waiting for transfers between devices: 94.6 us -> 111 us
  starting transfers between devices: 43.1 us -> 48.7 us
  local copies, waits for them, and re-layouts: 3.06 us -> 5.76 us
  Pallas kernels: 22.6 us -> 25.1 us
    all_to_all x2 -> x3, waiting for transfers between devices: 47.2 us -> 63.2 us  [the longest x1 28.1 us: on_device(): state = lax.all_to_all(home, 'col', split_axis=0, concat_axis=0, tiled=True)]
    all_to_all x2 -> x3, starting transfers between devices: 19.8 us -> 25.3 us  [the longest x1 13.8 us: poisson(): lax.all_to_all(modes.reshape(256, 2, 128), ('row', 'col'), split_axis=0,...]
    pallas_call x4, Pallas kernels: 17.8 us -> 20.3 us  [the longest x1 13.1 us: on_device(): call(euler_kernel, [(COLS, BRICK, 128), (512, 128)], (9, (0,)), [(5, BX +...]
  transfers between devices with their start and end apart: 10 -> 11, of which waited for: 7 -> 8; matrix products, arithmetic and copies ran while one was open for 0% -> 1% of each run, Pallas kernels for 0% -> 1%
where the time goes in v5:
time: 221 us; the launch traced here: 220 us
  waiting for transfers between devices  111 us (50%)
  starting transfers between devices  48.7 us (22%)
  blocking collectives  26.2 us (12%)
  Pallas kernels  25.1 us (11%)
  local copies, waits for them, and re-layouts  5.76 us (3%)
  between operations  2.91 us (1%)
    all_to_all x1, waiting for transfers between devices, on_device(): lax.all_to_all(sent.reshape(COLS, BRICK, 128), 'col', split_axis=0, conca...  32.3 us
    all_to_all x1, waiting for transfers between devices, on_device(): state = lax.all_to_all(home, 'col', split_axis=0, concat_axis=0, tiled=True)  28.1 us
    all_to_all x1, blocking collectives, poisson(): lax.all_to_all(strips.reshape(256, 3, 128), ('row', 'col'), split_axis=0,...  26.2 us
    all_to_all x1, waiting for transfers between devices, on_device(): lax.all_to_all(pulls, 'col', split_axis=0, concat_axis=0, tiled=True)  21.1 us
    all_to_all x1, waiting for transfers between devices, poisson(): lax.all_to_all(modes.reshape(256, 2, 128), ('row', 'col'), split_axis=0,...  13.9 us
    all_to_all x1, starting transfers between devices, poisson(): lax.all_to_all(modes.reshape(256, 2, 128), ('row', 'col'), split_axis=0,...  13.8 us
    pallas_call x1, Pallas kernels, on_device(): call(euler_kernel, [(COLS, BRICK, 128), (512, 128)], (9, (0,)), [(5, BX +...  13.1 us
    all_to_all x1, starting transfers between devices, gather_counts(): lax.all_to_all(copies, 'col', split_axis=0, concat_axis=0, tiled=True)  11.6 us
  transfers between devices with their start and end apart: 11, of which 8 were waited for; matrix products, arithmetic and copies ran while one was open for 1% of the time, Pallas kernels for 1%

profile of v5, /device:TPU:2, one launch (start us, length us, event | category | flops | bytes accessed | tf_op | source)
XLA Modules:
  0.0 220.1 jit_solution(5472777909307699512)
XLA Ops:
  0.7 0.6 broadcast_in_dim.31
  1.3 11.6 %all-to-all-start = ((s32[32,1,128]{2,1,0:T(1,128)}), s32[32,1,128]{2,1,0:T(1,128)S(1)}, u32[]{:S(2)}, u32[]{:S(2)}) async-start(s32[32,1,128]{2,1,0:T(1,128)} %broadcast_in_dim.31), calls=%async_computation | async-start | bytes 32768 | tf_op jit(solution)/shard_map/all_to_all | solution.py:330
  12.9 8.4 %all-to-all-done = s32[32,1,128]{2,1,0:T(1,128)S(1)} async-done(((s32[32,1,128]{2,1,0:T(1,128)}), s32[32,1,128]{2,1,0:T(1,128)S(1)}, u32[]{:S(2)}, u32[]{:S(2)}) %all-to-all-start) | async-done | bytes 16416 | tf_op jit(solution)/shard_map/all_to_all | solution.py:330
  21.3 0.7 slice_reduce_fusion
  22.0 0.6 fusion.1
  24.6 0.0 copy-start
  24.6 1.3 copy-done
  25.9 2.1 shard_map.73
  28.1 5.1 %all-to-all-start.1 = ((f32[32,80,128]{2,1,0:T(8,128)}), f32[32,80,128]{2,1,0:T(8,128)S(1)}, u32[]{:S(2)}, u32[]{:S(2)}) async-start(f32[32,80,128]{2,1,0:T(8,128)} %bitcast.5), calls=%async_computation.1 | async-start | bytes 2621440 | tf_op jit(solution)/shard_map/all_to_all | solution.py:350
  33.1 0.0 copy-start.1
  33.2 0.1 select_reduce_fusion
  33.3 0.2 convert_reduce_fusion
  33.5 32.3 %all-to-all-done.1.recv_ref = f32[32,80,128]{2,1,0:T(8,128)S(1)} async-done(((f32[32,80,128]{2,1,0:T(8,128)}), f32[32,80,128]{2,1,0:T(8,128)S(1)}, u32[]{:S(2)}, u32[]{:S(2)}) %all-to-all-start.1) | async-done | bytes 1310752 | tf_op jit(solution)/shard_map/all_to_all | solution.py:350
  65.7 2.7 %shard_map.74 = (f32[5,32,8,128]{3,2,1,0:T(8,128)S(1)}, f32[5,4,8,128]{3,2,1,0:T(8,128)S(1)}, f32[5,4,8,128]{3,2,1,0:T(8,128)S(1)}, f32[5,32,4,128]{3,2,1,0:T(4,128)S(1)}, f32[5,32,4,128]{3,2,1,0:T(4,128)S(1)}) custom-call(s32[16]{0:T(128)S(1)} %broadcast_add_fusion.owner_ref, f32[32,80,128]{2,1,0:T(8,128)S(1)} %all-to-all-done.1.recv_ref), custom_call_target="tpu_custom_call" | custom-call | tf_op jit(solution)/shard_map/pallas_call | solution.py:353
  68.4 0.0 copy-start.4
  68.4 1.5 collective-permute-start.2
  70.0 0.6 collective-permute-start.3
  70.5 0.0 collective-permute-start.1
  70.5 0.5 collective-permute-start
  71.0 1.6 collective-permute-done.1.xhigh_ref
  72.6 3.2 %collective-permute-done.xlow_ref = f32[5,4,8,128]{3,2,1,0:T(8,128)S(1)} collective-permute-done((f32[5,4,8,128]{3,2,1,0:T(8,128)S(1)}, f32[5,4,8,128]{3,2,1,0:T(8,128)S(1)}, u32[]{:S(2)}, u32[]{:S(2)}) %collective-permute-start) | collective-permute-done | bytes 81952 | tf_op jit(solution)/shard_map/ppermute | solution.py:369
  75.8 0.0 copy-start.2
  75.8 0.0 copy-start.3
  75.8 1.5 collective-permute-start.4
  77.4 2.5 %collective-permute-start.5 = (f32[5,4,4,128]{3,2,1,0:T(4,128)S(1)}, f32[5,4,4,128]{3,2,1,0:T(4,128)S(1)}, u32[]{:S(2)}, u32[]{:S(2)}) collective-permute-start(f32[5,4,4,128]{3,2,1,0:T(4,128)S(1)} %get-tuple-element.199), channel_id=1, source_target_pairs={{0,31},{1,0},{2,1},{3,2},{4,3},{5,4},{6,5},{7,6},{8,7},{9,8},{10,9... | collective-permute-start | bytes 122888 | tf_op jit(solution)/shard_map/ppermute | solution.py:375
  79.9 1.9 collective-permute-done.4.clow_ref
  81.8 0.0 collective-permute-done.5.chigh_ref
  81.8 0.0 collective-permute-done.2.ylow_ref
  81.8 0.0 collective-permute-done.3.yhigh_ref
  81.8 0.0 copy-done.1
  81.8 13.1 %shard_map.75 = (f32[32,80,128]{2,1,0:T(8,128)}, f32[512,128]{1,0:T(8,128)}) custom-call(s32[16]{0:T(128)S(1)} %broadcast_add_fusion.owner_ref, f32[5,32,8,128]{3,2,1,0:T(8,128)S(1)} %get-tuple-element.183.own_ref, f32[5,4,8,128]{3,2,1,0:T(8,128)S(1)} %collective-permute-done.xlow_ref, f32[5,4,8,128]{3,2,1,0:T(8,128)S(1)} %collective-permute-done.1.xhigh_ref, ...), custom_call_target="tpu_custom_call" | custom-call | tf_op jit(solution)/shard_map/pallas_call | solution.py:380
  94.9 13.8 %all-to-all-start.3 = ((f32[256,2,128]{2,1,0:T(2,128)}), f32[256,2,128]{2,1,0:T(2,128)S(1)}, u32[]{:S(2)}, u32[]{:S(2)}) async-start(f32[256,2,128]{2,1,0:T(2,128)} %bitcast.9), calls=%async_computation.3 | async-start | bytes 524288 | tf_op jit(solution)/shard_map/while/body/all_to_all | solution.py:392
  108.8 13.9 %all-to-all-done.3 = f32[256,2,128]{2,1,0:T(2,128)S(1)} async-done(((f32[256,2,128]{2,1,0:T(2,128)}), f32[256,2,128]{2,1,0:T(2,128)S(1)}, u32[]{:S(2)}, u32[]{:S(2)}) %all-to-all-start.3) | async-done | bytes 262176 | tf_op jit(solution)/shard_map/while/body/all_to_all | solution.py:392
  122.8 0.0 copy-done.4
  122.8 0.1 jit_solution_.3.eigy_ref
  122.9 0.0 copy-done.2
  122.9 0.0 copy-done.3
  122.9 2.0 body.3
  124.9 0.2 reshape.52
  125.1 26.2 %all_to_all.34 = f32[256,3,128]{2,1,0:T(4,128)S(1)} all-to-all(f32[256,3,128]{2,1,0:T(4,128)S(1)} %reshape.52), channel_id=1, replica_groups=mesh['row'=8,'col'=32] {'row','col'}, dimensions={0} | all-to-all | bytes 786432 | tf_op jit(solution)/shard_map/while/body/all_to_all | solution.py:403
  151.2 6.0 %all-to-all-start.2 = ((f32[32,80,128]{2,1,0:T(8,128)}), f32[32,80,128]{2,1,0:T(8,128)S(1)}, u32[]{:S(2)}, u32[]{:S(2)}) async-start(f32[32,80,128]{2,1,0:T(8,128)} %get-tuple-element.188), calls=%async_computation.2 | async-start | bytes 2621440 | tf_op jit(solution)/shard_map/all_to_all | solution.py:386
  157.2 0.9 broadcast_in_dim.35
  158.1 0.8 while.13
  158.1 0.8 copy.13
  158.9 1.2 reshape.53.modes_ref
  160.1 2.4 %shard_map.76 = f32[32,48,128]{2,1,0:T(8,128)} custom-call(s32[16]{0:T(128)S(1)} %broadcast_add_fusion.owner_ref, f32[768,128]{1,0:T(8,128)S(1)} %reshape.53.modes_ref, f32[256,128]{1,0:T(8,128)S(1)} %copy-done.1), custom_call_target="tpu_custom_call" | custom-call | tf_op jit(solution)/shard_map/pallas_call | solution.py:409
  162.5 28.1 %all-to-all-done.2 = f32[32,80,128]{2,1,0:T(8,128)S(1)} async-done(((f32[32,80,128]{2,1,0:T(8,128)}), f32[32,80,128]{2,1,0:T(8,128)S(1)}, u32[]{:S(2)}, u32[]{:S(2)}) %all-to-all-start.2) | async-done | bytes 1310752 | tf_op jit(solution)/shard_map/all_to_all | solution.py:386
  190.6 5.6 %all-to-all-start.5 = ((f32[32,48,128]{2,1,0:T(8,128)}), f32[32,48,128]{2,1,0:T(8,128)S(1)}, u32[]{:S(2)}, u32[]{:S(2)}) async-start(f32[32,48,128]{2,1,0:T(8,128)} %shard_map.76), calls=%async_computation.5 | async-start | bytes 1572864 | tf_op jit(solution)/shard_map/all_to_all | solution.py:415
  196.2 0.1 pad_add_fusion.place_ref
  196.2 21.1 %all-to-all-done.5 = f32[32,48,128]{2,1,0:T(8,128)S(1)} async-done(((f32[32,48,128]{2,1,0:T(8,128)}), f32[32,48,128]{2,1,0:T(8,128)S(1)}, u32[]{:S(2)}, u32[]{:S(2)}) %all-to-all-start.5) | async-done | bytes 786464 | tf_op jit(solution)/shard_map/all_to_all | solution.py:415
  217.3 2.8 %shard_map.77 = f32[5,16,4096]{2,1,0:T(8,128)} custom-call(s32[2]{0:T(128)S(1)} %pad_add_fusion.place_ref, f32[2560,128]{1,0:T(8,128)S(1)} %bitcast.16, f32[1536,128]{1,0:T(8,128)S(1)} %bitcast.17), custom_call_target="tpu_custom_call" | custom-call | tf_op jit(solution)/shard_map/pallas_call | solution.py:416
  (5 shorter events, 0.0 us)
Async XLA Ops:
  1.3 20.1 %all-to-all-start = ((s32[32,1,128]{2,1,0:T(1,128)}), s32[32,1,128]{2,1,0:T(1,128)S(1)}, u32[]{:S(2)}, u32[]{:S(2)}) async-start(s32[32,1,128]{2,1,0:T(1,128)} %broadcast_in_dim.31), calls=%async_computation | async-start | bytes 32768 | tf_op jit(solution)/shard_map/all_to_all | solution.py:330
  24.6 1.3 copy-start
  28.1 37.7 %all-to-all-start.1 = ((f32[32,80,128]{2,1,0:T(8,128)}), f32[32,80,128]{2,1,0:T(8,128)S(1)}, u32[]{:S(2)}, u32[]{:S(2)}) async-start(f32[32,80,128]{2,1,0:T(8,128)} %bitcast.5), calls=%async_computation.1 | async-start | bytes 2621440 | tf_op jit(solution)/shard_map/all_to_all | solution.py:350
  33.1 48.6 %copy-start.1 = (f32[256,128]{1,0:T(8,128)S(1)}, f32[256,128]{1,0:T(8,128)}, u32[]{:S(2)}) copy-start(f32[256,128]{1,0:T(8,128)} %constant.101.clone.table_ref) | copy-start | bytes 393220
  68.4 54.3 %copy-start.4 = (f32[256]{0:T(256)S(1)}, f32[256]{0:T(256)}, u32[]{:S(2)}) copy-start(f32[256]{0:T(256)} %constant.104.clone) | copy-start | bytes 3076
  68.4 13.3 %collective-permute-start.2 = (f32[5,32,4,128]{3,2,1,0:T(4,128)S(1)}, f32[5,32,4,128]{3,2,1,0:T(4,128)S(1)}, u32[]{:S(2)}, u32[]{:S(2)}) collective-permute-start(f32[5,32,4,128]{3,2,1,0:T(4,128)S(1)} %get-tuple-element.186), channel_id=1, source_target_pairs={{0,1},{1,2},{2,3},{3,4},{4,5},{5,6},{6,7},{7,8},{8,9},{9,10},{10,1... | collective-permute-start | bytes 983048 | tf_op jit(solution)/shard_map/ppermute | solution.py:371
  70.0 11.8 %collective-permute-start.3 = (f32[5,32,4,128]{3,2,1,0:T(4,128)S(1)}, f32[5,32,4,128]{3,2,1,0:T(4,128)S(1)}, u32[]{:S(2)}, u32[]{:S(2)}) collective-permute-start(f32[5,32,4,128]{3,2,1,0:T(4,128)S(1)} %get-tuple-element.187), channel_id=1, source_target_pairs={{0,31},{1,0},{2,1},{3,2},{4,3},{5,4},{6,5},{7,6},{8,7},{9,8},{10,9... | collective-permute-start | bytes 983048 | tf_op jit(solution)/shard_map/ppermute | solution.py:372
  70.5 2.1 collective-permute-start.1
  70.5 5.2 %collective-permute-start = (f32[5,4,8,128]{3,2,1,0:T(8,128)S(1)}, f32[5,4,8,128]{3,2,1,0:T(8,128)S(1)}, u32[]{:S(2)}, u32[]{:S(2)}) collective-permute-start(f32[5,4,8,128]{3,2,1,0:T(8,128)S(1)} %get-tuple-element.184), channel_id=1, source_target_pairs={{0,32},{32,64},{64,96},{96,128},{128,160},{160,192},{192,224},{224... | collective-permute-start | bytes 245768 | tf_op jit(solution)/shard_map/ppermute | solution.py:369
  75.8 47.1 %copy-start.2 = (f32[256,256]{1,0:T(8,128)S(1)}, f32[256,256]{1,0:T(8,128)}, u32[]{:S(2)}) copy-start(f32[256,256]{1,0:T(8,128)} %constant.102.clone.table_ref) | copy-start | bytes 786436
  75.8 47.1 %copy-start.3 = (f32[1,256]{1,0:T(1,128)S(1)}, f32[1,256]{1,0:T(1,128)}, u32[]{:S(2)}) copy-start(f32[1,256]{1,0:T(1,128)} %constant.103.clone.eigx_ref) | copy-start | bytes 3076
  75.8 5.9 %collective-permute-start.4 = (f32[5,4,4,128]{3,2,1,0:T(4,128)S(1)}, f32[5,4,4,128]{3,2,1,0:T(4,128)S(1)}, u32[]{:S(2)}, u32[]{:S(2)}) collective-permute-start(f32[5,4,4,128]{3,2,1,0:T(4,128)S(1)} %get-tuple-element.200), channel_id=1, source_target_pairs={{0,1},{1,2},{2,3},{3,4},{4,5},{5,6},{6,7},{7,8},{8,9},{9,10},{10,1... | collective-permute-start | bytes 122888 | tf_op jit(solution)/shard_map/ppermute | solution.py:374
  77.4 4.4 %collective-permute-start.5 = (f32[5,4,4,128]{3,2,1,0:T(4,128)S(1)}, f32[5,4,4,128]{3,2,1,0:T(4,128)S(1)}, u32[]{:S(2)}, u32[]{:S(2)}) collective-permute-start(f32[5,4,4,128]{3,2,1,0:T(4,128)S(1)} %get-tuple-element.199), channel_id=1, source_target_pairs={{0,31},{1,0},{2,1},{3,2},{4,3},{5,4},{6,5},{7,6},{8,7},{9,8},{10,9... | collective-permute-start | bytes 122888 | tf_op jit(solution)/shard_map/ppermute | solution.py:375
  94.9 27.9 %all-to-all-start.3 = ((f32[256,2,128]{2,1,0:T(2,128)}), f32[256,2,128]{2,1,0:T(2,128)S(1)}, u32[]{:S(2)}, u32[]{:S(2)}) async-start(f32[256,2,128]{2,1,0:T(2,128)} %bitcast.9), calls=%async_computation.3 | async-start | bytes 524288 | tf_op jit(solution)/shard_map/while/body/all_to_all | solution.py:392
  151.2 39.3 %all-to-all-start.2 = ((f32[32,80,128]{2,1,0:T(8,128)}), f32[32,80,128]{2,1,0:T(8,128)S(1)}, u32[]{:S(2)}, u32[]{:S(2)}) async-start(f32[32,80,128]{2,1,0:T(8,128)} %get-tuple-element.188), calls=%async_computation.2 | async-start | bytes 2621440 | tf_op jit(solution)/shard_map/all_to_all | solution.py:386
  190.6 26.7 %all-to-all-start.5 = ((f32[32,48,128]{2,1,0:T(8,128)}), f32[32,48,128]{2,1,0:T(8,128)S(1)}, u32[]{:S(2)}, u32[]{:S(2)}) async-start(f32[32,48,128]{2,1,0:T(8,128)} %shard_map.76), calls=%async_computation.5 | async-start | bytes 1572864 | tf_op jit(solution)/shard_map/all_to_all | solution.py:415

commit v6 on v4

--- a/solution.py
+++ b/solution.py
@@ -68,14 +68,22 @@
     return arrays
 
 
-def pack_kernel(start_ref, fields_ref, out_ref):
-    shift = start_ref[0]
+def stage_kernel(fields_ref, out_ref):
     for q in range(5):
         for tile in range(2 * PE):
             a, half = tile // 2, tile % 2
             slots = fields_ref[q, :, tile * 128 : (tile + 1) * 128]
-            turned = pltpu.roll(slots, shift, 0)
-            out_ref[pl.ds(half * BRICK + q * PE + a, CAP, stride=2 * BRICK), :] = turned
+            out_ref[pl.ds(half * BRICK + q * PE + a, CAP, stride=2 * BRICK), :] = slots
+
+
+def turn_kernel(column_ref, counts_ref, staged_ref, out_ref):
+    counts = counts_ref[...].reshape(COLS, 128)
+    before = lax.broadcasted_iota(jnp.int32, (COLS, 128), 0) < column_ref[0]
+    start = (jnp.sum(jnp.where(before, counts, 0.0)) * (1.0 / 128.0)).astype(jnp.int32)
+    size = 2 * BRICK
+    for y in range(CAP):
+        source = pl.multiple_of(((y - start) & (CAP - 1)) * size, 8)
+        out_ref[y * size : (y + 1) * size, :] = staged_ref[pl.ds(source, size), :]
 
 
 def unpack_kernel(owner_ref, recv_ref, own_ref, xfirst_ref, xlast_ref, yfirst_ref, ylast_ref, flat_ref):
@@ -318,14 +326,16 @@
 
 
 def gather_counts(counts):
-    copies = jnp.broadcast_to(counts.reshape(1, 1, 1), (COLS, 1, 128))
-    return lax.all_to_all(copies, "col", split_axis=0, concat_axis=0, tiled=True)[:, 0, 0]
+    copies = jnp.broadcast_to(counts.astype(jnp.float32).reshape(1, 1, 1), (COLS, 1, 128))
+    return lax.all_to_all(copies, "col", split_axis=0, concat_axis=0, tiled=True)
 
 
 def on_device(fields, counts):
     my_row = lax.axis_index("row")
     my_column = lax.axis_index("col")
-    row_counts = gather_counts(counts)
+    staged = call(stage_kernel, [(COLS * BRICK, 128)], (1, ()))(fields.transpose(1, 0, 2))
+    spread_counts = gather_counts(counts)
+    row_counts = spread_counts[:, 0, 0].astype(jnp.int32)
     column_ids = jnp.arange(COLS, dtype=jnp.int32)
     starts = jnp.sum(
         jnp.where(column_ids[None, :] < column_ids[:, None], row_counts[None, :], 0), axis=1
@@ -336,8 +346,8 @@
     owners = jnp.sum((starts[None, :] <= wanted[:, None]).astype(jnp.int32), axis=1) - 1
     turn = own_start % CAP
 
-    sent = call(pack_kernel, [(COLS * BRICK, 128)], (2, (0,)))(
-        turn.reshape(1), fields.transpose(1, 0, 2)
+    sent = call(turn_kernel, [(COLS * BRICK, 128)], (3, (0,)))(
+        my_column.reshape(1), spread_counts, staged
     )
     arrived = lax.all_to_all(
         sent.reshape(COLS, BRICK, 128), "col", split_axis=0, concat_axis=0, tiled=True
@@ -391,7 +401,7 @@
         jnp.asarray(np.broadcast_to(eig[:, None], (GX, 128))),
     )
     strips = lax.all_to_all(
-        strips.reshape(256, 3, 128), ("row", "col"), split_axis=0, concat_axis=0, tiled=True
+        strips.reshape(256, 1, 384), ("row", "col"), split_axis=0, concat_axis=0, tiled=True
     )
     returned = call(
         kick_kernel,

time: 194 us -> 185 us (0.954)
  waiting for transfers between devices: 94.6 us -> 88.9 us
  blocking collectives: 26.2 us -> 23.4 us
    all_to_all x1, blocking collectives: 26.2 us -> 23.4 us  [on_device(): lax.all_to_all(strips.reshape(256, 1, 384), ('row', 'col'), split_axis=0,...]
    all_to_all x1, waiting for transfers between devices: 33.3 us -> 30.7 us  [on_device(): lax.all_to_all(returned, 'col', split_axis=0, concat_axis=0, tiled=True)]
    all_to_all x1, waiting for transfers between devices: 8.44 us -> 6.03 us  [gather_counts(): lax.all_to_all(copies, 'col', split_axis=0, concat_axis=0, tiled=True)]
  transfers between devices with their start and end apart: 10 -> 10, of which waited for: 7 -> 7; matrix products, arithmetic and copies ran while one was open for 0% -> 1% of each run, Pallas kernels for 0% -> 1%
where the time goes in v6:
time: 185 us
  waiting for transfers between devices  88.9 us (48%)
  starting transfers between devices  42.9 us (23%)
  blocking collectives  23.4 us (13%)
  Pallas kernels  22.9 us (12%)
  between operations  2.86 us (2%)
  local copies, waits for them, and re-layouts  2.04 us (1%)
    all_to_all x1, waiting for transfers between devices, on_device(): lax.all_to_all(sent.reshape(COLS, BRICK, 128), 'col', split_axis=0, conca...  31.6 us
    all_to_all x1, waiting for transfers between devices, on_device(): lax.all_to_all(returned, 'col', split_axis=0, concat_axis=0, tiled=True)  30.7 us
    all_to_all x1, blocking collectives, on_device(): lax.all_to_all(strips.reshape(256, 1, 384), ('row', 'col'), split_axis=0,...  23.4 us
    all_to_all x1, waiting for transfers between devices, on_device(): lax.all_to_all(modes.reshape(256, 2, 128), ('row', 'col'), split_axis=0,...  13.9 us
    all_to_all x1, starting transfers between devices, on_device(): lax.all_to_all(modes.reshape(256, 2, 128), ('row', 'col'), split_axis=0,...  13.8 us
    all_to_all x1, starting transfers between devices, gather_counts(): lax.all_to_all(copies, 'col', split_axis=0, concat_axis=0, tiled=True)  11.6 us
    pallas_call x1, Pallas kernels, on_device(): call(euler_kernel, [(5, BX, BY, GZ), (512, 128)], (8, ()), [(5, BX + 2 *...  10.6 us
    all_to_all x1, waiting for transfers between devices, gather_counts(): lax.all_to_all(copies, 'col', split_axis=0, concat_axis=0, tiled=True)  6.03 us
  transfers between devices with their start and end apart: 10, of which 7 were waited for; matrix products, arithmetic and copies ran while one was open for 1% of the time, Pallas kernels for 1%

profile of v6, /device:TPU:2, one launch (start us, length us, event | category | flops | bytes accessed | tf_op | source)
XLA Modules:
  0.0 184.7 jit_solution(9638249282118399071)
XLA Ops:
  0.7 0.6 broadcast_in_dim.29
  1.3 11.6 %all-to-all-start = ((f32[32,1,128]{2,1,0:T(1,128)}), f32[32,1,128]{2,1,0:T(1,128)S(1)}, u32[]{:S(2)}, u32[]{:S(2)}) async-start(f32[32,1,128]{2,1,0:T(1,128)} %broadcast_in_dim.29), calls=%async_computation | async-start | bytes 32768 | tf_op jit(solution)/shard_map/all_to_all | solution.py:330
  12.9 0.0 copy-start
  12.9 1.3 copy-done
  14.2 1.1 shard_map.73.staged_ref
  15.3 6.0 %all-to-all-done.counts_ref = f32[32,1,128]{2,1,0:T(1,128)S(1)} async-done(((f32[32,1,128]{2,1,0:T(1,128)}), f32[32,1,128]{2,1,0:T(1,128)S(1)}, u32[]{:S(2)}, u32[]{:S(2)}) %all-to-all-start) | async-done | bytes 16416 | tf_op jit(solution)/shard_map/all_to_all | solution.py:330
  21.3 1.3 shard_map.74
  22.6 5.1 %all-to-all-start.1 = ((f32[32,80,128]{2,1,0:T(8,128)}), f32[32,80,128]{2,1,0:T(8,128)S(1)}, u32[]{:S(2)}, u32[]{:S(2)}) async-start(f32[32,80,128]{2,1,0:T(8,128)} %bitcast.5), calls=%async_computation.1 | async-start | bytes 2621440 | tf_op jit(solution)/shard_map/all_to_all | solution.py:352
  27.7 0.0 copy-start.1
  27.7 0.7 fusion.1
  28.4 0.1 select_reduce_fusion
  28.5 0.2 convert_reduce_fusion
  28.7 31.6 %all-to-all-done.1.recv_ref = f32[32,80,128]{2,1,0:T(8,128)S(1)} async-done(((f32[32,80,128]{2,1,0:T(8,128)}), f32[32,80,128]{2,1,0:T(8,128)S(1)}, u32[]{:S(2)}, u32[]{:S(2)}) %all-to-all-start.1) | async-done | bytes 1310752 | tf_op jit(solution)/shard_map/all_to_all | solution.py:352
  60.3 2.7 %shard_map.75 = (f32[5,32,8,128]{3,2,1,0:T(8,128)S(1)}, f32[5,4,8,128]{3,2,1,0:T(8,128)S(1)}, f32[5,4,8,128]{3,2,1,0:T(8,128)S(1)}, f32[5,32,4,128]{3,2,1,0:T(4,128)S(1)}, f32[5,32,4,128]{3,2,1,0:T(4,128)S(1)}) custom-call(s32[16]{0:T(128)S(1)} %broadcast_add_fusion.owner_ref, f32[32,80,128]{2,1,0:T(8,128)S(1)} %all-to-all-done.1.recv_ref), custom_call_target="tpu_custom_call" | custom-call | tf_op jit(solution)/shard_map/pallas_call | solution.py:355
  63.0 0.0 copy-start.4
  63.0 1.5 collective-permute-start.2
  64.5 0.6 collective-permute-start.3
  65.1 0.0 collective-permute-start.1
  65.1 0.5 collective-permute-start
  65.6 1.6 collective-permute-done.1.xhigh_ref
  67.1 0.0 copy-start.2
  67.1 0.0 copy-start.3
  67.1 3.2 %collective-permute-done.xlow_ref = f32[5,4,8,128]{3,2,1,0:T(8,128)S(1)} collective-permute-done((f32[5,4,8,128]{3,2,1,0:T(8,128)S(1)}, f32[5,4,8,128]{3,2,1,0:T(8,128)S(1)}, u32[]{:S(2)}, u32[]{:S(2)}) %collective-permute-start) | collective-permute-done | bytes 81952 | tf_op jit(solution)/shard_map/ppermute | solution.py:371
  70.3 1.5 collective-permute-start.4
  71.9 2.5 %collective-permute-start.5 = (f32[5,4,4,128]{3,2,1,0:T(4,128)S(1)}, f32[5,4,4,128]{3,2,1,0:T(4,128)S(1)}, u32[]{:S(2)}, u32[]{:S(2)}) collective-permute-start(f32[5,4,4,128]{3,2,1,0:T(4,128)S(1)} %get-tuple-element.19), channel_id=1, source_target_pairs={{0,31},{1,0},{2,1},{3,2},{4,3},{5,4},{6,5},{7,6},{8,7},{9,8},{10,9... | collective-permute-start | bytes 122888 | tf_op jit(solution)/shard_map/ppermute | solution.py:377
  74.4 1.9 %collective-permute-done.4.clow_ref = f32[5,4,4,128]{3,2,1,0:T(4,128)S(1)} collective-permute-done((f32[5,4,4,128]{3,2,1,0:T(4,128)S(1)}, f32[5,4,4,128]{3,2,1,0:T(4,128)S(1)}, u32[]{:S(2)}, u32[]{:S(2)}) %collective-permute-start.4) | collective-permute-done | bytes 40992 | tf_op jit(solution)/shard_map/ppermute | solution.py:376
  76.3 0.0 collective-permute-done.5.chigh_ref
  76.3 0.0 collective-permute-done.2.ylow_ref
  76.3 0.0 collective-permute-done.3.yhigh_ref
  76.3 0.0 copy-done.1
  76.3 10.6 %shard_map.76 = (f32[5,32,8,128]{3,2,1,0:T(8,128)S(1)}, f32[512,128]{1,0:T(8,128)}) custom-call(f32[5,32,8,128]{3,2,1,0:T(8,128)S(1)} %get-tuple-element.12.own_ref, f32[5,4,8,128]{3,2,1,0:T(8,128)S(1)} %collective-permute-done.xlow_ref, f32[5,4,8,128]{3,2,1,0:T(8,128)S(1)} %collective-permute-done.1.xhigh_ref, ...), custom_call_target="tpu_custom_call" | custom-call | tf_op jit(solution)/shard_map/pallas_call | solution.py:382
  86.9 13.8 %all-to-all-start.2 = ((f32[256,2,128]{2,1,0:T(2,128)}), f32[256,2,128]{2,1,0:T(2,128)S(1)}, u32[]{:S(2)}, u32[]{:S(2)}) async-start(f32[256,2,128]{2,1,0:T(2,128)} %bitcast.8), calls=%async_computation.2 | async-start | bytes 524288 | tf_op jit(solution)/shard_map/all_to_all | solution.py:388
  100.8 13.9 %all-to-all-done.2 = f32[256,2,128]{2,1,0:T(2,128)S(1)} async-done(((f32[256,2,128]{2,1,0:T(2,128)}), f32[256,2,128]{2,1,0:T(2,128)S(1)}, u32[]{:S(2)}, u32[]{:S(2)}) %all-to-all-start.2) | async-done | bytes 262176 | tf_op jit(solution)/shard_map/all_to_all | solution.py:388
  114.7 0.0 copy-done.4
  114.7 0.1 jit_solution_.3.eigy_ref
  114.8 0.0 copy-done.2
  114.8 0.0 copy-done.3
  114.9 2.0 %shard_map.77 = f32[768,128]{1,0:T(8,128)S(1)} custom-call(s32[1]{0:T(128)} %bitcast.6.place_ref, f32[1]{0:T(128)} %bitcast.7.wave_ref, f32[512,128]{1,0:T(8,128)S(1)} %bitcast.19, f32[256,256]{1,0:T(8,128)S(1)} %copy-done.2, f32[1,256]{1,0:T(1,128)S(1)} %copy-done.3, f32[256,128]{1,0:T(8,128)S(1)} %jit_solution_.3.eigy_ref), custom_call_target="tpu_custom_call" | custom-call | tf_op jit(solution)/shard_map/pallas_call | solution.py:395
  116.9 23.4 %all_to_all.25 = f32[256,1,384]{2,1,0:T(1,128)S(1)} all-to-all(f32[256,1,384]{2,1,0:T(1,128)S(1)} %bitcast.16), channel_id=1, replica_groups=mesh['row'=8,'col'=32] {'row','col'}, dimensions={0} | all-to-all | bytes 786432 | tf_op jit(solution)/shard_map/all_to_all | solution.py:403
  140.3 2.9 %shard_map.78 = f32[32,80,128]{2,1,0:T(8,128)} custom-call(s32[16]{0:T(128)S(1)} %broadcast_add_fusion.owner_ref, f32[5,32,8,128]{3,2,1,0:T(8,128)S(1)} %get-tuple-element.17.stepped_ref, f32[768,128]{1,0:T(8,128)S(1)} %bitcast.17, f32[256,128]{1,0:T(8,128)S(1)} %copy-done.1), custom_call_target="tpu_custom_call" | custom-call | tf_op jit(solution)/shard_map/pallas_call | solution.py:406
  143.2 5.8 %all-to-all-start.4 = ((f32[32,80,128]{2,1,0:T(8,128)}), f32[32,80,128]{2,1,0:T(8,128)S(1)}, u32[]{:S(2)}, u32[]{:S(2)}) async-start(f32[32,80,128]{2,1,0:T(8,128)} %shard_map.78), calls=%async_computation.4 | async-start | bytes 2621440 | tf_op jit(solution)/shard_map/all_to_all | solution.py:412
  148.9 0.7 fusion.2
  151.5 0.1 pad_add_fusion.place_ref
  151.6 30.7 %all-to-all-done.4 = f32[32,80,128]{2,1,0:T(8,128)S(1)} async-done(((f32[32,80,128]{2,1,0:T(8,128)}), f32[32,80,128]{2,1,0:T(8,128)S(1)}, u32[]{:S(2)}, u32[]{:S(2)}) %all-to-all-start.4) | async-done | bytes 1310752 | tf_op jit(solution)/shard_map/all_to_all | solution.py:412
  182.3 2.4 %shard_map.79 = f32[5,16,4096]{2,1,0:T(8,128)} custom-call(s32[2]{0:T(128)S(1)} %pad_add_fusion.place_ref, f32[2560,128]{1,0:T(8,128)S(1)} %bitcast.15), custom_call_target="tpu_custom_call" | custom-call | tf_op jit(solution)/shard_map/pallas_call | solution.py:414
  (5 shorter events, 0.0 us)
Async XLA Ops:
  1.3 20.1 %all-to-all-start = ((f32[32,1,128]{2,1,0:T(1,128)}), f32[32,1,128]{2,1,0:T(1,128)S(1)}, u32[]{:S(2)}, u32[]{:S(2)}) async-start(f32[32,1,128]{2,1,0:T(1,128)} %broadcast_in_dim.29), calls=%async_computation | async-start | bytes 32768 | tf_op jit(solution)/shard_map/all_to_all | solution.py:330
  12.9 1.3 copy-start
  22.6 37.7 %all-to-all-start.1 = ((f32[32,80,128]{2,1,0:T(8,128)}), f32[32,80,128]{2,1,0:T(8,128)S(1)}, u32[]{:S(2)}, u32[]{:S(2)}) async-start(f32[32,80,128]{2,1,0:T(8,128)} %bitcast.5), calls=%async_computation.1 | async-start | bytes 2621440 | tf_op jit(solution)/shard_map/all_to_all | solution.py:352
  27.7 48.6 %copy-start.1 = (f32[256,128]{1,0:T(8,128)S(1)}, f32[256,128]{1,0:T(8,128)}, u32[]{:S(2)}) copy-start(f32[256,128]{1,0:T(8,128)} %constant.76.clone.table_ref) | copy-start | bytes 393220
  63.0 51.8 %copy-start.4 = (f32[256]{0:T(256)S(1)}, f32[256]{0:T(256)}, u32[]{:S(2)}) copy-start(f32[256]{0:T(256)} %constant.79.clone) | copy-start | bytes 3076
  63.0 13.3 %collective-permute-start.2 = (f32[5,32,4,128]{3,2,1,0:T(4,128)S(1)}, f32[5,32,4,128]{3,2,1,0:T(4,128)S(1)}, u32[]{:S(2)}, u32[]{:S(2)}) collective-permute-start(f32[5,32,4,128]{3,2,1,0:T(4,128)S(1)} %get-tuple-element.15), channel_id=1, source_target_pairs={{0,1},{1,2},{2,3},{3,4},{4,5},{5,6},{6,7},{7,8},{8,9},{9,10},{10,1... | collective-permute-start | bytes 983048 | tf_op jit(solution)/shard_map/ppermute | solution.py:373
  64.5 11.8 %collective-permute-start.3 = (f32[5,32,4,128]{3,2,1,0:T(4,128)S(1)}, f32[5,32,4,128]{3,2,1,0:T(4,128)S(1)}, u32[]{:S(2)}, u32[]{:S(2)}) collective-permute-start(f32[5,32,4,128]{3,2,1,0:T(4,128)S(1)} %get-tuple-element.16), channel_id=1, source_target_pairs={{0,31},{1,0},{2,1},{3,2},{4,3},{5,4},{6,5},{7,6},{8,7},{9,8},{10,9... | collective-permute-start | bytes 983048 | tf_op jit(solution)/shard_map/ppermute | solution.py:374
  65.1 2.1 %collective-permute-start.1 = (f32[5,4,8,128]{3,2,1,0:T(8,128)S(1)}, f32[5,4,8,128]{3,2,1,0:T(8,128)S(1)}, u32[]{:S(2)}, u32[]{:S(2)}) collective-permute-start(f32[5,4,8,128]{3,2,1,0:T(8,128)S(1)} %get-tuple-element.14), channel_id=1, source_target_pairs={{0,224},{32,0},{64,32},{96,64},{128,96},{160,128},{192,160},{224,1... | collective-permute-start | bytes 245768 | tf_op jit(solution)/shard_map/ppermute | solution.py:372
  65.1 5.2 %collective-permute-start = (f32[5,4,8,128]{3,2,1,0:T(8,128)S(1)}, f32[5,4,8,128]{3,2,1,0:T(8,128)S(1)}, u32[]{:S(2)}, u32[]{:S(2)}) collective-permute-start(f32[5,4,8,128]{3,2,1,0:T(8,128)S(1)} %get-tuple-element.13), channel_id=1, source_target_pairs={{0,32},{32,64},{64,96},{96,128},{128,160},{160,192},{192,224},{224... | collective-permute-start | bytes 245768 | tf_op jit(solution)/shard_map/ppermute | solution.py:371
  67.1 47.7 %copy-start.2 = (f32[256,256]{1,0:T(8,128)S(1)}, f32[256,256]{1,0:T(8,128)}, u32[]{:S(2)}) copy-start(f32[256,256]{1,0:T(8,128)} %constant.77.clone.table_ref) | copy-start | bytes 786436
  67.1 47.7 %copy-start.3 = (f32[1,256]{1,0:T(1,128)S(1)}, f32[1,256]{1,0:T(1,128)}, u32[]{:S(2)}) copy-start(f32[1,256]{1,0:T(1,128)} %constant.78.clone.eigx_ref) | copy-start | bytes 3076
  70.3 5.9 %collective-permute-start.4 = (f32[5,4,4,128]{3,2,1,0:T(4,128)S(1)}, f32[5,4,4,128]{3,2,1,0:T(4,128)S(1)}, u32[]{:S(2)}, u32[]{:S(2)}) collective-permute-start(f32[5,4,4,128]{3,2,1,0:T(4,128)S(1)} %get-tuple-element.20), channel_id=1, source_target_pairs={{0,1},{1,2},{2,3},{3,4},{4,5},{5,6},{6,7},{7,8},{8,9},{9,10},{10,1... | collective-permute-start | bytes 122888 | tf_op jit(solution)/shard_map/ppermute | solution.py:376
  71.9 4.4 %collective-permute-start.5 = (f32[5,4,4,128]{3,2,1,0:T(4,128)S(1)}, f32[5,4,4,128]{3,2,1,0:T(4,128)S(1)}, u32[]{:S(2)}, u32[]{:S(2)}) collective-permute-start(f32[5,4,4,128]{3,2,1,0:T(4,128)S(1)} %get-tuple-element.19), channel_id=1, source_target_pairs={{0,31},{1,0},{2,1},{3,2},{4,3},{5,4},{6,5},{7,6},{8,7},{9,8},{10,9... | collective-permute-start | bytes 122888 | tf_op jit(solution)/shard_map/ppermute | solution.py:377
  86.9 27.9 %all-to-all-start.2 = ((f32[256,2,128]{2,1,0:T(2,128)}), f32[256,2,128]{2,1,0:T(2,128)S(1)}, u32[]{:S(2)}, u32[]{:S(2)}) async-start(f32[256,2,128]{2,1,0:T(2,128)} %bitcast.8), calls=%async_computation.2 | async-start | bytes 524288 | tf_op jit(solution)/shard_map/all_to_all | solution.py:388
  143.2 39.2 %all-to-all-start.4 = ((f32[32,80,128]{2,1,0:T(8,128)}), f32[32,80,128]{2,1,0:T(8,128)S(1)}, u32[]{:S(2)}, u32[]{:S(2)}) async-start(f32[32,80,128]{2,1,0:T(8,128)} %shard_map.78), calls=%async_computation.4 | async-start | bytes 2621440 | tf_op jit(solution)/shard_map/all_to_all | solution.py:412

commit v7 on v6

--- a/solution.py
+++ b/solution.py
@@ -24,7 +24,7 @@
 time_step = 0.03
 four_pi_g = 10.0
 
-PARAMS = pltpu.CompilerParams(vmem_limit_bytes=40 * 2**20)
+PARAMS = pltpu.CompilerParams(vmem_limit_bytes=16 * 2**20)
 VM = pl.BlockSpec(memory_space=pltpu.VMEM)
 SM = pl.BlockSpec(memory_space=pltpu.SMEM)
 
@@ -110,6 +110,8 @@
 
 
 def half_flux(states, direction, sign):
+    if len(states) == 2:
+        return [0.5 * states[1] + sign * 2.0 * states[0]]
     density, energy = states[0], states[4]
     inverse = 1.0 / density
     velocity = 0.5 * states[1 + direction] * inverse
@@ -143,12 +145,21 @@
     return [f - pltpu.roll(f, 1, axis) for f in faces]
 
 
-def euler_stage(load, store, first_row, count, keep):
+def all_fields(states, direction):
+    return states
+
+
+def mass_fields(states, direction):
+    return [states[0], states[1 + direction]]
+
+
+def euler_stage(load, store, first_row, count, keep, pick=all_fields):
     def slopes_of(low, mid, high):
         return [minmod(b - a, c - b) for a, b, c in zip(low, mid, high)]
 
     cut = lambda states: [u[:keep] for u in states]
-    r0, r1, r2, r3 = [cut(load(first_row + k)) for k in (-2, -1, 0, 1)]
+    cut_x = lambda states: cut(pick(states, 0))
+    r0, r1, r2, r3 = [cut_x(load(first_row + k)) for k in (-2, -1, 0, 1)]
     upper_prev, _ = edge_terms(r1, slopes_of(r0, r1, r2), 0)
     upper_now, lower_now = edge_terms(r2, slopes_of(r1, r2, r3), 0)
     face = [u + w for u, w in zip(upper_prev, lower_now)]
@@ -156,13 +167,13 @@
     def step(k, carry):
         face_low, upper_here = carry
         i = first_row + k
-        here, above, far = load(i), cut(load(i + 1)), cut(load(i + 2))
+        here, above, far = load(i), cut_x(load(i + 1)), cut_x(load(i + 2))
         mine = cut(here)
-        upper_next, lower_next = edge_terms(above, slopes_of(mine, above, far), 0)
+        upper_next, lower_next = edge_terms(above, slopes_of(pick(mine, 0), above, far), 0)
         face_high = [u + w for u, w in zip(upper_here, lower_next)]
         change = [h - l for h, l in zip(face_high, face_low)]
-        along_y = cut(line_change(here, 1, 0))
-        along_z = line_change(mine, 2, 1)
+        along_y = cut(line_change(pick(here, 1), 1, 0))
+        along_z = line_change(pick(mine, 2), 2, 1)
         rate = [-(a + b + c) for a, b, c in zip(change, along_y, along_z)]
         store(i, mine, rate)
         return tuple(face_high), tuple(upper_next)
@@ -172,7 +183,7 @@
 
 def euler_kernel(
     own_ref, xlow_ref, xhigh_ref, ylow_ref, yhigh_ref, clow_ref, chigh_ref, table_ref,
-    stepped_ref, modes_ref, ext_ref, first_ref, flat_ref,
+    first_ref, modes_ref, ext_ref, flat_ref,
 ):
     low, high = slice(BY + HALO, BY + 2 * HALO), slice(BY, BY + HALO)
     inner = slice(HALO, HALO + BX)
@@ -197,24 +208,33 @@
 
     euler_stage(load_ext, store_first, 2, BX + 4, BY + 2 * HALO)
 
+    def load_mass(i):
+        return [first_ref[q, i] for q in range(4)]
+
+    def store_density(i, states, rates):
+        second = states[0] + time_step * rates[0]
+        row = pl.multiple_of((i - HALO) * BY, BY)
+        flat_ref[pl.ds(row, BY), :] = 0.5 * ext_ref[0, i, 0:BY] + 0.5 * second
+
+    euler_stage(load_mass, store_density, HALO, BX, BY, mass_fields)
+    density = jnp.concatenate(
+        [flat_ref[pl.ds(b, BX, stride=BY), :] for b in range(BY)], axis=0
+    )
+    spread = dot(table_ref[...], density, ((1,), (1,)))
+    modes_ref[pl.ds(0, 256, stride=2), :] = spread[:, :128]
+    modes_ref[pl.ds(1, 256, stride=2), :] = spread[:, 128:]
+
+
+def second_kernel(own_ref, first_ref, stepped_ref):
     def load_first(i):
         return [first_ref[q, i] for q in range(5)]
 
     def store_stepped(i, states, rates):
         for q in range(5):
             second = states[q] + time_step * rates[q]
-            value = 0.5 * ext_ref[q, i, 0:BY] + 0.5 * second
-            stepped_ref[q, i - HALO] = value
-            if q == 0:
-                flat_ref[pl.ds(pl.multiple_of((i - HALO) * BY, BY), BY), :] = value
+            stepped_ref[q, i - HALO] = 0.5 * own_ref[q, i - HALO] + 0.5 * second
 
     euler_stage(load_first, store_stepped, HALO, BX, BY)
-    density = jnp.concatenate(
-        [flat_ref[pl.ds(b, BX, stride=BY), :] for b in range(BY)], axis=0
-    )
-    spread = dot(table_ref[...], density, ((1,), (1,)))
-    modes_ref[pl.ds(0, 256, stride=2), :] = spread[:, :128]
-    modes_ref[pl.ds(1, 256, stride=2), :] = spread[:, 128:]
 
 
 def plane_kernel(place_ref, wave_ref, modes_ref, table_ref, eigx_ref, eigy_ref, out_ref, plane_ref, wide_ref):
@@ -379,15 +399,15 @@
     table_z = hartley(GZ)
     table_x = hartley(GX)
     modes_of = np.arange(256) % GZ
-    stepped, modes = call(
-        euler_kernel,
-        [(5, BX, BY, GZ), (512, 128)],
-        (8, ()),
-        [(5, BX + 2 * HALO, BY + 2 * HALO, GZ), (5, BX + 2 * HALO, BY + 2 * HALO, GZ), (BX * BY, GZ)],
+    wide = (5, BX + 2 * HALO, BY + 2 * HALO, GZ)
+    first, modes = call(
+        euler_kernel, [wide, (512, 128)], (8, ()), [wide, (BX * BY, GZ)]
     )(own, xlow, xhigh, ylow, yhigh, clow, chigh, jnp.asarray(table_z[modes_of]))
     planes = lax.all_to_all(
         modes.reshape(256, 2, 128), ("row", "col"), split_axis=0, concat_axis=0, tiled=True
     )
+    stepped = call(second_kernel, [(5, BX, BY, GZ)], (2, ()))(own, first)
+    planes, stepped = lax.optimization_barrier((planes, stepped))
     place = my_row * COLS + my_column
     wave_z = place % GZ
     eig = eigenvalues(GX)

time: 185 us -> 185 us (level)
  waiting for transfers between devices: 88.9 us -> 83.6 us
  local copies, waits for them, and re-layouts: 2.04 us -> 4.67 us
  Pallas kernels: 22.9 us -> 25.3 us
    all_to_all x1, waiting for transfers between devices: 13.9 us -> 8.59 us  [on_device(): lax.all_to_all(modes.reshape(256, 2, 128), ('row', 'col'), split_axis=0,...]
    unnamed x10 -> x14, local copies, waits for them, and re-layouts: 1.33 us -> 3.96 us
    pallas_call x1 -> x2, Pallas kernels: 10.6 us -> 13 us  [the longest x1 9.04 us: on_device(): call(euler_kernel, [wide, (512, 128)], (8, ()), [wide, (BX * BY, GZ)])]
  transfers between devices with their start and end apart: 10 -> 10, of which waited for: 7 -> 7; matrix products, arithmetic and copies ran while one was open for 1% -> 1% of each run, Pallas kernels for 1% -> 3%
where the time goes in v7:
time: 185 us
  waiting for transfers between devices  83.6 us (45%)
  starting transfers between devices  42.9 us (23%)
  Pallas kernels  25.3 us (14%)
  blocking collectives  23.6 us (13%)
  local copies, waits for them, and re-layouts  4.67 us (3%)
  between operations  2.87 us (2%)
    all_to_all x1, waiting for transfers between devices, on_device(): lax.all_to_all(sent.reshape(COLS, BRICK, 128), 'col', split_axis=0, conca...  31.6 us
    all_to_all x1, waiting for transfers between devices, on_device(): lax.all_to_all(returned, 'col', split_axis=0, concat_axis=0, tiled=True)  30.7 us
    all_to_all x1, blocking collectives, on_device(): lax.all_to_all(strips.reshape(256, 1, 384), ('row', 'col'), split_axis=0,...  23.6 us
    all_to_all x1, starting transfers between devices, on_device(): lax.all_to_all(modes.reshape(256, 2, 128), ('row', 'col'), split_axis=0,...  13.8 us
    all_to_all x1, starting transfers between devices, gather_counts(): lax.all_to_all(copies, 'col', split_axis=0, concat_axis=0, tiled=True)  11.6 us
    pallas_call x1, Pallas kernels, on_device(): call(euler_kernel, [wide, (512, 128)], (8, ()), [wide, (BX * BY, GZ)])  9.04 us
    all_to_all x1, waiting for transfers between devices, on_device(): lax.all_to_all(modes.reshape(256, 2, 128), ('row', 'col'), split_axis=0,...  8.59 us
    all_to_all x1, waiting for transfers between devices, gather_counts(): lax.all_to_all(copies, 'col', split_axis=0, concat_axis=0, tiled=True)  6.03 us
  transfers between devices with their start and end apart: 10, of which 7 were waited for; matrix products, arithmetic and copies ran while one was open for 1% of the time, Pallas kernels for 3%

profile of v7, /device:TPU:2, one launch (start us, length us, event | category | flops | bytes accessed | tf_op | source)
XLA Modules:
  0.0 184.6 jit_solution(7774059846622417559)
XLA Ops:
  0.7 0.6 broadcast_in_dim.29
  1.3 11.6 %all-to-all-start = ((f32[32,1,128]{2,1,0:T(1,128)}), f32[32,1,128]{2,1,0:T(1,128)S(1)}, u32[]{:S(2)}, u32[]{:S(2)}) async-start(f32[32,1,128]{2,1,0:T(1,128)} %broadcast_in_dim.29), calls=%async_computation | async-start | bytes 32768 | tf_op jit(solution)/shard_map/all_to_all | solution.py:350
  12.9 0.0 copy-start.2
  12.9 1.3 copy-done.2
  14.2 1.1 shard_map.73.staged_ref
  15.3 6.0 %all-to-all-done.counts_ref = f32[32,1,128]{2,1,0:T(1,128)S(1)} async-done(((f32[32,1,128]{2,1,0:T(1,128)}), f32[32,1,128]{2,1,0:T(1,128)S(1)}, u32[]{:S(2)}, u32[]{:S(2)}) %all-to-all-start) | async-done | bytes 16416 | tf_op jit(solution)/shard_map/all_to_all | solution.py:350
  21.3 1.3 shard_map.74
  22.6 5.1 %all-to-all-start.1 = ((f32[32,80,128]{2,1,0:T(8,128)}), f32[32,80,128]{2,1,0:T(8,128)S(1)}, u32[]{:S(2)}, u32[]{:S(2)}) async-start(f32[32,80,128]{2,1,0:T(8,128)} %bitcast.5), calls=%async_computation.1 | async-start | bytes 2621440 | tf_op jit(solution)/shard_map/all_to_all | solution.py:372
  27.7 0.0 copy-start.3
  27.7 0.7 fusion.1
  28.4 0.1 select_reduce_fusion
  28.5 0.2 convert_reduce_fusion
  28.7 31.6 %all-to-all-done.1.recv_ref = f32[32,80,128]{2,1,0:T(8,128)S(1)} async-done(((f32[32,80,128]{2,1,0:T(8,128)}), f32[32,80,128]{2,1,0:T(8,128)S(1)}, u32[]{:S(2)}, u32[]{:S(2)}) %all-to-all-start.1) | async-done | bytes 1310752 | tf_op jit(solution)/shard_map/all_to_all | solution.py:372
  60.3 2.7 %shard_map.75 = (f32[5,32,8,128]{3,2,1,0:T(8,128)S(1)}, f32[5,4,8,128]{3,2,1,0:T(8,128)S(1)}, f32[5,4,8,128]{3,2,1,0:T(8,128)S(1)}, f32[5,32,4,128]{3,2,1,0:T(4,128)S(1)}, f32[5,32,4,128]{3,2,1,0:T(4,128)S(1)}) custom-call(s32[16]{0:T(128)S(1)} %broadcast_add_fusion.owner_ref, f32[32,80,128]{2,1,0:T(8,128)S(1)} %all-to-all-done.1.recv_ref), custom_call_target="tpu_custom_call" | custom-call | tf_op jit(solution)/shard_map/pallas_call | solution.py:375
  63.0 1.5 collective-permute-start.2
  64.5 0.6 collective-permute-start.3
  65.1 0.0 collective-permute-start.1
  65.1 0.5 collective-permute-start
  65.6 1.6 collective-permute-done.1.xhigh_ref
  67.1 3.2 %collective-permute-done.xlow_ref = f32[5,4,8,128]{3,2,1,0:T(8,128)S(1)} collective-permute-done((f32[5,4,8,128]{3,2,1,0:T(8,128)S(1)}, f32[5,4,8,128]{3,2,1,0:T(8,128)S(1)}, u32[]{:S(2)}, u32[]{:S(2)}) %collective-permute-start) | collective-permute-done | bytes 81952 | tf_op jit(solution)/shard_map/ppermute | solution.py:391
  70.3 1.5 collective-permute-start.4
  71.9 2.5 %collective-permute-start.5 = (f32[5,4,4,128]{3,2,1,0:T(4,128)S(1)}, f32[5,4,4,128]{3,2,1,0:T(4,128)S(1)}, u32[]{:S(2)}, u32[]{:S(2)}) collective-permute-start(f32[5,4,4,128]{3,2,1,0:T(4,128)S(1)} %get-tuple-element.23), channel_id=1, source_target_pairs={{0,31},{1,0},{2,1},{3,2},{4,3},{5,4},{6,5},{7,6},{8,7},{9,8},{10,9... | collective-permute-start | bytes 122888 | tf_op jit(solution)/shard_map/ppermute | solution.py:397
  74.4 1.9 %collective-permute-done.4.clow_ref = f32[5,4,4,128]{3,2,1,0:T(4,128)S(1)} collective-permute-done((f32[5,4,4,128]{3,2,1,0:T(4,128)S(1)}, f32[5,4,4,128]{3,2,1,0:T(4,128)S(1)}, u32[]{:S(2)}, u32[]{:S(2)}) %collective-permute-start.4) | collective-permute-done | bytes 40992 | tf_op jit(solution)/shard_map/ppermute | solution.py:396
  76.3 0.0 collective-permute-done.5.chigh_ref
  76.3 0.0 collective-permute-done.2.ylow_ref
  76.3 0.0 collective-permute-done.3.yhigh_ref
  76.3 0.0 copy-done.3
  76.3 9.0 %shard_map.76 = (f32[5,40,16,128]{3,2,1,0:T(8,128)S(1)}, f32[512,128]{1,0:T(8,128)}) custom-call(f32[5,32,8,128]{3,2,1,0:T(8,128)S(1)} %get-tuple-element.14.own_ref, f32[5,4,8,128]{3,2,1,0:T(8,128)S(1)} %collective-permute-done.xlow_ref, f32[5,4,8,128]{3,2,1,0:T(8,128)S(1)} %collective-permute-done.1.xhigh_ref, ...), custom_call_target="tpu_custom_call" | custom-call | tf_op jit(solution)/shard_map/pallas_call | solution.py:403
  85.3 0.0 copy-start
  85.3 1.2 copy-done
  86.5 13.8 %all-to-all-start.2 = ((f32[256,2,128]{2,1,0:T(2,128)}), f32[256,2,128]{2,1,0:T(2,128)S(1)}, u32[]{:S(2)}, u32[]{:S(2)}) async-start(f32[256,2,128]{2,1,0:T(2,128)} %bitcast.6), calls=%async_computation.2 | async-start | bytes 524288 | tf_op jit(solution)/shard_map/all_to_all | solution.py:406
  100.5 0.0 copy-start.1
  100.5 1.4 copy-done.1
  101.9 0.0 copy-start.6
  101.9 0.0 copy-start.4
  101.9 0.0 copy-start.5
  101.9 3.9 %shard_map.77.stepped_ref = f32[5,32,8,128]{3,2,1,0:T(8,128)S(1)} custom-call(f32[5,32,8,128]{3,2,1,0:T(8,128)S(1)} %get-tuple-element.14.own_ref, f32[5,40,16,128]{3,2,1,0:T(8,128)S(1)} %copy-done.1), custom_call_target="tpu_custom_call" | custom-call | tf_op jit(solution)/shard_map/pallas_call | solution.py:409
  105.8 8.6 %all-to-all-done.2 = f32[256,2,128]{2,1,0:T(2,128)S(1)} async-done(((f32[256,2,128]{2,1,0:T(2,128)}), f32[256,2,128]{2,1,0:T(2,128)S(1)}, u32[]{:S(2)}, u32[]{:S(2)}) %all-to-all-start.2) | async-done | bytes 262176 | tf_op jit(solution)/shard_map/all_to_all | solution.py:406
  114.4 0.0 copy-done.6
  114.4 0.1 jit_solution_.3.eigy_ref
  114.5 0.0 copy-done.4
  114.5 0.0 copy-done.5
  114.5 2.0 %shard_map.78 = f32[768,128]{1,0:T(8,128)S(1)} custom-call(s32[1]{0:T(128)} %bitcast.7.place_ref, f32[1]{0:T(128)} %bitcast.8.wave_ref, f32[512,128]{1,0:T(8,128)S(1)} %bitcast.19, f32[256,256]{1,0:T(8,128)S(1)} %copy-done.4, f32[1,256]{1,0:T(1,128)S(1)} %copy-done.5, f32[256,128]{1,0:T(8,128)S(1)} %jit_solution_.3.eigy_ref), custom_call_target="tpu_custom_call" | custom-call | tf_op jit(solution)/shard_map/pallas_call | solution.py:415
  116.6 23.6 %all_to_all.25 = f32[256,1,384]{2,1,0:T(1,128)S(1)} all-to-all(f32[256,1,384]{2,1,0:T(1,128)S(1)} %bitcast.16), channel_id=1, replica_groups=mesh['row'=8,'col'=32] {'row','col'}, dimensions={0} | all-to-all | bytes 786432 | tf_op jit(solution)/shard_map/all_to_all | solution.py:423
  140.1 2.9 %shard_map.79 = f32[32,80,128]{2,1,0:T(8,128)} custom-call(s32[16]{0:T(128)S(1)} %broadcast_add_fusion.owner_ref, f32[5,32,8,128]{3,2,1,0:T(8,128)S(1)} %shard_map.77.stepped_ref, f32[768,128]{1,0:T(8,128)S(1)} %bitcast.17, f32[256,128]{1,0:T(8,128)S(1)} %copy-done.3), custom_call_target="tpu_custom_call" | custom-call | tf_op jit(solution)/shard_map/pallas_call | solution.py:426
  143.0 5.8 %all-to-all-start.4 = ((f32[32,80,128]{2,1,0:T(8,128)}), f32[32,80,128]{2,1,0:T(8,128)S(1)}, u32[]{:S(2)}, u32[]{:S(2)}) async-start(f32[32,80,128]{2,1,0:T(8,128)} %shard_map.79), calls=%async_computation.4 | async-start | bytes 2621440 | tf_op jit(solution)/shard_map/all_to_all | solution.py:432
  148.8 0.7 fusion.2
  151.4 0.1 pad_add_fusion.place_ref
  151.5 30.7 %all-to-all-done.4 = f32[32,80,128]{2,1,0:T(8,128)S(1)} async-done(((f32[32,80,128]{2,1,0:T(8,128)}), f32[32,80,128]{2,1,0:T(8,128)S(1)}, u32[]{:S(2)}, u32[]{:S(2)}) %all-to-all-start.4) | async-done | bytes 1310752 | tf_op jit(solution)/shard_map/all_to_all | solution.py:432
  182.2 2.4 %shard_map.80 = f32[5,16,4096]{2,1,0:T(8,128)} custom-call(s32[2]{0:T(128)S(1)} %pad_add_fusion.place_ref, f32[2560,128]{1,0:T(8,128)S(1)} %bitcast.15), custom_call_target="tpu_custom_call" | custom-call | tf_op jit(solution)/shard_map/pallas_call | solution.py:434
  (5 shorter events, 0.0 us)
Async XLA Ops:
  1.3 20.1 %all-to-all-start = ((f32[32,1,128]{2,1,0:T(1,128)}), f32[32,1,128]{2,1,0:T(1,128)S(1)}, u32[]{:S(2)}, u32[]{:S(2)}) async-start(f32[32,1,128]{2,1,0:T(1,128)} %broadcast_in_dim.29), calls=%async_computation | async-start | bytes 32768 | tf_op jit(solution)/shard_map/all_to_all | solution.py:350
  12.9 1.3 copy-start.2
  22.6 37.7 %all-to-all-start.1 = ((f32[32,80,128]{2,1,0:T(8,128)}), f32[32,80,128]{2,1,0:T(8,128)S(1)}, u32[]{:S(2)}, u32[]{:S(2)}) async-start(f32[32,80,128]{2,1,0:T(8,128)} %bitcast.5), calls=%async_computation.1 | async-start | bytes 2621440 | tf_op jit(solution)/shard_map/all_to_all | solution.py:372
  27.7 48.6 %copy-start.3 = (f32[256,128]{1,0:T(8,128)S(1)}, f32[256,128]{1,0:T(8,128)}, u32[]{:S(2)}) copy-start(f32[256,128]{1,0:T(8,128)} %constant.76.clone.table_ref) | copy-start | bytes 393220
  63.0 13.3 %collective-permute-start.2 = (f32[5,32,4,128]{3,2,1,0:T(4,128)S(1)}, f32[5,32,4,128]{3,2,1,0:T(4,128)S(1)}, u32[]{:S(2)}, u32[]{:S(2)}) collective-permute-start(f32[5,32,4,128]{3,2,1,0:T(4,128)S(1)} %get-tuple-element.17), channel_id=1, source_target_pairs={{0,1},{1,2},{2,3},{3,4},{4,5},{5,6},{6,7},{7,8},{8,9},{9,10},{10,1... | collective-permute-start | bytes 983048 | tf_op jit(solution)/shard_map/ppermute | solution.py:393
  64.5 11.8 %collective-permute-start.3 = (f32[5,32,4,128]{3,2,1,0:T(4,128)S(1)}, f32[5,32,4,128]{3,2,1,0:T(4,128)S(1)}, u32[]{:S(2)}, u32[]{:S(2)}) collective-permute-start(f32[5,32,4,128]{3,2,1,0:T(4,128)S(1)} %get-tuple-element.18), channel_id=1, source_target_pairs={{0,31},{1,0},{2,1},{3,2},{4,3},{5,4},{6,5},{7,6},{8,7},{9,8},{10,9... | collective-permute-start | bytes 983048 | tf_op jit(solution)/shard_map/ppermute | solution.py:394
  65.1 2.1 %collective-permute-start.1 = (f32[5,4,8,128]{3,2,1,0:T(8,128)S(1)}, f32[5,4,8,128]{3,2,1,0:T(8,128)S(1)}, u32[]{:S(2)}, u32[]{:S(2)}) collective-permute-start(f32[5,4,8,128]{3,2,1,0:T(8,128)S(1)} %get-tuple-element.16), channel_id=1, source_target_pairs={{0,224},{32,0},{64,32},{96,64},{128,96},{160,128},{192,160},{224,1... | collective-permute-start | bytes 245768 | tf_op jit(solution)/shard_map/ppermute | solution.py:392
  65.1 5.2 %collective-permute-start = (f32[5,4,8,128]{3,2,1,0:T(8,128)S(1)}, f32[5,4,8,128]{3,2,1,0:T(8,128)S(1)}, u32[]{:S(2)}, u32[]{:S(2)}) collective-permute-start(f32[5,4,8,128]{3,2,1,0:T(8,128)S(1)} %get-tuple-element.15), channel_id=1, source_target_pairs={{0,32},{32,64},{64,96},{96,128},{128,160},{160,192},{192,224},{224... | collective-permute-start | bytes 245768 | tf_op jit(solution)/shard_map/ppermute | solution.py:391
  70.3 5.9 %collective-permute-start.4 = (f32[5,4,4,128]{3,2,1,0:T(4,128)S(1)}, f32[5,4,4,128]{3,2,1,0:T(4,128)S(1)}, u32[]{:S(2)}, u32[]{:S(2)}) collective-permute-start(f32[5,4,4,128]{3,2,1,0:T(4,128)S(1)} %get-tuple-element.24), channel_id=1, source_target_pairs={{0,1},{1,2},{2,3},{3,4},{4,5},{5,6},{6,7},{7,8},{8,9},{9,10},{10,1... | collective-permute-start | bytes 122888 | tf_op jit(solution)/shard_map/ppermute | solution.py:396
  71.9 4.4 %collective-permute-start.5 = (f32[5,4,4,128]{3,2,1,0:T(4,128)S(1)}, f32[5,4,4,128]{3,2,1,0:T(4,128)S(1)}, u32[]{:S(2)}, u32[]{:S(2)}) collective-permute-start(f32[5,4,4,128]{3,2,1,0:T(4,128)S(1)} %get-tuple-element.23), channel_id=1, source_target_pairs={{0,31},{1,0},{2,1},{3,2},{4,3},{5,4},{6,5},{7,6},{8,7},{9,8},{10,9... | collective-permute-start | bytes 122888 | tf_op jit(solution)/shard_map/ppermute | solution.py:397
  85.3 1.2 copy-start
  86.5 27.9 %all-to-all-start.2 = ((f32[256,2,128]{2,1,0:T(2,128)}), f32[256,2,128]{2,1,0:T(2,128)S(1)}, u32[]{:S(2)}, u32[]{:S(2)}) async-start(f32[256,2,128]{2,1,0:T(2,128)} %bitcast.6), calls=%async_computation.2 | async-start | bytes 524288 | tf_op jit(solution)/shard_map/all_to_all | solution.py:406
  100.5 1.4 copy-start.1
  101.9 12.5 %copy-start.6 = (f32[256]{0:T(256)S(1)}, f32[256]{0:T(256)}, u32[]{:S(2)}) copy-start(f32[256]{0:T(256)} %constant.79.clone) | copy-start | bytes 3076
  101.9 12.6 %copy-start.4 = (f32[256,256]{1,0:T(8,128)S(1)}, f32[256,256]{1,0:T(8,128)}, u32[]{:S(2)}) copy-start(f32[256,256]{1,0:T(8,128)} %constant.77.clone.table_ref) | copy-start | bytes 786436
  101.9 12.6 %copy-start.5 = (f32[1,256]{1,0:T(1,128)S(1)}, f32[1,256]{1,0:T(1,128)}, u32[]{:S(2)}) copy-start(f32[1,256]{1,0:T(1,128)} %constant.78.clone.eigx_ref) | copy-start | bytes 3076
  143.0 39.2 %all-to-all-start.4 = ((f32[32,80,128]{2,1,0:T(8,128)}), f32[32,80,128]{2,1,0:T(8,128)S(1)}, u32[]{:S(2)}, u32[]{:S(2)}) async-start(f32[32,80,128]{2,1,0:T(8,128)} %shard_map.79), calls=%async_computation.4 | async-start | bytes 2621440 | tf_op jit(solution)/shard_map/all_to_all | solution.py:432

commit v8 on v7

--- a/solution.py
+++ b/solution.py
@@ -153,7 +153,7 @@
     return [states[0], states[1 + direction]]
 
 
-def euler_stage(load, store, first_row, count, keep, pick=all_fields):
+def euler_stage(load, store, first_row, count, keep, unroll, pick=all_fields):
     def slopes_of(low, mid, high):
         return [minmod(b - a, c - b) for a, b, c in zip(low, mid, high)]
 
@@ -178,7 +178,7 @@
         store(i, mine, rate)
         return tuple(face_high), tuple(upper_next)
 
-    lax.fori_loop(0, count, step, (tuple(face), tuple(upper_now)), unroll=4)
+    lax.fori_loop(0, count, step, (tuple(face), tuple(upper_now)), unroll=unroll)
 
 
 def euler_kernel(
@@ -204,19 +204,19 @@
 
     def store_first(i, states, rates):
         for q in range(5):
-            first_ref[q, i] = states[q] + time_step * rates[q]
-
-    euler_stage(load_ext, store_first, 2, BX + 4, BY + 2 * HALO)
+            first_ref[q, i - 2] = states[q] + time_step * rates[q]
+
+    euler_stage(load_ext, store_first, 2, BX + 4, BY + 2 * HALO, 6)
 
     def load_mass(i):
-        return [first_ref[q, i] for q in range(4)]
+        return [first_ref[q, i - 2] for q in range(4)]
 
     def store_density(i, states, rates):
         second = states[0] + time_step * rates[0]
         row = pl.multiple_of((i - HALO) * BY, BY)
         flat_ref[pl.ds(row, BY), :] = 0.5 * ext_ref[0, i, 0:BY] + 0.5 * second
 
-    euler_stage(load_mass, store_density, HALO, BX, BY, mass_fields)
+    euler_stage(load_mass, store_density, HALO, BX, BY, 32, mass_fields)
     density = jnp.concatenate(
         [flat_ref[pl.ds(b, BX, stride=BY), :] for b in range(BY)], axis=0
     )
@@ -227,14 +227,14 @@
 
 def second_kernel(own_ref, first_ref, stepped_ref):
     def load_first(i):
-        return [first_ref[q, i] for q in range(5)]
+        return [first_ref[q, i - 2] for q in range(5)]
 
     def store_stepped(i, states, rates):
         for q in range(5):
             second = states[q] + time_step * rates[q]
             stepped_ref[q, i - HALO] = 0.5 * own_ref[q, i - HALO] + 0.5 * second
 
-    euler_stage(load_first, store_stepped, HALO, BX, BY)
+    euler_stage(load_first, store_stepped, HALO, BX, BY, 8)
 
 
 def plane_kernel(place_ref, wave_ref, modes_ref, table_ref, eigx_ref, eigy_ref, out_ref, plane_ref, wide_ref):
@@ -401,7 +401,7 @@
     modes_of = np.arange(256) % GZ
     wide = (5, BX + 2 * HALO, BY + 2 * HALO, GZ)
     first, modes = call(
-        euler_kernel, [wide, (512, 128)], (8, ()), [wide, (BX * BY, GZ)]
+        euler_kernel, [(5, BX + HALO, BY + 2 * HALO, GZ), (512, 128)], (8, ()), [wide, (BX * BY, GZ)]
     )(own, xlow, xhigh, ylow, yhigh, clow, chigh, jnp.asarray(table_z[modes_of]))
     planes = lax.all_to_all(
         modes.reshape(256, 2, 128), ("row", "col"), split_axis=0, concat_axis=0, tiled=True

time: 185 us -> 183 us (0.989)
  Pallas kernels: 25.3 us -> 22.3 us
  waiting for transfers between devices: 83.6 us -> 86.1 us
    all_to_all x1, waiting for transfers between devices: 8.59 us -> 10.8 us  [on_device(): lax.all_to_all(modes.reshape(256, 2, 128), ('row', 'col'), split_axis=0,...]
    pallas_call x1, Pallas kernels: 9.04 us -> 6.9 us  [on_device(): call(euler_kernel, [(5, BX + HALO, BY + 2 * HALO, GZ), (512, 128)], (8, (...]
    unnamed x14 -> x12, local copies, waits for them, and re-layouts: 3.96 us -> 2.24 us
  transfers between devices with their start and end apart: 10 -> 10, of which waited for: 7 -> 7; matrix products, arithmetic and copies ran while one was open for 1% -> 1% of each run, Pallas kernels for 3% -> 2%
where the time goes in v8:
time: 183 us; the launch traced here: 182 us
  waiting for transfers between devices  86.1 us (47%)
  starting transfers between devices  42.9 us (23%)
  blocking collectives  23.6 us (13%)
  Pallas kernels  22.3 us (12%)
  local copies, waits for them, and re-layouts  2.95 us (2%)
  between operations  2.66 us (1%)
    all_to_all x1, waiting for transfers between devices, on_device(): lax.all_to_all(sent.reshape(COLS, BRICK, 128), 'col', split_axis=0, conca...  31.6 us
    all_to_all x1, waiting for transfers between devices, on_device(): lax.all_to_all(returned, 'col', split_axis=0, concat_axis=0, tiled=True)  31 us
    all_to_all x1, blocking collectives, on_device(): lax.all_to_all(strips.reshape(256, 1, 384), ('row', 'col'), split_axis=0,...  23.6 us
    all_to_all x1, starting transfers between devices, on_device(): lax.all_to_all(modes.reshape(256, 2, 128), ('row', 'col'), split_axis=0,...  13.8 us
    all_to_all x1, starting transfers between devices, gather_counts(): lax.all_to_all(copies, 'col', split_axis=0, concat_axis=0, tiled=True)  11.6 us
    all_to_all x1, waiting for transfers between devices, on_device(): lax.all_to_all(modes.reshape(256, 2, 128), ('row', 'col'), split_axis=0,...  10.8 us
    pallas_call x1, Pallas kernels, on_device(): call(euler_kernel, [(5, BX + HALO, BY + 2 * HALO, GZ), (512, 128)], (8, (...  6.9 us
    all_to_all x1, waiting for transfers between devices, gather_counts(): lax.all_to_all(copies, 'col', split_axis=0, concat_axis=0, tiled=True)  6.03 us
  transfers between devices with their start and end apart: 10, of which 7 were waited for; matrix products, arithmetic and copies ran while one was open for 1% of the time, Pallas kernels for 2%

profile of v8, /device:TPU:2, one launch (start us, length us, event | category | flops | bytes accessed | tf_op | source)
XLA Modules:
  0.0 182.1 jit_solution(12855360153681435533)
XLA Ops:
  0.7 0.6 broadcast_in_dim.29
  1.3 11.6 %all-to-all-start = ((f32[32,1,128]{2,1,0:T(1,128)}), f32[32,1,128]{2,1,0:T(1,128)S(1)}, u32[]{:S(2)}, u32[]{:S(2)}) async-start(f32[32,1,128]{2,1,0:T(1,128)} %broadcast_in_dim.29), calls=%async_computation | async-start | bytes 32768 | tf_op jit(solution)/shard_map/all_to_all | solution.py:350
  12.9 0.0 copy-start
  12.9 1.3 copy-done
  14.2 1.1 shard_map.73.staged_ref
  15.3 6.0 %all-to-all-done.counts_ref = f32[32,1,128]{2,1,0:T(1,128)S(1)} async-done(((f32[32,1,128]{2,1,0:T(1,128)}), f32[32,1,128]{2,1,0:T(1,128)S(1)}, u32[]{:S(2)}, u32[]{:S(2)}) %all-to-all-start) | async-done | bytes 16416 | tf_op jit(solution)/shard_map/all_to_all | solution.py:350
  21.3 1.3 shard_map.74
  22.6 5.1 %all-to-all-start.1 = ((f32[32,80,128]{2,1,0:T(8,128)}), f32[32,80,128]{2,1,0:T(8,128)S(1)}, u32[]{:S(2)}, u32[]{:S(2)}) async-start(f32[32,80,128]{2,1,0:T(8,128)} %bitcast.5), calls=%async_computation.1 | async-start | bytes 2621440 | tf_op jit(solution)/shard_map/all_to_all | solution.py:372
  27.7 0.7 fusion.1
  28.4 0.1 select_reduce_fusion
  28.5 0.2 convert_reduce_fusion
  28.7 31.6 %all-to-all-done.1.recv_ref = f32[32,80,128]{2,1,0:T(8,128)S(1)} async-done(((f32[32,80,128]{2,1,0:T(8,128)}), f32[32,80,128]{2,1,0:T(8,128)S(1)}, u32[]{:S(2)}, u32[]{:S(2)}) %all-to-all-start.1) | async-done | bytes 1310752 | tf_op jit(solution)/shard_map/all_to_all | solution.py:372
  60.3 2.7 %shard_map.75 = (f32[5,32,8,128]{3,2,1,0:T(8,128)S(1)}, f32[5,4,8,128]{3,2,1,0:T(8,128)S(1)}, f32[5,4,8,128]{3,2,1,0:T(8,128)S(1)}, f32[5,32,4,128]{3,2,1,0:T(4,128)S(1)}, f32[5,32,4,128]{3,2,1,0:T(4,128)S(1)}) custom-call(s32[16]{0:T(128)S(1)} %broadcast_add_fusion.owner_ref, f32[32,80,128]{2,1,0:T(8,128)S(1)} %all-to-all-done.1.recv_ref), custom_call_target="tpu_custom_call" | custom-call | tf_op jit(solution)/shard_map/pallas_call | solution.py:375
  63.0 1.5 collective-permute-start.2
  64.5 0.6 collective-permute-start.3
  65.1 0.0 collective-permute-start.1
  65.1 0.5 collective-permute-start
  65.6 1.6 collective-permute-done.1.xhigh_ref
  67.1 3.2 %collective-permute-done.xlow_ref = f32[5,4,8,128]{3,2,1,0:T(8,128)S(1)} collective-permute-done((f32[5,4,8,128]{3,2,1,0:T(8,128)S(1)}, f32[5,4,8,128]{3,2,1,0:T(8,128)S(1)}, u32[]{:S(2)}, u32[]{:S(2)}) %collective-permute-start) | collective-permute-done | bytes 81952 | tf_op jit(solution)/shard_map/ppermute | solution.py:391
  70.3 1.5 collective-permute-start.4
  71.9 2.5 %collective-permute-start.5 = (f32[5,4,4,128]{3,2,1,0:T(4,128)S(1)}, f32[5,4,4,128]{3,2,1,0:T(4,128)S(1)}, u32[]{:S(2)}, u32[]{:S(2)}) collective-permute-start(f32[5,4,4,128]{3,2,1,0:T(4,128)S(1)} %get-tuple-element.23), channel_id=1, source_target_pairs={{0,31},{1,0},{2,1},{3,2},{4,3},{5,4},{6,5},{7,6},{8,7},{9,8},{10,9... | collective-permute-start | bytes 122888 | tf_op jit(solution)/shard_map/ppermute | solution.py:397
  74.4 1.9 %collective-permute-done.4.clow_ref = f32[5,4,4,128]{3,2,1,0:T(4,128)S(1)} collective-permute-done((f32[5,4,4,128]{3,2,1,0:T(4,128)S(1)}, f32[5,4,4,128]{3,2,1,0:T(4,128)S(1)}, u32[]{:S(2)}, u32[]{:S(2)}) %collective-permute-start.4) | collective-permute-done | bytes 40992 | tf_op jit(solution)/shard_map/ppermute | solution.py:396
  76.3 0.0 collective-permute-done.5.chigh_ref
  76.3 0.0 collective-permute-done.2.ylow_ref
  76.3 0.0 collective-permute-done.3.yhigh_ref
  76.3 0.0 copy-start.1
  76.3 0.9 copy-done.1
  77.2 6.9 %shard_map.76 = (f32[5,36,16,128]{3,2,1,0:T(8,128)S(1)}, f32[512,128]{1,0:T(8,128)}) custom-call(f32[5,32,8,128]{3,2,1,0:T(8,128)S(1)} %get-tuple-element.14.own_ref, f32[5,4,8,128]{3,2,1,0:T(8,128)S(1)} %collective-permute-done.xlow_ref, f32[5,4,8,128]{3,2,1,0:T(8,128)S(1)} %collective-permute-done.1.xhigh_ref, ...), custom_call_target="tpu_custom_call" | custom-call | tf_op jit(solution)/shard_map/pallas_call | solution.py:403
  84.1 13.8 %all-to-all-start.2 = ((f32[256,2,128]{2,1,0:T(2,128)}), f32[256,2,128]{2,1,0:T(2,128)S(1)}, u32[]{:S(2)}, u32[]{:S(2)}) async-start(f32[256,2,128]{2,1,0:T(2,128)} %bitcast.6), calls=%async_computation.2 | async-start | bytes 524288 | tf_op jit(solution)/shard_map/all_to_all | solution.py:406
  98.0 0.0 copy-start.5
  98.0 0.0 copy-start.3
  98.0 0.0 copy-start.4
  98.1 3.1 %shard_map.77.stepped_ref = f32[5,32,8,128]{3,2,1,0:T(8,128)S(1)} custom-call(f32[5,32,8,128]{3,2,1,0:T(8,128)S(1)} %get-tuple-element.14.own_ref, f32[5,36,16,128]{3,2,1,0:T(8,128)S(1)} %get-tuple-element.20.first_ref), custom_call_target="tpu_custom_call" | custom-call | tf_op jit(solution)/shard_map/pallas_call | solution.py:409
  101.1 0.0 copy-start.2
  101.1 10.8 %all-to-all-done.2 = f32[256,2,128]{2,1,0:T(2,128)S(1)} async-done(((f32[256,2,128]{2,1,0:T(2,128)}), f32[256,2,128]{2,1,0:T(2,128)S(1)}, u32[]{:S(2)}, u32[]{:S(2)}) %all-to-all-start.2) | async-done | bytes 262176 | tf_op jit(solution)/shard_map/all_to_all | solution.py:406
  112.0 0.0 copy-done.5
  112.0 0.1 jit_solution_.3.eigy_ref
  112.1 0.0 copy-done.3
  112.1 0.0 copy-done.4
  112.1 2.0 %shard_map.78 = f32[768,128]{1,0:T(8,128)S(1)} custom-call(s32[1]{0:T(128)} %bitcast.7.place_ref, f32[1]{0:T(128)} %bitcast.8.wave_ref, f32[512,128]{1,0:T(8,128)S(1)} %bitcast.19, f32[256,256]{1,0:T(8,128)S(1)} %copy-done.3, f32[1,256]{1,0:T(1,128)S(1)} %copy-done.4, f32[256,128]{1,0:T(8,128)S(1)} %jit_solution_.3.eigy_ref), custom_call_target="tpu_custom_call" | custom-call | tf_op jit(solution)/shard_map/pallas_call | solution.py:415
  114.1 23.6 %all_to_all.25 = f32[256,1,384]{2,1,0:T(1,128)S(1)} all-to-all(f32[256,1,384]{2,1,0:T(1,128)S(1)} %bitcast.16), channel_id=1, replica_groups=mesh['row'=8,'col'=32] {'row','col'}, dimensions={0} | all-to-all | bytes 786432 | tf_op jit(solution)/shard_map/all_to_all | solution.py:423
  137.7 0.0 copy-done.2
  137.7 2.9 %shard_map.79 = f32[32,80,128]{2,1,0:T(8,128)} custom-call(s32[16]{0:T(128)S(1)} %broadcast_add_fusion.owner_ref, f32[5,32,8,128]{3,2,1,0:T(8,128)S(1)} %shard_map.77.stepped_ref, f32[768,128]{1,0:T(8,128)S(1)} %bitcast.17, f32[256,128]{1,0:T(8,128)S(1)} %copy-done.2), custom_call_target="tpu_custom_call" | custom-call | tf_op jit(solution)/shard_map/pallas_call | solution.py:426
  140.6 5.8 %all-to-all-start.4 = ((f32[32,80,128]{2,1,0:T(8,128)}), f32[32,80,128]{2,1,0:T(8,128)S(1)}, u32[]{:S(2)}, u32[]{:S(2)}) async-start(f32[32,80,128]{2,1,0:T(8,128)} %shard_map.79), calls=%async_computation.4 | async-start | bytes 2621440 | tf_op jit(solution)/shard_map/all_to_all | solution.py:432
  146.4 0.6 fusion.2
  148.7 0.1 pad_add_fusion.place_ref
  148.8 31.0 %all-to-all-done.4 = f32[32,80,128]{2,1,0:T(8,128)S(1)} async-done(((f32[32,80,128]{2,1,0:T(8,128)}), f32[32,80,128]{2,1,0:T(8,128)S(1)}, u32[]{:S(2)}, u32[]{:S(2)}) %all-to-all-start.4) | async-done | bytes 1310752 | tf_op jit(solution)/shard_map/all_to_all | solution.py:432
  179.7 2.4 %shard_map.80 = f32[5,16,4096]{2,1,0:T(8,128)} custom-call(s32[2]{0:T(128)S(1)} %pad_add_fusion.place_ref, f32[2560,128]{1,0:T(8,128)S(1)} %bitcast.15), custom_call_target="tpu_custom_call" | custom-call | tf_op jit(solution)/shard_map/pallas_call | solution.py:434
  (5 shorter events, 0.0 us)
Async XLA Ops:
  1.3 20.1 %all-to-all-start = ((f32[32,1,128]{2,1,0:T(1,128)}), f32[32,1,128]{2,1,0:T(1,128)S(1)}, u32[]{:S(2)}, u32[]{:S(2)}) async-start(f32[32,1,128]{2,1,0:T(1,128)} %broadcast_in_dim.29), calls=%async_computation | async-start | bytes 32768 | tf_op jit(solution)/shard_map/all_to_all | solution.py:350
  12.9 1.3 copy-start
  22.6 37.7 %all-to-all-start.1 = ((f32[32,80,128]{2,1,0:T(8,128)}), f32[32,80,128]{2,1,0:T(8,128)S(1)}, u32[]{:S(2)}, u32[]{:S(2)}) async-start(f32[32,80,128]{2,1,0:T(8,128)} %bitcast.5), calls=%async_computation.1 | async-start | bytes 2621440 | tf_op jit(solution)/shard_map/all_to_all | solution.py:372
  63.0 13.3 %collective-permute-start.2 = (f32[5,32,4,128]{3,2,1,0:T(4,128)S(1)}, f32[5,32,4,128]{3,2,1,0:T(4,128)S(1)}, u32[]{:S(2)}, u32[]{:S(2)}) collective-permute-start(f32[5,32,4,128]{3,2,1,0:T(4,128)S(1)} %get-tuple-element.17), channel_id=1, source_target_pairs={{0,1},{1,2},{2,3},{3,4},{4,5},{5,6},{6,7},{7,8},{8,9},{9,10},{10,1... | collective-permute-start | bytes 983048 | tf_op jit(solution)/shard_map/ppermute | solution.py:393
  64.5 11.8 %collective-permute-start.3 = (f32[5,32,4,128]{3,2,1,0:T(4,128)S(1)}, f32[5,32,4,128]{3,2,1,0:T(4,128)S(1)}, u32[]{:S(2)}, u32[]{:S(2)}) collective-permute-start(f32[5,32,4,128]{3,2,1,0:T(4,128)S(1)} %get-tuple-element.18), channel_id=1, source_target_pairs={{0,31},{1,0},{2,1},{3,2},{4,3},{5,4},{6,5},{7,6},{8,7},{9,8},{10,9... | collective-permute-start | bytes 983048 | tf_op jit(solution)/shard_map/ppermute | solution.py:394
  65.1 2.1 %collective-permute-start.1 = (f32[5,4,8,128]{3,2,1,0:T(8,128)S(1)}, f32[5,4,8,128]{3,2,1,0:T(8,128)S(1)}, u32[]{:S(2)}, u32[]{:S(2)}) collective-permute-start(f32[5,4,8,128]{3,2,1,0:T(8,128)S(1)} %get-tuple-element.16), channel_id=1, source_target_pairs={{0,224},{32,0},{64,32},{96,64},{128,96},{160,128},{192,160},{224,1... | collective-permute-start | bytes 245768 | tf_op jit(solution)/shard_map/ppermute | solution.py:392
  65.1 5.2 %collective-permute-start = (f32[5,4,8,128]{3,2,1,0:T(8,128)S(1)}, f32[5,4,8,128]{3,2,1,0:T(8,128)S(1)}, u32[]{:S(2)}, u32[]{:S(2)}) collective-permute-start(f32[5,4,8,128]{3,2,1,0:T(8,128)S(1)} %get-tuple-element.15), channel_id=1, source_target_pairs={{0,32},{32,64},{64,96},{96,128},{128,160},{160,192},{192,224},{224... | collective-permute-start | bytes 245768 | tf_op jit(solution)/shard_map/ppermute | solution.py:391
  70.3 5.9 %collective-permute-start.4 = (f32[5,4,4,128]{3,2,1,0:T(4,128)S(1)}, f32[5,4,4,128]{3,2,1,0:T(4,128)S(1)}, u32[]{:S(2)}, u32[]{:S(2)}) collective-permute-start(f32[5,4,4,128]{3,2,1,0:T(4,128)S(1)} %get-tuple-element.24), channel_id=1, source_target_pairs={{0,1},{1,2},{2,3},{3,4},{4,5},{5,6},{6,7},{7,8},{8,9},{9,10},{10,1... | collective-permute-start | bytes 122888 | tf_op jit(solution)/shard_map/ppermute | solution.py:396
  71.9 4.4 %collective-permute-start.5 = (f32[5,4,4,128]{3,2,1,0:T(4,128)S(1)}, f32[5,4,4,128]{3,2,1,0:T(4,128)S(1)}, u32[]{:S(2)}, u32[]{:S(2)}) collective-permute-start(f32[5,4,4,128]{3,2,1,0:T(4,128)S(1)} %get-tuple-element.23), channel_id=1, source_target_pairs={{0,31},{1,0},{2,1},{3,2},{4,3},{5,4},{6,5},{7,6},{8,7},{9,8},{10,9... | collective-permute-start | bytes 122888 | tf_op jit(solution)/shard_map/ppermute | solution.py:397
  76.3 0.9 copy-start.1
  84.1 27.9 %all-to-all-start.2 = ((f32[256,2,128]{2,1,0:T(2,128)}), f32[256,2,128]{2,1,0:T(2,128)S(1)}, u32[]{:S(2)}, u32[]{:S(2)}) async-start(f32[256,2,128]{2,1,0:T(2,128)} %bitcast.6), calls=%async_computation.2 | async-start | bytes 524288 | tf_op jit(solution)/shard_map/all_to_all | solution.py:406
  98.0 14.0 %copy-start.5 = (f32[256]{0:T(256)S(1)}, f32[256]{0:T(256)}, u32[]{:S(2)}) copy-start(f32[256]{0:T(256)} %constant.79.clone) | copy-start | bytes 3076
  98.0 14.0 %copy-start.3 = (f32[256,256]{1,0:T(8,128)S(1)}, f32[256,256]{1,0:T(8,128)}, u32[]{:S(2)}) copy-start(f32[256,256]{1,0:T(8,128)} %constant.77.clone.table_ref) | copy-start | bytes 786436
  98.0 14.0 %copy-start.4 = (f32[1,256]{1,0:T(1,128)S(1)}, f32[1,256]{1,0:T(1,128)}, u32[]{:S(2)}) copy-start(f32[1,256]{1,0:T(1,128)} %constant.78.clone.eigx_ref) | copy-start | bytes 3076
  101.1 36.6 %copy-start.2 = (f32[256,128]{1,0:T(8,128)S(1)}, f32[256,128]{1,0:T(8,128)}, u32[]{:S(2)}) copy-start(f32[256,128]{1,0:T(8,128)} %constant.76.clone.table_ref) | copy-start | bytes 393220
  140.6 39.2 %all-to-all-start.4 = ((f32[32,80,128]{2,1,0:T(8,128)}), f32[32,80,128]{2,1,0:T(8,128)S(1)}, u32[]{:S(2)}, u32[]{:S(2)}) async-start(f32[32,80,128]{2,1,0:T(8,128)} %shard_map.79), calls=%async_computation.4 | async-start | bytes 2621440 | tf_op jit(solution)/shard_map/all_to_all | solution.py:432

commit v9 on v8

--- a/solution.py
+++ b/solution.py
@@ -35,8 +35,36 @@
     return ((np.cos(angle) + np.sin(angle)) / math.sqrt(length)).astype(np.float32)
 
 
-def eigenvalues(length):
-    return (-4.0 * np.sin(np.pi * np.arange(length) / length) ** 2).astype(np.float32)
+def kappas():
+    wave_y = np.sin(np.pi * np.arange(GY) / GY) ** 2
+    wave_z = np.sin(np.pi * np.arange(GZ) / GZ) ** 2
+    return 2.0 * np.arcsinh(np.sqrt(wave_z[:, None] + wave_y[None, :]))
+
+
+def lane_spans():
+    inner = np.arange(128) % BX
+    return np.concatenate([inner, np.where(inner == 0, -1, BX)]).astype(np.float32)
+
+
+def lane_expand():
+    lanes = np.arange(256) % 128 // BX
+    return 0.5 * (np.arange(8)[:, None] // 2 == lanes[None, :]).astype(np.float32)
+
+
+def lane_picks():
+    picks = np.zeros((16, 128), np.float32)
+    for k in range(4):
+        picks[2 * k, k * BX + BX - 1] = 1.0
+        picks[8 + 2 * k + 1, k * BX] = 1.0
+    return picks
+
+
+def mean_line():
+    lanes = np.arange(256)
+    used = (lanes < BX) | (lanes == 128) | (lanes == 129)
+    gap = np.arange(GX)[:, None] // BX * BX + lane_spans()[None, :] - np.arange(GX)[:, None] % BX
+    gap = np.abs(gap)
+    return (four_pi_g * np.where(used[None, :], gap / 2.0 - gap * gap / (2.0 * GX), 0.0)).astype(np.float32)
 
 
 def dot(left, right, dims=((1,), (0,))):
@@ -221,8 +249,8 @@
         [flat_ref[pl.ds(b, BX, stride=BY), :] for b in range(BY)], axis=0
     )
     spread = dot(table_ref[...], density, ((1,), (1,)))
-    modes_ref[pl.ds(0, 256, stride=2), :] = spread[:, :128]
-    modes_ref[pl.ds(1, 256, stride=2), :] = spread[:, 128:]
+    modes_ref[pl.ds(0, GZ, stride=2), :] = spread[:, :128]
+    modes_ref[pl.ds(1, GZ, stride=2), :] = spread[:, 128:]
 
 
 def second_kernel(own_ref, first_ref, stepped_ref):
@@ -237,56 +265,108 @@
     euler_stage(load_first, store_stepped, HALO, BX, BY, 8)
 
 
-def plane_kernel(place_ref, wave_ref, modes_ref, table_ref, eigx_ref, eigy_ref, out_ref, plane_ref, wide_ref):
-    for high in range(2):
-        for tile in range(2):
-            lines = [
-                modes_ref[pl.ds((high * 4 + r) * COLS * 2 + tile, COLS, stride=2), :]
-                for r in range(4)
-            ]
-            for p, value in enumerate(swap_groups(lines, 32)):
-                plane_ref[pl.ds(high * GY + tile * 4 + p, COLS, stride=BY), :] = value
-    half = pl.multiple_of(place_ref[0] * 128, 128)
-    table = table_ref[...]
-    half_table = table_ref[pl.ds(half, 128), :]
-    plane = jnp.concatenate([plane_ref[0:GY, :], plane_ref[GY:, :]], axis=1)
-    spectrum = dot(dot(half_table, plane), table)
-    eigen = eigx_ref[...] + eigy_ref[pl.ds(half, 128), :][:, 0:1] + wave_ref[0]
-    flat = eigen >= 0.0
-    green = jnp.where(flat, 0.0, four_pi_g / jnp.where(flat, -1.0, eigen))
-    back = dot(spectrum * green, table)
-    potential = dot(half_table, back, ((0,), (0,)))
-    for high in range(2):
-        base, side = high * (GY + 16), potential[:, high * 128 : high * 128 + 128]
+def table_kernel(kappa_ref, expand_ref, span_ref, decay_ref, scale_ref, left_ref, right_ref):
+    kappa = dot(kappa_ref[...], expand_ref[...], ((0,), (0,)))
+    flat = kappa <= 0.0
+    decay = jnp.exp(-kappa)
+    width = jnp.where(flat, 1.0, jnp.exp(kappa) - decay)
+    scale = jnp.where(flat, 0.0, -four_pi_g / width)
+    images = scale / jnp.where(flat, 1.0, 1.0 - jnp.exp(-GX * kappa))
+    span = span_ref[...]
+    decay_ref[...] = decay
+    scale_ref[...] = scale
+    left_ref[...] = images * jnp.exp(-kappa * (span + 1.0))
+    right_ref[...] = images * jnp.exp(-kappa * (BX - span))
+
+
+def ends_kernel(modes_ref, table_ref, decay_ref, scale_ref, pick_ref, local_ref, ends_ref, plane_ref):
+    for tile in range(2):
+        lines = [modes_ref[pl.ds(k * 2 + tile, COLS, stride=8), :] for k in range(4)]
+        for g, value in enumerate(swap_groups(lines, 32)):
+            plane_ref[pl.ds(tile * 4 + g, COLS, stride=BY), :] = value
+    source = dot(table_ref[...], plane_ref[...])
+    x = lax.broadcasted_iota(jnp.int32, (GY, 128), 1) % BX
+    power = decay_ref[:, :128]
+    rising, falling = source, source
+    step = 1
+    while step < BX:
+        rising = rising + jnp.where(x >= step, power * pltpu.roll(rising, step, 1), 0.0)
+        falling = falling + jnp.where(x < BX - step, power * pltpu.roll(falling, 128 - step, 1), 0.0)
+        power = power * power
+        step *= 2
+    local_ref[:, :128] = scale_ref[:, :128] * (rising + falling - source)
+    side = jnp.where(x == 0, falling, pltpu.roll(rising, 128 - BX + 2, 1))
+    local_ref[:, 128:] = scale_ref[:, 128:] * decay_ref[:, 128:] * side
+    ends = dot(pick_ref[0:8, :], rising, ((1,), (1,))) + dot(pick_ref[8:16, :], falling, ((1,), (1,)))
+    for r in range(ROWS):
+        ends_ref[r * 24 : r * 24 + 8, :] = ends[:, :128]
+        ends_ref[r * 24 + 8 : r * 24 + 16, :] = ends[:, 128:]
+        ends_ref[r * 24 + 16 : r * 24 + 24, :] = source[0:8]
+
+
+def join_kernel(
+    place_ref, ends_ref, local_ref, left_ref, right_ref, kappa_ref, expand_ref, line_ref, table_ref,
+    out_ref, wide_ref,
+):
+    row = place_ref[0]
+
+    def slab(step):
+        return pl.multiple_of(((row + step) & (ROWS - 1)) * 24, 8)
+
+    rising = lax.broadcasted_iota(jnp.int32, (8, GY), 0) % 2 == 0
+    block = jnp.exp(-BX * kappa_ref[...])
+    total = None
+    for d in range(ROWS, 0, -1):
+        below, above = slab(ROWS - d), slab(d)
+        both = []
+        for part in (0, 8):
+            both.append((ends_ref[pl.ds(below + part, 8), :], ends_ref[pl.ds(above + part, 8), :]))
+        low = jnp.concatenate([both[0][0], both[1][0]], axis=1)
+        high = jnp.concatenate([both[0][1], both[1][1]], axis=1)
+        value = jnp.where(rising, low, high)
+        total = value if total is None else value + block * total
+    from_left = dot(jnp.where(rising, total, 0.0), expand_ref[0:8, :] * 2.0, ((0,), (0,)))
+    from_right = dot(jnp.where(rising, 0.0, total), expand_ref[0:8, :] * 2.0, ((0,), (0,)))
+    field = local_ref[...] + left_ref[...] * from_left + right_ref[...] * from_right
+    lane = lax.broadcasted_iota(jnp.int32, (8, 128), 1)
+    halves = []
+    for half in range(2):
+        line = jnp.zeros((8, 128), jnp.float32)
+        for g in range(4):
+            values = ends_ref[pl.ds(slab(ROWS - half * 4 - g) + 16, 8), :]
+            values = jnp.where(lane < BX, values, 0.0)
+            line = line + (pltpu.roll(values, g * BX, 1) if g else values)
+        halves.append(line)
+    mean = dot(jnp.concatenate(halves, axis=1), line_ref[...])
+    first = lax.broadcasted_iota(jnp.int32, (8, 256), 0) == 0
+    mean = jnp.where(jnp.logical_and(first, place_ref[1] == 0), mean, 0.0)
+    field = jnp.concatenate([field[0:8] + mean, field[8:]], axis=0)
+    potential = dot(table_ref[...], field)
+    for part in range(2):
+        base, side = part * (GY + 16), potential[:, part * 128 : part * 128 + 128]
         wide_ref[base + 8 : base + 8 + GY, :] = side
         wide_ref[base : base + 8, :] = side[GY - 8 :]
         wide_ref[base + 8 + GY : base + 16 + GY, :] = side[:8]
-
-    def strip(row):
-        return jnp.concatenate(
-            [wide_ref[pl.ds(b + row, COLS, stride=BY), :] for b in (0, GY + 16)], axis=1
-        )
-
-    strips = [strip(8 + yl) for yl in range(BY)]
-    below, above = strip(7), strip(16)
-    lane = lax.broadcasted_iota(jnp.int32, (COLS, GX), 1) % 32
-    sides = jnp.zeros((COLS, GX), jnp.float32)
+    strips = [wide_ref[pl.ds(8 + yl, COLS, stride=BY), :] for yl in range(BY)]
+    below = wide_ref[pl.ds(7, COLS, stride=BY), :]
+    above = wide_ref[pl.ds(16, COLS, stride=BY), :]
+    x = lax.broadcasted_iota(jnp.int32, (COLS, 128), 1) % BX
+    sides = jnp.zeros((COLS, 128), jnp.float32)
     for yl in range(BY):
-        sides = jnp.where(lane == yl, pltpu.roll(strips[yl], 1 + yl, 1), sides)
-        sides = jnp.where(lane == 8 + yl, pltpu.roll(strips[yl], GX - 24 + yl, 1), sides)
+        edge = wide_ref[pl.ds(GY + 16 + 8 + yl, COLS, stride=BY), :]
+        sides = jnp.where(x == yl, pltpu.roll(edge, yl, 1) if yl else edge, sides)
+        sides = jnp.where(x == BY + yl, pltpu.roll(edge, BY - 1 + yl, 1), sides)
     strips = strips + [below, above, sides, sides]
-    for high in range(2):
-        for quad in range(3):
-            lines = [s[:, high * 128 : high * 128 + 128] for s in strips[quad * 4 : quad * 4 + 4]]
-            for p, value in enumerate(swap_groups(lines, 32)):
-                out_ref[pl.ds((high * 4 + p) * COLS * 3 + quad, COLS, stride=3), :] = value
+    for quad in range(3):
+        for k, value in enumerate(swap_groups(strips[quad * 4 : quad * 4 + 4], 32)):
+            out_ref[pl.ds(k * 3 + quad, COLS, stride=12), :] = value
 
 
 def kick_kernel(owner_ref, stepped_ref, modes_ref, table_ref, out_ref, phi_ref, kicked_ref):
     table = table_ref[...]
     parts = []
     for quad in range(3):
-        block = modes_ref[pl.ds(quad, 256, stride=3), :]
+        block = modes_ref[pl.ds(quad, GZ, stride=3), :]
         parts.append(dot(block, table, ((0,), (0,))))
     for yl in range(BY):
         phi_ref[pl.ds(BY + yl, BX, stride=BY), :] = parts[yl // 4][(yl % 4) * 32 : (yl % 4) * 32 + 32]
@@ -398,37 +478,48 @@
 
     table_z = hartley(GZ)
     table_x = hartley(GX)
-    modes_of = np.arange(256) % GZ
     wide = (5, BX + 2 * HALO, BY + 2 * HALO, GZ)
     first, modes = call(
-        euler_kernel, [(5, BX + HALO, BY + 2 * HALO, GZ), (512, 128)], (8, ()), [wide, (BX * BY, GZ)]
-    )(own, xlow, xhigh, ylow, yhigh, clow, chigh, jnp.asarray(table_z[modes_of]))
+        euler_kernel, [(5, BX + HALO, BY + 2 * HALO, GZ), (256, 128)], (8, ()), [wide, (BX * BY, GZ)]
+    )(own, xlow, xhigh, ylow, yhigh, clow, chigh, jnp.asarray(table_z))
     planes = lax.all_to_all(
-        modes.reshape(256, 2, 128), ("row", "col"), split_axis=0, concat_axis=0, tiled=True
+        modes.reshape(COLS, 8, 128), "col", split_axis=0, concat_axis=0, tiled=True
+    )
+    kappa = jnp.asarray(np.repeat(kappas(), 2, axis=0).astype(np.float32))
+    kappa = lax.dynamic_slice_in_dim(kappa, my_column * 8, 8, axis=0)
+    expand = jnp.asarray(lane_expand())
+    square = (GY, 256)
+    decay, scale, left, right = call(table_kernel, [square] * 4, (3, ()))(
+        kappa, expand, jnp.asarray(lane_spans()[None, :])
     )
     stepped = call(second_kernel, [(5, BX, BY, GZ)], (2, ()))(own, first)
-    planes, stepped = lax.optimization_barrier((planes, stepped))
-    place = my_row * COLS + my_column
-    wave_z = place % GZ
-    eig = eigenvalues(GX)
-    eig_z = -4.0 * jnp.sin((math.pi / GZ) * wave_z.astype(jnp.float32)) ** 2
-    strips = call(plane_kernel, [(768, 128)], (6, (0, 1)), [(2 * GY, 128), (2 * (GY + 16), 128)])(
-        (place // GZ).reshape(1),
-        eig_z.reshape(1),
-        planes.reshape(512, 128),
+    planes, stepped, decay = lax.optimization_barrier((planes, stepped, decay))
+    local, ends = call(ends_kernel, [square, (ROWS * 24, 128)], (5, ()), [(GY, 128)])(
+        planes.reshape(256, 128), jnp.asarray(table_x), decay, scale, jnp.asarray(lane_picks())
+    )
+    ends = lax.all_to_all(
+        ends.reshape(ROWS, 24, 128), "row", split_axis=0, concat_axis=0, tiled=True
+    )
+    strips = call(join_kernel, [(COLS * 12, 128)], (9, (0,)), [(2 * (GY + 16), 128)])(
+        jnp.stack([my_row, my_column]),
+        ends.reshape(ROWS * 24, 128),
+        local,
+        left,
+        right,
+        kappa,
+        expand,
+        jnp.asarray(mean_line()),
         jnp.asarray(table_x),
-        jnp.asarray(eig[None, :]),
-        jnp.asarray(np.broadcast_to(eig[:, None], (GX, 128))),
     )
     strips = lax.all_to_all(
-        strips.reshape(256, 1, 384), ("row", "col"), split_axis=0, concat_axis=0, tiled=True
+        strips.reshape(COLS, 1, 1536), "col", split_axis=0, concat_axis=0, tiled=True
     )
     returned = call(
         kick_kernel,
         [(COLS, BRICK, 128)],
         (4, (0,)),
         [((BX + 2) * BY, GZ), (5 * BX * BY, GZ)],
-    )(owners, stepped, strips.reshape(768, 128), jnp.asarray(table_z[modes_of]))
+    )(owners, stepped, strips.reshape(COLS * 12, 128), jnp.asarray(table_z))
     came_back = lax.all_to_all(returned, "col", split_axis=0, concat_axis=0, tiled=True)
     home = jnp.stack([(CAP - turn) % CAP, counts[0, 0]])
     result = call(spread_kernel, [(5, CAP, PE * PE * PE)], (2, (0,)))(

time: 183 us -> 181 us (0.989)
  blocking collectives: 23.6 us -> 16.9 us
  waiting for transfers between devices: 86.1 us -> 82 us
  local copies, waits for them, and re-layouts: 2.95 us -> 6.67 us
  Pallas kernels: 22.3 us -> 25.2 us
    all_to_all x1, blocking collectives: 23.6 us -> 16.9 us  [on_device(): lax.all_to_all(strips.reshape(COLS, 1, 1536), 'col', split_axis=0, concat...]
    unnamed x12 -> x26, local copies, waits for them, and re-layouts: 2.24 us -> 5.34 us
    pallas_call x2 -> x4, Pallas kernels: 8.92 us -> 12 us  [the longest x1 6.76 us: on_device(): call(euler_kernel, [(5, BX + HALO, BY + 2 * HALO, GZ), (256, 128)], (8, (...]
    all_to_all x1 -> x2, waiting for transfers between devices: 10.8 us -> 7.83 us  [the longest x1 5.46 us: on_device(): lax.all_to_all(ends.reshape(ROWS, 24, 128), 'row', split_axis=0, concat_a...]
    all_to_all x1 -> x2, starting transfers between devices: 13.8 us -> 15.6 us  [the longest x1 12.1 us: on_device(): lax.all_to_all(modes.reshape(COLS, 8, 128), 'col', split_axis=0, concat_a...]
  transfers between devices with their start and end apart: 10 -> 11, of which waited for: 7 -> 8; matrix products, arithmetic and copies ran while one was open for 1% -> 1% of each run, Pallas kernels for 2% -> 3%
where the time goes in v9:
time: 181 us; the launch traced here: 180 us
  waiting for transfers between devices  82 us (45%)
  starting transfers between devices  44.7 us (25%)
  Pallas kernels  25.2 us (14%)
  blocking collectives  16.9 us (9%)
  local copies, waits for them, and re-layouts  6.67 us (4%)
  between operations  2.76 us (2%)
    all_to_all x1, waiting for transfers between devices, on_device(): lax.all_to_all(sent.reshape(COLS, BRICK, 128), 'col', split_axis=0, conca...  31.6 us
    all_to_all x1, waiting for transfers between devices, on_device(): lax.all_to_all(returned, 'col', split_axis=0, concat_axis=0, tiled=True)  29.9 us
    all_to_all x1, blocking collectives, on_device(): lax.all_to_all(strips.reshape(COLS, 1, 1536), 'col', split_axis=0, concat...  16.9 us
    all_to_all x1, starting transfers between devices, on_device(): lax.all_to_all(modes.reshape(COLS, 8, 128), 'col', split_axis=0, concat_a...  12.1 us
    all_to_all x1, starting transfers between devices, gather_counts(): lax.all_to_all(copies, 'col', split_axis=0, concat_axis=0, tiled=True)  11.6 us
    pallas_call x1, Pallas kernels, on_device(): call(euler_kernel, [(5, BX + HALO, BY + 2 * HALO, GZ), (256, 128)], (8, (...  6.76 us
    all_to_all x1, waiting for transfers between devices, gather_counts(): lax.all_to_all(copies, 'col', split_axis=0, concat_axis=0, tiled=True)  6.03 us
    all_to_all x1, starting transfers between devices, on_device(): lax.all_to_all(returned, 'col', split_axis=0, concat_axis=0, tiled=True)  5.74 us
  transfers between devices with their start and end apart: 11, of which 8 were waited for; matrix products, arithmetic and copies ran while one was open for 1% of the time, Pallas kernels for 3%

profile of v9, /device:TPU:2, one launch (start us, length us, event | category | flops | bytes accessed | tf_op | source)
XLA Modules:
  0.0 180.1 jit_solution(14233550670069330723)
XLA Ops:
  0.7 0.6 broadcast_in_dim.29
  1.3 11.6 %all-to-all-start = ((f32[32,1,128]{2,1,0:T(1,128)}), f32[32,1,128]{2,1,0:T(1,128)S(1)}, u32[]{:S(2)}, u32[]{:S(2)}) async-start(f32[32,1,128]{2,1,0:T(1,128)} %broadcast_in_dim.29), calls=%async_computation | async-start | bytes 32768 | tf_op jit(solution)/shard_map/all_to_all | solution.py:430
  12.9 0.0 copy-start
  12.9 1.3 copy-done
  14.2 1.1 shard_map.91.staged_ref
  15.3 6.0 %all-to-all-done.counts_ref = f32[32,1,128]{2,1,0:T(1,128)S(1)} async-done(((f32[32,1,128]{2,1,0:T(1,128)}), f32[32,1,128]{2,1,0:T(1,128)S(1)}, u32[]{:S(2)}, u32[]{:S(2)}) %all-to-all-start) | async-done | bytes 16416 | tf_op jit(solution)/shard_map/all_to_all | solution.py:430
  21.3 1.3 shard_map.92
  22.6 5.1 %all-to-all-start.1 = ((f32[32,80,128]{2,1,0:T(8,128)}), f32[32,80,128]{2,1,0:T(8,128)S(1)}, u32[]{:S(2)}, u32[]{:S(2)}) async-start(f32[32,80,128]{2,1,0:T(8,128)} %bitcast.5), calls=%async_computation.1 | async-start | bytes 2621440 | tf_op jit(solution)/shard_map/all_to_all | solution.py:452
  27.7 0.0 copy-start.4
  27.7 0.7 fusion.1
  28.4 0.1 select_reduce_fusion
  28.5 0.2 convert_reduce_fusion
  28.7 31.6 %all-to-all-done.1.recv_ref = f32[32,80,128]{2,1,0:T(8,128)S(1)} async-done(((f32[32,80,128]{2,1,0:T(8,128)}), f32[32,80,128]{2,1,0:T(8,128)S(1)}, u32[]{:S(2)}, u32[]{:S(2)}) %all-to-all-start.1) | async-done | bytes 1310752 | tf_op jit(solution)/shard_map/all_to_all | solution.py:452
  60.3 2.7 %shard_map.93 = (f32[5,32,8,128]{3,2,1,0:T(8,128)S(1)}, f32[5,4,8,128]{3,2,1,0:T(8,128)S(1)}, f32[5,4,8,128]{3,2,1,0:T(8,128)S(1)}, f32[5,32,4,128]{3,2,1,0:T(4,128)S(1)}, f32[5,32,4,128]{3,2,1,0:T(4,128)S(1)}) custom-call(s32[16]{0:T(128)S(1)} %broadcast_add_fusion.owner_ref, f32[32,80,128]{2,1,0:T(8,128)S(1)} %all-to-all-done.1.recv_ref), custom_call_target="tpu_custom_call" | custom-call | tf_op jit(solution)/shard_map/pallas_call | solution.py:455
  63.0 0.0 copy-start.10
  63.0 0.0 copy-start.12
  63.0 1.5 collective-permute-start.2
  64.5 0.6 collective-permute-start.3
  65.1 0.0 collective-permute-start.1
  65.1 0.5 collective-permute-start
  65.6 1.6 collective-permute-done.1.xhigh_ref
  67.1 3.2 %collective-permute-done.xlow_ref = f32[5,4,8,128]{3,2,1,0:T(8,128)S(1)} collective-permute-done((f32[5,4,8,128]{3,2,1,0:T(8,128)S(1)}, f32[5,4,8,128]{3,2,1,0:T(8,128)S(1)}, u32[]{:S(2)}, u32[]{:S(2)}) %collective-permute-start) | collective-permute-done | bytes 81952 | tf_op jit(solution)/shard_map/ppermute | solution.py:471
  70.4 1.5 collective-permute-start.4
  71.9 2.5 %collective-permute-start.5 = (f32[5,4,4,128]{3,2,1,0:T(4,128)S(1)}, f32[5,4,4,128]{3,2,1,0:T(4,128)S(1)}, u32[]{:S(2)}, u32[]{:S(2)}) collective-permute-start(f32[5,4,4,128]{3,2,1,0:T(4,128)S(1)} %get-tuple-element.37), channel_id=1, source_target_pairs={{0,31},{1,0},{2,1},{3,2},{4,3},{5,4},{6,5},{7,6},{8,7},{9,8},{10,9... | collective-permute-start | bytes 122888 | tf_op jit(solution)/shard_map/ppermute | solution.py:477
  74.4 1.9 %collective-permute-done.4.clow_ref = f32[5,4,4,128]{3,2,1,0:T(4,128)S(1)} collective-permute-done((f32[5,4,4,128]{3,2,1,0:T(4,128)S(1)}, f32[5,4,4,128]{3,2,1,0:T(4,128)S(1)}, u32[]{:S(2)}, u32[]{:S(2)}) %collective-permute-start.4) | collective-permute-done | bytes 40992 | tf_op jit(solution)/shard_map/ppermute | solution.py:476
  76.3 0.0 collective-permute-done.5.chigh_ref
  76.3 0.0 collective-permute-done.2.ylow_ref
  76.3 0.0 collective-permute-done.3.yhigh_ref
  76.3 0.0 copy-done.4
  76.3 6.8 %shard_map.94 = (f32[5,36,16,128]{3,2,1,0:T(8,128)S(1)}, f32[256,128]{1,0:T(8,128)}) custom-call(f32[5,32,8,128]{3,2,1,0:T(8,128)S(1)} %get-tuple-element.21.own_ref, f32[5,4,8,128]{3,2,1,0:T(8,128)S(1)} %collective-permute-done.xlow_ref, f32[5,4,8,128]{3,2,1,0:T(8,128)S(1)} %collective-permute-done.1.xhigh_ref, ...), custom_call_target="tpu_custom_call" | custom-call | tf_op jit(solution)/shard_map/pallas_call | solution.py:482
  83.1 12.1 %all-to-all-start.2 = ((f32[32,8,128]{2,1,0:T(8,128)}), f32[32,8,128]{2,1,0:T(8,128)S(1)}, u32[]{:S(2)}, u32[]{:S(2)}) async-start(f32[32,8,128]{2,1,0:T(8,128)} %bitcast.6), calls=%async_computation.2 | async-start | bytes 262144 | tf_op jit(solution)/shard_map/all_to_all | solution.py:485
  95.2 0.7 constant_dynamic-slice_fusion.kappa_ref
  95.9 0.0 copy-done.10
  95.9 0.0 copy-done.12
  95.9 0.6 shard_map.96
  96.5 0.0 copy-start.2
  96.5 0.7 copy-done.2
  97.2 0.0 copy-start.6
  97.2 0.7 copy-done.6
  97.9 0.0 copy-start.8
  97.9 0.7 copy-done.8
  98.6 0.0 copy-start.1
  98.6 0.0 copy-start.11
  98.6 3.1 %shard_map.95.stepped_ref = f32[5,32,8,128]{3,2,1,0:T(8,128)S(1)} custom-call(f32[5,32,8,128]{3,2,1,0:T(8,128)S(1)} %get-tuple-element.21.own_ref, f32[5,36,16,128]{3,2,1,0:T(8,128)S(1)} %get-tuple-element.27.first_ref), custom_call_target="tpu_custom_call" | custom-call | tf_op jit(solution)/shard_map/pallas_call | solution.py:495
  101.7 2.4 %all-to-all-done.2 = f32[32,8,128]{2,1,0:T(8,128)S(1)} async-done(((f32[32,8,128]{2,1,0:T(8,128)}), f32[32,8,128]{2,1,0:T(8,128)S(1)}, u32[]{:S(2)}, u32[]{:S(2)}) %all-to-all-start.2) | async-done | bytes 131104 | tf_op jit(solution)/shard_map/all_to_all | solution.py:485
  104.1 0.0 copy-done.1
  104.1 0.0 copy-done.11
  104.1 0.0 copy-start.3
  104.1 0.9 copy-done.3
  105.0 2.3 %shard_map.97 = (f32[256,256]{1,0:T(8,128)S(1)}, f32[192,128]{1,0:T(8,128)}) custom-call(f32[256,128]{1,0:T(8,128)S(1)} %bitcast.20, f32[256,256]{1,0:T(8,128)S(1)} %copy-done.1, f32[256,256]{1,0:T(8,128)S(1)} %get-tuple-element.31.decay_ref, f32[256,256]{1,0:T(8,128)S(1)} %copy-done.3, f32[16,128]{1,0:T(8,128)S(1)} %copy-done.11), custom_call_target="tpu_custom_call" | custom-call | tf_op jit(solution)/shard_map/pallas_call | solution.py:497
  107.4 3.5 %all-to-all-start.3 = ((f32[8,24,128]{2,1,0:T(8,128)}), f32[8,24,128]{2,1,0:T(8,128)S(1)}, u32[]{:S(2)}, u32[]{:S(2)}) async-start(f32[8,24,128]{2,1,0:T(8,128)} %bitcast.9), calls=%async_computation.3 | async-start | bytes 196608 | tf_op jit(solution)/shard_map/all_to_all | solution.py:500
  110.9 0.1 pad_add_fusion.1.place_ref
  111.0 5.5 %all-to-all-done.3 = f32[8,24,128]{2,1,0:T(8,128)S(1)} async-done(((f32[8,24,128]{2,1,0:T(8,128)}), f32[8,24,128]{2,1,0:T(8,128)S(1)}, u32[]{:S(2)}, u32[]{:S(2)}) %all-to-all-start.3) | async-done | bytes 98336 | tf_op jit(solution)/shard_map/all_to_all | solution.py:500
  116.4 0.0 copy-done.7
  116.4 0.0 copy-done.9
  116.4 0.9 copy-done.5
  117.4 2.3 %shard_map.98 = f32[384,128]{1,0:T(8,128)S(1)} custom-call(s32[2]{0:T(128)S(1)} %pad_add_fusion.1.place_ref, f32[192,128]{1,0:T(8,128)S(1)} %bitcast.21, f32[256,256]{1,0:T(8,128)S(1)} %get-tuple-element.34.local_ref, f32[256,256]{1,0:T(8,128)S(1)} %copy-done.7, f32[256,256]{1,0:T(8,128)S(1)} %copy-done.9, ...), custom_call_target="tpu_custom_call" | custom-call | tf_op jit(solution)/shard_map/pallas_call | solution.py:503
  119.7 16.9 %all_to_all.30 = f32[32,1,1536]{2,1,0:T(1,128)S(1)} all-to-all(f32[32,1,1536]{2,1,0:T(1,128)S(1)} %bitcast.18), channel_id=1, replica_groups=mesh['row'=8,'col'=32] {'col'}, dimensions={0} | all-to-all | bytes 393216 | tf_op jit(solution)/shard_map/all_to_all | solution.py:514
  136.6 2.8 %shard_map.99 = f32[32,80,128]{2,1,0:T(8,128)} custom-call(s32[16]{0:T(128)S(1)} %broadcast_add_fusion.owner_ref, f32[5,32,8,128]{3,2,1,0:T(8,128)S(1)} %shard_map.95.stepped_ref, f32[384,128]{1,0:T(8,128)S(1)} %bitcast.19, f32[128,128]{1,0:T(8,128)S(1)} %copy-done.4), custom_call_target="tpu_custom_call" | custom-call | tf_op jit(solution)/shard_map/pallas_call | solution.py:517
  139.4 5.7 %all-to-all-start.5 = ((f32[32,80,128]{2,1,0:T(8,128)}), f32[32,80,128]{2,1,0:T(8,128)S(1)}, u32[]{:S(2)}, u32[]{:S(2)}) async-start(f32[32,80,128]{2,1,0:T(8,128)} %shard_map.99), calls=%async_computation.5 | async-start | bytes 2621440 | tf_op jit(solution)/shard_map/all_to_all | solution.py:523
  145.1 0.7 fusion.2
  147.7 0.1 pad_add_fusion.place_ref
  147.8 29.9 %all-to-all-done.5 = f32[32,80,128]{2,1,0:T(8,128)S(1)} async-done(((f32[32,80,128]{2,1,0:T(8,128)}), f32[32,80,128]{2,1,0:T(8,128)S(1)}, u32[]{:S(2)}, u32[]{:S(2)}) %all-to-all-start.5) | async-done | bytes 1310752 | tf_op jit(solution)/shard_map/all_to_all | solution.py:523
  177.7 2.4 %shard_map.100 = f32[5,16,4096]{2,1,0:T(8,128)} custom-call(s32[2]{0:T(128)S(1)} %pad_add_fusion.place_ref, f32[2560,128]{1,0:T(8,128)S(1)} %bitcast.16), custom_call_target="tpu_custom_call" | custom-call | tf_op jit(solution)/shard_map/pallas_call | solution.py:525
  (8 shorter events, 0.0 us)
Async XLA Ops:
  1.3 20.1 %all-to-all-start = ((f32[32,1,128]{2,1,0:T(1,128)}), f32[32,1,128]{2,1,0:T(1,128)S(1)}, u32[]{:S(2)}, u32[]{:S(2)}) async-start(f32[32,1,128]{2,1,0:T(1,128)} %broadcast_in_dim.29), calls=%async_computation | async-start | bytes 32768 | tf_op jit(solution)/shard_map/all_to_all | solution.py:430
  12.9 1.3 copy-start
  22.6 37.7 %all-to-all-start.1 = ((f32[32,80,128]{2,1,0:T(8,128)}), f32[32,80,128]{2,1,0:T(8,128)S(1)}, u32[]{:S(2)}, u32[]{:S(2)}) async-start(f32[32,80,128]{2,1,0:T(8,128)} %bitcast.5), calls=%async_computation.1 | async-start | bytes 2621440 | tf_op jit(solution)/shard_map/all_to_all | solution.py:452
  27.7 48.6 %copy-start.4 = (f32[128,128]{1,0:T(8,128)S(1)}, f32[128,128]{1,0:T(8,128)}, u32[]{:S(2)}) copy-start(f32[128,128]{1,0:T(8,128)} %constant.61.clone.table_ref) | copy-start | bytes 196612
  63.0 33.0 %copy-start.10 = (f32[8,256]{1,0:T(8,128)S(1)}, f32[8,256]{1,0:T(8,128)}, u32[]{:S(2)}) copy-start(f32[8,256]{1,0:T(8,128)} %constant.63.clone.expand_ref) | copy-start | bytes 24580
  63.0 33.0 %copy-start.12 = (f32[1,256]{1,0:T(1,128)S(1)}, f32[1,256]{1,0:T(1,128)}, u32[]{:S(2)}) copy-start(f32[1,256]{1,0:T(1,128)} %constant.64.clone.span_ref) | copy-start | bytes 3076
  63.0 13.3 %collective-permute-start.2 = (f32[5,32,4,128]{3,2,1,0:T(4,128)S(1)}, f32[5,32,4,128]{3,2,1,0:T(4,128)S(1)}, u32[]{:S(2)}, u32[]{:S(2)}) collective-permute-start(f32[5,32,4,128]{3,2,1,0:T(4,128)S(1)} %get-tuple-element.24), channel_id=1, source_target_pairs={{0,1},{1,2},{2,3},{3,4},{4,5},{5,6},{6,7},{7,8},{8,9},{9,10},{10,1... | collective-permute-start | bytes 983048 | tf_op jit(solution)/shard_map/ppermute | solution.py:473
  64.5 11.8 %collective-permute-start.3 = (f32[5,32,4,128]{3,2,1,0:T(4,128)S(1)}, f32[5,32,4,128]{3,2,1,0:T(4,128)S(1)}, u32[]{:S(2)}, u32[]{:S(2)}) collective-permute-start(f32[5,32,4,128]{3,2,1,0:T(4,128)S(1)} %get-tuple-element.25), channel_id=1, source_target_pairs={{0,31},{1,0},{2,1},{3,2},{4,3},{5,4},{6,5},{7,6},{8,7},{9,8},{10,9... | collective-permute-start | bytes 983048 | tf_op jit(solution)/shard_map/ppermute | solution.py:474
  65.1 2.1 %collective-permute-start.1 = (f32[5,4,8,128]{3,2,1,0:T(8,128)S(1)}, f32[5,4,8,128]{3,2,1,0:T(8,128)S(1)}, u32[]{:S(2)}, u32[]{:S(2)}) collective-permute-start(f32[5,4,8,128]{3,2,1,0:T(8,128)S(1)} %get-tuple-element.23), channel_id=1, source_target_pairs={{0,224},{32,0},{64,32},{96,64},{128,96},{160,128},{192,160},{224,1... | collective-permute-start | bytes 245768 | tf_op jit(solution)/shard_map/ppermute | solution.py:472
  65.1 5.2 %collective-permute-start = (f32[5,4,8,128]{3,2,1,0:T(8,128)S(1)}, f32[5,4,8,128]{3,2,1,0:T(8,128)S(1)}, u32[]{:S(2)}, u32[]{:S(2)}) collective-permute-start(f32[5,4,8,128]{3,2,1,0:T(8,128)S(1)} %get-tuple-element.22), channel_id=1, source_target_pairs={{0,32},{32,64},{64,96},{96,128},{128,160},{160,192},{192,224},{224... | collective-permute-start | bytes 245768 | tf_op jit(solution)/shard_map/ppermute | solution.py:471
  70.4 5.9 %collective-permute-start.4 = (f32[5,4,4,128]{3,2,1,0:T(4,128)S(1)}, f32[5,4,4,128]{3,2,1,0:T(4,128)S(1)}, u32[]{:S(2)}, u32[]{:S(2)}) collective-permute-start(f32[5,4,4,128]{3,2,1,0:T(4,128)S(1)} %get-tuple-element.38), channel_id=1, source_target_pairs={{0,1},{1,2},{2,3},{3,4},{4,5},{5,6},{6,7},{7,8},{8,9},{9,10},{10,1... | collective-permute-start | bytes 122888 | tf_op jit(solution)/shard_map/ppermute | solution.py:476
  71.9 4.4 %collective-permute-start.5 = (f32[5,4,4,128]{3,2,1,0:T(4,128)S(1)}, f32[5,4,4,128]{3,2,1,0:T(4,128)S(1)}, u32[]{:S(2)}, u32[]{:S(2)}) collective-permute-start(f32[5,4,4,128]{3,2,1,0:T(4,128)S(1)} %get-tuple-element.37), channel_id=1, source_target_pairs={{0,31},{1,0},{2,1},{3,2},{4,3},{5,4},{6,5},{7,6},{8,7},{9,8},{10,9... | collective-permute-start | bytes 122888 | tf_op jit(solution)/shard_map/ppermute | solution.py:477
  83.1 21.0 %all-to-all-start.2 = ((f32[32,8,128]{2,1,0:T(8,128)}), f32[32,8,128]{2,1,0:T(8,128)S(1)}, u32[]{:S(2)}, u32[]{:S(2)}) async-start(f32[32,8,128]{2,1,0:T(8,128)} %bitcast.6), calls=%async_computation.2 | async-start | bytes 262144 | tf_op jit(solution)/shard_map/all_to_all | solution.py:485
  96.5 0.7 copy-start.2
  97.2 0.7 copy-start.6
  97.9 0.7 copy-start.8
  98.6 5.4 %copy-start.1 = (f32[256,256]{1,0:T(8,128)S(1)}, f32[256,256]{1,0:T(8,128)}, u32[]{:S(2)}) copy-start(f32[256,256]{1,0:T(8,128)} %constant.65.clone.table_ref) | copy-start | bytes 786436
  98.6 5.4 %copy-start.11 = (f32[16,128]{1,0:T(8,128)S(1)}, f32[16,128]{1,0:T(8,128)}, u32[]{:S(2)}) copy-start(f32[16,128]{1,0:T(8,128)} %constant.66.clone.pick_ref) | copy-start | bytes 24580
  104.1 1.0 copy-start.3
  105.0 11.4 %copy-start.7 = (f32[256,256]{1,0:T(8,128)S(1)}, f32[256,256]{1,0:T(8,128)}, u32[]{:S(2)}) copy-start(f32[256,256]{1,0:T(8,128)} %copy-done.6) | copy-start | bytes 786436
  105.0 11.4 %copy-start.9 = (f32[256,256]{1,0:T(8,128)S(1)}, f32[256,256]{1,0:T(8,128)}, u32[]{:S(2)}) copy-start(f32[256,256]{1,0:T(8,128)} %copy-done.8) | copy-start | bytes 786436
  107.4 9.1 %all-to-all-start.3 = ((f32[8,24,128]{2,1,0:T(8,128)}), f32[8,24,128]{2,1,0:T(8,128)S(1)}, u32[]{:S(2)}, u32[]{:S(2)}) async-start(f32[8,24,128]{2,1,0:T(8,128)} %bitcast.9), calls=%async_computation.3 | async-start | bytes 196608 | tf_op jit(solution)/shard_map/all_to_all | solution.py:500
  116.4 1.0 copy-start.5
  139.4 38.3 %all-to-all-start.5 = ((f32[32,80,128]{2,1,0:T(8,128)}), f32[32,80,128]{2,1,0:T(8,128)S(1)}, u32[]{:S(2)}, u32[]{:S(2)}) async-start(f32[32,80,128]{2,1,0:T(8,128)} %shard_map.99), calls=%async_computation.5 | async-start | bytes 2621440 | tf_op jit(solution)/shard_map/all_to_all | solution.py:523

commit v10 on v9

--- a/solution.py
+++ b/solution.py
@@ -64,7 +64,9 @@
     used = (lanes < BX) | (lanes == 128) | (lanes == 129)
     gap = np.arange(GX)[:, None] // BX * BX + lane_spans()[None, :] - np.arange(GX)[:, None] % BX
     gap = np.abs(gap)
-    return (four_pi_g * np.where(used[None, :], gap / 2.0 - gap * gap / (2.0 * GX), 0.0)).astype(np.float32)
+    shape = gap / 2.0 - gap * gap / (2.0 * GX)
+    shape = shape - shape[:, 0].mean()
+    return (four_pi_g * np.where(used[None, :], shape, 0.0)).astype(np.float32)
 
 
 def dot(left, right, dims=((1,), (0,))):
@@ -265,28 +267,14 @@
     euler_stage(load_first, store_stepped, HALO, BX, BY, 8)
 
 
-def table_kernel(kappa_ref, expand_ref, span_ref, decay_ref, scale_ref, left_ref, right_ref):
-    kappa = dot(kappa_ref[...], expand_ref[...], ((0,), (0,)))
-    flat = kappa <= 0.0
-    decay = jnp.exp(-kappa)
-    width = jnp.where(flat, 1.0, jnp.exp(kappa) - decay)
-    scale = jnp.where(flat, 0.0, -four_pi_g / width)
-    images = scale / jnp.where(flat, 1.0, 1.0 - jnp.exp(-GX * kappa))
-    span = span_ref[...]
-    decay_ref[...] = decay
-    scale_ref[...] = scale
-    left_ref[...] = images * jnp.exp(-kappa * (span + 1.0))
-    right_ref[...] = images * jnp.exp(-kappa * (BX - span))
-
-
-def ends_kernel(modes_ref, table_ref, decay_ref, scale_ref, pick_ref, local_ref, ends_ref, plane_ref):
+def ends_kernel(modes_ref, table_ref, kappa_ref, expand_ref, pick_ref, raw_ref, ends_ref, plane_ref):
     for tile in range(2):
         lines = [modes_ref[pl.ds(k * 2 + tile, COLS, stride=8), :] for k in range(4)]
         for g, value in enumerate(swap_groups(lines, 32)):
             plane_ref[pl.ds(tile * 4 + g, COLS, stride=BY), :] = value
+    power = jnp.exp(-dot(kappa_ref[...], expand_ref[:, :128], ((0,), (0,))))
     source = dot(table_ref[...], plane_ref[...])
     x = lax.broadcasted_iota(jnp.int32, (GY, 128), 1) % BX
-    power = decay_ref[:, :128]
     rising, falling = source, source
     step = 1
     while step < BX:
@@ -294,14 +282,28 @@
         falling = falling + jnp.where(x < BX - step, power * pltpu.roll(falling, 128 - step, 1), 0.0)
         power = power * power
         step *= 2
-    local_ref[:, :128] = scale_ref[:, :128] * (rising + falling - source)
-    side = jnp.where(x == 0, falling, pltpu.roll(rising, 128 - BX + 2, 1))
-    local_ref[:, 128:] = scale_ref[:, 128:] * decay_ref[:, 128:] * side
     ends = dot(pick_ref[0:8, :], rising, ((1,), (1,))) + dot(pick_ref[8:16, :], falling, ((1,), (1,)))
     for r in range(ROWS):
         ends_ref[r * 24 : r * 24 + 8, :] = ends[:, :128]
         ends_ref[r * 24 + 8 : r * 24 + 16, :] = ends[:, 128:]
         ends_ref[r * 24 + 16 : r * 24 + 24, :] = source[0:8]
+    raw_ref[:, :128] = rising + falling - source
+    raw_ref[:, 128:] = jnp.where(x == 0, falling, pltpu.roll(rising, 128 - BX + 2, 1))
+
+
+def weigh_kernel(kappa_ref, expand_ref, span_ref, raw_ref, local_ref, left_ref, right_ref):
+    kappa = dot(kappa_ref[...], expand_ref[:, :128], ((0,), (0,)))
+    flat = kappa <= 0.0
+    decay = jnp.exp(-kappa)
+    width = jnp.where(flat, 1.0, jnp.exp(kappa) - decay)
+    scale = jnp.where(flat, 0.0, -four_pi_g / width)
+    images = scale / jnp.where(flat, 1.0, 1.0 - jnp.exp(-GX * kappa))
+    for half in range(2):
+        lanes = slice(half * 128, half * 128 + 128)
+        span = span_ref[:, lanes]
+        local_ref[:, lanes] = (scale * decay if half else scale) * raw_ref[:, lanes]
+        left_ref[:, lanes] = images * jnp.exp(-kappa * (span + 1.0))
+        right_ref[:, lanes] = images * jnp.exp(-kappa * (BX - span))
 
 
 def join_kernel(
@@ -337,7 +339,9 @@
             values = jnp.where(lane < BX, values, 0.0)
             line = line + (pltpu.roll(values, g * BX, 1) if g else values)
         halves.append(line)
-    mean = dot(jnp.concatenate(halves, axis=1), line_ref[...])
+    line = jnp.concatenate(halves, axis=1)
+    line = line - jnp.sum(line, axis=1, keepdims=True) * (1.0 / GX)
+    mean = dot(line, line_ref[...])
     first = lax.broadcasted_iota(jnp.int32, (8, 256), 0) == 0
     mean = jnp.where(jnp.logical_and(first, place_ref[1] == 0), mean, 0.0)
     field = jnp.concatenate([field[0:8] + mean, field[8:]], axis=0)
@@ -489,13 +493,13 @@
     kappa = lax.dynamic_slice_in_dim(kappa, my_column * 8, 8, axis=0)
     expand = jnp.asarray(lane_expand())
     square = (GY, 256)
-    decay, scale, left, right = call(table_kernel, [square] * 4, (3, ()))(
-        kappa, expand, jnp.asarray(lane_spans()[None, :])
-    )
     stepped = call(second_kernel, [(5, BX, BY, GZ)], (2, ()))(own, first)
-    planes, stepped, decay = lax.optimization_barrier((planes, stepped, decay))
-    local, ends = call(ends_kernel, [square, (ROWS * 24, 128)], (5, ()), [(GY, 128)])(
-        planes.reshape(256, 128), jnp.asarray(table_x), decay, scale, jnp.asarray(lane_picks())
+    planes, stepped, kappa = lax.optimization_barrier((planes, stepped, kappa))
+    raw, ends = call(ends_kernel, [square, (ROWS * 24, 128)], (5, ()), [(GY, 128)])(
+        planes.reshape(256, 128), jnp.asarray(table_x), kappa, expand, jnp.asarray(lane_picks())
+    )
+    local, left, right = call(weigh_kernel, [square] * 3, (4, ()))(
+        kappa, expand, jnp.asarray(lane_spans()[None, :]), raw
     )
     ends = lax.all_to_all(
         ends.reshape(ROWS, 24, 128), "row", split_axis=0, concat_axis=0, tiled=True

time: 181 us -> 177 us (0.978)
  local copies, waits for them, and re-layouts: 6.67 us -> 3.64 us
  blocking collectives: 16.9 us -> 14.6 us
  waiting for transfers between devices: 82 us -> 84 us
    unnamed x26 -> x14, local copies, waits for them, and re-layouts: 5.34 us -> 2.28 us
    all_to_all x1, waiting for transfers between devices: 2.37 us -> 5.05 us  [on_device(): lax.all_to_all(modes.reshape(COLS, 8, 128), 'col', split_axis=0, concat_a...]
    all_to_all x1, blocking collectives: 16.9 us -> 14.6 us  [on_device(): lax.all_to_all(strips.reshape(COLS, 1, 1536), 'col', split_axis=0, concat...]
where the time goes in v10:
time: 177 us
  waiting for transfers between devices  84 us (47%)
  starting transfers between devices  44.7 us (25%)
  Pallas kernels  25.1 us (14%)
  blocking collectives  14.6 us (8%)
  local copies, waits for them, and re-layouts  3.64 us (2%)
  between operations  2.92 us (2%)
  other arithmetic  1.85 us (1%)
    all_to_all x1, waiting for transfers between devices, on_device(): lax.all_to_all(sent.reshape(COLS, BRICK, 128), 'col', split_axis=0, conca...  31.6 us
    all_to_all x1, waiting for transfers between devices, on_device(): lax.all_to_all(returned, 'col', split_axis=0, concat_axis=0, tiled=True)  29.7 us
    all_to_all x1, blocking collectives, on_device(): lax.all_to_all(strips.reshape(COLS, 1, 1536), 'col', split_axis=0, concat...  14.6 us
    all_to_all x1, starting transfers between devices, on_device(): lax.all_to_all(modes.reshape(COLS, 8, 128), 'col', split_axis=0, concat_a...  12.1 us
    all_to_all x1, starting transfers between devices, gather_counts(): lax.all_to_all(copies, 'col', split_axis=0, concat_axis=0, tiled=True)  11.6 us
    pallas_call x1, Pallas kernels, on_device(): call(euler_kernel, [(5, BX + HALO, BY + 2 * HALO, GZ), (256, 128)], (8, (...  6.76 us
    all_to_all x1, waiting for transfers between devices, gather_counts(): lax.all_to_all(copies, 'col', split_axis=0, concat_axis=0, tiled=True)  6.03 us
    all_to_all x1, starting transfers between devices, on_device(): lax.all_to_all(returned, 'col', split_axis=0, concat_axis=0, tiled=True)  5.74 us
  transfers between devices with their start and end apart: 11, of which 8 were waited for; matrix products, arithmetic and copies ran while one was open for 1% of the time, Pallas kernels for 3%

profile of v10, /device:TPU:2, one launch (start us, length us, event | category | flops | bytes accessed | tf_op | source)
XLA Modules:
  0.0 176.8 jit_solution(16017376017936633115)
XLA Ops:
  0.7 0.6 broadcast_in_dim.29
  1.3 11.6 %all-to-all-start = ((f32[32,1,128]{2,1,0:T(1,128)}), f32[32,1,128]{2,1,0:T(1,128)S(1)}, u32[]{:S(2)}, u32[]{:S(2)}) async-start(f32[32,1,128]{2,1,0:T(1,128)} %broadcast_in_dim.29), calls=%async_computation | async-start | bytes 32768 | tf_op jit(solution)/shard_map/all_to_all | solution.py:434
  12.9 0.0 copy-start
  12.9 1.3 copy-done
  14.2 1.1 shard_map.91.staged_ref
  15.3 6.0 %all-to-all-done.counts_ref = f32[32,1,128]{2,1,0:T(1,128)S(1)} async-done(((f32[32,1,128]{2,1,0:T(1,128)}), f32[32,1,128]{2,1,0:T(1,128)S(1)}, u32[]{:S(2)}, u32[]{:S(2)}) %all-to-all-start) | async-done | bytes 16416 | tf_op jit(solution)/shard_map/all_to_all | solution.py:434
  21.3 1.3 shard_map.92
  22.6 5.1 %all-to-all-start.1 = ((f32[32,80,128]{2,1,0:T(8,128)}), f32[32,80,128]{2,1,0:T(8,128)S(1)}, u32[]{:S(2)}, u32[]{:S(2)}) async-start(f32[32,80,128]{2,1,0:T(8,128)} %bitcast.5), calls=%async_computation.1 | async-start | bytes 2621440 | tf_op jit(solution)/shard_map/all_to_all | solution.py:456
  27.7 0.0 copy-start.2
  27.7 0.7 fusion.1
  28.4 0.1 select_reduce_fusion
  28.5 0.2 convert_reduce_fusion
  28.7 31.6 %all-to-all-done.1.recv_ref = f32[32,80,128]{2,1,0:T(8,128)S(1)} async-done(((f32[32,80,128]{2,1,0:T(8,128)}), f32[32,80,128]{2,1,0:T(8,128)S(1)}, u32[]{:S(2)}, u32[]{:S(2)}) %all-to-all-start.1) | async-done | bytes 1310752 | tf_op jit(solution)/shard_map/all_to_all | solution.py:456
  60.3 2.7 %shard_map.93 = (f32[5,32,8,128]{3,2,1,0:T(8,128)S(1)}, f32[5,4,8,128]{3,2,1,0:T(8,128)S(1)}, f32[5,4,8,128]{3,2,1,0:T(8,128)S(1)}, f32[5,32,4,128]{3,2,1,0:T(4,128)S(1)}, f32[5,32,4,128]{3,2,1,0:T(4,128)S(1)}) custom-call(s32[16]{0:T(128)S(1)} %broadcast_add_fusion.owner_ref, f32[32,80,128]{2,1,0:T(8,128)S(1)} %all-to-all-done.1.recv_ref), custom_call_target="tpu_custom_call" | custom-call | tf_op jit(solution)/shard_map/pallas_call | solution.py:459
  63.0 1.5 collective-permute-start.2
  64.5 0.6 collective-permute-start.3
  65.1 0.0 collective-permute-start.1
  65.1 0.5 collective-permute-start
  65.6 1.6 collective-permute-done.1.xhigh_ref
  67.1 3.2 %collective-permute-done.xlow_ref = f32[5,4,8,128]{3,2,1,0:T(8,128)S(1)} collective-permute-done((f32[5,4,8,128]{3,2,1,0:T(8,128)S(1)}, f32[5,4,8,128]{3,2,1,0:T(8,128)S(1)}, u32[]{:S(2)}, u32[]{:S(2)}) %collective-permute-start) | collective-permute-done | bytes 81952 | tf_op jit(solution)/shard_map/ppermute | solution.py:475
  70.3 1.5 collective-permute-start.4
  71.9 2.5 %collective-permute-start.5 = (f32[5,4,4,128]{3,2,1,0:T(4,128)S(1)}, f32[5,4,4,128]{3,2,1,0:T(4,128)S(1)}, u32[]{:S(2)}, u32[]{:S(2)}) collective-permute-start(f32[5,4,4,128]{3,2,1,0:T(4,128)S(1)} %get-tuple-element.35), channel_id=1, source_target_pairs={{0,31},{1,0},{2,1},{3,2},{4,3},{5,4},{6,5},{7,6},{8,7},{9,8},{10,9... | collective-permute-start | bytes 122888 | tf_op jit(solution)/shard_map/ppermute | solution.py:481
  74.4 1.9 %collective-permute-done.4.clow_ref = f32[5,4,4,128]{3,2,1,0:T(4,128)S(1)} collective-permute-done((f32[5,4,4,128]{3,2,1,0:T(4,128)S(1)}, f32[5,4,4,128]{3,2,1,0:T(4,128)S(1)}, u32[]{:S(2)}, u32[]{:S(2)}) %collective-permute-start.4) | collective-permute-done | bytes 40992 | tf_op jit(solution)/shard_map/ppermute | solution.py:480
  76.3 0.0 collective-permute-done.5.chigh_ref
  76.3 0.0 collective-permute-done.2.ylow_ref
  76.3 0.0 collective-permute-done.3.yhigh_ref
  76.3 0.0 copy-done.2
  76.3 6.8 %shard_map.94 = (f32[5,36,16,128]{3,2,1,0:T(8,128)S(1)}, f32[256,128]{1,0:T(8,128)}) custom-call(f32[5,32,8,128]{3,2,1,0:T(8,128)S(1)} %get-tuple-element.20.own_ref, f32[5,4,8,128]{3,2,1,0:T(8,128)S(1)} %collective-permute-done.xlow_ref, f32[5,4,8,128]{3,2,1,0:T(8,128)S(1)} %collective-permute-done.1.xhigh_ref, ...), custom_call_target="tpu_custom_call" | custom-call | tf_op jit(solution)/shard_map/pallas_call | solution.py:486
  83.1 12.1 %all-to-all-start.2 = ((f32[32,8,128]{2,1,0:T(8,128)}), f32[32,8,128]{2,1,0:T(8,128)S(1)}, u32[]{:S(2)}, u32[]{:S(2)}) async-start(f32[32,8,128]{2,1,0:T(8,128)} %bitcast.6), calls=%async_computation.2 | async-start | bytes 262144 | tf_op jit(solution)/shard_map/all_to_all | solution.py:489
  95.2 0.7 constant_dynamic-slice_fusion.kappa_ref
  95.9 0.0 copy-start.1
  95.9 0.0 copy-start.4
  95.9 0.0 copy-start.5
  95.9 0.0 copy-start.6
  95.9 3.1 %shard_map.95.stepped_ref = f32[5,32,8,128]{3,2,1,0:T(8,128)S(1)} custom-call(f32[5,32,8,128]{3,2,1,0:T(8,128)S(1)} %get-tuple-element.20.own_ref, f32[5,36,16,128]{3,2,1,0:T(8,128)S(1)} %get-tuple-element.26.first_ref), custom_call_target="tpu_custom_call" | custom-call | tf_op jit(solution)/shard_map/pallas_call | solution.py:496
  99.0 5.0 %all-to-all-done.2 = f32[32,8,128]{2,1,0:T(8,128)S(1)} async-done(((f32[32,8,128]{2,1,0:T(8,128)}), f32[32,8,128]{2,1,0:T(8,128)S(1)}, u32[]{:S(2)}, u32[]{:S(2)}) %all-to-all-start.2) | async-done | bytes 131104 | tf_op jit(solution)/shard_map/all_to_all | solution.py:489
  104.0 0.0 copy-done.1
  104.0 0.0 copy-done.4
  104.0 0.0 copy-done.5
  104.0 2.4 %shard_map.96 = (f32[256,256]{1,0:T(8,128)S(1)}, f32[192,128]{1,0:T(8,128)}) custom-call(f32[256,128]{1,0:T(8,128)S(1)} %bitcast.20, f32[256,256]{1,0:T(8,128)S(1)} %copy-done.1, f32[8,256]{1,0:T(8,128)S(1)} %constant_dynamic-slice_fusion.kappa_ref, f32[8,256]{1,0:T(8,128)S(1)} %copy-done.4, f32[16,128]{1,0:T(8,128)S(1)} %copy-done.5), custom_call_target="tpu_custom_call" | custom-call | tf_op jit(solution)/shard_map/pallas_call | solution.py:498
  106.4 3.5 %all-to-all-start.3 = ((f32[8,24,128]{2,1,0:T(8,128)}), f32[8,24,128]{2,1,0:T(8,128)S(1)}, u32[]{:S(2)}, u32[]{:S(2)}) async-start(f32[8,24,128]{2,1,0:T(8,128)} %bitcast.9), calls=%async_computation.3 | async-start | bytes 196608 | tf_op jit(solution)/shard_map/all_to_all | solution.py:504
  110.0 0.1 pad_add_fusion.1.place_ref
  110.1 0.0 copy-done.6
  110.1 0.5 shard_map.97
  110.5 5.0 %all-to-all-done.3 = f32[8,24,128]{2,1,0:T(8,128)S(1)} async-done(((f32[8,24,128]{2,1,0:T(8,128)}), f32[8,24,128]{2,1,0:T(8,128)S(1)}, u32[]{:S(2)}, u32[]{:S(2)}) %all-to-all-start.3) | async-done | bytes 98336 | tf_op jit(solution)/shard_map/all_to_all | solution.py:504
  115.5 0.0 copy-start.3
  115.5 0.9 copy-done.3
  116.5 2.3 %shard_map.98 = f32[384,128]{1,0:T(8,128)S(1)} custom-call(s32[2]{0:T(128)S(1)} %pad_add_fusion.1.place_ref, f32[192,128]{1,0:T(8,128)S(1)} %bitcast.21, f32[256,256]{1,0:T(8,128)S(1)} %get-tuple-element.32.local_ref, f32[256,256]{1,0:T(8,128)S(1)} %get-tuple-element.33.left_ref, f32[256,256]{1,0:T(8,128)S(1)} %get-tuple-element.34.right_ref, ...), custom_call_target="tpu_custom_call" | custom-call | tf_op jit(solution)/shard_map/pallas_call | solution.py:507
  118.8 14.6 %all_to_all.30 = f32[32,1,1536]{2,1,0:T(1,128)S(1)} all-to-all(f32[32,1,1536]{2,1,0:T(1,128)S(1)} %bitcast.18), channel_id=1, replica_groups=mesh['row'=8,'col'=32] {'col'}, dimensions={0} | all-to-all | bytes 393216 | tf_op jit(solution)/shard_map/all_to_all | solution.py:518
  133.4 2.8 %shard_map.99 = f32[32,80,128]{2,1,0:T(8,128)} custom-call(s32[16]{0:T(128)S(1)} %broadcast_add_fusion.owner_ref, f32[5,32,8,128]{3,2,1,0:T(8,128)S(1)} %shard_map.95.stepped_ref, f32[384,128]{1,0:T(8,128)S(1)} %bitcast.19, f32[128,128]{1,0:T(8,128)S(1)} %copy-done.2), custom_call_target="tpu_custom_call" | custom-call | tf_op jit(solution)/shard_map/pallas_call | solution.py:521
  136.1 5.7 %all-to-all-start.5 = ((f32[32,80,128]{2,1,0:T(8,128)}), f32[32,80,128]{2,1,0:T(8,128)S(1)}, u32[]{:S(2)}, u32[]{:S(2)}) async-start(f32[32,80,128]{2,1,0:T(8,128)} %shard_map.99), calls=%async_computation.5 | async-start | bytes 2621440 | tf_op jit(solution)/shard_map/all_to_all | solution.py:527
  141.9 0.7 fusion.2
  144.7 0.1 pad_add_fusion.place_ref
  144.8 29.7 %all-to-all-done.5 = f32[32,80,128]{2,1,0:T(8,128)S(1)} async-done(((f32[32,80,128]{2,1,0:T(8,128)}), f32[32,80,128]{2,1,0:T(8,128)S(1)}, u32[]{:S(2)}, u32[]{:S(2)}) %all-to-all-start.5) | async-done | bytes 1310752 | tf_op jit(solution)/shard_map/all_to_all | solution.py:527
  174.5 2.4 %shard_map.100 = f32[5,16,4096]{2,1,0:T(8,128)} custom-call(s32[2]{0:T(128)S(1)} %pad_add_fusion.place_ref, f32[2560,128]{1,0:T(8,128)S(1)} %bitcast.16), custom_call_target="tpu_custom_call" | custom-call | tf_op jit(solution)/shard_map/pallas_call | solution.py:529
  (5 shorter events, 0.0 us)
Async XLA Ops:
  1.3 20.1 %all-to-all-start = ((f32[32,1,128]{2,1,0:T(1,128)}), f32[32,1,128]{2,1,0:T(1,128)S(1)}, u32[]{:S(2)}, u32[]{:S(2)}) async-start(f32[32,1,128]{2,1,0:T(1,128)} %broadcast_in_dim.29), calls=%async_computation | async-start | bytes 32768 | tf_op jit(solution)/shard_map/all_to_all | solution.py:434
  12.9 1.3 copy-start
  22.6 37.7 %all-to-all-start.1 = ((f32[32,80,128]{2,1,0:T(8,128)}), f32[32,80,128]{2,1,0:T(8,128)S(1)}, u32[]{:S(2)}, u32[]{:S(2)}) async-start(f32[32,80,128]{2,1,0:T(8,128)} %bitcast.5), calls=%async_computation.1 | async-start | bytes 2621440 | tf_op jit(solution)/shard_map/all_to_all | solution.py:456
  27.7 48.6 %copy-start.2 = (f32[128,128]{1,0:T(8,128)S(1)}, f32[128,128]{1,0:T(8,128)}, u32[]{:S(2)}) copy-start(f32[128,128]{1,0:T(8,128)} %constant.61.clone.table_ref) | copy-start | bytes 196612
  63.0 13.3 %collective-permute-start.2 = (f32[5,32,4,128]{3,2,1,0:T(4,128)S(1)}, f32[5,32,4,128]{3,2,1,0:T(4,128)S(1)}, u32[]{:S(2)}, u32[]{:S(2)}) collective-permute-start(f32[5,32,4,128]{3,2,1,0:T(4,128)S(1)} %get-tuple-element.23), channel_id=1, source_target_pairs={{0,1},{1,2},{2,3},{3,4},{4,5},{5,6},{6,7},{7,8},{8,9},{9,10},{10,1... | collective-permute-start | bytes 983048 | tf_op jit(solution)/shard_map/ppermute | solution.py:477
  64.5 11.8 %collective-permute-start.3 = (f32[5,32,4,128]{3,2,1,0:T(4,128)S(1)}, f32[5,32,4,128]{3,2,1,0:T(4,128)S(1)}, u32[]{:S(2)}, u32[]{:S(2)}) collective-permute-start(f32[5,32,4,128]{3,2,1,0:T(4,128)S(1)} %get-tuple-element.24), channel_id=1, source_target_pairs={{0,31},{1,0},{2,1},{3,2},{4,3},{5,4},{6,5},{7,6},{8,7},{9,8},{10,9... | collective-permute-start | bytes 983048 | tf_op jit(solution)/shard_map/ppermute | solution.py:478
  65.1 2.1 %collective-permute-start.1 = (f32[5,4,8,128]{3,2,1,0:T(8,128)S(1)}, f32[5,4,8,128]{3,2,1,0:T(8,128)S(1)}, u32[]{:S(2)}, u32[]{:S(2)}) collective-permute-start(f32[5,4,8,128]{3,2,1,0:T(8,128)S(1)} %get-tuple-element.22), channel_id=1, source_target_pairs={{0,224},{32,0},{64,32},{96,64},{128,96},{160,128},{192,160},{224,1... | collective-permute-start | bytes 245768 | tf_op jit(solution)/shard_map/ppermute | solution.py:476
  65.1 5.2 %collective-permute-start = (f32[5,4,8,128]{3,2,1,0:T(8,128)S(1)}, f32[5,4,8,128]{3,2,1,0:T(8,128)S(1)}, u32[]{:S(2)}, u32[]{:S(2)}) collective-permute-start(f32[5,4,8,128]{3,2,1,0:T(8,128)S(1)} %get-tuple-element.21), channel_id=1, source_target_pairs={{0,32},{32,64},{64,96},{96,128},{128,160},{160,192},{192,224},{224... | collective-permute-start | bytes 245768 | tf_op jit(solution)/shard_map/ppermute | solution.py:475
  70.3 5.9 %collective-permute-start.4 = (f32[5,4,4,128]{3,2,1,0:T(4,128)S(1)}, f32[5,4,4,128]{3,2,1,0:T(4,128)S(1)}, u32[]{:S(2)}, u32[]{:S(2)}) collective-permute-start(f32[5,4,4,128]{3,2,1,0:T(4,128)S(1)} %get-tuple-element.36), channel_id=1, source_target_pairs={{0,1},{1,2},{2,3},{3,4},{4,5},{5,6},{6,7},{7,8},{8,9},{9,10},{10,1... | collective-permute-start | bytes 122888 | tf_op jit(solution)/shard_map/ppermute | solution.py:480
  71.9 4.4 %collective-permute-start.5 = (f32[5,4,4,128]{3,2,1,0:T(4,128)S(1)}, f32[5,4,4,128]{3,2,1,0:T(4,128)S(1)}, u32[]{:S(2)}, u32[]{:S(2)}) collective-permute-start(f32[5,4,4,128]{3,2,1,0:T(4,128)S(1)} %get-tuple-element.35), channel_id=1, source_target_pairs={{0,31},{1,0},{2,1},{3,2},{4,3},{5,4},{6,5},{7,6},{8,7},{9,8},{10,9... | collective-permute-start | bytes 122888 | tf_op jit(solution)/shard_map/ppermute | solution.py:481
  83.1 21.0 %all-to-all-start.2 = ((f32[32,8,128]{2,1,0:T(8,128)}), f32[32,8,128]{2,1,0:T(8,128)S(1)}, u32[]{:S(2)}, u32[]{:S(2)}) async-start(f32[32,8,128]{2,1,0:T(8,128)} %bitcast.6), calls=%async_computation.2 | async-start | bytes 262144 | tf_op jit(solution)/shard_map/all_to_all | solution.py:489
  95.9 8.1 %copy-start.1 = (f32[256,256]{1,0:T(8,128)S(1)}, f32[256,256]{1,0:T(8,128)}, u32[]{:S(2)}) copy-start(f32[256,256]{1,0:T(8,128)} %constant.64.clone.table_ref) | copy-start | bytes 786436
  95.9 8.1 %copy-start.4 = (f32[8,256]{1,0:T(8,128)S(1)}, f32[8,256]{1,0:T(8,128)}, u32[]{:S(2)}) copy-start(f32[8,256]{1,0:T(8,128)} %constant.63.clone.expand_ref) | copy-start | bytes 24580
  95.9 8.1 %copy-start.5 = (f32[16,128]{1,0:T(8,128)S(1)}, f32[16,128]{1,0:T(8,128)}, u32[]{:S(2)}) copy-start(f32[16,128]{1,0:T(8,128)} %constant.65.clone.pick_ref) | copy-start | bytes 24580
  95.9 14.1 %copy-start.6 = (f32[1,256]{1,0:T(1,128)S(1)}, f32[1,256]{1,0:T(1,128)}, u32[]{:S(2)}) copy-start(f32[1,256]{1,0:T(1,128)} %constant.66.clone.span_ref) | copy-start | bytes 3076
  106.4 9.1 %all-to-all-start.3 = ((f32[8,24,128]{2,1,0:T(8,128)}), f32[8,24,128]{2,1,0:T(8,128)S(1)}, u32[]{:S(2)}, u32[]{:S(2)}) async-start(f32[8,24,128]{2,1,0:T(8,128)} %bitcast.9), calls=%async_computation.3 | async-start | bytes 196608 | tf_op jit(solution)/shard_map/all_to_all | solution.py:504
  115.5 1.0 copy-start.3
  136.1 38.3 %all-to-all-start.5 = ((f32[32,80,128]{2,1,0:T(8,128)}), f32[32,80,128]{2,1,0:T(8,128)S(1)}, u32[]{:S(2)}, u32[]{:S(2)}) async-start(f32[32,80,128]{2,1,0:T(8,128)} %shard_map.99), calls=%async_computation.5 | async-start | bytes 2621440 | tf_op jit(solution)/shard_map/all_to_all | solution.py:527

commit v11 on v10

--- a/solution.py
+++ b/solution.py
@@ -57,16 +57,6 @@
         picks[2 * k, k * BX + BX - 1] = 1.0
         picks[8 + 2 * k + 1, k * BX] = 1.0
     return picks
-
-
-def mean_line():
-    lanes = np.arange(256)
-    used = (lanes < BX) | (lanes == 128) | (lanes == 129)
-    gap = np.arange(GX)[:, None] // BX * BX + lane_spans()[None, :] - np.arange(GX)[:, None] % BX
-    gap = np.abs(gap)
-    shape = gap / 2.0 - gap * gap / (2.0 * GX)
-    shape = shape - shape[:, 0].mean()
-    return (four_pi_g * np.where(used[None, :], shape, 0.0)).astype(np.float32)
 
 
 def dot(left, right, dims=((1,), (0,))):
@@ -133,6 +123,12 @@
     xlast_ref[...] = block[:, BX - HALO :]
     yfirst_ref[...] = block[:, :, :HALO]
     ylast_ref[...] = block[:, :, BY - HALO :]
+
+
+def corner_kernel(ylow_ref, yhigh_ref, up_ref, down_ref):
+    for ref, first in ((up_ref, BX - 2), (down_ref, 0)):
+        ref[:, :, :HALO] = yhigh_ref[:, first : first + 2]
+        ref[:, :, HALO:] = ylow_ref[:, first : first + 2]
 
 
 def minmod(p, q):
@@ -222,12 +218,9 @@
     ext_ref[:, HALO + BX :, 0:BY] = xhigh_ref[...]
     ext_ref[:, inner, high] = yhigh_ref[...]
     ext_ref[:, inner, low] = ylow_ref[...]
-    for part, ref in ((low, clow_ref), (high, chigh_ref)):
-        corner = ref[...]
-        ext_ref[:, 0:2, part] = corner[:, 0:2]
-        ext_ref[:, 2:4, part] = corner[:, 0:2]
-        ext_ref[:, HALO + BX : HALO + BX + 2, part] = corner[:, 2:4]
-        ext_ref[:, HALO + BX + 2 :, part] = corner[:, 2:4]
+    for start, ref in ((0, clow_ref), (HALO + BX, chigh_ref)):
+        ext_ref[:, start : start + 2, BY:] = ref[...]
+        ext_ref[:, start + 2 : start + 4, BY:] = ref[...]
 
     def load_ext(i):
         return [ext_ref[q, i] for q in range(5)]
@@ -307,7 +300,7 @@
 
 
 def join_kernel(
-    place_ref, ends_ref, local_ref, left_ref, right_ref, kappa_ref, expand_ref, line_ref, table_ref,
+    place_ref, ends_ref, local_ref, left_ref, right_ref, kappa_ref, expand_ref, table_ref,
     out_ref, wide_ref,
 ):
     row = place_ref[0]
@@ -341,9 +334,18 @@
         halves.append(line)
     line = jnp.concatenate(halves, axis=1)
     line = line - jnp.sum(line, axis=1, keepdims=True) * (1.0 / GX)
-    mean = dot(line, line_ref[...])
-    first = lax.broadcasted_iota(jnp.int32, (8, 256), 0) == 0
+    source = lax.broadcasted_iota(jnp.int32, (GX, 128), 0)
+    target = lax.broadcasted_iota(jnp.int32, (GX, 128), 1)
+    target = jnp.where(target == BX + 1, -1, target)
+    gap = jnp.abs(source // BX * BX + target - source % BX).astype(jnp.float32)
+    shape = four_pi_g * (gap * (0.5 - gap * (0.5 / GX)) - (GX * GX - 1.0) / (12.0 * GX))
+    mean = dot(line, shape)
+    first = lax.broadcasted_iota(jnp.int32, (8, 128), 0) == 0
     mean = jnp.where(jnp.logical_and(first, place_ref[1] == 0), mean, 0.0)
+    inner = jnp.where(lane < BX, mean, 0.0)
+    low, high = pltpu.roll(mean, 128 - BX - 1, 1), pltpu.roll(mean, 128 - BX + 1, 1)
+    outer = jnp.where(lane == 0, low, jnp.where(lane == 1, high, 0.0))
+    mean = jnp.concatenate([inner, outer], axis=1)
     field = jnp.concatenate([field[0:8] + mean, field[8:]], axis=0)
     potential = dot(table_ref[...], field)
     for part in range(2):
@@ -408,12 +410,12 @@
 def spread_kernel(place_ref, recv_ref, out_ref):
     shift = place_ref[0]
     live = lax.broadcasted_iota(jnp.int32, (CAP, 128), 0) < place_ref[1]
-    for q in range(5):
-        for tile in range(2 * PE):
-            a, half = tile // 2, tile % 2
-            lines = recv_ref[pl.ds(half * BRICK + q * PE + a, CAP, stride=2 * BRICK), :]
-            turned = pltpu.roll(lines, shift, 0)
-            out_ref[q, :, tile * 128 : (tile + 1) * 128] = jnp.where(live, turned, 0.0)
+    field = pl.program_id(0) * PE
+    for tile in range(2 * PE):
+        a, half = tile // 2, tile % 2
+        lines = recv_ref[pl.ds(field + (half * BRICK + a), CAP, stride=2 * BRICK), :]
+        turned = pltpu.roll(lines, shift, 0)
+        out_ref[:, tile * 128 : (tile + 1) * 128] = jnp.where(live, turned, 0.0)
 
 
 def call(kernel, outs, ins, scratch=()):
@@ -476,9 +478,9 @@
     xhigh = lax.ppermute(xfirst, "row", ring(ROWS, -1))
     ylow = lax.ppermute(ylast, "col", ring(COLS, 1))
     yhigh = lax.ppermute(yfirst, "col", ring(COLS, -1))
-    edges = jnp.concatenate([xlow[:, 2:4], xhigh[:, 0:2]], axis=1)
-    clow = lax.ppermute(edges[:, :, BY - HALO :], "col", ring(COLS, 1))
-    chigh = lax.ppermute(edges[:, :, :HALO], "col", ring(COLS, -1))
+    up, down = call(corner_kernel, [(5, 2, BY, GZ)] * 2, (2, ()))(ylow, yhigh)
+    clow = lax.ppermute(up, "row", ring(ROWS, 1))
+    chigh = lax.ppermute(down, "row", ring(ROWS, -1))
 
     table_z = hartley(GZ)
     table_x = hartley(GX)
@@ -504,7 +506,7 @@
     ends = lax.all_to_all(
         ends.reshape(ROWS, 24, 128), "row", split_axis=0, concat_axis=0, tiled=True
     )
-    strips = call(join_kernel, [(COLS * 12, 128)], (9, (0,)), [(2 * (GY + 16), 128)])(
+    strips = call(join_kernel, [(COLS * 12, 128)], (8, (0,)), [(2 * (GY + 16), 128)])(
         jnp.stack([my_row, my_column]),
         ends.reshape(ROWS * 24, 128),
         local,
@@ -512,7 +514,6 @@
         right,
         kappa,
         expand,
-        jnp.asarray(mean_line()),
         jnp.asarray(table_x),
     )
     strips = lax.all_to_all(
@@ -526,9 +527,14 @@
     )(owners, stepped, strips.reshape(COLS * 12, 128), jnp.asarray(table_z))
     came_back = lax.all_to_all(returned, "col", split_axis=0, concat_axis=0, tiled=True)
     home = jnp.stack([(CAP - turn) % CAP, counts[0, 0]])
-    result = call(spread_kernel, [(5, CAP, PE * PE * PE)], (2, (0,)))(
-        home, came_back.reshape(COLS * BRICK, 128)
-    )
+    result = pl.pallas_call(
+        spread_kernel,
+        grid=(5,),
+        out_shape=jax.ShapeDtypeStruct((5, CAP, PE * PE * PE), jnp.float32),
+        in_specs=[SM, VM],
+        out_specs=pl.BlockSpec((None, CAP, PE * PE * PE), lambda q: (q, 0, 0)),
+        compiler_params=PARAMS,
+    )(home, came_back.reshape(COLS * BRICK, 128))
     return result.transpose(1, 0, 2)
 
 

time: 177 us -> 175 us (0.989)
    ppermute x1, waiting for transfers between devices: 3.19 us -> 0.01 us  [on_device(): xlow = lax.ppermute(xlast, 'row', ring(ROWS, 1))]
    ppermute x1, starting transfers between devices: 0.01 us -> 2.95 us  [on_device(): xhigh = lax.ppermute(xfirst, 'row', ring(ROWS, -1))]
    all_to_all x1, starting transfers between devices: 12.1 us -> 9.19 us  [on_device(): lax.all_to_all(modes.reshape(COLS, 8, 128), 'col', split_axis=0, concat_a...]
    ppermute x1, waiting for transfers between devices: 0.01 us -> 2.09 us  [on_device(): ylow = lax.ppermute(ylast, 'col', ring(COLS, 1))]
    pallas_call x2 -> x3, Pallas kernels: 4.67 us -> 5.5 us  [the longest x1 3.14 us: on_device(): pl.pallas_call(spread_kernel, grid=(5,), out_shape=jax.ShapeDtypeStruct((...]
where the time goes in v11:
time: 175 us
  waiting for transfers between devices  83.7 us (48%)
  starting transfers between devices  43.4 us (25%)
  Pallas kernels  25.9 us (15%)
  blocking collectives  14.9 us (9%)
  local copies, waits for them, and re-layouts  2.65 us (2%)
  between operations  2.48 us (1%)
    all_to_all x1, waiting for transfers between devices, on_device(): lax.all_to_all(sent.reshape(COLS, BRICK, 128), 'col', split_axis=0, conca...  31.6 us
    all_to_all x1, waiting for transfers between devices, on_device(): lax.all_to_all(returned, 'col', split_axis=0, concat_axis=0, tiled=True)  30.2 us
    all_to_all x1, blocking collectives, on_device(): lax.all_to_all(strips.reshape(COLS, 1, 1536), 'col', split_axis=0, concat...  14.9 us
    all_to_all x1, starting transfers between devices, gather_counts(): lax.all_to_all(copies, 'col', split_axis=0, concat_axis=0, tiled=True)  11.6 us
    all_to_all x1, starting transfers between devices, on_device(): lax.all_to_all(modes.reshape(COLS, 8, 128), 'col', split_axis=0, concat_a...  9.19 us
    pallas_call x1, Pallas kernels, on_device(): call(euler_kernel, [(5, BX + HALO, BY + 2 * HALO, GZ), (256, 128)], (8, (...  6.74 us
    all_to_all x1, waiting for transfers between devices, gather_counts(): lax.all_to_all(copies, 'col', split_axis=0, concat_axis=0, tiled=True)  6.03 us
    all_to_all x1, starting transfers between devices, on_device(): lax.all_to_all(returned, 'col', split_axis=0, concat_axis=0, tiled=True)  5.74 us
  transfers between devices with their start and end apart: 11, of which 8 were waited for; matrix products, arithmetic and copies ran while one was open for 1% of the time, Pallas kernels for 3%

profile of v11, /device:TPU:2, one launch (start us, length us, event | category | flops | bytes accessed | tf_op | source)
XLA Modules:
  0.0 174.8 jit_solution(7715418646605577972)
XLA Ops:
  0.7 0.6 broadcast_in_dim.29
  1.3 11.6 %all-to-all-start = ((f32[32,1,128]{2,1,0:T(1,128)}), f32[32,1,128]{2,1,0:T(1,128)S(1)}, u32[]{:S(2)}, u32[]{:S(2)}) async-start(f32[32,1,128]{2,1,0:T(1,128)} %broadcast_in_dim.29), calls=%async_computation | async-start | bytes 32768 | tf_op jit(solution)/shard_map/all_to_all | solution.py:436
  12.9 0.0 copy-start
  12.9 1.3 copy-done
  14.2 1.1 shard_map.82.staged_ref
  15.3 6.0 %all-to-all-done.counts_ref = f32[32,1,128]{2,1,0:T(1,128)S(1)} async-done(((f32[32,1,128]{2,1,0:T(1,128)}), f32[32,1,128]{2,1,0:T(1,128)S(1)}, u32[]{:S(2)}, u32[]{:S(2)}) %all-to-all-start) | async-done | bytes 16416 | tf_op jit(solution)/shard_map/all_to_all | solution.py:436
  21.3 1.3 shard_map.83
  22.6 5.1 %all-to-all-start.1 = ((f32[32,80,128]{2,1,0:T(8,128)}), f32[32,80,128]{2,1,0:T(8,128)S(1)}, u32[]{:S(2)}, u32[]{:S(2)}) async-start(f32[32,80,128]{2,1,0:T(8,128)} %bitcast.5), calls=%async_computation.1 | async-start | bytes 2621440 | tf_op jit(solution)/shard_map/all_to_all | solution.py:458
  27.7 0.0 copy-start.2
  27.7 0.7 fusion
  28.4 0.1 select_reduce_fusion
  28.5 0.2 convert_reduce_fusion
  28.7 31.6 %all-to-all-done.1.recv_ref = f32[32,80,128]{2,1,0:T(8,128)S(1)} async-done(((f32[32,80,128]{2,1,0:T(8,128)}), f32[32,80,128]{2,1,0:T(8,128)S(1)}, u32[]{:S(2)}, u32[]{:S(2)}) %all-to-all-start.1) | async-done | bytes 1310752 | tf_op jit(solution)/shard_map/all_to_all | solution.py:458
  60.3 2.7 %shard_map.84 = (f32[5,32,8,128]{3,2,1,0:T(8,128)S(1)}, f32[5,4,8,128]{3,2,1,0:T(8,128)S(1)}, f32[5,4,8,128]{3,2,1,0:T(8,128)S(1)}, f32[5,32,4,128]{3,2,1,0:T(4,128)S(1)}, f32[5,32,4,128]{3,2,1,0:T(4,128)S(1)}) custom-call(s32[16]{0:T(128)S(1)} %broadcast_add_fusion.owner_ref, f32[32,80,128]{2,1,0:T(8,128)S(1)} %all-to-all-done.1.recv_ref), custom_call_target="tpu_custom_call" | custom-call | tf_op jit(solution)/shard_map/pallas_call | solution.py:461
  63.0 1.5 collective-permute-start.2
  64.5 0.6 collective-permute-start.3
  65.1 0.0 collective-permute-start
  65.1 3.0 %collective-permute-start.1 = (f32[5,4,8,128]{3,2,1,0:T(8,128)S(1)}, f32[5,4,8,128]{3,2,1,0:T(8,128)S(1)}, u32[]{:S(2)}, u32[]{:S(2)}) collective-permute-start(f32[5,4,8,128]{3,2,1,0:T(8,128)S(1)} %get-tuple-element.24), channel_id=1, source_target_pairs={{0,224},{32,0},{64,32},{96,64},{128,96},{160,128},{192,160},{224,1... | collective-permute-start | bytes 245768 | tf_op jit(solution)/shard_map/ppermute | solution.py:478
  68.0 2.1 %collective-permute-done.2.ylow_ref = f32[5,32,4,128]{3,2,1,0:T(4,128)S(1)} collective-permute-done((f32[5,32,4,128]{3,2,1,0:T(4,128)S(1)}, f32[5,32,4,128]{3,2,1,0:T(4,128)S(1)}, u32[]{:S(2)}, u32[]{:S(2)}) %collective-permute-start.2) | collective-permute-done | bytes 327712 | tf_op jit(solution)/shard_map/ppermute | solution.py:479
  70.1 1.5 collective-permute-done.3.yhigh_ref
  71.6 0.0 collective-permute-start.4
  71.6 2.9 %collective-permute-start.5 = (f32[5,2,8,128]{3,2,1,0:T(8,128)S(1)}, f32[5,2,8,128]{3,2,1,0:T(8,128)S(1)}, u32[]{:S(2)}, u32[]{:S(2)}) collective-permute-start(f32[5,2,8,128]{3,2,1,0:T(8,128)S(1)} %get-tuple-element.28), channel_id=1, source_target_pairs={{0,224},{32,0},{64,32},{96,64},{128,96},{160,128},{192,160},{224,1... | collective-permute-start | bytes 122888 | tf_op jit(solution)/shard_map/ppermute | solution.py:483
  74.6 0.0 collective-permute-done.xlow_ref
  74.6 0.0 collective-permute-done.1.xhigh_ref
  74.6 1.7 collective-permute-done.4.clow_ref
  76.2 0.0 collective-permute-done.5.chigh_ref
  76.2 0.0 copy-done.2
  76.2 6.7 %shard_map.86 = (f32[5,36,16,128]{3,2,1,0:T(8,128)S(1)}, f32[256,128]{1,0:T(8,128)}) custom-call(f32[5,32,8,128]{3,2,1,0:T(8,128)S(1)} %get-tuple-element.22.own_ref, f32[5,4,8,128]{3,2,1,0:T(8,128)S(1)} %collective-permute-done.xlow_ref, f32[5,4,8,128]{3,2,1,0:T(8,128)S(1)} %collective-permute-done.1.xhigh_ref, ...), custom_call_target="tpu_custom_call" | custom-call | tf_op jit(solution)/shard_map/pallas_call | solution.py:488
  83.0 9.2 %all-to-all-start.2 = ((f32[32,8,128]{2,1,0:T(8,128)}), f32[32,8,128]{2,1,0:T(8,128)S(1)}, u32[]{:S(2)}, u32[]{:S(2)}) async-start(f32[32,8,128]{2,1,0:T(8,128)} %bitcast.6), calls=%async_computation.2 | async-start | bytes 262144 | tf_op jit(solution)/shard_map/all_to_all | solution.py:491
  92.2 0.7 constant_dynamic-slice_fusion.kappa_ref
  92.9 0.0 copy-start.1
  92.9 0.0 copy-start.3
  92.9 0.0 copy-start.4
  92.9 0.0 copy-start.5
  92.9 3.1 %shard_map.87.stepped_ref = f32[5,32,8,128]{3,2,1,0:T(8,128)S(1)} custom-call(f32[5,32,8,128]{3,2,1,0:T(8,128)S(1)} %get-tuple-element.22.own_ref, f32[5,36,16,128]{3,2,1,0:T(8,128)S(1)} %get-tuple-element.30.first_ref), custom_call_target="tpu_custom_call" | custom-call | tf_op jit(solution)/shard_map/pallas_call | solution.py:498
  96.0 5.4 %all-to-all-done.2 = f32[32,8,128]{2,1,0:T(8,128)S(1)} async-done(((f32[32,8,128]{2,1,0:T(8,128)}), f32[32,8,128]{2,1,0:T(8,128)S(1)}, u32[]{:S(2)}, u32[]{:S(2)}) %all-to-all-start.2) | async-done | bytes 131104 | tf_op jit(solution)/shard_map/all_to_all | solution.py:491
  101.3 0.0 copy-done.1
  101.3 0.0 copy-done.3
  101.3 0.0 copy-done.4
  101.4 2.4 %shard_map.88 = (f32[256,256]{1,0:T(8,128)S(1)}, f32[192,128]{1,0:T(8,128)}) custom-call(f32[256,128]{1,0:T(8,128)S(1)} %bitcast.20, f32[256,256]{1,0:T(8,128)S(1)} %copy-done.1, f32[8,256]{1,0:T(8,128)S(1)} %constant_dynamic-slice_fusion.kappa_ref, f32[8,256]{1,0:T(8,128)S(1)} %copy-done.3, f32[16,128]{1,0:T(8,128)S(1)} %copy-done.4), custom_call_target="tpu_custom_call" | custom-call | tf_op jit(solution)/shard_map/pallas_call | solution.py:500
  103.7 3.7 %all-to-all-start.3 = ((f32[8,24,128]{2,1,0:T(8,128)}), f32[8,24,128]{2,1,0:T(8,128)S(1)}, u32[]{:S(2)}, u32[]{:S(2)}) async-start(f32[8,24,128]{2,1,0:T(8,128)} %bitcast.9), calls=%async_computation.3 | async-start | bytes 196608 | tf_op jit(solution)/shard_map/all_to_all | solution.py:506
  107.5 0.1 pad_add_fusion.1.place_ref
  107.6 0.0 copy-done.5
  107.6 0.5 shard_map.89
  108.0 5.2 %all-to-all-done.3 = f32[8,24,128]{2,1,0:T(8,128)S(1)} async-done(((f32[8,24,128]{2,1,0:T(8,128)}), f32[8,24,128]{2,1,0:T(8,128)S(1)}, u32[]{:S(2)}, u32[]{:S(2)}) %all-to-all-start.3) | async-done | bytes 98336 | tf_op jit(solution)/shard_map/all_to_all | solution.py:506
  113.3 2.3 %shard_map.90 = f32[384,128]{1,0:T(8,128)S(1)} custom-call(s32[2]{0:T(128)S(1)} %pad_add_fusion.1.place_ref, f32[192,128]{1,0:T(8,128)S(1)} %bitcast.21, f32[256,256]{1,0:T(8,128)S(1)} %get-tuple-element.36.local_ref, f32[256,256]{1,0:T(8,128)S(1)} %get-tuple-element.37.left_ref, f32[256,256]{1,0:T(8,128)S(1)} %get-tuple-element.38.right_ref, ...), custom_call_target="tpu_custom_call" | custom-call | tf_op jit(solution)/shard_map/pallas_call | solution.py:509
  115.6 14.9 %all_to_all.30 = f32[32,1,1536]{2,1,0:T(1,128)S(1)} all-to-all(f32[32,1,1536]{2,1,0:T(1,128)S(1)} %bitcast.18), channel_id=1, replica_groups=mesh['row'=8,'col'=32] {'col'}, dimensions={0} | all-to-all | bytes 393216 | tf_op jit(solution)/shard_map/all_to_all | solution.py:519
  130.5 2.8 %shard_map.91 = f32[32,80,128]{2,1,0:T(8,128)} custom-call(s32[16]{0:T(128)S(1)} %broadcast_add_fusion.owner_ref, f32[5,32,8,128]{3,2,1,0:T(8,128)S(1)} %shard_map.87.stepped_ref, f32[384,128]{1,0:T(8,128)S(1)} %bitcast.19, f32[128,128]{1,0:T(8,128)S(1)} %copy-done.2), custom_call_target="tpu_custom_call" | custom-call | tf_op jit(solution)/shard_map/pallas_call | solution.py:522
  133.3 5.7 %all-to-all-start.5 = ((f32[32,80,128]{2,1,0:T(8,128)}), f32[32,80,128]{2,1,0:T(8,128)S(1)}, u32[]{:S(2)}, u32[]{:S(2)}) async-start(f32[32,80,128]{2,1,0:T(8,128)} %shard_map.91), calls=%async_computation.5 | async-start | bytes 2621440 | tf_op jit(solution)/shard_map/all_to_all | solution.py:528
  139.0 0.6 fusion.1
  141.3 0.1 pad_add_fusion.place_ref
  141.4 30.2 %all-to-all-done.5 = f32[32,80,128]{2,1,0:T(8,128)S(1)} async-done(((f32[32,80,128]{2,1,0:T(8,128)}), f32[32,80,128]{2,1,0:T(8,128)S(1)}, u32[]{:S(2)}, u32[]{:S(2)}) %all-to-all-start.5) | async-done | bytes 1310752 | tf_op jit(solution)/shard_map/all_to_all | solution.py:528
  171.6 3.1 %shard_map.92 = f32[5,16,4096]{2,1,0:T(8,128)} custom-call(s32[2]{0:T(128)S(1)} %pad_add_fusion.place_ref, f32[2560,128]{1,0:T(8,128)S(1)} %bitcast.16), custom_call_target="tpu_custom_call" | custom-call | tf_op jit(solution)/shard_map/pallas_call | solution.py:530
  (3 shorter events, 0.0 us)
Async XLA Ops:
  1.3 20.1 %all-to-all-start = ((f32[32,1,128]{2,1,0:T(1,128)}), f32[32,1,128]{2,1,0:T(1,128)S(1)}, u32[]{:S(2)}, u32[]{:S(2)}) async-start(f32[32,1,128]{2,1,0:T(1,128)} %broadcast_in_dim.29), calls=%async_computation | async-start | bytes 32768 | tf_op jit(solution)/shard_map/all_to_all | solution.py:436
  12.9 1.3 copy-start
  22.6 37.7 %all-to-all-start.1 = ((f32[32,80,128]{2,1,0:T(8,128)}), f32[32,80,128]{2,1,0:T(8,128)S(1)}, u32[]{:S(2)}, u32[]{:S(2)}) async-start(f32[32,80,128]{2,1,0:T(8,128)} %bitcast.5), calls=%async_computation.1 | async-start | bytes 2621440 | tf_op jit(solution)/shard_map/all_to_all | solution.py:458
  27.7 48.6 %copy-start.2 = (f32[128,128]{1,0:T(8,128)S(1)}, f32[128,128]{1,0:T(8,128)}, u32[]{:S(2)}) copy-start(f32[128,128]{1,0:T(8,128)} %constant.59.clone.table_ref) | copy-start | bytes 196612
  63.0 7.2 %collective-permute-start.2 = (f32[5,32,4,128]{3,2,1,0:T(4,128)S(1)}, f32[5,32,4,128]{3,2,1,0:T(4,128)S(1)}, u32[]{:S(2)}, u32[]{:S(2)}) collective-permute-start(f32[5,32,4,128]{3,2,1,0:T(4,128)S(1)} %get-tuple-element.25), channel_id=1, source_target_pairs={{0,1},{1,2},{2,3},{3,4},{4,5},{5,6},{6,7},{7,8},{8,9},{9,10},{10,1... | collective-permute-start | bytes 983048 | tf_op jit(solution)/shard_map/ppermute | solution.py:479
  64.5 7.1 %collective-permute-start.3 = (f32[5,32,4,128]{3,2,1,0:T(4,128)S(1)}, f32[5,32,4,128]{3,2,1,0:T(4,128)S(1)}, u32[]{:S(2)}, u32[]{:S(2)}) collective-permute-start(f32[5,32,4,128]{3,2,1,0:T(4,128)S(1)} %get-tuple-element.26), channel_id=1, source_target_pairs={{0,31},{1,0},{2,1},{3,2},{4,3},{5,4},{6,5},{7,6},{8,7},{9,8},{10,9... | collective-permute-start | bytes 983048 | tf_op jit(solution)/shard_map/ppermute | solution.py:480
  65.1 9.5 %collective-permute-start = (f32[5,4,8,128]{3,2,1,0:T(8,128)S(1)}, f32[5,4,8,128]{3,2,1,0:T(8,128)S(1)}, u32[]{:S(2)}, u32[]{:S(2)}) collective-permute-start(f32[5,4,8,128]{3,2,1,0:T(8,128)S(1)} %get-tuple-element.23), channel_id=1, source_target_pairs={{0,32},{32,64},{64,96},{96,128},{128,160},{160,192},{192,224},{224... | collective-permute-start | bytes 245768 | tf_op jit(solution)/shard_map/ppermute | solution.py:477
  65.1 9.5 %collective-permute-start.1 = (f32[5,4,8,128]{3,2,1,0:T(8,128)S(1)}, f32[5,4,8,128]{3,2,1,0:T(8,128)S(1)}, u32[]{:S(2)}, u32[]{:S(2)}) collective-permute-start(f32[5,4,8,128]{3,2,1,0:T(8,128)S(1)} %get-tuple-element.24), channel_id=1, source_target_pairs={{0,224},{32,0},{64,32},{96,64},{128,96},{160,128},{192,160},{224,1... | collective-permute-start | bytes 245768 | tf_op jit(solution)/shard_map/ppermute | solution.py:478
  71.6 4.7 %collective-permute-start.4 = (f32[5,2,8,128]{3,2,1,0:T(8,128)S(1)}, f32[5,2,8,128]{3,2,1,0:T(8,128)S(1)}, u32[]{:S(2)}, u32[]{:S(2)}) collective-permute-start(f32[5,2,8,128]{3,2,1,0:T(8,128)S(1)} %get-tuple-element.27), channel_id=1, source_target_pairs={{0,32},{32,64},{64,96},{96,128},{128,160},{160,192},{192,224},{224... | collective-permute-start | bytes 122888 | tf_op jit(solution)/shard_map/ppermute | solution.py:482
  71.6 4.6 %collective-permute-start.5 = (f32[5,2,8,128]{3,2,1,0:T(8,128)S(1)}, f32[5,2,8,128]{3,2,1,0:T(8,128)S(1)}, u32[]{:S(2)}, u32[]{:S(2)}) collective-permute-start(f32[5,2,8,128]{3,2,1,0:T(8,128)S(1)} %get-tuple-element.28), channel_id=1, source_target_pairs={{0,224},{32,0},{64,32},{96,64},{128,96},{160,128},{192,160},{224,1... | collective-permute-start | bytes 122888 | tf_op jit(solution)/shard_map/ppermute | solution.py:483
  83.0 18.4 %all-to-all-start.2 = ((f32[32,8,128]{2,1,0:T(8,128)}), f32[32,8,128]{2,1,0:T(8,128)S(1)}, u32[]{:S(2)}, u32[]{:S(2)}) async-start(f32[32,8,128]{2,1,0:T(8,128)} %bitcast.6), calls=%async_computation.2 | async-start | bytes 262144 | tf_op jit(solution)/shard_map/all_to_all | solution.py:491
  92.9 8.4 %copy-start.1 = (f32[256,256]{1,0:T(8,128)S(1)}, f32[256,256]{1,0:T(8,128)}, u32[]{:S(2)}) copy-start(f32[256,256]{1,0:T(8,128)} %constant.62.clone.table_ref) | copy-start | bytes 786436
  92.9 8.4 %copy-start.3 = (f32[8,256]{1,0:T(8,128)S(1)}, f32[8,256]{1,0:T(8,128)}, u32[]{:S(2)}) copy-start(f32[8,256]{1,0:T(8,128)} %constant.61.clone.expand_ref) | copy-start | bytes 24580
  92.9 8.4 %copy-start.4 = (f32[16,128]{1,0:T(8,128)S(1)}, f32[16,128]{1,0:T(8,128)}, u32[]{:S(2)}) copy-start(f32[16,128]{1,0:T(8,128)} %constant.63.clone.pick_ref) | copy-start | bytes 24580
  92.9 14.6 %copy-start.5 = (f32[1,256]{1,0:T(1,128)S(1)}, f32[1,256]{1,0:T(1,128)}, u32[]{:S(2)}) copy-start(f32[1,256]{1,0:T(1,128)} %constant.64.clone.span_ref) | copy-start | bytes 3076
  103.7 9.5 %all-to-all-start.3 = ((f32[8,24,128]{2,1,0:T(8,128)}), f32[8,24,128]{2,1,0:T(8,128)S(1)}, u32[]{:S(2)}, u32[]{:S(2)}) async-start(f32[8,24,128]{2,1,0:T(8,128)} %bitcast.9), calls=%async_computation.3 | async-start | bytes 196608 | tf_op jit(solution)/shard_map/all_to_all | solution.py:506
  133.3 38.3 %all-to-all-start.5 = ((f32[32,80,128]{2,1,0:T(8,128)}), f32[32,80,128]{2,1,0:T(8,128)S(1)}, u32[]{:S(2)}, u32[]{:S(2)}) async-start(f32[32,80,128]{2,1,0:T(8,128)} %shard_map.91), calls=%async_computation.5 | async-start | bytes 2621440 | tf_op jit(solution)/shard_map/all_to_all | solution.py:528

commit v12 on v11

--- a/solution.py
+++ b/solution.py
@@ -52,19 +52,19 @@
 
 
 def lane_picks():
-    picks = np.zeros((16, 128), np.float32)
+    picks = np.zeros((8, 256), np.float32)
     for k in range(4):
         picks[2 * k, k * BX + BX - 1] = 1.0
-        picks[8 + 2 * k + 1, k * BX] = 1.0
+        picks[2 * k + 1, 128 + k * BX] = 1.0
     return picks
 
 
-def dot(left, right, dims=((1,), (0,))):
+def dot(left, right, dims=((1,), (0,)), precision=lax.Precision.HIGHEST):
     return lax.dot_general(
         left,
         right,
         (dims, ((), ())),
-        precision=lax.Precision.HIGHEST,
+        precision=precision,
         preferred_element_type=jnp.float32,
     )
 
@@ -106,7 +106,7 @@
         out_ref[y * size : (y + 1) * size, :] = staged_ref[pl.ds(source, size), :]
 
 
-def unpack_kernel(owner_ref, recv_ref, own_ref, xfirst_ref, xlast_ref, yfirst_ref, ylast_ref, flat_ref):
+def unpack_kernel(owner_ref, recv_ref, own_ref, xfirst_ref, xlast_ref, yfirst_ref, ylast_ref):
     for q in range(5):
         for xl in range(2):
             for part in range(2):
@@ -116,9 +116,8 @@
                 ]
                 for b, value in enumerate(swap_groups(lines, PE)):
                     base = (q * BX + xl * PE + part * 8) * BY + b
-                    flat_ref[pl.ds(base, 8, stride=BY), :] = value
-    block = flat_ref[...].reshape(5, BX, BY, GZ)
-    own_ref[...] = block
+                    own_ref[pl.ds(base, 8, stride=BY), :] = value
+    block = own_ref[...].reshape(5, BX, BY, GZ)
     xfirst_ref[...] = block[:, :HALO]
     xlast_ref[...] = block[:, BX - HALO :]
     yfirst_ref[...] = block[:, :, :HALO]
@@ -275,7 +274,7 @@
         falling = falling + jnp.where(x < BX - step, power * pltpu.roll(falling, 128 - step, 1), 0.0)
         power = power * power
         step *= 2
-    ends = dot(pick_ref[0:8, :], rising, ((1,), (1,))) + dot(pick_ref[8:16, :], falling, ((1,), (1,)))
+    ends = dot(pick_ref[...], jnp.concatenate([rising, falling], axis=1), ((1,), (1,)))
     for r in range(ROWS):
         ends_ref[r * 24 : r * 24 + 8, :] = ends[:, :128]
         ends_ref[r * 24 + 8 : r * 24 + 16, :] = ends[:, 128:]
@@ -320,9 +319,15 @@
         high = jnp.concatenate([both[0][1], both[1][1]], axis=1)
         value = jnp.where(rising, low, high)
         total = value if total is None else value + block * total
-    from_left = dot(jnp.where(rising, total, 0.0), expand_ref[0:8, :] * 2.0, ((0,), (0,)))
-    from_right = dot(jnp.where(rising, 0.0, total), expand_ref[0:8, :] * 2.0, ((0,), (0,)))
-    field = local_ref[...] + left_ref[...] * from_left + right_ref[...] * from_right
+    end = lax.broadcasted_iota(jnp.int32, (8, 256), 0) % 2
+    side = lax.broadcasted_iota(jnp.int32, (8, 256), 1) // 128
+    spread = jnp.where(end == side, 2.0 * expand_ref[...], 0.0)
+    incoming = dot(total, spread, ((0,), (0,)))
+    halves = []
+    for lanes in (slice(0, 128), slice(128, 256)):
+        moved = left_ref[:, lanes] * incoming[:, :128] + right_ref[:, lanes] * incoming[:, 128:]
+        halves.append(local_ref[:, lanes] + moved)
+    field = jnp.concatenate(halves, axis=1)
     lane = lax.broadcasted_iota(jnp.int32, (8, 128), 1)
     halves = []
     for half in range(2):
@@ -347,7 +352,7 @@
     outer = jnp.where(lane == 0, low, jnp.where(lane == 1, high, 0.0))
     mean = jnp.concatenate([inner, outer], axis=1)
     field = jnp.concatenate([field[0:8] + mean, field[8:]], axis=0)
-    potential = dot(table_ref[...], field)
+    potential = dot(table_ref[...], field, precision=lax.Precision.HIGH)
     for part in range(2):
         base, side = part * (GY + 16), potential[:, part * 128 : part * 128 + 128]
         wide_ref[base + 8 : base + 8 + GY, :] = side
@@ -410,12 +415,12 @@
 def spread_kernel(place_ref, recv_ref, out_ref):
     shift = place_ref[0]
     live = lax.broadcasted_iota(jnp.int32, (CAP, 128), 0) < place_ref[1]
-    field = pl.program_id(0) * PE
-    for tile in range(2 * PE):
-        a, half = tile // 2, tile % 2
-        lines = recv_ref[pl.ds(field + (half * BRICK + a), CAP, stride=2 * BRICK), :]
-        turned = pltpu.roll(lines, shift, 0)
-        out_ref[:, tile * 128 : (tile + 1) * 128] = jnp.where(live, turned, 0.0)
+    for q in range(5):
+        for tile in range(2 * PE):
+            a, half = tile // 2, tile % 2
+            lines = recv_ref[pl.ds(half * BRICK + q * PE + a, CAP, stride=2 * BRICK), :]
+            turned = pltpu.roll(lines, shift, 0)
+            out_ref[q, :, tile * 128 : (tile + 1) * 128] = jnp.where(live, turned, 0.0)
 
 
 def call(kernel, outs, ins, scratch=()):
@@ -461,15 +466,15 @@
     own, xfirst, xlast, yfirst, ylast = call(
         unpack_kernel,
         [
-            (5, BX, BY, GZ),
+            (5 * BX * BY, GZ),
             (5, HALO, BY, GZ),
             (5, HALO, BY, GZ),
             (5, BX, HALO, GZ),
             (5, BX, HALO, GZ),
         ],
         (2, (0,)),
-        [(5 * BX * BY, GZ)],
     )(owners, arrived)
+    own = own.reshape(5, BX, BY, GZ)
 
     def ring(count, step):
         return [(i, (i + step) % count) for i in range(count)]
@@ -527,14 +532,9 @@
     )(owners, stepped, strips.reshape(COLS * 12, 128), jnp.asarray(table_z))
     came_back = lax.all_to_all(returned, "col", split_axis=0, concat_axis=0, tiled=True)
     home = jnp.stack([(CAP - turn) % CAP, counts[0, 0]])
-    result = pl.pallas_call(
-        spread_kernel,
-        grid=(5,),
-        out_shape=jax.ShapeDtypeStruct((5, CAP, PE * PE * PE), jnp.float32),
-        in_specs=[SM, VM],
-        out_specs=pl.BlockSpec((None, CAP, PE * PE * PE), lambda q: (q, 0, 0)),
-        compiler_params=PARAMS,
-    )(home, came_back.reshape(COLS * BRICK, 128))
+    result = call(spread_kernel, [(5, CAP, PE * PE * PE)], (2, (0,)))(
+        home, came_back.reshape(COLS * BRICK, 128)
+    )
     return result.transpose(1, 0, 2)
 
 

time: 175 us -> 174 us (level)
  no operation moved by 1% of the time
where the time goes in v12:
time: 174 us; the launch traced here: 173 us
  waiting for transfers between devices  83.7 us (48%)
  starting transfers between devices  43.4 us (25%)
  Pallas kernels  24.3 us (14%)
  blocking collectives  14.9 us (9%)
  local copies, waits for them, and re-layouts  2.65 us (2%)
  between operations  2.48 us (1%)
    all_to_all x1, waiting for transfers between devices, on_device(): lax.all_to_all(sent.reshape(COLS, BRICK, 128), 'col', split_axis=0, conca...  31.6 us
    all_to_all x1, waiting for transfers between devices, on_device(): lax.all_to_all(returned, 'col', split_axis=0, concat_axis=0, tiled=True)  30.2 us
    all_to_all x1, blocking collectives, on_device(): lax.all_to_all(strips.reshape(COLS, 1, 1536), 'col', split_axis=0, concat...  14.9 us
    all_to_all x1, starting transfers between devices, gather_counts(): lax.all_to_all(copies, 'col', split_axis=0, concat_axis=0, tiled=True)  11.6 us
    all_to_all x1, starting transfers between devices, on_device(): lax.all_to_all(modes.reshape(COLS, 8, 128), 'col', split_axis=0, concat_a...  9.19 us
    pallas_call x1, Pallas kernels, on_device(): call(euler_kernel, [(5, BX + HALO, BY + 2 * HALO, GZ), (256, 128)], (8, (...  6.74 us
    all_to_all x1, waiting for transfers between devices, gather_counts(): lax.all_to_all(copies, 'col', split_axis=0, concat_axis=0, tiled=True)  6.03 us
    all_to_all x1, starting transfers between devices, on_device(): lax.all_to_all(returned, 'col', split_axis=0, concat_axis=0, tiled=True)  5.74 us
  transfers between devices with their start and end apart: 11, of which 8 were waited for; matrix products, arithmetic and copies ran while one was open for 1% of the time, Pallas kernels for 3%

profile of v12, /device:TPU:2, one launch (start us, length us, event | category | flops | bytes accessed | tf_op | source)
XLA Modules:
  0.0 173.2 jit_solution(6938541786509628948)
XLA Ops:
  0.7 0.6 broadcast_in_dim.29
  1.3 11.6 %all-to-all-start = ((f32[32,1,128]{2,1,0:T(1,128)}), f32[32,1,128]{2,1,0:T(1,128)S(1)}, u32[]{:S(2)}, u32[]{:S(2)}) async-start(f32[32,1,128]{2,1,0:T(1,128)} %broadcast_in_dim.29), calls=%async_computation | async-start | bytes 32768 | tf_op jit(solution)/shard_map/all_to_all | solution.py:441
  12.9 0.0 copy-start
  12.9 1.3 copy-done
  14.2 1.1 shard_map.82.staged_ref
  15.3 6.0 %all-to-all-done.counts_ref = f32[32,1,128]{2,1,0:T(1,128)S(1)} async-done(((f32[32,1,128]{2,1,0:T(1,128)}), f32[32,1,128]{2,1,0:T(1,128)S(1)}, u32[]{:S(2)}, u32[]{:S(2)}) %all-to-all-start) | async-done | bytes 16416 | tf_op jit(solution)/shard_map/all_to_all | solution.py:441
  21.3 1.3 shard_map.83
  22.6 5.1 %all-to-all-start.1 = ((f32[32,80,128]{2,1,0:T(8,128)}), f32[32,80,128]{2,1,0:T(8,128)S(1)}, u32[]{:S(2)}, u32[]{:S(2)}) async-start(f32[32,80,128]{2,1,0:T(8,128)} %bitcast.5), calls=%async_computation.1 | async-start | bytes 2621440 | tf_op jit(solution)/shard_map/all_to_all | solution.py:463
  27.7 0.0 copy-start.2
  27.7 0.7 fusion
  28.4 0.1 select_reduce_fusion
  28.5 0.2 convert_reduce_fusion
  28.7 31.6 %all-to-all-done.1.recv_ref = f32[32,80,128]{2,1,0:T(8,128)S(1)} async-done(((f32[32,80,128]{2,1,0:T(8,128)}), f32[32,80,128]{2,1,0:T(8,128)S(1)}, u32[]{:S(2)}, u32[]{:S(2)}) %all-to-all-start.1) | async-done | bytes 1310752 | tf_op jit(solution)/shard_map/all_to_all | solution.py:463
  60.3 2.6 %shard_map.84 = (f32[1280,128]{1,0:T(8,128)S(1)}, f32[5,4,8,128]{3,2,1,0:T(8,128)S(1)}, f32[5,4,8,128]{3,2,1,0:T(8,128)S(1)}, f32[5,32,4,128]{3,2,1,0:T(4,128)S(1)}, f32[5,32,4,128]{3,2,1,0:T(4,128)S(1)}) custom-call(s32[16]{0:T(128)S(1)} %broadcast_add_fusion.owner_ref, f32[32,80,128]{2,1,0:T(8,128)S(1)} %all-to-all-done.1.recv_ref), custom_call_target="tpu_custom_call" | custom-call | tf_op jit(solution)/shard_map/pallas_call | solution.py:466
  62.9 1.5 collective-permute-start.2
  64.5 0.6 collective-permute-start.3
  65.0 0.0 collective-permute-start
  65.0 3.0 %collective-permute-start.1 = (f32[5,4,8,128]{3,2,1,0:T(8,128)S(1)}, f32[5,4,8,128]{3,2,1,0:T(8,128)S(1)}, u32[]{:S(2)}, u32[]{:S(2)}) collective-permute-start(f32[5,4,8,128]{3,2,1,0:T(8,128)S(1)} %get-tuple-element.24), channel_id=1, source_target_pairs={{0,224},{32,0},{64,32},{96,64},{128,96},{160,128},{192,160},{224,1... | collective-permute-start | bytes 245768 | tf_op jit(solution)/shard_map/ppermute | solution.py:483
  68.0 2.1 %collective-permute-done.2.ylow_ref = f32[5,32,4,128]{3,2,1,0:T(4,128)S(1)} collective-permute-done((f32[5,32,4,128]{3,2,1,0:T(4,128)S(1)}, f32[5,32,4,128]{3,2,1,0:T(4,128)S(1)}, u32[]{:S(2)}, u32[]{:S(2)}) %collective-permute-start.2) | collective-permute-done | bytes 327712 | tf_op jit(solution)/shard_map/ppermute | solution.py:484
  70.1 1.5 collective-permute-done.3.yhigh_ref
  71.6 0.0 collective-permute-start.4
  71.6 2.9 %collective-permute-start.5 = (f32[5,2,8,128]{3,2,1,0:T(8,128)S(1)}, f32[5,2,8,128]{3,2,1,0:T(8,128)S(1)}, u32[]{:S(2)}, u32[]{:S(2)}) collective-permute-start(f32[5,2,8,128]{3,2,1,0:T(8,128)S(1)} %get-tuple-element.28), channel_id=1, source_target_pairs={{0,224},{32,0},{64,32},{96,64},{128,96},{160,128},{192,160},{224,1... | collective-permute-start | bytes 122888 | tf_op jit(solution)/shard_map/ppermute | solution.py:488
  74.6 0.0 collective-permute-done.xlow_ref
  74.6 0.0 collective-permute-done.1.xhigh_ref
  74.6 1.7 collective-permute-done.4.clow_ref
  76.2 0.0 collective-permute-done.5.chigh_ref
  76.2 0.0 copy-done.2
  76.2 6.7 %shard_map.86 = (f32[5,36,16,128]{3,2,1,0:T(8,128)S(1)}, f32[256,128]{1,0:T(8,128)}) custom-call(f32[5,32,8,128]{3,2,1,0:T(8,128)S(1)} %bitcast.18, f32[5,4,8,128]{3,2,1,0:T(8,128)S(1)} %collective-permute-done.xlow_ref, f32[5,4,8,128]{3,2,1,0:T(8,128)S(1)} %collective-permute-done.1.xhigh_ref, f32[5,32,4,128]{3,2,1,0:T(4,128)S(1)} %collective-permute-done.2.ylow_ref, ...), custom_call_target="tpu_custom_call" | custom-call | tf_op jit(solution)/shard_map/pallas_call | solution.py:493
  83.0 9.2 %all-to-all-start.2 = ((f32[32,8,128]{2,1,0:T(8,128)}), f32[32,8,128]{2,1,0:T(8,128)S(1)}, u32[]{:S(2)}, u32[]{:S(2)}) async-start(f32[32,8,128]{2,1,0:T(8,128)} %bitcast.7), calls=%async_computation.2 | async-start | bytes 262144 | tf_op jit(solution)/shard_map/all_to_all | solution.py:496
  92.2 0.7 constant_dynamic-slice_fusion.kappa_ref
  92.9 0.0 copy-start.1
  92.9 0.0 copy-start.3
  92.9 0.0 copy-start.4
  92.9 0.0 copy-start.5
  92.9 3.1 %shard_map.87.stepped_ref = f32[5,32,8,128]{3,2,1,0:T(8,128)S(1)} custom-call(f32[5,32,8,128]{3,2,1,0:T(8,128)S(1)} %bitcast.19, f32[5,36,16,128]{3,2,1,0:T(8,128)S(1)} %get-tuple-element.30.first_ref), custom_call_target="tpu_custom_call" | custom-call | tf_op jit(solution)/shard_map/pallas_call | solution.py:503
  96.0 5.4 %all-to-all-done.2 = f32[32,8,128]{2,1,0:T(8,128)S(1)} async-done(((f32[32,8,128]{2,1,0:T(8,128)}), f32[32,8,128]{2,1,0:T(8,128)S(1)}, u32[]{:S(2)}, u32[]{:S(2)}) %all-to-all-start.2) | async-done | bytes 131104 | tf_op jit(solution)/shard_map/all_to_all | solution.py:496
  101.3 0.0 copy-done.1
  101.3 0.0 copy-done.3
  101.3 0.0 copy-done.4
  101.3 2.2 %shard_map.88 = (f32[256,256]{1,0:T(8,128)S(1)}, f32[192,128]{1,0:T(8,128)}) custom-call(f32[256,128]{1,0:T(8,128)S(1)} %bitcast.23, f32[256,256]{1,0:T(8,128)S(1)} %copy-done.1, f32[8,256]{1,0:T(8,128)S(1)} %constant_dynamic-slice_fusion.kappa_ref, f32[8,256]{1,0:T(8,128)S(1)} %copy-done.3, f32[8,256]{1,0:T(8,128)S(1)} %copy-done.4), custom_call_target="tpu_custom_call" | custom-call | tf_op jit(solution)/shard_map/pallas_call | solution.py:505
  103.5 3.7 %all-to-all-start.3 = ((f32[8,24,128]{2,1,0:T(8,128)}), f32[8,24,128]{2,1,0:T(8,128)S(1)}, u32[]{:S(2)}, u32[]{:S(2)}) async-start(f32[8,24,128]{2,1,0:T(8,128)} %bitcast.10), calls=%async_computation.3 | async-start | bytes 196608 | tf_op jit(solution)/shard_map/all_to_all | solution.py:511
  107.3 0.1 pad_add_fusion.1.place_ref
  107.3 0.0 copy-done.5
  107.3 0.5 shard_map.89
  107.8 5.2 %all-to-all-done.3 = f32[8,24,128]{2,1,0:T(8,128)S(1)} async-done(((f32[8,24,128]{2,1,0:T(8,128)}), f32[8,24,128]{2,1,0:T(8,128)S(1)}, u32[]{:S(2)}, u32[]{:S(2)}) %all-to-all-start.3) | async-done | bytes 98336 | tf_op jit(solution)/shard_map/all_to_all | solution.py:511
  113.1 1.7 shard_map.90
  114.8 14.9 %all_to_all.30 = f32[32,1,1536]{2,1,0:T(1,128)S(1)} all-to-all(f32[32,1,1536]{2,1,0:T(1,128)S(1)} %bitcast.21), channel_id=1, replica_groups=mesh['row'=8,'col'=32] {'col'}, dimensions={0} | all-to-all | bytes 393216 | tf_op jit(solution)/shard_map/all_to_all | solution.py:524
  129.7 2.8 %shard_map.91 = f32[32,80,128]{2,1,0:T(8,128)} custom-call(s32[16]{0:T(128)S(1)} %broadcast_add_fusion.owner_ref, f32[5,32,8,128]{3,2,1,0:T(8,128)S(1)} %shard_map.87.stepped_ref, f32[384,128]{1,0:T(8,128)S(1)} %bitcast.22, f32[128,128]{1,0:T(8,128)S(1)} %copy-done.2), custom_call_target="tpu_custom_call" | custom-call | tf_op jit(solution)/shard_map/pallas_call | solution.py:527
  132.5 5.7 %all-to-all-start.5 = ((f32[32,80,128]{2,1,0:T(8,128)}), f32[32,80,128]{2,1,0:T(8,128)S(1)}, u32[]{:S(2)}, u32[]{:S(2)}) async-start(f32[32,80,128]{2,1,0:T(8,128)} %shard_map.91), calls=%async_computation.5 | async-start | bytes 2621440 | tf_op jit(solution)/shard_map/all_to_all | solution.py:533
  138.2 0.6 fusion.1
  140.5 0.1 pad_add_fusion.place_ref
  140.6 30.2 %all-to-all-done.5 = f32[32,80,128]{2,1,0:T(8,128)S(1)} async-done(((f32[32,80,128]{2,1,0:T(8,128)}), f32[32,80,128]{2,1,0:T(8,128)S(1)}, u32[]{:S(2)}, u32[]{:S(2)}) %all-to-all-start.5) | async-done | bytes 1310752 | tf_op jit(solution)/shard_map/all_to_all | solution.py:533
  170.8 2.4 %shard_map.92 = f32[5,16,4096]{2,1,0:T(8,128)} custom-call(s32[2]{0:T(128)S(1)} %pad_add_fusion.place_ref, f32[2560,128]{1,0:T(8,128)S(1)} %bitcast.17), custom_call_target="tpu_custom_call" | custom-call | tf_op jit(solution)/shard_map/pallas_call | solution.py:535
  (3 shorter events, 0.0 us)
Async XLA Ops:
  1.3 20.1 %all-to-all-start = ((f32[32,1,128]{2,1,0:T(1,128)}), f32[32,1,128]{2,1,0:T(1,128)S(1)}, u32[]{:S(2)}, u32[]{:S(2)}) async-start(f32[32,1,128]{2,1,0:T(1,128)} %broadcast_in_dim.29), calls=%async_computation | async-start | bytes 32768 | tf_op jit(solution)/shard_map/all_to_all | solution.py:441
  12.9 1.3 copy-start
  22.6 37.7 %all-to-all-start.1 = ((f32[32,80,128]{2,1,0:T(8,128)}), f32[32,80,128]{2,1,0:T(8,128)S(1)}, u32[]{:S(2)}, u32[]{:S(2)}) async-start(f32[32,80,128]{2,1,0:T(8,128)} %bitcast.5), calls=%async_computation.1 | async-start | bytes 2621440 | tf_op jit(solution)/shard_map/all_to_all | solution.py:463
  27.7 48.6 %copy-start.2 = (f32[128,128]{1,0:T(8,128)S(1)}, f32[128,128]{1,0:T(8,128)}, u32[]{:S(2)}) copy-start(f32[128,128]{1,0:T(8,128)} %constant.59.clone.table_ref) | copy-start | bytes 196612
  62.9 7.2 %collective-permute-start.2 = (f32[5,32,4,128]{3,2,1,0:T(4,128)S(1)}, f32[5,32,4,128]{3,2,1,0:T(4,128)S(1)}, u32[]{:S(2)}, u32[]{:S(2)}) collective-permute-start(f32[5,32,4,128]{3,2,1,0:T(4,128)S(1)} %get-tuple-element.25), channel_id=1, source_target_pairs={{0,1},{1,2},{2,3},{3,4},{4,5},{5,6},{6,7},{7,8},{8,9},{9,10},{10,1... | collective-permute-start | bytes 983048 | tf_op jit(solution)/shard_map/ppermute | solution.py:484
  64.5 7.1 %collective-permute-start.3 = (f32[5,32,4,128]{3,2,1,0:T(4,128)S(1)}, f32[5,32,4,128]{3,2,1,0:T(4,128)S(1)}, u32[]{:S(2)}, u32[]{:S(2)}) collective-permute-start(f32[5,32,4,128]{3,2,1,0:T(4,128)S(1)} %get-tuple-element.26), channel_id=1, source_target_pairs={{0,31},{1,0},{2,1},{3,2},{4,3},{5,4},{6,5},{7,6},{8,7},{9,8},{10,9... | collective-permute-start | bytes 983048 | tf_op jit(solution)/shard_map/ppermute | solution.py:485
  65.0 9.5 %collective-permute-start = (f32[5,4,8,128]{3,2,1,0:T(8,128)S(1)}, f32[5,4,8,128]{3,2,1,0:T(8,128)S(1)}, u32[]{:S(2)}, u32[]{:S(2)}) collective-permute-start(f32[5,4,8,128]{3,2,1,0:T(8,128)S(1)} %get-tuple-element.23), channel_id=1, source_target_pairs={{0,32},{32,64},{64,96},{96,128},{128,160},{160,192},{192,224},{224... | collective-permute-start | bytes 245768 | tf_op jit(solution)/shard_map/ppermute | solution.py:482
  65.0 9.5 %collective-permute-start.1 = (f32[5,4,8,128]{3,2,1,0:T(8,128)S(1)}, f32[5,4,8,128]{3,2,1,0:T(8,128)S(1)}, u32[]{:S(2)}, u32[]{:S(2)}) collective-permute-start(f32[5,4,8,128]{3,2,1,0:T(8,128)S(1)} %get-tuple-element.24), channel_id=1, source_target_pairs={{0,224},{32,0},{64,32},{96,64},{128,96},{160,128},{192,160},{224,1... | collective-permute-start | bytes 245768 | tf_op jit(solution)/shard_map/ppermute | solution.py:483
  71.6 4.7 %collective-permute-start.4 = (f32[5,2,8,128]{3,2,1,0:T(8,128)S(1)}, f32[5,2,8,128]{3,2,1,0:T(8,128)S(1)}, u32[]{:S(2)}, u32[]{:S(2)}) collective-permute-start(f32[5,2,8,128]{3,2,1,0:T(8,128)S(1)} %get-tuple-element.27), channel_id=1, source_target_pairs={{0,32},{32,64},{64,96},{96,128},{128,160},{160,192},{192,224},{224... | collective-permute-start | bytes 122888 | tf_op jit(solution)/shard_map/ppermute | solution.py:487
  71.6 4.6 %collective-permute-start.5 = (f32[5,2,8,128]{3,2,1,0:T(8,128)S(1)}, f32[5,2,8,128]{3,2,1,0:T(8,128)S(1)}, u32[]{:S(2)}, u32[]{:S(2)}) collective-permute-start(f32[5,2,8,128]{3,2,1,0:T(8,128)S(1)} %get-tuple-element.28), channel_id=1, source_target_pairs={{0,224},{32,0},{64,32},{96,64},{128,96},{160,128},{192,160},{224,1... | collective-permute-start | bytes 122888 | tf_op jit(solution)/shard_map/ppermute | solution.py:488
  83.0 18.3 %all-to-all-start.2 = ((f32[32,8,128]{2,1,0:T(8,128)}), f32[32,8,128]{2,1,0:T(8,128)S(1)}, u32[]{:S(2)}, u32[]{:S(2)}) async-start(f32[32,8,128]{2,1,0:T(8,128)} %bitcast.7), calls=%async_computation.2 | async-start | bytes 262144 | tf_op jit(solution)/shard_map/all_to_all | solution.py:496
  92.9 8.4 %copy-start.1 = (f32[256,256]{1,0:T(8,128)S(1)}, f32[256,256]{1,0:T(8,128)}, u32[]{:S(2)}) copy-start(f32[256,256]{1,0:T(8,128)} %constant.62.clone.table_ref) | copy-start | bytes 786436
  92.9 8.4 %copy-start.3 = (f32[8,256]{1,0:T(8,128)S(1)}, f32[8,256]{1,0:T(8,128)}, u32[]{:S(2)}) copy-start(f32[8,256]{1,0:T(8,128)} %constant.61.clone.expand_ref) | copy-start | bytes 24580
  92.9 8.4 %copy-start.4 = (f32[8,256]{1,0:T(8,128)S(1)}, f32[8,256]{1,0:T(8,128)}, u32[]{:S(2)}) copy-start(f32[8,256]{1,0:T(8,128)} %constant.63.clone.pick_ref) | copy-start | bytes 24580
  92.9 14.5 %copy-start.5 = (f32[1,256]{1,0:T(1,128)S(1)}, f32[1,256]{1,0:T(1,128)}, u32[]{:S(2)}) copy-start(f32[1,256]{1,0:T(1,128)} %constant.64.clone.span_ref) | copy-start | bytes 3076
  103.5 9.5 %all-to-all-start.3 = ((f32[8,24,128]{2,1,0:T(8,128)}), f32[8,24,128]{2,1,0:T(8,128)S(1)}, u32[]{:S(2)}, u32[]{:S(2)}) async-start(f32[8,24,128]{2,1,0:T(8,128)} %bitcast.10), calls=%async_computation.3 | async-start | bytes 196608 | tf_op jit(solution)/shard_map/all_to_all | solution.py:511
  132.5 38.3 %all-to-all-start.5 = ((f32[32,80,128]{2,1,0:T(8,128)}), f32[32,80,128]{2,1,0:T(8,128)S(1)}, u32[]{:S(2)}, u32[]{:S(2)}) async-start(f32[32,80,128]{2,1,0:T(8,128)} %shard_map.91), calls=%async_computation.5 | async-start | bytes 2621440 | tf_op jit(solution)/shard_map/all_to_all | solution.py:533

commit v13 on v12

--- a/solution.py
+++ b/solution.py
@@ -19,6 +19,8 @@
 CAP = 16
 LINES = 16
 BRICK = 5 * PE
+EARLY = 8 + PE
+LATE = 4 * PE
 HALO = 4
 
 time_step = 0.03
@@ -207,8 +209,8 @@
 
 
 def euler_kernel(
-    own_ref, xlow_ref, xhigh_ref, ylow_ref, yhigh_ref, clow_ref, chigh_ref, table_ref,
-    first_ref, modes_ref, ext_ref, flat_ref,
+    owner_ref, own_ref, xlow_ref, xhigh_ref, ylow_ref, yhigh_ref, clow_ref, chigh_ref, table_ref,
+    own_first_ref, side_first_ref, modes_ref, ext_ref, first_ref, flat_ref,
 ):
     low, high = slice(BY + HALO, BY + 2 * HALO), slice(BY, BY + HALO)
     inner = slice(HALO, HALO + BX)
@@ -239,15 +241,32 @@
         flat_ref[pl.ds(row, BY), :] = 0.5 * ext_ref[0, i, 0:BY] + 0.5 * second
 
     euler_stage(load_mass, store_density, HALO, BX, BY, 32, mass_fields)
+    own_first_ref[...] = first_ref[:, :, 0:BY]
+    side_first_ref[:, :, 0:2] = first_ref[:, 2 : 2 + BX, BY : BY + 2]
+    side_first_ref[:, :, 2:4] = first_ref[:, 2 : 2 + BX, BY + 6 : BY + 8]
     density = jnp.concatenate(
         [flat_ref[pl.ds(b, BX, stride=BY), :] for b in range(BY)], axis=0
     )
     spread = dot(table_ref[...], density, ((1,), (1,)))
-    modes_ref[pl.ds(0, GZ, stride=2), :] = spread[:, :128]
-    modes_ref[pl.ds(1, GZ, stride=2), :] = spread[:, 128:]
-
-
-def second_kernel(own_ref, first_ref, stepped_ref):
+    for k in range(4):
+        for tile in range(2):
+            piece = spread[k * COLS : (k + 1) * COLS, tile * 128 : tile * 128 + 128]
+            modes_ref[pl.ds(k * 2 + tile, COLS, stride=EARLY), :] = piece
+    for xl in range(2):
+        for part in range(2):
+            base = (xl * PE + part * 8) * BY
+            lines = [flat_ref[pl.ds(base + b, 8, stride=BY), :] for b in range(BY)]
+            for zl, value in enumerate(swap_groups(lines, PE)):
+                row = owner_ref[xl * 8 + zl] * EARLY + 8 + part * 8
+                modes_ref[pl.ds(pl.multiple_of(row, 8), 8), :] = value
+
+
+def second_kernel(own_ref, own_first_ref, side_first_ref, stepped_ref, first_ref):
+    first_ref[:, :, 0:BY] = own_first_ref[...]
+    first_ref[:, :, BY:] = own_first_ref[...]
+    first_ref[:, 2 : 2 + BX, BY : BY + 2] = side_first_ref[:, :, 0:2]
+    first_ref[:, 2 : 2 + BX, BY + 6 : BY + 8] = side_first_ref[:, :, 2:4]
+
     def load_first(i):
         return [first_ref[q, i - 2] for q in range(5)]
 
@@ -261,7 +280,7 @@
 
 def ends_kernel(modes_ref, table_ref, kappa_ref, expand_ref, pick_ref, raw_ref, ends_ref, plane_ref):
     for tile in range(2):
-        lines = [modes_ref[pl.ds(k * 2 + tile, COLS, stride=8), :] for k in range(4)]
+        lines = [modes_ref[pl.ds(k * 2 + tile, COLS, stride=EARLY), :] for k in range(4)]
         for g, value in enumerate(swap_groups(lines, 32)):
             plane_ref[pl.ds(tile * 4 + g, COLS, stride=BY), :] = value
     power = jnp.exp(-dot(kappa_ref[...], expand_ref[:, :128], ((0,), (0,))))
@@ -397,12 +416,11 @@
     momenta = [stepped_ref[1 + d] for d in range(3)]
     work = momenta[0] * grad_x + momenta[1] * grad_y + momenta[2] * grad_z
     cells = BX * BY
-    kicked_ref[0:cells, :] = density.reshape(cells, GZ)
     for d in range(3):
         value = momenta[d] - time_step * density * grads[d]
-        kicked_ref[(1 + d) * cells : (2 + d) * cells, :] = value.reshape(cells, GZ)
-    kicked_ref[4 * cells :, :] = (stepped_ref[4] - time_step * work).reshape(cells, GZ)
-    for q in range(5):
+        kicked_ref[d * cells : (1 + d) * cells, :] = value.reshape(cells, GZ)
+    kicked_ref[3 * cells :, :] = (stepped_ref[4] - time_step * work).reshape(cells, GZ)
+    for q in range(4):
         for xl in range(2):
             for part in range(2):
                 base = (q * BX + xl * PE + part * 8) * BY
@@ -412,13 +430,16 @@
                     out_ref[owner_ref[xl * 8 + zl], rows : rows + 8, :] = value
 
 
-def spread_kernel(place_ref, recv_ref, out_ref):
+def spread_kernel(place_ref, early_ref, late_ref, out_ref):
     shift = place_ref[0]
     live = lax.broadcasted_iota(jnp.int32, (CAP, 128), 0) < place_ref[1]
     for q in range(5):
         for tile in range(2 * PE):
             a, half = tile // 2, tile % 2
-            lines = recv_ref[pl.ds(half * BRICK + q * PE + a, CAP, stride=2 * BRICK), :]
+            if q:
+                lines = late_ref[pl.ds(half * LATE + (q - 1) * PE + a, CAP, stride=2 * LATE), :]
+            else:
+                lines = early_ref[pl.ds(half * EARLY + 8 + a, CAP, stride=2 * EARLY), :]
             turned = pltpu.roll(lines, shift, 0)
             out_ref[q, :, tile * 128 : (tile + 1) * 128] = jnp.where(live, turned, 0.0)
 
@@ -488,22 +509,29 @@
     chigh = lax.ppermute(down, "row", ring(ROWS, -1))
 
     table_z = hartley(GZ)
+    order_z = np.arange(GZ).reshape(COLS, 4).T.reshape(GZ)
     table_x = hartley(GX)
     wide = (5, BX + 2 * HALO, BY + 2 * HALO, GZ)
-    first, modes = call(
-        euler_kernel, [(5, BX + HALO, BY + 2 * HALO, GZ), (256, 128)], (8, ()), [wide, (BX * BY, GZ)]
-    )(own, xlow, xhigh, ylow, yhigh, clow, chigh, jnp.asarray(table_z))
+    ring_shape = (5, BX + HALO, BY + 2 * HALO, GZ)
+    own_first, side_first, modes = call(
+        euler_kernel,
+        [(5, BX + HALO, BY, GZ), (5, BX, HALO, GZ), (COLS * EARLY, 128)],
+        (9, (0,)),
+        [wide, ring_shape, (BX * BY, GZ)],
+    )(owners, own, xlow, xhigh, ylow, yhigh, clow, chigh, jnp.asarray(table_z[order_z]))
     planes = lax.all_to_all(
-        modes.reshape(COLS, 8, 128), "col", split_axis=0, concat_axis=0, tiled=True
+        modes.reshape(COLS, EARLY, 128), "col", split_axis=0, concat_axis=0, tiled=True
     )
     kappa = jnp.asarray(np.repeat(kappas(), 2, axis=0).astype(np.float32))
     kappa = lax.dynamic_slice_in_dim(kappa, my_column * 8, 8, axis=0)
     expand = jnp.asarray(lane_expand())
     square = (GY, 256)
-    stepped = call(second_kernel, [(5, BX, BY, GZ)], (2, ()))(own, first)
+    stepped = call(second_kernel, [(5, BX, BY, GZ)], (3, ()), [ring_shape])(
+        own, own_first, side_first
+    )
     planes, stepped, kappa = lax.optimization_barrier((planes, stepped, kappa))
     raw, ends = call(ends_kernel, [square, (ROWS * 24, 128)], (5, ()), [(GY, 128)])(
-        planes.reshape(256, 128), jnp.asarray(table_x), kappa, expand, jnp.asarray(lane_picks())
+        planes.reshape(COLS * EARLY, 128), jnp.asarray(table_x), kappa, expand, jnp.asarray(lane_picks())
     )
     local, left, right = call(weigh_kernel, [square] * 3, (4, ()))(
         kappa, expand, jnp.asarray(lane_spans()[None, :]), raw
@@ -526,14 +554,14 @@
     )
     returned = call(
         kick_kernel,
-        [(COLS, BRICK, 128)],
+        [(COLS, LATE, 128)],
         (4, (0,)),
-        [((BX + 2) * BY, GZ), (5 * BX * BY, GZ)],
+        [((BX + 2) * BY, GZ), (4 * BX * BY, GZ)],
     )(owners, stepped, strips.reshape(COLS * 12, 128), jnp.asarray(table_z))
     came_back = lax.all_to_all(returned, "col", split_axis=0, concat_axis=0, tiled=True)
     home = jnp.stack([(CAP - turn) % CAP, counts[0, 0]])
-    result = call(spread_kernel, [(5, CAP, PE * PE * PE)], (2, (0,)))(
-        home, came_back.reshape(COLS * BRICK, 128)
+    result = call(spread_kernel, [(5, CAP, PE * PE * PE)], (3, (0,)))(
+        home, planes.reshape(COLS * EARLY, 128), came_back.reshape(COLS * LATE, 128)
     )
     return result.transpose(1, 0, 2)
 

time: 174 us -> 174 us (level)
    all_to_all x1, waiting for transfers between devices: 30.2 us -> 24.1 us  [on_device(): lax.all_to_all(returned, 'col', split_axis=0, concat_axis=0, tiled=True)]
    all_to_all x1, waiting for transfers between devices: 5.36 us -> 10.6 us  [on_device(): lax.all_to_all(modes.reshape(COLS, EARLY, 128), 'col', split_axis=0, conc...]
where the time goes in v13:
time: 174 us
  waiting for transfers between devices  82.9 us (48%)
  starting transfers between devices  43.4 us (25%)
  Pallas kernels  24.9 us (14%)
  blocking collectives  14.9 us (9%)
  between operations  2.93 us (2%)
  local copies, waits for them, and re-layouts  2.7 us (2%)
  other arithmetic  1.83 us (1%)
    all_to_all x1, waiting for transfers between devices, on_device(): lax.all_to_all(sent.reshape(COLS, BRICK, 128), 'col', split_axis=0, conca...  31.6 us
    all_to_all x1, waiting for transfers between devices, on_device(): lax.all_to_all(returned, 'col', split_axis=0, concat_axis=0, tiled=True)  24.1 us
    all_to_all x1, blocking collectives, on_device(): lax.all_to_all(strips.reshape(COLS, 1, 1536), 'col', split_axis=0, concat...  14.9 us
    all_to_all x1, starting transfers between devices, gather_counts(): lax.all_to_all(copies, 'col', split_axis=0, concat_axis=0, tiled=True)  11.6 us
    all_to_all x1, waiting for transfers between devices, on_device(): lax.all_to_all(modes.reshape(COLS, EARLY, 128), 'col', split_axis=0, conc...  10.6 us
    all_to_all x1, starting transfers between devices, on_device(): lax.all_to_all(modes.reshape(COLS, EARLY, 128), 'col', split_axis=0, conc...  9.19 us
    pallas_call x1, Pallas kernels, on_device(): call(euler_kernel, [(5, BX + HALO, BY, GZ), (5, BX, HALO, GZ), (COLS * EA...  7.5 us
    all_to_all x1, waiting for transfers between devices, gather_counts(): lax.all_to_all(copies, 'col', split_axis=0, concat_axis=0, tiled=True)  6.03 us
  transfers between devices with their start and end apart: 11, of which 8 were waited for; matrix products, arithmetic and copies ran while one was open for 1% of the time, Pallas kernels for 3%

profile of v13, /device:TPU:2, one launch (start us, length us, event | category | flops | bytes accessed | tf_op | source)
XLA Modules:
  0.0 173.5 jit_solution(4806020033224870313)
XLA Ops:
  0.7 0.6 broadcast_in_dim.29
  1.3 11.6 %all-to-all-start = ((f32[32,1,128]{2,1,0:T(1,128)}), f32[32,1,128]{2,1,0:T(1,128)S(1)}, u32[]{:S(2)}, u32[]{:S(2)}) async-start(f32[32,1,128]{2,1,0:T(1,128)} %broadcast_in_dim.29), calls=%async_computation | async-start | bytes 32768 | tf_op jit(solution)/shard_map/all_to_all | solution.py:462
  12.9 0.0 copy-start
  12.9 1.3 copy-done
  14.2 1.1 shard_map.91.staged_ref
  15.3 6.0 %all-to-all-done.counts_ref = f32[32,1,128]{2,1,0:T(1,128)S(1)} async-done(((f32[32,1,128]{2,1,0:T(1,128)}), f32[32,1,128]{2,1,0:T(1,128)S(1)}, u32[]{:S(2)}, u32[]{:S(2)}) %all-to-all-start) | async-done | bytes 16416 | tf_op jit(solution)/shard_map/all_to_all | solution.py:462
  21.3 1.3 shard_map.92
  22.6 5.1 %all-to-all-start.1 = ((f32[32,80,128]{2,1,0:T(8,128)}), f32[32,80,128]{2,1,0:T(8,128)S(1)}, u32[]{:S(2)}, u32[]{:S(2)}) async-start(f32[32,80,128]{2,1,0:T(8,128)} %bitcast.5), calls=%async_computation.1 | async-start | bytes 2621440 | tf_op jit(solution)/shard_map/all_to_all | solution.py:484
  27.7 0.0 copy-start.4
  27.7 0.7 fusion
  28.4 0.1 select_reduce_fusion
  28.5 0.2 convert_reduce_fusion
  28.7 31.6 %all-to-all-done.1.recv_ref = f32[32,80,128]{2,1,0:T(8,128)S(1)} async-done(((f32[32,80,128]{2,1,0:T(8,128)}), f32[32,80,128]{2,1,0:T(8,128)S(1)}, u32[]{:S(2)}, u32[]{:S(2)}) %all-to-all-start.1) | async-done | bytes 1310752 | tf_op jit(solution)/shard_map/all_to_all | solution.py:484
  60.3 2.6 %shard_map.93 = (f32[1280,128]{1,0:T(8,128)S(1)}, f32[5,4,8,128]{3,2,1,0:T(8,128)S(1)}, f32[5,4,8,128]{3,2,1,0:T(8,128)S(1)}, f32[5,32,4,128]{3,2,1,0:T(4,128)S(1)}, f32[5,32,4,128]{3,2,1,0:T(4,128)S(1)}) custom-call(s32[16]{0:T(128)S(1)} %broadcast_add_fusion.owner_ref, f32[32,80,128]{2,1,0:T(8,128)S(1)} %all-to-all-done.1.recv_ref), custom_call_target="tpu_custom_call" | custom-call | tf_op jit(solution)/shard_map/pallas_call | solution.py:487
  62.9 1.5 collective-permute-start.2
  64.5 0.6 collective-permute-start.3
  65.0 0.0 collective-permute-start
  65.0 3.0 %collective-permute-start.1 = (f32[5,4,8,128]{3,2,1,0:T(8,128)S(1)}, f32[5,4,8,128]{3,2,1,0:T(8,128)S(1)}, u32[]{:S(2)}, u32[]{:S(2)}) collective-permute-start(f32[5,4,8,128]{3,2,1,0:T(8,128)S(1)} %get-tuple-element.25), channel_id=1, source_target_pairs={{0,224},{32,0},{64,32},{96,64},{128,96},{160,128},{192,160},{224,1... | collective-permute-start | bytes 245768 | tf_op jit(solution)/shard_map/ppermute | solution.py:504
  68.0 2.1 %collective-permute-done.2.ylow_ref = f32[5,32,4,128]{3,2,1,0:T(4,128)S(1)} collective-permute-done((f32[5,32,4,128]{3,2,1,0:T(4,128)S(1)}, f32[5,32,4,128]{3,2,1,0:T(4,128)S(1)}, u32[]{:S(2)}, u32[]{:S(2)}) %collective-permute-start.2) | collective-permute-done | bytes 327712 | tf_op jit(solution)/shard_map/ppermute | solution.py:505
  70.1 1.5 collective-permute-done.3.yhigh_ref
  71.6 0.0 collective-permute-start.4
  71.6 2.9 %collective-permute-start.5 = (f32[5,2,8,128]{3,2,1,0:T(8,128)S(1)}, f32[5,2,8,128]{3,2,1,0:T(8,128)S(1)}, u32[]{:S(2)}, u32[]{:S(2)}) collective-permute-start(f32[5,2,8,128]{3,2,1,0:T(8,128)S(1)} %get-tuple-element.29), channel_id=1, source_target_pairs={{0,224},{32,0},{64,32},{96,64},{128,96},{160,128},{192,160},{224,1... | collective-permute-start | bytes 122888 | tf_op jit(solution)/shard_map/ppermute | solution.py:509
  74.6 0.0 collective-permute-done.xlow_ref
  74.6 0.0 collective-permute-done.1.xhigh_ref
  74.6 1.7 collective-permute-done.4.clow_ref
  76.2 0.0 collective-permute-done.5.chigh_ref
  76.2 0.0 copy-done.4
  76.2 7.5 %shard_map.95 = (f32[5,36,8,128]{3,2,1,0:T(8,128)S(1)}, f32[5,32,4,128]{3,2,1,0:T(4,128)S(1)}, f32[768,128]{1,0:T(8,128)}) custom-call(s32[16]{0:T(128)S(1)} %broadcast_add_fusion.owner_ref, f32[5,32,8,128]{3,2,1,0:T(8,128)S(1)} %bitcast.20, f32[5,4,8,128]{3,2,1,0:T(8,128)S(1)} %collective-permute-done.xlow_ref, ...), custom_call_target="tpu_custom_call" | custom-call | tf_op jit(solution)/shard_map/pallas_call | solution.py:516
  83.7 9.2 %all-to-all-start.2 = ((f32[32,24,128]{2,1,0:T(8,128)}), f32[32,24,128]{2,1,0:T(8,128)S(1)}, u32[]{:S(2)}, u32[]{:S(2)}) async-start(f32[32,24,128]{2,1,0:T(8,128)} %bitcast.7), calls=%async_computation.2 | async-start | bytes 786432 | tf_op jit(solution)/shard_map/all_to_all | solution.py:522
  92.9 0.0 copy-start.1
  93.0 0.0 copy-start.2
  93.0 0.0 copy-start.5
  93.0 0.7 constant_dynamic-slice_fusion.kappa_ref
  93.7 0.0 copy-start.6
  93.7 3.3 %shard_map.96.stepped_ref = f32[5,32,8,128]{3,2,1,0:T(8,128)S(1)} custom-call(f32[5,32,8,128]{3,2,1,0:T(8,128)S(1)} %bitcast.21, f32[5,36,8,128]{3,2,1,0:T(8,128)S(1)} %get-tuple-element.31.own_first_ref, f32[5,32,4,128]{3,2,1,0:T(4,128)S(1)} %get-tuple-element.32.side_first_ref), custom_call_target="tpu_custom_call" | custom-call | tf_op jit(solution)/shard_map/pallas_call | solution.py:529
  97.0 10.6 %all-to-all-done.2 = f32[32,24,128]{2,1,0:T(8,128)S(1)} async-done(((f32[32,24,128]{2,1,0:T(8,128)}), f32[32,24,128]{2,1,0:T(8,128)S(1)}, u32[]{:S(2)}, u32[]{:S(2)}) %all-to-all-start.2) | async-done | bytes 393248 | tf_op jit(solution)/shard_map/all_to_all | solution.py:522
  107.6 0.0 copy-done.1
  107.6 0.0 copy-done.2
  107.6 0.0 copy-done.5
  107.6 0.0 copy-start.3
  107.6 2.2 %shard_map.97 = (f32[256,256]{1,0:T(8,128)S(1)}, f32[192,128]{1,0:T(8,128)}) custom-call(f32[768,128]{1,0:T(8,128)S(1)} %bitcast.18, f32[256,256]{1,0:T(8,128)S(1)} %copy-done.1, f32[8,256]{1,0:T(8,128)S(1)} %constant_dynamic-slice_fusion.kappa_ref, f32[8,256]{1,0:T(8,128)S(1)} %copy-done.2, f32[8,256]{1,0:T(8,128)S(1)} %copy-done.5), custom_call_target="tpu_custom_call" | custom-call | tf_op jit(solution)/shard_map/pallas_call | solution.py:533
  109.8 3.8 %all-to-all-start.3 = ((f32[8,24,128]{2,1,0:T(8,128)}), f32[8,24,128]{2,1,0:T(8,128)S(1)}, u32[]{:S(2)}, u32[]{:S(2)}) async-start(f32[8,24,128]{2,1,0:T(8,128)} %bitcast.10), calls=%async_computation.3 | async-start | bytes 196608 | tf_op jit(solution)/shard_map/all_to_all | solution.py:539
  113.6 0.1 pad_add_fusion.1.place_ref
  113.7 0.0 copy-done.6
  113.7 0.5 shard_map.98
  114.1 5.2 %all-to-all-done.3 = f32[8,24,128]{2,1,0:T(8,128)S(1)} async-done(((f32[8,24,128]{2,1,0:T(8,128)}), f32[8,24,128]{2,1,0:T(8,128)S(1)}, u32[]{:S(2)}, u32[]{:S(2)}) %all-to-all-start.3) | async-done | bytes 98336 | tf_op jit(solution)/shard_map/all_to_all | solution.py:539
  119.4 1.7 shard_map.99
  121.1 14.9 %all_to_all.30 = f32[32,1,1536]{2,1,0:T(1,128)S(1)} all-to-all(f32[32,1,1536]{2,1,0:T(1,128)S(1)} %bitcast.23), channel_id=1, replica_groups=mesh['row'=8,'col'=32] {'col'}, dimensions={0} | all-to-all | bytes 393216 | tf_op jit(solution)/shard_map/all_to_all | solution.py:552
  136.0 0.0 copy-done.3
  136.0 2.5 %shard_map.100 = f32[32,64,128]{2,1,0:T(8,128)} custom-call(s32[16]{0:T(128)S(1)} %broadcast_add_fusion.owner_ref, f32[5,32,8,128]{3,2,1,0:T(8,128)S(1)} %shard_map.96.stepped_ref, f32[384,128]{1,0:T(8,128)S(1)} %bitcast.24, f32[128,128]{1,0:T(8,128)S(1)} %copy-done.3), custom_call_target="tpu_custom_call" | custom-call | tf_op jit(solution)/shard_map/pallas_call | solution.py:555
  138.5 5.7 %all-to-all-start.5 = ((f32[32,64,128]{2,1,0:T(8,128)}), f32[32,64,128]{2,1,0:T(8,128)S(1)}, u32[]{:S(2)}, u32[]{:S(2)}) async-start(f32[32,64,128]{2,1,0:T(8,128)} %shard_map.100), calls=%async_computation.5 | async-start | bytes 2097152 | tf_op jit(solution)/shard_map/all_to_all | solution.py:561
  144.2 0.7 fusion.1
  147.0 0.1 pad_add_fusion.place_ref
  147.1 24.1 %all-to-all-done.5 = f32[32,64,128]{2,1,0:T(8,128)S(1)} async-done(((f32[32,64,128]{2,1,0:T(8,128)}), f32[32,64,128]{2,1,0:T(8,128)S(1)}, u32[]{:S(2)}, u32[]{:S(2)}) %all-to-all-start.5) | async-done | bytes 1048608 | tf_op jit(solution)/shard_map/all_to_all | solution.py:561
  171.2 2.3 %shard_map.101 = f32[5,16,4096]{2,1,0:T(8,128)} custom-call(s32[2]{0:T(128)S(1)} %pad_add_fusion.place_ref, f32[768,128]{1,0:T(8,128)S(1)} %bitcast.19, f32[2048,128]{1,0:T(8,128)S(1)} %bitcast.17), custom_call_target="tpu_custom_call" | custom-call | tf_op jit(solution)/shard_map/pallas_call | solution.py:563
  (3 shorter events, 0.0 us)
Async XLA Ops:
  1.3 20.1 %all-to-all-start = ((f32[32,1,128]{2,1,0:T(1,128)}), f32[32,1,128]{2,1,0:T(1,128)S(1)}, u32[]{:S(2)}, u32[]{:S(2)}) async-start(f32[32,1,128]{2,1,0:T(1,128)} %broadcast_in_dim.29), calls=%async_computation | async-start | bytes 32768 | tf_op jit(solution)/shard_map/all_to_all | solution.py:462
  12.9 1.3 copy-start
  22.6 37.7 %all-to-all-start.1 = ((f32[32,80,128]{2,1,0:T(8,128)}), f32[32,80,128]{2,1,0:T(8,128)S(1)}, u32[]{:S(2)}, u32[]{:S(2)}) async-start(f32[32,80,128]{2,1,0:T(8,128)} %bitcast.5), calls=%async_computation.1 | async-start | bytes 2621440 | tf_op jit(solution)/shard_map/all_to_all | solution.py:484
  27.7 48.6 %copy-start.4 = (f32[128,128]{1,0:T(8,128)S(1)}, f32[128,128]{1,0:T(8,128)}, u32[]{:S(2)}) copy-start(f32[128,128]{1,0:T(8,128)} %constant.61.clone.table_ref) | copy-start | bytes 196612
  62.9 7.2 %collective-permute-start.2 = (f32[5,32,4,128]{3,2,1,0:T(4,128)S(1)}, f32[5,32,4,128]{3,2,1,0:T(4,128)S(1)}, u32[]{:S(2)}, u32[]{:S(2)}) collective-permute-start(f32[5,32,4,128]{3,2,1,0:T(4,128)S(1)} %get-tuple-element.26), channel_id=1, source_target_pairs={{0,1},{1,2},{2,3},{3,4},{4,5},{5,6},{6,7},{7,8},{8,9},{9,10},{10,1... | collective-permute-start | bytes 983048 | tf_op jit(solution)/shard_map/ppermute | solution.py:505
  64.5 7.1 %collective-permute-start.3 = (f32[5,32,4,128]{3,2,1,0:T(4,128)S(1)}, f32[5,32,4,128]{3,2,1,0:T(4,128)S(1)}, u32[]{:S(2)}, u32[]{:S(2)}) collective-permute-start(f32[5,32,4,128]{3,2,1,0:T(4,128)S(1)} %get-tuple-element.27), channel_id=1, source_target_pairs={{0,31},{1,0},{2,1},{3,2},{4,3},{5,4},{6,5},{7,6},{8,7},{9,8},{10,9... | collective-permute-start | bytes 983048 | tf_op jit(solution)/shard_map/ppermute | solution.py:506
  65.0 9.5 %collective-permute-start = (f32[5,4,8,128]{3,2,1,0:T(8,128)S(1)}, f32[5,4,8,128]{3,2,1,0:T(8,128)S(1)}, u32[]{:S(2)}, u32[]{:S(2)}) collective-permute-start(f32[5,4,8,128]{3,2,1,0:T(8,128)S(1)} %get-tuple-element.24), channel_id=1, source_target_pairs={{0,32},{32,64},{64,96},{96,128},{128,160},{160,192},{192,224},{224... | collective-permute-start | bytes 245768 | tf_op jit(solution)/shard_map/ppermute | solution.py:503
  65.0 9.5 %collective-permute-start.1 = (f32[5,4,8,128]{3,2,1,0:T(8,128)S(1)}, f32[5,4,8,128]{3,2,1,0:T(8,128)S(1)}, u32[]{:S(2)}, u32[]{:S(2)}) collective-permute-start(f32[5,4,8,128]{3,2,1,0:T(8,128)S(1)} %get-tuple-element.25), channel_id=1, source_target_pairs={{0,224},{32,0},{64,32},{96,64},{128,96},{160,128},{192,160},{224,1... | collective-permute-start | bytes 245768 | tf_op jit(solution)/shard_map/ppermute | solution.py:504
  71.6 4.7 %collective-permute-start.4 = (f32[5,2,8,128]{3,2,1,0:T(8,128)S(1)}, f32[5,2,8,128]{3,2,1,0:T(8,128)S(1)}, u32[]{:S(2)}, u32[]{:S(2)}) collective-permute-start(f32[5,2,8,128]{3,2,1,0:T(8,128)S(1)} %get-tuple-element.28), channel_id=1, source_target_pairs={{0,32},{32,64},{64,96},{96,128},{128,160},{160,192},{192,224},{224... | collective-permute-start | bytes 122888 | tf_op jit(solution)/shard_map/ppermute | solution.py:508
  71.6 4.6 %collective-permute-start.5 = (f32[5,2,8,128]{3,2,1,0:T(8,128)S(1)}, f32[5,2,8,128]{3,2,1,0:T(8,128)S(1)}, u32[]{:S(2)}, u32[]{:S(2)}) collective-permute-start(f32[5,2,8,128]{3,2,1,0:T(8,128)S(1)} %get-tuple-element.29), channel_id=1, source_target_pairs={{0,224},{32,0},{64,32},{96,64},{128,96},{160,128},{192,160},{224,1... | collective-permute-start | bytes 122888 | tf_op jit(solution)/shard_map/ppermute | solution.py:509
  83.7 23.9 %all-to-all-start.2 = ((f32[32,24,128]{2,1,0:T(8,128)}), f32[32,24,128]{2,1,0:T(8,128)S(1)}, u32[]{:S(2)}, u32[]{:S(2)}) async-start(f32[32,24,128]{2,1,0:T(8,128)} %bitcast.7), calls=%async_computation.2 | async-start | bytes 786432 | tf_op jit(solution)/shard_map/all_to_all | solution.py:522
  92.9 14.7 %copy-start.1 = (f32[256,256]{1,0:T(8,128)S(1)}, f32[256,256]{1,0:T(8,128)}, u32[]{:S(2)}) copy-start(f32[256,256]{1,0:T(8,128)} %constant.64.clone.table_ref) | copy-start | bytes 786436
  93.0 14.7 %copy-start.2 = (f32[8,256]{1,0:T(8,128)S(1)}, f32[8,256]{1,0:T(8,128)}, u32[]{:S(2)}) copy-start(f32[8,256]{1,0:T(8,128)} %constant.63.clone.expand_ref) | copy-start | bytes 24580
  93.0 14.6 %copy-start.5 = (f32[8,256]{1,0:T(8,128)S(1)}, f32[8,256]{1,0:T(8,128)}, u32[]{:S(2)}) copy-start(f32[8,256]{1,0:T(8,128)} %constant.65.clone.pick_ref) | copy-start | bytes 24580
  93.7 19.9 %copy-start.6 = (f32[1,256]{1,0:T(1,128)S(1)}, f32[1,256]{1,0:T(1,128)}, u32[]{:S(2)}) copy-start(f32[1,256]{1,0:T(1,128)} %constant.66.clone.span_ref) | copy-start | bytes 3076
  107.6 28.4 %copy-start.3 = (f32[128,128]{1,0:T(8,128)S(1)}, f32[128,128]{1,0:T(8,128)}, u32[]{:S(2)}) copy-start(f32[128,128]{1,0:T(8,128)} %constant.67.clone.table_ref) | copy-start | bytes 196612
  109.8 9.6 %all-to-all-start.3 = ((f32[8,24,128]{2,1,0:T(8,128)}), f32[8,24,128]{2,1,0:T(8,128)S(1)}, u32[]{:S(2)}, u32[]{:S(2)}) async-start(f32[8,24,128]{2,1,0:T(8,128)} %bitcast.10), calls=%async_computation.3 | async-start | bytes 196608 | tf_op jit(solution)/shard_map/all_to_all | solution.py:539
  138.5 32.7 %all-to-all-start.5 = ((f32[32,64,128]{2,1,0:T(8,128)}), f32[32,64,128]{2,1,0:T(8,128)S(1)}, u32[]{:S(2)}, u32[]{:S(2)}) async-start(f32[32,64,128]{2,1,0:T(8,128)} %shard_map.100), calls=%async_computation.5 | async-start | bytes 2097152 | tf_op jit(solution)/shard_map/all_to_all | solution.py:561

commit v14 on v12

--- a/solution.py
+++ b/solution.py
@@ -265,7 +265,12 @@
         for g, value in enumerate(swap_groups(lines, 32)):
             plane_ref[pl.ds(tile * 4 + g, COLS, stride=BY), :] = value
     power = jnp.exp(-dot(kappa_ref[...], expand_ref[:, :128], ((0,), (0,))))
-    source = dot(table_ref[...], plane_ref[...])
+    plane = plane_ref[...]
+    mean = jnp.sum(plane, axis=0, keepdims=True) * (1.0 / GY)
+    source = dot(table_ref[...], plane - mean, precision=lax.Precision.HIGH)
+    head = lax.broadcasted_iota(jnp.int32, (8, 128), 0) == 0
+    head = source[0:8] + jnp.where(head, math.sqrt(GY) * mean, 0.0)
+    source = jnp.concatenate([head, source[8:]], axis=0)
     x = lax.broadcasted_iota(jnp.int32, (GY, 128), 1) % BX
     rising, falling = source, source
     step = 1

time: 174 us -> 174 us (level)
  no operation moved by 1% of the time
where the time goes in v14:
time: 174 us; the launch traced here: 173 us
  waiting for transfers between devices  83.7 us (48%)
  starting transfers between devices  43.4 us (25%)
  Pallas kernels  24.1 us (14%)
  blocking collectives  14.9 us (9%)
  local copies, waits for them, and re-layouts  2.65 us (2%)
  between operations  2.48 us (1%)
    all_to_all x1, waiting for transfers between devices, on_device(): lax.all_to_all(sent.reshape(COLS, BRICK, 128), 'col', split_axis=0, conca...  31.6 us
    all_to_all x1, waiting for transfers between devices, on_device(): lax.all_to_all(returned, 'col', split_axis=0, concat_axis=0, tiled=True)  30.2 us
    all_to_all x1, blocking collectives, on_device(): lax.all_to_all(strips.reshape(COLS, 1, 1536), 'col', split_axis=0, concat...  14.9 us
    all_to_all x1, starting transfers between devices, gather_counts(): lax.all_to_all(copies, 'col', split_axis=0, concat_axis=0, tiled=True)  11.6 us
    all_to_all x1, starting transfers between devices, on_device(): lax.all_to_all(modes.reshape(COLS, 8, 128), 'col', split_axis=0, concat_a...  9.19 us
    pallas_call x1, Pallas kernels, on_device(): call(euler_kernel, [(5, BX + HALO, BY + 2 * HALO, GZ), (256, 128)], (8, (...  6.74 us
    all_to_all x1, waiting for transfers between devices, gather_counts(): lax.all_to_all(copies, 'col', split_axis=0, concat_axis=0, tiled=True)  6.03 us
    all_to_all x1, starting transfers between devices, on_device(): lax.all_to_all(returned, 'col', split_axis=0, concat_axis=0, tiled=True)  5.74 us
  transfers between devices with their start and end apart: 11, of which 8 were waited for; matrix products, arithmetic and copies ran while one was open for 1% of the time, Pallas kernels for 3%

profile of v14, /device:TPU:2, one launch (start us, length us, event | category | flops | bytes accessed | tf_op | source)
XLA Modules:
  0.0 173.0 jit_solution(7625176228766589300)
XLA Ops:
  0.7 0.6 broadcast_in_dim.29
  1.3 11.6 %all-to-all-start = ((f32[32,1,128]{2,1,0:T(1,128)}), f32[32,1,128]{2,1,0:T(1,128)S(1)}, u32[]{:S(2)}, u32[]{:S(2)}) async-start(f32[32,1,128]{2,1,0:T(1,128)} %broadcast_in_dim.29), calls=%async_computation | async-start | bytes 32768 | tf_op jit(solution)/shard_map/all_to_all | solution.py:446
  12.9 0.0 copy-start
  12.9 1.3 copy-done
  14.2 1.1 shard_map.82.staged_ref
  15.3 6.0 %all-to-all-done.counts_ref = f32[32,1,128]{2,1,0:T(1,128)S(1)} async-done(((f32[32,1,128]{2,1,0:T(1,128)}), f32[32,1,128]{2,1,0:T(1,128)S(1)}, u32[]{:S(2)}, u32[]{:S(2)}) %all-to-all-start) | async-done | bytes 16416 | tf_op jit(solution)/shard_map/all_to_all | solution.py:446
  21.3 1.3 shard_map.83
  22.6 5.1 %all-to-all-start.1 = ((f32[32,80,128]{2,1,0:T(8,128)}), f32[32,80,128]{2,1,0:T(8,128)S(1)}, u32[]{:S(2)}, u32[]{:S(2)}) async-start(f32[32,80,128]{2,1,0:T(8,128)} %bitcast.5), calls=%async_computation.1 | async-start | bytes 2621440 | tf_op jit(solution)/shard_map/all_to_all | solution.py:468
  27.7 0.0 copy-start.2
  27.7 0.7 fusion
  28.4 0.1 select_reduce_fusion
  28.5 0.2 convert_reduce_fusion
  28.7 31.6 %all-to-all-done.1.recv_ref = f32[32,80,128]{2,1,0:T(8,128)S(1)} async-done(((f32[32,80,128]{2,1,0:T(8,128)}), f32[32,80,128]{2,1,0:T(8,128)S(1)}, u32[]{:S(2)}, u32[]{:S(2)}) %all-to-all-start.1) | async-done | bytes 1310752 | tf_op jit(solution)/shard_map/all_to_all | solution.py:468
  60.3 2.6 %shard_map.84 = (f32[1280,128]{1,0:T(8,128)S(1)}, f32[5,4,8,128]{3,2,1,0:T(8,128)S(1)}, f32[5,4,8,128]{3,2,1,0:T(8,128)S(1)}, f32[5,32,4,128]{3,2,1,0:T(4,128)S(1)}, f32[5,32,4,128]{3,2,1,0:T(4,128)S(1)}) custom-call(s32[16]{0:T(128)S(1)} %broadcast_add_fusion.owner_ref, f32[32,80,128]{2,1,0:T(8,128)S(1)} %all-to-all-done.1.recv_ref), custom_call_target="tpu_custom_call" | custom-call | tf_op jit(solution)/shard_map/pallas_call | solution.py:471
  62.9 1.5 collective-permute-start.2
  64.5 0.6 collective-permute-start.3
  65.0 0.0 collective-permute-start
  65.0 3.0 %collective-permute-start.1 = (f32[5,4,8,128]{3,2,1,0:T(8,128)S(1)}, f32[5,4,8,128]{3,2,1,0:T(8,128)S(1)}, u32[]{:S(2)}, u32[]{:S(2)}) collective-permute-start(f32[5,4,8,128]{3,2,1,0:T(8,128)S(1)} %get-tuple-element.24), channel_id=1, source_target_pairs={{0,224},{32,0},{64,32},{96,64},{128,96},{160,128},{192,160},{224,1... | collective-permute-start | bytes 245768 | tf_op jit(solution)/shard_map/ppermute | solution.py:488
  68.0 2.1 %collective-permute-done.2.ylow_ref = f32[5,32,4,128]{3,2,1,0:T(4,128)S(1)} collective-permute-done((f32[5,32,4,128]{3,2,1,0:T(4,128)S(1)}, f32[5,32,4,128]{3,2,1,0:T(4,128)S(1)}, u32[]{:S(2)}, u32[]{:S(2)}) %collective-permute-start.2) | collective-permute-done | bytes 327712 | tf_op jit(solution)/shard_map/ppermute | solution.py:489
  70.1 1.5 collective-permute-done.3.yhigh_ref
  71.6 0.0 collective-permute-start.4
  71.6 2.9 %collective-permute-start.5 = (f32[5,2,8,128]{3,2,1,0:T(8,128)S(1)}, f32[5,2,8,128]{3,2,1,0:T(8,128)S(1)}, u32[]{:S(2)}, u32[]{:S(2)}) collective-permute-start(f32[5,2,8,128]{3,2,1,0:T(8,128)S(1)} %get-tuple-element.28), channel_id=1, source_target_pairs={{0,224},{32,0},{64,32},{96,64},{128,96},{160,128},{192,160},{224,1... | collective-permute-start | bytes 122888 | tf_op jit(solution)/shard_map/ppermute | solution.py:493
  74.6 0.0 collective-permute-done.xlow_ref
  74.6 0.0 collective-permute-done.1.xhigh_ref
  74.6 1.7 collective-permute-done.4.clow_ref
  76.2 0.0 collective-permute-done.5.chigh_ref
  76.2 0.0 copy-done.2
  76.2 6.7 %shard_map.86 = (f32[5,36,16,128]{3,2,1,0:T(8,128)S(1)}, f32[256,128]{1,0:T(8,128)}) custom-call(f32[5,32,8,128]{3,2,1,0:T(8,128)S(1)} %bitcast.18, f32[5,4,8,128]{3,2,1,0:T(8,128)S(1)} %collective-permute-done.xlow_ref, f32[5,4,8,128]{3,2,1,0:T(8,128)S(1)} %collective-permute-done.1.xhigh_ref, f32[5,32,4,128]{3,2,1,0:T(4,128)S(1)} %collective-permute-done.2.ylow_ref, ...), custom_call_target="tpu_custom_call" | custom-call | tf_op jit(solution)/shard_map/pallas_call | solution.py:498
  83.0 9.2 %all-to-all-start.2 = ((f32[32,8,128]{2,1,0:T(8,128)}), f32[32,8,128]{2,1,0:T(8,128)S(1)}, u32[]{:S(2)}, u32[]{:S(2)}) async-start(f32[32,8,128]{2,1,0:T(8,128)} %bitcast.7), calls=%async_computation.2 | async-start | bytes 262144 | tf_op jit(solution)/shard_map/all_to_all | solution.py:501
  92.2 0.7 constant_dynamic-slice_fusion.kappa_ref
  92.9 0.0 copy-start.1
  92.9 0.0 copy-start.3
  92.9 0.0 copy-start.4
  92.9 0.0 copy-start.5
  92.9 3.1 %shard_map.87.stepped_ref = f32[5,32,8,128]{3,2,1,0:T(8,128)S(1)} custom-call(f32[5,32,8,128]{3,2,1,0:T(8,128)S(1)} %bitcast.19, f32[5,36,16,128]{3,2,1,0:T(8,128)S(1)} %get-tuple-element.30.first_ref), custom_call_target="tpu_custom_call" | custom-call | tf_op jit(solution)/shard_map/pallas_call | solution.py:508
  96.0 5.4 %all-to-all-done.2 = f32[32,8,128]{2,1,0:T(8,128)S(1)} async-done(((f32[32,8,128]{2,1,0:T(8,128)}), f32[32,8,128]{2,1,0:T(8,128)S(1)}, u32[]{:S(2)}, u32[]{:S(2)}) %all-to-all-start.2) | async-done | bytes 131104 | tf_op jit(solution)/shard_map/all_to_all | solution.py:501
  101.3 0.0 copy-done.1
  101.3 0.0 copy-done.3
  101.3 0.0 copy-done.4
  101.3 2.0 %shard_map.88 = (f32[256,256]{1,0:T(8,128)S(1)}, f32[192,128]{1,0:T(8,128)}) custom-call(f32[256,128]{1,0:T(8,128)S(1)} %bitcast.23, f32[256,256]{1,0:T(8,128)S(1)} %copy-done.1, f32[8,256]{1,0:T(8,128)S(1)} %constant_dynamic-slice_fusion.kappa_ref, f32[8,256]{1,0:T(8,128)S(1)} %copy-done.3, f32[8,256]{1,0:T(8,128)S(1)} %copy-done.4), custom_call_target="tpu_custom_call" | custom-call | tf_op jit(solution)/shard_map/pallas_call | solution.py:510
  103.3 3.7 %all-to-all-start.3 = ((f32[8,24,128]{2,1,0:T(8,128)}), f32[8,24,128]{2,1,0:T(8,128)S(1)}, u32[]{:S(2)}, u32[]{:S(2)}) async-start(f32[8,24,128]{2,1,0:T(8,128)} %bitcast.10), calls=%async_computation.3 | async-start | bytes 196608 | tf_op jit(solution)/shard_map/all_to_all | solution.py:516
  107.1 0.1 pad_add_fusion.1.place_ref
  107.1 0.0 copy-done.5
  107.1 0.5 shard_map.89
  107.6 5.2 %all-to-all-done.3 = f32[8,24,128]{2,1,0:T(8,128)S(1)} async-done(((f32[8,24,128]{2,1,0:T(8,128)}), f32[8,24,128]{2,1,0:T(8,128)S(1)}, u32[]{:S(2)}, u32[]{:S(2)}) %all-to-all-start.3) | async-done | bytes 98336 | tf_op jit(solution)/shard_map/all_to_all | solution.py:516
  112.9 1.7 shard_map.90
  114.6 14.9 %all_to_all.30 = f32[32,1,1536]{2,1,0:T(1,128)S(1)} all-to-all(f32[32,1,1536]{2,1,0:T(1,128)S(1)} %bitcast.21), channel_id=1, replica_groups=mesh['row'=8,'col'=32] {'col'}, dimensions={0} | all-to-all | bytes 393216 | tf_op jit(solution)/shard_map/all_to_all | solution.py:529
  129.5 2.8 %shard_map.91 = f32[32,80,128]{2,1,0:T(8,128)} custom-call(s32[16]{0:T(128)S(1)} %broadcast_add_fusion.owner_ref, f32[5,32,8,128]{3,2,1,0:T(8,128)S(1)} %shard_map.87.stepped_ref, f32[384,128]{1,0:T(8,128)S(1)} %bitcast.22, f32[128,128]{1,0:T(8,128)S(1)} %copy-done.2), custom_call_target="tpu_custom_call" | custom-call | tf_op jit(solution)/shard_map/pallas_call | solution.py:532
  132.3 5.7 %all-to-all-start.5 = ((f32[32,80,128]{2,1,0:T(8,128)}), f32[32,80,128]{2,1,0:T(8,128)S(1)}, u32[]{:S(2)}, u32[]{:S(2)}) async-start(f32[32,80,128]{2,1,0:T(8,128)} %shard_map.91), calls=%async_computation.5 | async-start | bytes 2621440 | tf_op jit(solution)/shard_map/all_to_all | solution.py:538
  138.0 0.6 fusion.1
  140.3 0.1 pad_add_fusion.place_ref
  140.4 30.2 %all-to-all-done.5 = f32[32,80,128]{2,1,0:T(8,128)S(1)} async-done(((f32[32,80,128]{2,1,0:T(8,128)}), f32[32,80,128]{2,1,0:T(8,128)S(1)}, u32[]{:S(2)}, u32[]{:S(2)}) %all-to-all-start.5) | async-done | bytes 1310752 | tf_op jit(solution)/shard_map/all_to_all | solution.py:538
  170.6 2.4 %shard_map.92 = f32[5,16,4096]{2,1,0:T(8,128)} custom-call(s32[2]{0:T(128)S(1)} %pad_add_fusion.place_ref, f32[2560,128]{1,0:T(8,128)S(1)} %bitcast.17), custom_call_target="tpu_custom_call" | custom-call | tf_op jit(solution)/shard_map/pallas_call | solution.py:540
  (3 shorter events, 0.0 us)
Async XLA Ops:
  1.3 20.1 %all-to-all-start = ((f32[32,1,128]{2,1,0:T(1,128)}), f32[32,1,128]{2,1,0:T(1,128)S(1)}, u32[]{:S(2)}, u32[]{:S(2)}) async-start(f32[32,1,128]{2,1,0:T(1,128)} %broadcast_in_dim.29), calls=%async_computation | async-start | bytes 32768 | tf_op jit(solution)/shard_map/all_to_all | solution.py:446
  12.9 1.3 copy-start
  22.6 37.7 %all-to-all-start.1 = ((f32[32,80,128]{2,1,0:T(8,128)}), f32[32,80,128]{2,1,0:T(8,128)S(1)}, u32[]{:S(2)}, u32[]{:S(2)}) async-start(f32[32,80,128]{2,1,0:T(8,128)} %bitcast.5), calls=%async_computation.1 | async-start | bytes 2621440 | tf_op jit(solution)/shard_map/all_to_all | solution.py:468
  27.7 48.6 %copy-start.2 = (f32[128,128]{1,0:T(8,128)S(1)}, f32[128,128]{1,0:T(8,128)}, u32[]{:S(2)}) copy-start(f32[128,128]{1,0:T(8,128)} %constant.59.clone.table_ref) | copy-start | bytes 196612
  62.9 7.2 %collective-permute-start.2 = (f32[5,32,4,128]{3,2,1,0:T(4,128)S(1)}, f32[5,32,4,128]{3,2,1,0:T(4,128)S(1)}, u32[]{:S(2)}, u32[]{:S(2)}) collective-permute-start(f32[5,32,4,128]{3,2,1,0:T(4,128)S(1)} %get-tuple-element.25), channel_id=1, source_target_pairs={{0,1},{1,2},{2,3},{3,4},{4,5},{5,6},{6,7},{7,8},{8,9},{9,10},{10,1... | collective-permute-start | bytes 983048 | tf_op jit(solution)/shard_map/ppermute | solution.py:489
  64.5 7.1 %collective-permute-start.3 = (f32[5,32,4,128]{3,2,1,0:T(4,128)S(1)}, f32[5,32,4,128]{3,2,1,0:T(4,128)S(1)}, u32[]{:S(2)}, u32[]{:S(2)}) collective-permute-start(f32[5,32,4,128]{3,2,1,0:T(4,128)S(1)} %get-tuple-element.26), channel_id=1, source_target_pairs={{0,31},{1,0},{2,1},{3,2},{4,3},{5,4},{6,5},{7,6},{8,7},{9,8},{10,9... | collective-permute-start | bytes 983048 | tf_op jit(solution)/shard_map/ppermute | solution.py:490
  65.0 9.5 %collective-permute-start = (f32[5,4,8,128]{3,2,1,0:T(8,128)S(1)}, f32[5,4,8,128]{3,2,1,0:T(8,128)S(1)}, u32[]{:S(2)}, u32[]{:S(2)}) collective-permute-start(f32[5,4,8,128]{3,2,1,0:T(8,128)S(1)} %get-tuple-element.23), channel_id=1, source_target_pairs={{0,32},{32,64},{64,96},{96,128},{128,160},{160,192},{192,224},{224... | collective-permute-start | bytes 245768 | tf_op jit(solution)/shard_map/ppermute | solution.py:487
  65.0 9.5 %collective-permute-start.1 = (f32[5,4,8,128]{3,2,1,0:T(8,128)S(1)}, f32[5,4,8,128]{3,2,1,0:T(8,128)S(1)}, u32[]{:S(2)}, u32[]{:S(2)}) collective-permute-start(f32[5,4,8,128]{3,2,1,0:T(8,128)S(1)} %get-tuple-element.24), channel_id=1, source_target_pairs={{0,224},{32,0},{64,32},{96,64},{128,96},{160,128},{192,160},{224,1... | collective-permute-start | bytes 245768 | tf_op jit(solution)/shard_map/ppermute | solution.py:488
  71.6 4.7 %collective-permute-start.4 = (f32[5,2,8,128]{3,2,1,0:T(8,128)S(1)}, f32[5,2,8,128]{3,2,1,0:T(8,128)S(1)}, u32[]{:S(2)}, u32[]{:S(2)}) collective-permute-start(f32[5,2,8,128]{3,2,1,0:T(8,128)S(1)} %get-tuple-element.27), channel_id=1, source_target_pairs={{0,32},{32,64},{64,96},{96,128},{128,160},{160,192},{192,224},{224... | collective-permute-start | bytes 122888 | tf_op jit(solution)/shard_map/ppermute | solution.py:492
  71.6 4.6 %collective-permute-start.5 = (f32[5,2,8,128]{3,2,1,0:T(8,128)S(1)}, f32[5,2,8,128]{3,2,1,0:T(8,128)S(1)}, u32[]{:S(2)}, u32[]{:S(2)}) collective-permute-start(f32[5,2,8,128]{3,2,1,0:T(8,128)S(1)} %get-tuple-element.28), channel_id=1, source_target_pairs={{0,224},{32,0},{64,32},{96,64},{128,96},{160,128},{192,160},{224,1... | collective-permute-start | bytes 122888 | tf_op jit(solution)/shard_map/ppermute | solution.py:493
  83.0 18.4 %all-to-all-start.2 = ((f32[32,8,128]{2,1,0:T(8,128)}), f32[32,8,128]{2,1,0:T(8,128)S(1)}, u32[]{:S(2)}, u32[]{:S(2)}) async-start(f32[32,8,128]{2,1,0:T(8,128)} %bitcast.7), calls=%async_computation.2 | async-start | bytes 262144 | tf_op jit(solution)/shard_map/all_to_all | solution.py:501
  92.9 8.4 %copy-start.1 = (f32[256,256]{1,0:T(8,128)S(1)}, f32[256,256]{1,0:T(8,128)}, u32[]{:S(2)}) copy-start(f32[256,256]{1,0:T(8,128)} %constant.62.clone.table_ref) | copy-start | bytes 786436
  92.9 8.4 %copy-start.3 = (f32[8,256]{1,0:T(8,128)S(1)}, f32[8,256]{1,0:T(8,128)}, u32[]{:S(2)}) copy-start(f32[8,256]{1,0:T(8,128)} %constant.61.clone.expand_ref) | copy-start | bytes 24580
  92.9 8.4 %copy-start.4 = (f32[8,256]{1,0:T(8,128)S(1)}, f32[8,256]{1,0:T(8,128)}, u32[]{:S(2)}) copy-start(f32[8,256]{1,0:T(8,128)} %constant.63.clone.pick_ref) | copy-start | bytes 24580
  92.9 14.2 %copy-start.5 = (f32[1,256]{1,0:T(1,128)S(1)}, f32[1,256]{1,0:T(1,128)}, u32[]{:S(2)}) copy-start(f32[1,256]{1,0:T(1,128)} %constant.64.clone.span_ref) | copy-start | bytes 3076
  103.3 9.5 %all-to-all-start.3 = ((f32[8,24,128]{2,1,0:T(8,128)}), f32[8,24,128]{2,1,0:T(8,128)S(1)}, u32[]{:S(2)}, u32[]{:S(2)}) async-start(f32[8,24,128]{2,1,0:T(8,128)} %bitcast.10), calls=%async_computation.3 | async-start | bytes 196608 | tf_op jit(solution)/shard_map/all_to_all | solution.py:516
  132.3 38.3 %all-to-all-start.5 = ((f32[32,80,128]{2,1,0:T(8,128)}), f32[32,80,128]{2,1,0:T(8,128)S(1)}, u32[]{:S(2)}, u32[]{:S(2)}) async-start(f32[32,80,128]{2,1,0:T(8,128)} %shard_map.91), calls=%async_computation.5 | async-start | bytes 2621440 | tf_op jit(solution)/shard_map/all_to_all | solution.py:538
